TPU v7x, 128 devices: a whole 4x4x4 slice. The times are simulated.
128 devices in a mesh: gx: 16 (over z_hi, x, core), gy: 4 (over y), gz: 2 (over z_lo).
Axes of the slice: x: 4, y: 4, z: 4 (z_hi: 2, z_lo: 2; z = z_hi * 2 + z_lo), core: 2. Of those that a mesh axis runs over, the one named last changes fastest.
Arguments:
- cells: bfloat16 [4, 64, 256, 256], P(None, 'gx', 'gy', 'gz'), may hold values from -6 to 6
- weight: bfloat16 [32, 4, 3, 3, 3], replicated, may hold values from -0.625 to 0.625
- bias: float32 [32], replicated, may hold values from -3 to 3
- cotangent: bfloat16 [32, 32, 128, 128], P(None, 'gx', 'gy', 'gz'), may hold values from -6 to 6
Outputs:
- pooled: bfloat16 [32, 32, 128, 128], P(None, 'gx', 'gy', 'gz')
- weight_grad: float32 [32, 4, 3, 3, 3], replicated
- bias_grad: float32 [32], replicated
- input_grad: float32 [4, 64, 256, 256], P(None, 'gx', 'gy', 'gz')
All inputs are finite; a program needn't handle non-finite values.
Results may differ from a plain program's by a relative error of at most 0.0029.
Values may be sent and summed in bfloat16 or wider, within the bound.
A program may use at most 128 MiB of HBM per device.

v0:
```python
import jax
import jax.numpy as jnp
from jax import lax
from jax.sharding import PartitionSpec as P

leak_slope = 0.3
soft_scale = 10.0


def extended(cells, sides, width):
    for axis, dim in sides:
        count = lax.axis_size(axis)
        head = lax.slice_in_dim(cells, 0, width, axis=dim)
        tail = lax.slice_in_dim(cells, cells.shape[dim] - width, cells.shape[dim], axis=dim)
        cells = jnp.concatenate(
            [
                lax.ppermute(tail, axis, [(i, (i + 1) % count) for i in range(count)]),
                cells,
                lax.ppermute(head, axis, [((i + 1) % count, i) for i in range(count)]),
            ],
            axis=dim,
        )
    return cells


def activate(preact):
    return leak_slope * preact + (1.0 - leak_slope) / soft_scale * jax.nn.softplus(
        soft_scale * preact
    )


def slope_of(preact):
    return leak_slope + (1.0 - leak_slope) * jax.nn.sigmoid(soft_scale * preact)


def on_device(cells, weight, bias, cotangent):
    chan_in, cells_x, cells_y, cells_z = cells.shape
    chan_out = weight.shape[0]
    stencil = [
        (shift_a, shift_b, shift_e)
        for shift_a in range(3)
        for shift_b in range(3)
        for shift_e in range(3)
    ]
    widened = extended(cells, (("gx", 1), ("gy", 2), ("gz", 3)), 1)
    patches = jnp.stack(
        [
            widened[:, sa : sa + cells_x, sb : sb + cells_y, se : se + cells_z]
            for sa, sb, se in stencil
        ],
        axis=1,
    )
    patches = patches.reshape(chan_in * 27, cells_x, cells_y, cells_z)
    weight_mat = weight.reshape(chan_out, chan_in * 27)
    preact = (
        jnp.einsum("ok,kxyz->oxyz", weight_mat, patches, preferred_element_type=jnp.float32)
        + bias[:, None, None, None]
    )
    activated = activate(preact)
    pooled = (
        activated.reshape(chan_out, cells_x // 2, 2, cells_y // 2, 2, cells_z // 2, 2)
        .mean(axis=(2, 4, 6))
        .astype(jnp.bfloat16)
    )
    spread = jnp.broadcast_to(
        cotangent.astype(jnp.float32)[:, :, None, :, None, :, None],
        (chan_out, cells_x // 2, 2, cells_y // 2, 2, cells_z // 2, 2),
    )
    spread = spread.reshape(chan_out, cells_x, cells_y, cells_z)
    delta = (slope_of(preact) * spread * 0.125).astype(jnp.bfloat16)
    weight_local = jnp.einsum("oxyz,kxyz->ok", delta, patches, preferred_element_type=jnp.float32)
    bias_local = jnp.sum(delta, axis=(1, 2, 3), dtype=jnp.float32)
    weight_total, bias_grad = lax.psum((weight_local, bias_local), ("gx", "gy", "gz"))
    weight_grad = weight_total.reshape(chan_out, chan_in, 3, 3, 3)
    delta_wide = extended(delta, (("gx", 1), ("gy", 2), ("gz", 3)), 1)
    input_grad = jnp.zeros((chan_in, cells_x, cells_y, cells_z), jnp.float32)
    for sa, sb, se in stencil:
        window = delta_wide[:, sa : sa + cells_x, sb : sb + cells_y, se : se + cells_z]
        input_grad = input_grad + jnp.einsum(
            "oc,oxyz->cxyz",
            weight[:, :, 2 - sa, 2 - sb, 2 - se],
            window,
            preferred_element_type=jnp.float32,
        )
    return (pooled, weight_grad, bias_grad, input_grad)


def solution(mesh):
    in_specs = (P(None, "gx", "gy", "gz"), P(), P(), P(None, "gx", "gy", "gz"))
    out_specs = (P(None, "gx", "gy", "gz"), P(), P(), P(None, "gx", "gy", "gz"))
    return jax.shard_map(
        on_device, mesh=mesh, in_specs=in_specs, out_specs=out_specs, check_vma=False
    )
```

profile of v0, /device:TPU:0, one launch (start us, length us, event | category | flops | bytes accessed | tf_op | source)
XLA Modules:
  0.0 232.9 jit_solution(10944951480757157942)
XLA Ops:
  1.6 5.7 %collective-permute-start.1 = (bf16[4,1,64,128]{3,2,1,0:T(8,128)(2,1)S(1)}, bf16[4,1,64,128]{3,2,1,0:T(8,128)(2,1)S(1)}, u32[]{:S(2)}, u32[]{:S(2)}) collective-permute-start(bf16[4,1,64,128]{3,2,1,0:T(8,128)(2,1)S(1)} %get-tuple-element.35), channel_id=1, source_target_pairs={{8,0},{16,8},{24,16},{32,24},{40,32},{48,40},{56,48},{64,56},{72,6... | collective-permute-start | bytes 196616 | tf_op jit(solution)/shard_map/ppermute | solution.py:19
  7.3 1.9 collective-permute-done
  10.2 3.1 %collective-permute-start.3 = (bf16[4,6,1,128]{3,2,1,0:T(2,128)(2,1)S(1)}, bf16[4,6,1,128]{3,2,1,0:T(2,128)(2,1)S(1)}, u32[]{:S(2)}, u32[]{:S(2)}) collective-permute-start(bf16[4,6,1,128]{3,2,1,0:T(2,128)(2,1)S(1)} %get-tuple-element.34), channel_id=1, source_target_pairs={{2,0},{4,2},{6,4},{0,6},{3,1},{5,3},{7,5},{1,7},{10,8},{12,10},{14... | collective-permute-start | bytes 18440 | tf_op jit(solution)/shard_map/ppermute | solution.py:19
  14.7 3.5 %collective-permute-done.2 = bf16[4,6,1,128]{3,2,1,0:T(2,128)(2,1)S(1)} collective-permute-done((bf16[4,6,1,128]{3,2,1,0:T(2,128)(2,1)S(1)}, bf16[4,6,1,128]{3,2,1,0:T(2,128)(2,1)S(1)}, u32[]{:S(2)}, u32[]{:S(2)}) %collective-permute-start.2) | collective-permute-done | bytes 6176 | tf_op jit(solution)/shard_map/ppermute | solution.py:17
  18.6 1.8 collective-permute-start.5
  20.9 1.7 copy.72
  22.7 7.9 %broadcast_in_dim.2 = f32[32,2,2,32,2,64,2]{0,6,5,4,3,2,1:T(2,128)} broadcast(f32[32,2,32,64]{0,3,2,1:T(8,128)S(1)} %copy.72), dimensions={0,1,3,5} | broadcast | bytes 4718592 | tf_op jit(solution)/shard_map/broadcast_in_dim | solution.py:65
  30.5 11.4 %copy.73 = f32[32,4,64,128]{3,0,2,1:T(8,128)} copy(f32[32,4,64,128]{0,3,2,1:T(8,128)} %bitcast.435) | data formatting | bytes 8388608 | tf_op jit(solution)/shard_map/reshape | solution.py:69
  42.0 2.2 pad_maximum_fusion.3
  48.1 9.9 %convert_reduce_fusion = (f32[32]{0:T(128)S(1)}, bf16[32,4,64,128]{3,0,2,1:T(8,128)(2,1)S(1)}, f32[32,4,64,128]{3,0,2,1:T(8,128)}) fusion(f32[32,4,64,128]{3,0,2,1:T(8,128)S(1)} %copy-done.1, f32[32]{0:T(128)S(1)} %copy-done.13, bf16[32,108]{0,1:T(8,128)(2,1)S(1)} %reshape.26, bf16[108,4,64,128]{3,2,1,0:T(8,128)(2,1)S(1)} %bitcast.437), kind=kOutput, calls=%fused_computation.23 | convolution fusion | flops 248512480 | bytes 17570816 | tf_op jit(solution)/shard_map/ok,kxyz->oxyz/dot_general | solution.py:56
  57.9 6.6 %fusion.167 = f32[32,108]{0,1:T(8,128)S(1)} fusion(bf16[32,4,64,128]{3,0,2,1:T(8,128)(2,1)S(1)} %get-tuple-element.19, bf16[108,4,64,128]{3,2,1,0:T(8,128)(2,1)S(1)} %bitcast.438), kind=kOutput, calls=%fused_computation.110 | convolution fusion | flops 226492416 | bytes 9188864 | tf_op jit(solution)/shard_map/oxyz,kxyz->ok/dot_general | solution.py:71
  65.6 10.5 %copy.71 = f32[32,4,64,128]{0,3,2,1:T(8,128)} copy(f32[32,4,64,128]{3,0,2,1:T(8,128)} %get-tuple-element.20) | data formatting | bytes 8388608 | tf_op jit(solution)/shard_map/add | solution.py:27
  76.1 3.1 %collective-permute-start.7 = (bf16[32,1,64,128]{3,0,2,1:T(8,128)(2,1)}, bf16[32,1,64,128]{3,0,2,1:T(8,128)(2,1)S(1)}, u32[]{:S(2)}, u32[]{:S(2)}) collective-permute-start(bf16[32,1,64,128]{3,0,2,1:T(8,128)(2,1)} %get-tuple-element.28), channel_id=1, source_target_pairs={{8,0},{16,8},{24,16},{32,24},{40,32},{48,40},{56,48},{64,56},{72,6... | collective-permute-start | bytes 1572872 | tf_op jit(solution)/shard_map/ppermute | solution.py:19
  79.2 13.1 %reduce_sum.18 = f32[32,2,32,64]{0,3,2,1:T(8,128)} reduce(f32[32,2,2,32,2,64,2]{0,6,5,4,3,2,1:T(2,128)} %bitcast.436, f32[]{:T(128)} %constant.2.clone.1), dimensions={2,4,6}, to_apply=%region_0.1 | reduce | flops 917504 | bytes 4718596 | tf_op jit(solution)/shard_map/reduce_sum | solution.py:62
  92.3 2.9 %multiply_convert_fusion = bf16[32,2,32,64]{0,3,2,1:T(8,128)(2,1)} fusion(f32[32,2,32,64]{0,3,2,1:T(8,128)} %reduce_sum.18), kind=kLoop, calls=%fused_computation.72 | loop fusion | flops 262144 | bytes 786432 | tf_op jit(solution)/shard_map/convert_element_type | solution.py:63
  95.1 2.8 %copy.80 = bf16[32,2,32,64]{3,2,1,0:T(8,128)(2,1)} copy(bf16[32,2,32,64]{0,3,2,1:T(8,128)(2,1)} %multiply_convert_fusion) | data formatting | bytes 524288
  97.9 68.2 %all-reduce = (f32[32,4,3,3,3]{0,4,3,2,1:T(4,128)S(1)}, f32[32]{0:T(128)}) all-reduce(f32[32,4,3,3,3]{0,4,3,2,1:T(4,128)S(1)} %reshape.29, f32[32]{0:T(128)S(1)} %get-tuple-element.18), channel_id=1, replica_groups=mesh['gx'=16,'gy'=4,'gz'=2] {'gx','gy','gz'}, use_global_device_ids=true, to_apply=%region_1.2 | all-reduce | flops 3488 | bytes 27904 | tf_op jit(solution)/shard_map/psum | solution.py:73
  172.6 1.6 collective-permute-done.8
  174.9 4.1 %fusion.271 = (bf16[32,6,66,1]{3,0,2,1:T(8,128)(2,1)}, bf16[32,6,66,1]{3,0,2,1:T(8,128)(2,1)}) fusion(bf16[32,6,66,128]{3,0,2,1:T(8,128)(2,1)S(1)} %pad_maximum_fusion.1), kind=kLoop, calls=%fused_computation.251 | loop fusion | bytes 101376 | tf_op jit(solution)/shard_map/slice | solution.py:14
  179.0 4.8 %copy.76 = bf16[32,6,66,1]{2,0,3,1:T(8,128)(2,1)S(1)} copy(bf16[32,6,66,1]{3,0,2,1:T(8,128)(2,1)} %get-tuple-element.23) | data formatting | bytes 50688 | tf_op jit(solution)/shard_map/slice | solution.py:14
  185.0 4.8 %copy.78 = bf16[32,6,66,1]{2,0,3,1:T(8,128)(2,1)S(1)} copy(bf16[32,6,66,1]{3,0,2,1:T(8,128)(2,1)} %get-tuple-element.24) | data formatting | bytes 50688 | tf_op jit(solution)/shard_map/slice | solution.py:13
  197.9 6.0 %copy.77 = bf16[32,6,66,1]{3,0,2,1:T(8,128)(2,1)} copy(bf16[32,6,66,1]{2,0,3,1:T(8,128)(2,1)S(1)} %collective-permute-done.10) | data formatting | bytes 50688 | tf_op jit(solution)/shard_map/ppermute | solution.py:17
  203.9 6.0 %copy.79 = bf16[32,6,66,1]{3,0,2,1:T(8,128)(2,1)} copy(bf16[32,6,66,1]{2,0,3,1:T(8,128)(2,1)S(1)} %collective-permute-done.11) | data formatting | bytes 50688 | tf_op jit(solution)/shard_map/ppermute | solution.py:19
  209.9 9.5 %maximum_maximum_fusion = (bf16[32,6,66,129]{3,0,2,1:T(8,128)(2,1)S(1)}, bf16[32,6,66,129]{3,0,2,1:T(8,128)(2,1)S(1)}) fusion(bf16[32,6,1,128]{3,0,2,1:T(8,128)(2,1)S(1)} %collective-permute-done.9, bf16[32,1,64,128]{3,0,2,1:T(8,128)(2,1)S(1)} %collective-permute-done.7, bf16[32,4,64,128]{3,0,2,1:T(8,128)(2,1)S(1)} %get-tuple-element.19, ...), kind=kLoop, calls=%fused_computation.5 | loop fusion | flops 39232512 | bytes 9833472 | tf_op jit(solution)/shard_map/concatenate | solution.py:15
  (114 shorter events, 38.5 us)
Async XLA Ops:
  1.5 7.6 %collective-permute-start = (bf16[4,1,64,128]{3,2,1,0:T(8,128)(2,1)S(1)}, bf16[4,1,64,128]{3,2,1,0:T(8,128)(2,1)S(1)}, u32[]{:S(2)}, u32[]{:S(2)}) collective-permute-start(bf16[4,1,64,128]{3,2,1,0:T(8,128)(2,1)S(1)} %get-tuple-element.36), channel_id=1, source_target_pairs={{0,8},{8,16},{16,24},{24,32},{32,40},{40,48},{48,56},{56,64},{64,7... | collective-permute-start | bytes 196616 | tf_op jit(solution)/shard_map/ppermute | solution.py:17
  1.6 8.5 %collective-permute-start.1 = (bf16[4,1,64,128]{3,2,1,0:T(8,128)(2,1)S(1)}, bf16[4,1,64,128]{3,2,1,0:T(8,128)(2,1)S(1)}, u32[]{:S(2)}, u32[]{:S(2)}) collective-permute-start(bf16[4,1,64,128]{3,2,1,0:T(8,128)(2,1)S(1)} %get-tuple-element.35), channel_id=1, source_target_pairs={{8,0},{16,8},{24,16},{32,24},{40,32},{48,40},{56,48},{64,56},{72,6... | collective-permute-start | bytes 196616 | tf_op jit(solution)/shard_map/ppermute | solution.py:19
  10.2 4.5 %collective-permute-start.3 = (bf16[4,6,1,128]{3,2,1,0:T(2,128)(2,1)S(1)}, bf16[4,6,1,128]{3,2,1,0:T(2,128)(2,1)S(1)}, u32[]{:S(2)}, u32[]{:S(2)}) collective-permute-start(bf16[4,6,1,128]{3,2,1,0:T(2,128)(2,1)S(1)} %get-tuple-element.34), channel_id=1, source_target_pairs={{2,0},{4,2},{6,4},{0,6},{3,1},{5,3},{7,5},{1,7},{10,8},{12,10},{14... | collective-permute-start | bytes 18440 | tf_op jit(solution)/shard_map/ppermute | solution.py:19
  13.3 4.9 %collective-permute-start.2 = (bf16[4,6,1,128]{3,2,1,0:T(2,128)(2,1)S(1)}, bf16[4,6,1,128]{3,2,1,0:T(2,128)(2,1)S(1)}, u32[]{:S(2)}, u32[]{:S(2)}) collective-permute-start(bf16[4,6,1,128]{3,2,1,0:T(2,128)(2,1)S(1)} %get-tuple-element.33), channel_id=1, source_target_pairs={{0,2},{2,4},{4,6},{6,0},{1,3},{3,5},{5,7},{7,1},{8,10},{10,12},{12... | collective-permute-start | bytes 18440 | tf_op jit(solution)/shard_map/ppermute | solution.py:17
  18.6 23.5 %collective-permute-start.5 = (bf16[4,6,66,1]{3,2,1,0:T(8,128)(2,1)S(1)}, bf16[4,6,66,1]{3,2,1,0:T(8,128)(2,1)}, u32[]{:S(2)}, u32[]{:S(2)}) collective-permute-start(bf16[4,6,66,1]{3,2,1,0:T(8,128)(2,1)S(1)} %get-tuple-element.29), channel_id=1, source_target_pairs={{1,0},{0,1},{3,2},{2,3},{5,4},{4,5},{7,6},{6,7},{9,8},{8,9},{11,10... | collective-permute-start | bytes 9512 | tf_op jit(solution)/shard_map/ppermute | solution.py:19
  20.4 21.6 %collective-permute-start.4 = (bf16[4,6,66,1]{3,2,1,0:T(8,128)(2,1)S(1)}, bf16[4,6,66,1]{3,2,1,0:T(8,128)(2,1)}, u32[]{:S(2)}, u32[]{:S(2)}) collective-permute-start(bf16[4,6,66,1]{3,2,1,0:T(8,128)(2,1)S(1)} %get-tuple-element.30), channel_id=1, source_target_pairs={{0,1},{1,0},{2,3},{3,2},{4,5},{5,4},{6,7},{7,6},{8,9},{9,8},{10,11... | collective-permute-start | bytes 9512 | tf_op jit(solution)/shard_map/ppermute | solution.py:17
  30.5 11.4 %copy-start.11 = (bf16[32,4,3,3,3]{0,1,4,3,2:T(4,128)(2,1)S(1)}, bf16[32,4,3,3,3]{0,1,4,3,2:T(4,128)(2,1)}, u32[]{:S(2)}) copy-start(bf16[32,4,3,3,3]{0,1,4,3,2:T(4,128)(2,1)} %param.5) | copy-start | bytes 20740
  30.5 14.2 %copy-start = (bf16[4,4,64,128]{3,2,1,0:T(8,128)(2,1)S(1)}, bf16[4,4,64,128]{3,2,1,0:T(8,128)(2,1)}, u32[]{:S(2)}) copy-start(bf16[4,4,64,128]{3,2,1,0:T(8,128)(2,1)} %param.4) | copy-start | bytes 786436
  44.8 3.3 %copy-start.1 = (f32[32,4,64,128]{3,0,2,1:T(8,128)S(1)}, f32[32,4,64,128]{3,0,2,1:T(8,128)}, u32[]{:S(2)}) copy-start(f32[32,4,64,128]{3,0,2,1:T(8,128)} %copy.73) | copy-start | bytes 12582916
  44.8 3.3 %copy-start.13 = (f32[32]{0:T(128)S(1)}, f32[32]{0:T(128)}, u32[]{:S(2)}) copy-start(f32[32]{0:T(128)} %param.6) | copy-start | bytes 388
  76.1 91.8 %collective-permute-start.7 = (bf16[32,1,64,128]{3,0,2,1:T(8,128)(2,1)}, bf16[32,1,64,128]{3,0,2,1:T(8,128)(2,1)S(1)}, u32[]{:S(2)}, u32[]{:S(2)}) collective-permute-start(bf16[32,1,64,128]{3,0,2,1:T(8,128)(2,1)} %get-tuple-element.28), channel_id=1, source_target_pairs={{8,0},{16,8},{24,16},{32,24},{40,32},{48,40},{56,48},{64,56},{72,6... | collective-permute-start | bytes 1572872 | tf_op jit(solution)/shard_map/ppermute | solution.py:19
  79.2 88.7 %collective-permute-start.6 = (bf16[32,1,64,128]{3,0,2,1:T(8,128)(2,1)}, bf16[32,1,64,128]{3,0,2,1:T(8,128)(2,1)S(1)}, u32[]{:S(2)}, u32[]{:S(2)}) collective-permute-start(bf16[32,1,64,128]{3,0,2,1:T(8,128)(2,1)} %get-tuple-element.27), channel_id=1, source_target_pairs={{0,8},{8,16},{16,24},{24,32},{32,40},{40,48},{48,56},{56,64},{64,7... | collective-permute-start | bytes 1572872 | tf_op jit(solution)/shard_map/ppermute | solution.py:17
  79.2 87.6 %copy-start.12 = (bf16[32,4,3,3,3]{0,1,4,3,2:T(4,128)(2,1)S(1)}, bf16[32,4,3,3,3]{0,1,4,3,2:T(4,128)(2,1)}, u32[]{:S(2)}) copy-start(bf16[32,4,3,3,3]{0,1,4,3,2:T(4,128)(2,1)} %param.5) | copy-start | bytes 20740
  167.9 4.7 %collective-permute-start.9 = (bf16[32,6,1,128]{3,0,2,1:T(8,128)(2,1)S(1)}, bf16[32,6,1,128]{3,0,2,1:T(8,128)(2,1)S(1)}, u32[]{:S(2)}, u32[]{:S(2)}) collective-permute-start(bf16[32,6,1,128]{3,0,2,1:T(8,128)(2,1)S(1)} %get-tuple-element.26), channel_id=1, source_target_pairs={{2,0},{4,2},{6,4},{0,6},{3,1},{5,3},{7,5},{1,7},{10,8},{12,10},{14... | collective-permute-start | bytes 147464 | tf_op jit(solution)/shard_map/ppermute | solution.py:19
  168.9 5.3 %collective-permute-start.8 = (bf16[32,6,1,128]{3,0,2,1:T(8,128)(2,1)S(1)}, bf16[32,6,1,128]{3,0,2,1:T(8,128)(2,1)S(1)}, u32[]{:S(2)}, u32[]{:S(2)}) collective-permute-start(bf16[32,6,1,128]{3,0,2,1:T(8,128)(2,1)S(1)} %get-tuple-element.25), channel_id=1, source_target_pairs={{0,2},{2,4},{4,6},{6,0},{1,3},{3,5},{5,7},{7,1},{8,10},{10,12},{12... | collective-permute-start | bytes 147464 | tf_op jit(solution)/shard_map/ppermute | solution.py:17
  183.8 14.1 %collective-permute-start.10 = (bf16[32,6,66,1]{2,0,3,1:T(8,128)(2,1)S(1)}, bf16[32,6,66,1]{2,0,3,1:T(8,128)(2,1)S(1)}, u32[]{:S(2)}, u32[]{:S(2)}) collective-permute-start(bf16[32,6,66,1]{2,0,3,1:T(8,128)(2,1)S(1)} %copy.76), channel_id=1, source_target_pairs={{0,1},{1,0},{2,3},{3,2},{4,5},{5,4},{6,7},{7,6},{8,9},{9,8},{10,11... | collective-permute-start | bytes 76040 | tf_op jit(solution)/shard_map/ppermute | solution.py:17
  189.7 14.2 %collective-permute-start.11 = (bf16[32,6,66,1]{2,0,3,1:T(8,128)(2,1)S(1)}, bf16[32,6,66,1]{2,0,3,1:T(8,128)(2,1)S(1)}, u32[]{:S(2)}, u32[]{:S(2)}) collective-permute-start(bf16[32,6,66,1]{2,0,3,1:T(8,128)(2,1)S(1)} %copy.78), channel_id=1, source_target_pairs={{1,0},{0,1},{3,2},{2,3},{5,4},{4,5},{7,6},{6,7},{9,8},{8,9},{11,10... | collective-permute-start | bytes 76040 | tf_op jit(solution)/shard_map/ppermute | solution.py:19
  226.0 3.4 %copy-start.2 = (f32[4,64,128,4]{2,3,1,0:T(4,128)S(1)}, f32[4,64,128,4]{2,3,1,0:T(4,128)}, u32[]{:S(2)}) copy-start(f32[4,64,128,4]{2,3,1,0:T(4,128)} %fusion.223) | copy-start | bytes 1572868
  226.0 3.4 %copy-start.4 = (f32[4,64,128,4]{2,3,1,0:T(4,128)S(1)}, f32[4,64,128,4]{2,3,1,0:T(4,128)}, u32[]{:S(2)}) copy-start(f32[4,64,128,4]{2,3,1,0:T(4,128)} %fusion.18) | copy-start | bytes 1572868
  226.0 3.4 %copy-start.8 = (f32[4,64,128,4]{2,3,1,0:T(4,128)S(1)}, f32[4,64,128,4]{2,3,1,0:T(4,128)}, u32[]{:S(2)}) copy-start(f32[4,64,128,4]{2,3,1,0:T(4,128)} %fusion.227) | copy-start | bytes 1572868
  226.0 3.4 %copy-start.9 = (f32[4,64,128,4]{2,3,1,0:T(4,128)S(1)}, f32[4,64,128,4]{2,3,1,0:T(4,128)}, u32[]{:S(2)}) copy-start(f32[4,64,128,4]{2,3,1,0:T(4,128)} %fusion.231) | copy-start | bytes 1572868
  226.0 3.4 %copy-start.10 = (f32[4,64,128,4]{2,3,1,0:T(4,128)S(1)}, f32[4,64,128,4]{2,3,1,0:T(4,128)}, u32[]{:S(2)}) copy-start(f32[4,64,128,4]{2,3,1,0:T(4,128)} %fusion.238) | copy-start | bytes 1572868
  228.5 1.9 copy-start.3
  228.5 1.9 copy-start.5
  (2 other events, 3.7 us)
where the time goes:
time: 236 us; the launch traced here: 233 us
  blocking collectives  68.2 us (29%)
  local copies, waits for them, and re-layouts  67.6 us (29%)
  matrix products  39.4 us (17%)
  other arithmetic  29.3 us (12%)
  starting transfers between devices  18.7 us (8%)
  waiting for transfers between devices  8.38 us (4%)
    psum x1, blocking collectives, on_device(): lax.psum((weight_local, bias_local), ('gx', 'gy', 'gz'))  68.2 us
    dot_general x27, matrix products, on_device(): jnp.einsum('oc,oxyz->cxyz', weight[:, :, 2 - sa, 2 - sb, 2 - se], window,...  22.9 us
    ppermute x6, starting transfers between devices, extended(): lax.ppermute(head, axis, [((i + 1) % count, i) for i in range(count)])  15.6 us
    reduce_sum x1, other arithmetic, on_device(): pooled = activated.reshape(chan_out, cells_x // 2, 2, cells_y // 2, 2, ce...  13.1 us
    concatenate x4, other arithmetic, extended(): jnp.concatenate([lax.ppermute(tail, axis, [(i, (i + 1) % count) for i in...  12.6 us
    reshape x1, local copies, waits for them, and re-layouts, on_device(): spread = spread.reshape(chan_out, cells_x, cells_y, cells_z)  11.4 us
    add x1, local copies, waits for them, and re-layouts, activate(): leak_slope * preact  10.5 us
    slice x4, local copies, waits for them, and re-layouts, extended(): lax.slice_in_dim(cells, cells.shape[dim] - width, cells.shape[dim], axis=...  9.99 us
  transfers between devices with their start and end apart: 12, of which 4 were waited for; matrix products, arithmetic and copies ran while one was open for 27% of the time, Pallas kernels for 0%

commit v1 on v0

--- a/solution.py
+++ b/solution.py
@@ -1,7 +1,12 @@
 import jax
 import jax.numpy as jnp
 from jax import lax
+from jax.experimental import pallas as pl
+from jax.experimental.pallas import tpu as pltpu
 from jax.sharding import PartitionSpec as P
+
+MESH = pl.DeviceIdType.MESH
+AXES = ("gx", "gy", "gz")
 
 leak_slope = 0.3
 soft_scale = 10.0
@@ -21,6 +26,87 @@
             axis=dim,
         )
     return cells
+
+
+def allreduce_kernel(sizes, x_ref, o_ref, slots_x, slots_y, slots_z, acc_x, acc_y,
+                     send_x, recv_x, send_y, recv_y, send_z, recv_z):
+    me = tuple(lax.axis_index(a) for a in AXES)
+    slots = (slots_x, slots_y, slots_z)
+    sends = (send_x, send_y, send_z)
+    recvs = (recv_x, recv_y, recv_z)
+    sources = (x_ref, acc_x, acc_y)
+    sinks = (acc_x, acc_y, o_ref)
+
+    def peer(axis, index):
+        return tuple(index if k == axis else me[k] for k in range(3))
+
+    barrier = pltpu.get_barrier_semaphore()
+    count = 0
+    for axis, n in enumerate(sizes):
+        for d in range(1, n):
+            target = lax.rem(me[axis] + d, n)
+            pl.semaphore_signal(barrier, inc=1, device_id=peer(axis, target), device_id_type=MESH)
+            count += 1
+    pl.semaphore_wait(barrier, count)
+
+    for axis, n in enumerate(sizes):
+        src, held, sink = sources[axis], slots[axis], sinks[axis]
+        mine = me[axis]
+        copies = []
+        for d in range(1, n):
+            target = lax.rem(mine + d, n)
+            copy = pltpu.make_async_remote_copy(
+                src_ref=src,
+                dst_ref=held.at[mine],
+                send_sem=sends[axis].at[d],
+                recv_sem=recvs[axis].at[mine],
+                device_id=peer(axis, target),
+                device_id_type=MESH,
+            )
+            copy.start()
+            copies.append(copy)
+        held[mine] = src[...]
+        for d in range(1, n):
+            origin = lax.rem(mine + n - d, n)
+            incoming = pltpu.make_async_remote_copy(
+                src_ref=src,
+                dst_ref=held.at[origin],
+                send_sem=sends[axis].at[d],
+                recv_sem=recvs[axis].at[origin],
+                device_id=peer(axis, origin),
+                device_id_type=MESH,
+            )
+            incoming.wait_recv()
+        for copy in copies:
+            copy.wait_send()
+        total = held[0]
+        for k in range(1, n):
+            total = total + held[k]
+        sink[...] = total
+
+
+def allreduce(x, sizes):
+    shape = x.shape
+    return pl.pallas_call(
+        lambda *refs: allreduce_kernel(sizes, *refs),
+        out_shape=jax.ShapeDtypeStruct(shape, jnp.float32),
+        in_specs=[pl.BlockSpec(memory_space=pltpu.VMEM)],
+        out_specs=pl.BlockSpec(memory_space=pltpu.VMEM),
+        scratch_shapes=[
+            pltpu.VMEM((sizes[0],) + shape, jnp.float32),
+            pltpu.VMEM((sizes[1],) + shape, jnp.float32),
+            pltpu.VMEM((sizes[2],) + shape, jnp.float32),
+            pltpu.VMEM(shape, jnp.float32),
+            pltpu.VMEM(shape, jnp.float32),
+            pltpu.SemaphoreType.DMA((sizes[0],)),
+            pltpu.SemaphoreType.DMA((sizes[0],)),
+            pltpu.SemaphoreType.DMA((sizes[1],)),
+            pltpu.SemaphoreType.DMA((sizes[1],)),
+            pltpu.SemaphoreType.DMA((sizes[2],)),
+            pltpu.SemaphoreType.DMA((sizes[2],)),
+        ],
+        compiler_params=pltpu.CompilerParams(collective_id=0, has_side_effects=True),
+    )(x)
 
 
 def activate(preact):
@@ -70,8 +156,16 @@
     delta = (slope_of(preact) * spread * 0.125).astype(jnp.bfloat16)
     weight_local = jnp.einsum("oxyz,kxyz->ok", delta, patches, preferred_element_type=jnp.float32)
     bias_local = jnp.sum(delta, axis=(1, 2, 3), dtype=jnp.float32)
-    weight_total, bias_grad = lax.psum((weight_local, bias_local), ("gx", "gy", "gz"))
-    weight_grad = weight_total.reshape(chan_out, chan_in, 3, 3, 3)
+    taps = chan_in * 27
+    width = -(-(taps + 1) // 128) * 128
+    partial = jnp.concatenate(
+        [weight_local, bias_local[:, None], jnp.zeros((chan_out, width - taps - 1), jnp.float32)],
+        axis=1,
+    )
+    sizes = tuple(lax.axis_size(a) for a in AXES)
+    both = allreduce(partial, sizes)
+    weight_grad = both[:, :taps].reshape(chan_out, chan_in, 3, 3, 3)
+    bias_grad = both[:, taps]
     delta_wide = extended(delta, (("gx", 1), ("gy", 2), ("gz", 3)), 1)
     input_grad = jnp.zeros((chan_in, cells_x, cells_y, cells_z), jnp.float32)
     for sa, sb, se in stencil:

time: 236 us -> 192 us (0.81)
  blocking collectives: 68.2 us -> 0 us
  Pallas kernels: 0 us -> 20.2 us
    psum x1 -> x0, blocking collectives: 68.2 us -> none  [on_device(): lax.psum((weight_local, bias_local), ('gx', 'gy', 'gz'))]
    pallas_call x0 -> x1, Pallas kernels: none -> 20.2 us  [allreduce(): pl.pallas_call(lambda *refs: allreduce_kernel(sizes, *refs), out_shape=ja...]
  transfers between devices with their start and end apart: 12 -> 12, of which waited for: 4 -> 4; matrix products, arithmetic and copies ran while one was open for 27% -> 25% of each run, Pallas kernels for 0% -> 11%
where the time goes in v1:
time: 192 us; the launch traced here: 188 us
  local copies, waits for them, and re-layouts  68.8 us (36%)
  matrix products  39.5 us (21%)
  other arithmetic  29 us (15%)
  Pallas kernels  20.2 us (11%)
  starting transfers between devices  19.6 us (10%)
  waiting for transfers between devices  9.65 us (5%)
    dot_general x27, matrix products, on_device(): jnp.einsum('oc,oxyz->cxyz', weight[:, :, 2 - sa, 2 - sb, 2 - se], window,...  22.9 us
    pallas_call x1, Pallas kernels, allreduce(): pl.pallas_call(lambda *refs: allreduce_kernel(sizes, *refs), out_shape=ja...  20.2 us
    ppermute x6, starting transfers between devices, extended(): lax.ppermute(head, axis, [((i + 1) % count, i) for i in range(count)])  17.8 us
    reduce_sum x1, other arithmetic, on_device(): pooled = activated.reshape(chan_out, cells_x // 2, 2, cells_y // 2, 2, ce...  13.1 us
    concatenate x4, other arithmetic, extended(): jnp.concatenate([lax.ppermute(tail, axis, [(i, (i + 1) % count) for i in...  12.6 us
    reshape x1, local copies, waits for them, and re-layouts, on_device(): spread = spread.reshape(chan_out, cells_x, cells_y, cells_z)  11.4 us
    add x1, local copies, waits for them, and re-layouts, activate(): leak_slope * preact  10.5 us
    slice x4, local copies, waits for them, and re-layouts, extended(): lax.slice_in_dim(cells, cells.shape[dim] - width, cells.shape[dim], axis=...  9.97 us
  transfers between devices with their start and end apart: 12, of which 4 were waited for; matrix products, arithmetic and copies ran while one was open for 25% of the time, Pallas kernels for 11%

profile of v1, /device:TPU:0, one launch (start us, length us, event | category | flops | bytes accessed | tf_op | source)
XLA Modules:
  0.0 188.1 jit_solution(17935949328235689359)
XLA Ops:
  1.6 5.7 %collective-permute-start.1 = (bf16[4,1,64,128]{3,2,1,0:T(8,128)(2,1)S(1)}, bf16[4,1,64,128]{3,2,1,0:T(8,128)(2,1)S(1)}, u32[]{:S(2)}, u32[]{:S(2)}) collective-permute-start(bf16[4,1,64,128]{3,2,1,0:T(8,128)(2,1)S(1)} %get-tuple-element.33), channel_id=1, source_target_pairs={{8,0},{16,8},{24,16},{32,24},{40,32},{48,40},{56,48},{64,56},{72,6... | collective-permute-start | bytes 196616 | tf_op jit(solution)/shard_map/ppermute | solution.py:24
  7.3 1.9 collective-permute-done
  10.2 3.1 %collective-permute-start.3 = (bf16[4,6,1,128]{3,2,1,0:T(2,128)(2,1)S(1)}, bf16[4,6,1,128]{3,2,1,0:T(2,128)(2,1)S(1)}, u32[]{:S(2)}, u32[]{:S(2)}) collective-permute-start(bf16[4,6,1,128]{3,2,1,0:T(2,128)(2,1)S(1)} %get-tuple-element.32), channel_id=1, source_target_pairs={{2,0},{4,2},{6,4},{0,6},{3,1},{5,3},{7,5},{1,7},{10,8},{12,10},{14... | collective-permute-start | bytes 18440 | tf_op jit(solution)/shard_map/ppermute | solution.py:24
  14.7 3.5 %collective-permute-done.2 = bf16[4,6,1,128]{3,2,1,0:T(2,128)(2,1)S(1)} collective-permute-done((bf16[4,6,1,128]{3,2,1,0:T(2,128)(2,1)S(1)}, bf16[4,6,1,128]{3,2,1,0:T(2,128)(2,1)S(1)}, u32[]{:S(2)}, u32[]{:S(2)}) %collective-permute-start.2) | collective-permute-done | bytes 6176 | tf_op jit(solution)/shard_map/ppermute | solution.py:22
  18.6 1.8 collective-permute-start.5
  20.9 1.7 copy.74
  22.7 7.9 %broadcast_in_dim.6 = f32[32,2,2,32,2,64,2]{0,6,5,4,3,2,1:T(2,128)} broadcast(f32[32,2,32,64]{0,3,2,1:T(8,128)S(1)} %copy.74), dimensions={0,1,3,5} | broadcast | bytes 4718592 | tf_op jit(solution)/shard_map/broadcast_in_dim | solution.py:151
  30.5 11.4 %copy.75 = f32[32,4,64,128]{3,0,2,1:T(8,128)} copy(f32[32,4,64,128]{0,3,2,1:T(8,128)} %bitcast.439) | data formatting | bytes 8388608 | tf_op jit(solution)/shard_map/reshape | solution.py:155
  42.1 2.2 %pad_maximum_fusion.3 = (bf16[4,6,66,129]{3,2,1,0:T(8,128)(2,1)S(1)}, bf16[4,6,66,129]{3,2,1,0:T(8,128)(2,1)S(1)}) fusion(bf16[4,6,66,1]{3,2,1,0:T(8,128)(2,1)} %collective-permute-done.5, bf16[4,6,1,128]{3,2,1,0:T(2,128)(2,1)S(1)} %collective-permute-done.3, bf16[4,6,64,128]{3,2,1,0:T(8,128)(2,1)S(1)} %constant_dynamic-update-slice_fusion, ...), kind=kLoop, calls=%fused_computation.112 | loop fusion | flops 3269376 | bytes 1229184 | tf_op jit(solution)/shard_map/concatenate | solution.py:20
  48.1 9.8 %convert_reduce_fusion = (f32[32]{0:T(128)S(1)}, bf16[32,4,64,128]{3,0,2,1:T(8,128)(2,1)S(1)}, f32[32,4,64,128]{3,0,2,1:T(8,128)}) fusion(f32[32,4,64,128]{3,0,2,1:T(8,128)S(1)} %copy-done.1, f32[32]{0:T(128)S(1)} %copy-done.13, bf16[32,108]{0,1:T(8,128)(2,1)S(1)} %reshape.26, bf16[108,4,64,128]{3,2,1,0:T(8,128)(2,1)S(1)} %bitcast.441), kind=kOutput, calls=%fused_computation.23 | convolution fusion | flops 248512480 | bytes 17570816 | tf_op jit(solution)/shard_map/ok,kxyz->oxyz/dot_general | solution.py:142
  58.0 6.8 %fusion.167 = f32[32,108]{1,0:T(8,128)S(1)} fusion(bf16[32,4,64,128]{3,0,2,1:T(8,128)(2,1)S(1)} %get-tuple-element.17, bf16[108,4,64,128]{3,2,1,0:T(8,128)(2,1)S(1)} %bitcast.442), kind=kOutput, calls=%fused_computation.110 | convolution fusion | flops 226492416 | bytes 9188864 | tf_op jit(solution)/shard_map/oxyz,kxyz->ok/dot_general | solution.py:157
  65.8 10.5 %copy.73 = f32[32,4,64,128]{0,3,2,1:T(8,128)} copy(f32[32,4,64,128]{3,0,2,1:T(8,128)} %get-tuple-element.18) | data formatting | bytes 8388608 | tf_op jit(solution)/shard_map/add | solution.py:113
  76.3 13.1 %reduce_sum.18 = f32[32,2,32,64]{0,3,2,1:T(8,128)} reduce(f32[32,2,2,32,2,64,2]{0,6,5,4,3,2,1:T(2,128)} %bitcast.440, f32[]{:T(128)} %constant.9.clone.1), dimensions={2,4,6}, to_apply=%region_0.1 | reduce | flops 917504 | bytes 4718596 | tf_op jit(solution)/shard_map/reduce_sum | solution.py:148
  89.3 1.9 multiply_convert_fusion
  93.0 3.1 %collective-permute-start.7 = (bf16[32,1,64,128]{3,0,2,1:T(8,128)(2,1)}, bf16[32,1,64,128]{3,0,2,1:T(8,128)(2,1)S(1)}, u32[]{:S(2)}, u32[]{:S(2)}) collective-permute-start(bf16[32,1,64,128]{3,0,2,1:T(8,128)(2,1)} %get-tuple-element.26), channel_id=1, source_target_pairs={{8,0},{16,8},{24,16},{32,24},{40,32},{48,40},{56,48},{64,56},{72,6... | collective-permute-start | bytes 1572872 | tf_op jit(solution)/shard_map/ppermute | solution.py:24
  96.7 20.2 %shard_map.75 = f32[32,128]{1,0:T(8,128)} custom-call(f32[32,128]{1,0:T(8,128)} %maximum_maximum_fusion.3.refs_0_), custom_call_target="tpu_custom_call" | custom-call | tf_op jit(solution)/shard_map/pallas_call | solution.py:90
  121.0 3.0 %collective-permute-start.9 = (bf16[32,6,1,128]{3,0,2,1:T(8,128)(2,1)S(1)}, bf16[32,6,1,128]{3,0,2,1:T(8,128)(2,1)S(1)}, u32[]{:S(2)}, u32[]{:S(2)}) collective-permute-start(bf16[32,6,1,128]{3,0,2,1:T(8,128)(2,1)S(1)} %get-tuple-element.24), channel_id=1, source_target_pairs={{2,0},{4,2},{6,4},{0,6},{3,1},{5,3},{7,5},{1,7},{10,8},{12,10},{14... | collective-permute-start | bytes 147464 | tf_op jit(solution)/shard_map/ppermute | solution.py:24
  126.6 2.9 %collective-permute-done.8 = bf16[32,6,1,128]{3,0,2,1:T(8,128)(2,1)S(1)} collective-permute-done((bf16[32,6,1,128]{3,0,2,1:T(8,128)(2,1)S(1)}, bf16[32,6,1,128]{3,0,2,1:T(8,128)(2,1)S(1)}, u32[]{:S(2)}, u32[]{:S(2)}) %collective-permute-start.8) | collective-permute-done | bytes 49184 | tf_op jit(solution)/shard_map/ppermute | solution.py:22
  130.2 4.1 %fusion.271 = (bf16[32,6,66,1]{3,0,2,1:T(8,128)(2,1)}, bf16[32,6,66,1]{3,0,2,1:T(8,128)(2,1)}) fusion(bf16[32,6,66,128]{3,0,2,1:T(8,128)(2,1)S(1)} %pad_maximum_fusion.1), kind=kLoop, calls=%fused_computation.253 | loop fusion | bytes 101376 | tf_op jit(solution)/shard_map/slice | solution.py:19
  134.3 4.8 %copy.79 = bf16[32,6,66,1]{2,0,3,1:T(8,128)(2,1)S(1)} copy(bf16[32,6,66,1]{3,0,2,1:T(8,128)(2,1)} %get-tuple-element.21) | data formatting | bytes 50688 | tf_op jit(solution)/shard_map/slice | solution.py:19
  140.2 4.8 %copy.81 = bf16[32,6,66,1]{2,0,3,1:T(8,128)(2,1)S(1)} copy(bf16[32,6,66,1]{3,0,2,1:T(8,128)(2,1)} %get-tuple-element.22) | data formatting | bytes 50688 | tf_op jit(solution)/shard_map/slice | solution.py:18
  153.2 6.0 %copy.80 = bf16[32,6,66,1]{3,0,2,1:T(8,128)(2,1)} copy(bf16[32,6,66,1]{2,0,3,1:T(8,128)(2,1)S(1)} %collective-permute-done.10) | data formatting | bytes 50688 | tf_op jit(solution)/shard_map/ppermute | solution.py:22
  159.2 6.0 %copy.82 = bf16[32,6,66,1]{3,0,2,1:T(8,128)(2,1)} copy(bf16[32,6,66,1]{2,0,3,1:T(8,128)(2,1)S(1)} %collective-permute-done.11) | data formatting | bytes 50688 | tf_op jit(solution)/shard_map/ppermute | solution.py:24
  165.2 9.5 %maximum_maximum_fusion = (bf16[32,6,66,129]{3,0,2,1:T(8,128)(2,1)S(1)}, bf16[32,6,66,129]{3,0,2,1:T(8,128)(2,1)S(1)}) fusion(bf16[32,6,1,128]{3,0,2,1:T(8,128)(2,1)S(1)} %collective-permute-done.9, bf16[32,1,64,128]{3,0,2,1:T(8,128)(2,1)S(1)} %collective-permute-done.7, bf16[32,4,64,128]{3,0,2,1:T(8,128)(2,1)S(1)} %get-tuple-element.17, ...), kind=kLoop, calls=%fused_computation.5 | loop fusion | flops 39232512 | bytes 9833472 | tf_op jit(solution)/shard_map/concatenate | solution.py:20
  (120 shorter events, 41.2 us)
Async XLA Ops:
  1.5 7.6 %collective-permute-start = (bf16[4,1,64,128]{3,2,1,0:T(8,128)(2,1)S(1)}, bf16[4,1,64,128]{3,2,1,0:T(8,128)(2,1)S(1)}, u32[]{:S(2)}, u32[]{:S(2)}) collective-permute-start(bf16[4,1,64,128]{3,2,1,0:T(8,128)(2,1)S(1)} %get-tuple-element.34), channel_id=1, source_target_pairs={{0,8},{8,16},{16,24},{24,32},{32,40},{40,48},{48,56},{56,64},{64,7... | collective-permute-start | bytes 196616 | tf_op jit(solution)/shard_map/ppermute | solution.py:22
  1.6 8.5 %collective-permute-start.1 = (bf16[4,1,64,128]{3,2,1,0:T(8,128)(2,1)S(1)}, bf16[4,1,64,128]{3,2,1,0:T(8,128)(2,1)S(1)}, u32[]{:S(2)}, u32[]{:S(2)}) collective-permute-start(bf16[4,1,64,128]{3,2,1,0:T(8,128)(2,1)S(1)} %get-tuple-element.33), channel_id=1, source_target_pairs={{8,0},{16,8},{24,16},{32,24},{40,32},{48,40},{56,48},{64,56},{72,6... | collective-permute-start | bytes 196616 | tf_op jit(solution)/shard_map/ppermute | solution.py:24
  10.2 4.5 %collective-permute-start.3 = (bf16[4,6,1,128]{3,2,1,0:T(2,128)(2,1)S(1)}, bf16[4,6,1,128]{3,2,1,0:T(2,128)(2,1)S(1)}, u32[]{:S(2)}, u32[]{:S(2)}) collective-permute-start(bf16[4,6,1,128]{3,2,1,0:T(2,128)(2,1)S(1)} %get-tuple-element.32), channel_id=1, source_target_pairs={{2,0},{4,2},{6,4},{0,6},{3,1},{5,3},{7,5},{1,7},{10,8},{12,10},{14... | collective-permute-start | bytes 18440 | tf_op jit(solution)/shard_map/ppermute | solution.py:24
  13.3 4.9 %collective-permute-start.2 = (bf16[4,6,1,128]{3,2,1,0:T(2,128)(2,1)S(1)}, bf16[4,6,1,128]{3,2,1,0:T(2,128)(2,1)S(1)}, u32[]{:S(2)}, u32[]{:S(2)}) collective-permute-start(bf16[4,6,1,128]{3,2,1,0:T(2,128)(2,1)S(1)} %get-tuple-element.31), channel_id=1, source_target_pairs={{0,2},{2,4},{4,6},{6,0},{1,3},{3,5},{5,7},{7,1},{8,10},{10,12},{12... | collective-permute-start | bytes 18440 | tf_op jit(solution)/shard_map/ppermute | solution.py:22
  18.6 23.5 %collective-permute-start.5 = (bf16[4,6,66,1]{3,2,1,0:T(8,128)(2,1)S(1)}, bf16[4,6,66,1]{3,2,1,0:T(8,128)(2,1)}, u32[]{:S(2)}, u32[]{:S(2)}) collective-permute-start(bf16[4,6,66,1]{3,2,1,0:T(8,128)(2,1)S(1)} %get-tuple-element.27), channel_id=1, source_target_pairs={{1,0},{0,1},{3,2},{2,3},{5,4},{4,5},{7,6},{6,7},{9,8},{8,9},{11,10... | collective-permute-start | bytes 9512 | tf_op jit(solution)/shard_map/ppermute | solution.py:24
  20.4 21.7 %collective-permute-start.4 = (bf16[4,6,66,1]{3,2,1,0:T(8,128)(2,1)S(1)}, bf16[4,6,66,1]{3,2,1,0:T(8,128)(2,1)}, u32[]{:S(2)}, u32[]{:S(2)}) collective-permute-start(bf16[4,6,66,1]{3,2,1,0:T(8,128)(2,1)S(1)} %get-tuple-element.28), channel_id=1, source_target_pairs={{0,1},{1,0},{2,3},{3,2},{4,5},{5,4},{6,7},{7,6},{8,9},{9,8},{10,11... | collective-permute-start | bytes 9512 | tf_op jit(solution)/shard_map/ppermute | solution.py:22
  30.5 11.4 %copy-start.11 = (bf16[32,4,3,3,3]{0,1,4,3,2:T(4,128)(2,1)S(1)}, bf16[32,4,3,3,3]{0,1,4,3,2:T(4,128)(2,1)}, u32[]{:S(2)}) copy-start(bf16[32,4,3,3,3]{0,1,4,3,2:T(4,128)(2,1)} %param.5) | copy-start | bytes 20740
  30.5 14.3 %copy-start = (bf16[4,4,64,128]{3,2,1,0:T(8,128)(2,1)S(1)}, bf16[4,4,64,128]{3,2,1,0:T(8,128)(2,1)}, u32[]{:S(2)}) copy-start(bf16[4,4,64,128]{3,2,1,0:T(8,128)(2,1)} %param.4) | copy-start | bytes 786436
  44.8 3.3 %copy-start.1 = (f32[32,4,64,128]{3,0,2,1:T(8,128)S(1)}, f32[32,4,64,128]{3,0,2,1:T(8,128)}, u32[]{:S(2)}) copy-start(f32[32,4,64,128]{3,0,2,1:T(8,128)} %copy.75) | copy-start | bytes 12582916
  44.8 3.3 %copy-start.13 = (f32[32]{0:T(128)S(1)}, f32[32]{0:T(128)}, u32[]{:S(2)}) copy-start(f32[32]{0:T(128)} %param.6) | copy-start | bytes 388
  76.3 43.6 %copy-start.12 = (bf16[32,4,3,3,3]{0,1,4,3,2:T(4,128)(2,1)S(1)}, bf16[32,4,3,3,3]{0,1,4,3,2:T(4,128)(2,1)}, u32[]{:S(2)}) copy-start(bf16[32,4,3,3,3]{0,1,4,3,2:T(4,128)(2,1)} %param.5) | copy-start | bytes 20740
  93.0 28.0 %collective-permute-start.7 = (bf16[32,1,64,128]{3,0,2,1:T(8,128)(2,1)}, bf16[32,1,64,128]{3,0,2,1:T(8,128)(2,1)S(1)}, u32[]{:S(2)}, u32[]{:S(2)}) collective-permute-start(bf16[32,1,64,128]{3,0,2,1:T(8,128)(2,1)} %get-tuple-element.26), channel_id=1, source_target_pairs={{8,0},{16,8},{24,16},{32,24},{40,32},{48,40},{56,48},{64,56},{72,6... | collective-permute-start | bytes 1572872 | tf_op jit(solution)/shard_map/ppermute | solution.py:24
  96.0 25.0 %collective-permute-start.6 = (bf16[32,1,64,128]{3,0,2,1:T(8,128)(2,1)}, bf16[32,1,64,128]{3,0,2,1:T(8,128)(2,1)S(1)}, u32[]{:S(2)}, u32[]{:S(2)}) collective-permute-start(bf16[32,1,64,128]{3,0,2,1:T(8,128)(2,1)} %get-tuple-element.25), channel_id=1, source_target_pairs={{0,8},{8,16},{16,24},{24,32},{32,40},{40,48},{48,56},{56,64},{64,7... | collective-permute-start | bytes 1572872 | tf_op jit(solution)/shard_map/ppermute | solution.py:22
  121.0 5.6 %collective-permute-start.9 = (bf16[32,6,1,128]{3,0,2,1:T(8,128)(2,1)S(1)}, bf16[32,6,1,128]{3,0,2,1:T(8,128)(2,1)S(1)}, u32[]{:S(2)}, u32[]{:S(2)}) collective-permute-start(bf16[32,6,1,128]{3,0,2,1:T(8,128)(2,1)S(1)} %get-tuple-element.24), channel_id=1, source_target_pairs={{2,0},{4,2},{6,4},{0,6},{3,1},{5,3},{7,5},{1,7},{10,8},{12,10},{14... | collective-permute-start | bytes 147464 | tf_op jit(solution)/shard_map/ppermute | solution.py:24
  124.1 5.5 %collective-permute-start.8 = (bf16[32,6,1,128]{3,0,2,1:T(8,128)(2,1)S(1)}, bf16[32,6,1,128]{3,0,2,1:T(8,128)(2,1)S(1)}, u32[]{:S(2)}, u32[]{:S(2)}) collective-permute-start(bf16[32,6,1,128]{3,0,2,1:T(8,128)(2,1)S(1)} %get-tuple-element.23), channel_id=1, source_target_pairs={{0,2},{2,4},{4,6},{6,0},{1,3},{3,5},{5,7},{7,1},{8,10},{10,12},{12... | collective-permute-start | bytes 147464 | tf_op jit(solution)/shard_map/ppermute | solution.py:22
  139.1 14.1 %collective-permute-start.10 = (bf16[32,6,66,1]{2,0,3,1:T(8,128)(2,1)S(1)}, bf16[32,6,66,1]{2,0,3,1:T(8,128)(2,1)S(1)}, u32[]{:S(2)}, u32[]{:S(2)}) collective-permute-start(bf16[32,6,66,1]{2,0,3,1:T(8,128)(2,1)S(1)} %copy.79), channel_id=1, source_target_pairs={{0,1},{1,0},{2,3},{3,2},{4,5},{5,4},{6,7},{7,6},{8,9},{9,8},{10,11... | collective-permute-start | bytes 76040 | tf_op jit(solution)/shard_map/ppermute | solution.py:22
  144.9 14.3 %collective-permute-start.11 = (bf16[32,6,66,1]{2,0,3,1:T(8,128)(2,1)S(1)}, bf16[32,6,66,1]{2,0,3,1:T(8,128)(2,1)S(1)}, u32[]{:S(2)}, u32[]{:S(2)}) collective-permute-start(bf16[32,6,66,1]{2,0,3,1:T(8,128)(2,1)S(1)} %copy.81), channel_id=1, source_target_pairs={{1,0},{0,1},{3,2},{2,3},{5,4},{4,5},{7,6},{6,7},{9,8},{8,9},{11,10... | collective-permute-start | bytes 76040 | tf_op jit(solution)/shard_map/ppermute | solution.py:24
  181.3 3.4 %copy-start.2 = (f32[4,64,128,4]{2,3,1,0:T(4,128)S(1)}, f32[4,64,128,4]{2,3,1,0:T(4,128)}, u32[]{:S(2)}) copy-start(f32[4,64,128,4]{2,3,1,0:T(4,128)} %fusion.223) | copy-start | bytes 1572868
  181.3 3.4 %copy-start.4 = (f32[4,64,128,4]{2,3,1,0:T(4,128)S(1)}, f32[4,64,128,4]{2,3,1,0:T(4,128)}, u32[]{:S(2)}) copy-start(f32[4,64,128,4]{2,3,1,0:T(4,128)} %fusion.18) | copy-start | bytes 1572868
  181.3 3.4 %copy-start.8 = (f32[4,64,128,4]{2,3,1,0:T(4,128)S(1)}, f32[4,64,128,4]{2,3,1,0:T(4,128)}, u32[]{:S(2)}) copy-start(f32[4,64,128,4]{2,3,1,0:T(4,128)} %fusion.227) | copy-start | bytes 1572868
  181.3 3.4 %copy-start.9 = (f32[4,64,128,4]{2,3,1,0:T(4,128)S(1)}, f32[4,64,128,4]{2,3,1,0:T(4,128)}, u32[]{:S(2)}) copy-start(f32[4,64,128,4]{2,3,1,0:T(4,128)} %fusion.231) | copy-start | bytes 1572868
  181.3 3.4 %copy-start.10 = (f32[4,64,128,4]{2,3,1,0:T(4,128)S(1)}, f32[4,64,128,4]{2,3,1,0:T(4,128)}, u32[]{:S(2)}) copy-start(f32[4,64,128,4]{2,3,1,0:T(4,128)} %fusion.238) | copy-start | bytes 1572868
  183.8 1.9 copy-start.3
  183.8 1.9 copy-start.5
  (2 other events, 3.7 us)

commit v2 on v1

--- a/solution.py
+++ b/solution.py
@@ -119,9 +119,84 @@
     return leak_slope + (1.0 - leak_slope) * jax.nn.sigmoid(soft_scale * preact)
 
 
+def forward_kernel(chunk, w_ref, b_ref, p_ref, cot_ref, pooled_ref, delta_ref, wg_ref, bg_ref,
+                   pool_acc, wg_acc, bg_acc):
+    step = pl.program_id(0)
+    steps = pl.num_programs(0)
+    lanes = p_ref.shape[-1]
+
+    @pl.when(step == 0)
+    def _():
+        pool_acc[...] = jnp.zeros_like(pool_acc)
+        wg_acc[...] = jnp.zeros_like(wg_acc)
+        bg_acc[...] = jnp.zeros_like(bg_acc)
+
+    weight = w_ref[...]
+    bias = b_ref[...]
+
+    @pl.loop(0, lanes // chunk)
+    def _(q):
+        cols = pl.ds(pl.multiple_of(q * chunk, chunk), chunk)
+        patch = p_ref[0, :, cols]
+        preact = jnp.dot(weight, patch, preferred_element_type=jnp.float32) + bias
+        scaled = soft_scale * preact
+        e = jnp.exp(-jnp.abs(scaled))
+        softplus = jnp.maximum(scaled, 0.0) + jnp.log1p(e)
+        activated = leak_slope * preact + (1.0 - leak_slope) / soft_scale * softplus
+        pool_acc[:, cols] += activated
+        sigmoid = jnp.where(scaled >= 0.0, 1.0, e) / (1.0 + e)
+        slope = leak_slope + (1.0 - leak_slope) * sigmoid
+        delta = (slope * cot_ref[:, cols].astype(jnp.float32) * 0.125).astype(jnp.bfloat16)
+        delta_ref[0, :, cols] = delta
+        wg_acc[...] += lax.dot_general(
+            delta, patch, (((1,), (1,)), ((), ())), preferred_element_type=jnp.float32
+        )
+        bg_acc[...] += jnp.sum(delta.astype(jnp.float32), axis=1, keepdims=True)
+
+    @pl.when(step == steps - 1)
+    def _():
+        pooled_ref[...] = (pool_acc[...] * 0.125).astype(pooled_ref.dtype)
+        wg_ref[...] = wg_acc[...]
+        bg_ref[...] = bg_acc[...]
+
+
+def forward(weight_mat, bias, patches, cot):
+    parities, taps, lanes = patches.shape
+    chan_out = weight_mat.shape[0]
+    full = lambda shape: pl.BlockSpec(shape, lambda p: (0,) * len(shape))
+    return pl.pallas_call(
+        lambda *refs: forward_kernel(512, *refs),
+        grid=(parities,),
+        out_shape=(
+            jax.ShapeDtypeStruct((chan_out, lanes), jnp.bfloat16),
+            jax.ShapeDtypeStruct((parities, chan_out, lanes), jnp.bfloat16),
+            jax.ShapeDtypeStruct((chan_out, taps), jnp.float32),
+            jax.ShapeDtypeStruct((chan_out, 1), jnp.float32),
+        ),
+        in_specs=[
+            full((chan_out, taps)),
+            full((chan_out, 1)),
+            pl.BlockSpec((1, taps, lanes), lambda p: (p, 0, 0)),
+            full((chan_out, lanes)),
+        ],
+        out_specs=(
+            full((chan_out, lanes)),
+            pl.BlockSpec((1, chan_out, lanes), lambda p: (p, 0, 0)),
+            full((chan_out, taps)),
+            full((chan_out, 1)),
+        ),
+        scratch_shapes=[
+            pltpu.VMEM((chan_out, lanes), jnp.float32),
+            pltpu.VMEM((chan_out, taps), jnp.float32),
+            pltpu.VMEM((chan_out, 1), jnp.float32),
+        ],
+    )(weight_mat, bias, patches, cot)
+
+
 def on_device(cells, weight, bias, cotangent):
     chan_in, cells_x, cells_y, cells_z = cells.shape
     chan_out = weight.shape[0]
+    hx, hy, hz = cells_x // 2, cells_y // 2, cells_z // 2
     stencil = [
         (shift_a, shift_b, shift_e)
         for shift_a in range(3)
@@ -129,37 +204,39 @@
         for shift_e in range(3)
     ]
     widened = extended(cells, (("gx", 1), ("gy", 2), ("gz", 3)), 1)
+    subgrids = {}
+    for ox in range(4):
+        for oy in range(4):
+            for oz in range(4):
+                sub = widened[:, ox : ox + cells_x - 1 : 2, oy : oy + cells_y - 1 : 2, oz : oz + cells_z - 1 : 2]
+                subgrids[ox, oy, oz] = sub.reshape(chan_in, 1, hx * hy * hz)
     patches = jnp.stack(
         [
-            widened[:, sa : sa + cells_x, sb : sb + cells_y, se : se + cells_z]
-            for sa, sb, se in stencil
-        ],
-        axis=1,
-    )
-    patches = patches.reshape(chan_in * 27, cells_x, cells_y, cells_z)
+            jnp.concatenate(
+                [subgrids[px + sa, py + sb, pz + se] for sa, sb, se in stencil], axis=1
+            ).reshape(chan_in * 27, hx * hy * hz)
+            for px in range(2)
+            for py in range(2)
+            for pz in range(2)
+        ],
+        axis=0,
+    )
     weight_mat = weight.reshape(chan_out, chan_in * 27)
-    preact = (
-        jnp.einsum("ok,kxyz->oxyz", weight_mat, patches, preferred_element_type=jnp.float32)
-        + bias[:, None, None, None]
-    )
-    activated = activate(preact)
-    pooled = (
-        activated.reshape(chan_out, cells_x // 2, 2, cells_y // 2, 2, cells_z // 2, 2)
-        .mean(axis=(2, 4, 6))
-        .astype(jnp.bfloat16)
-    )
-    spread = jnp.broadcast_to(
-        cotangent.astype(jnp.float32)[:, :, None, :, None, :, None],
-        (chan_out, cells_x // 2, 2, cells_y // 2, 2, cells_z // 2, 2),
-    )
-    spread = spread.reshape(chan_out, cells_x, cells_y, cells_z)
-    delta = (slope_of(preact) * spread * 0.125).astype(jnp.bfloat16)
-    weight_local = jnp.einsum("oxyz,kxyz->ok", delta, patches, preferred_element_type=jnp.float32)
-    bias_local = jnp.sum(delta, axis=(1, 2, 3), dtype=jnp.float32)
+    cot = cotangent.reshape(chan_out, hx * hy * hz)
+    pooled, delta_par, weight_local, bias_local = forward(
+        weight_mat, bias.reshape(chan_out, 1), patches, cot
+    )
+    pooled = pooled.reshape(chan_out, hx, hy, hz)
+    delta = jnp.zeros((chan_out, cells_x, cells_y, cells_z), jnp.bfloat16)
+    for px in range(2):
+        for py in range(2):
+            for pz in range(2):
+                block = delta_par[px * 4 + py * 2 + pz].reshape(chan_out, hx, hy, hz)
+                delta = delta.at[:, px::2, py::2, pz::2].set(block)
     taps = chan_in * 27
     width = -(-(taps + 1) // 128) * 128
     partial = jnp.concatenate(
-        [weight_local, bias_local[:, None], jnp.zeros((chan_out, width - taps - 1), jnp.float32)],
+        [weight_local, bias_local, jnp.zeros((chan_out, width - taps - 1), jnp.float32)],
         axis=1,
     )
     sizes = tuple(lax.axis_size(a) for a in AXES)

time: 192 us -> 637 us (3.32)
  the two profiles are of different devices: /device:TPU:0 before, /device:TPU:7 now
where the time goes in v2:
time: 637 us; the launch traced here: 626 us
  local copies, waits for them, and re-layouts  511 us (80%)
  Pallas kernels  43.7 us (7%)
  matrix products  28 us (4%)
  starting transfers between devices  19.4 us (3%)
  other arithmetic  15.4 us (2%)
    slice x64, local copies, waits for them, and re-layouts, on_device(): widened[:, ox:ox + cells_x - 1:2, oy:oy + cells_y - 1:2, oz:oz + cells_z...  173 us
    unnamed x118, local copies, waits for them, and re-layouts  173 us
    concatenate x8, local copies, waits for them, and re-layouts, on_device(): jnp.concatenate([subgrids[px + sa, py + sb, pz + se] for sa, sb, se in st...  42.2 us
    reshape x64, local copies, waits for them, and re-layouts, on_device(): subgrids[ox, oy, oz] = sub.reshape(chan_in, 1, hx * hy * hz)  37.8 us
    another operation x16, local copies, waits for them, and re-layouts, on_device(): block = delta_par[px * 4 + py * 2 + pz].reshape(chan_out, hx, hy, hz)  29.5 us
    dot_general x27, matrix products, on_device(): jnp.einsum('oc,oxyz->cxyz', weight[:, :, 2 - sa, 2 - sb, 2 - se], window,...  28 us
    pallas_call x1, Pallas kernels, forward(): pl.pallas_call(lambda *refs: forward_kernel(512, *refs), grid=(parities,)...  22.9 us
    pallas_call x1, Pallas kernels, allreduce(): pl.pallas_call(lambda *refs: allreduce_kernel(sizes, *refs), out_shape=ja...  20.7 us
  transfers between devices with their start and end apart: 12, of which 1 were waited for; matrix products, arithmetic and copies ran while one was open for 20% of the time, Pallas kernels for 0%

profile of v2, /device:TPU:7, one launch (start us, length us, event | category | flops | bytes accessed | tf_op | source)
XLA Modules:
  0.0 625.5 jit_solution(10968489477147425293)
XLA Ops:
  238.2 5.0 concatenate.108
  244.4 5.0 concatenate.112
  250.6 5.7 concatenate.114
  257.5 5.0 concatenate.110
  263.7 5.7 concatenate.111
  270.7 5.0 concatenate.115
  277.0 5.9 concatenate.113
  282.9 5.0 concatenate.109
  303.4 22.9 %shard_map.75 = (bf16[32,4096]{1,0:T(8,128)(2,1)}, bf16[8,32,4096]{2,1,0:T(8,128)(2,1)}, f32[32,108]{1,0:T(8,128)}, f32[32,1]{1,0:T(8,128)}) custom-call(bf16[32,108]{1,0:T(8,128)(2,1)} %copy.690.refs_0_, f32[32,1]{1,0:T(8,128)} %copy.691.refs_1_, bf16[8,108,4096]{2,1,0:T(8,128)(2,1)} %constant_dynamic-update-slice_fusion.3.refs_2_, ...), custom_call_target="tpu_custom_call" | custom-call | tf_op jit(solution)/shard_map/pallas_call | solution.py:167
  327.7 20.7 %shard_map.76 = f32[32,128]{1,0:T(8,128)} custom-call(f32[32,128]{1,0:T(8,128)} %maximum_maximum_fusion.2.refs_0_), custom_call_target="tpu_custom_call" | custom-call | tf_op jit(solution)/shard_map/pallas_call | solution.py:90
  385.7 16.5 %scatter_custom_fusion = bf16[32,32768]{0,1:T(8,128)(2,1)} fusion(s32[4096]{0:T(1024)} %reshape.323, bf16[4096,32]{1,0:T(8,128)(2,1)} %bitcast.410, bf16[]{:T(256)} %constant.5.clone.1), kind=kCustom, calls=%fused_computation.10 | custom fusion | bytes 2097664
  402.2 19.5 %scatter_fusion = bf16[32,32768]{0,1:T(8,128)(2,1)} fusion(bf16[32,32768]{0,1:T(8,128)(2,1)} %scatter_custom_fusion, s32[4096]{0:T(1024)S(1)} %reshape.329, bf16[4096,32]{1,0:T(8,128)(2,1)} %bitcast.401), kind=kCustom, calls=%fused_computation.1 | custom fusion | bytes 802816
  421.6 19.6 %scatter_fusion.1 = bf16[32,32768]{0,1:T(8,128)(2,1)} fusion(bf16[32,32768]{0,1:T(8,128)(2,1)} %scatter_fusion, s32[4096]{0:T(1024)S(1)} %reshape.335, bf16[4096,32]{1,0:T(8,128)(2,1)} %bitcast.400), kind=kCustom, calls=%fused_computation.2 | custom fusion | bytes 802816
  441.3 19.5 %scatter_fusion.2 = bf16[32,32768]{0,1:T(8,128)(2,1)} fusion(bf16[32,32768]{0,1:T(8,128)(2,1)} %scatter_fusion.1, s32[4096]{0:T(1024)S(1)} %reshape.341, bf16[4096,32]{1,0:T(8,128)(2,1)} %bitcast.399), kind=kCustom, calls=%fused_computation.3 | custom fusion | bytes 802816
  460.7 19.7 %scatter_fusion.3 = bf16[32,32768]{0,1:T(8,128)(2,1)} fusion(bf16[32,32768]{0,1:T(8,128)(2,1)} %scatter_fusion.2, s32[4096]{0:T(1024)S(1)} %copy-done.40, bf16[4096,32]{1,0:T(8,128)(2,1)} %bitcast.398), kind=kCustom, calls=%fused_computation.4 | custom fusion | bytes 802816
  480.4 19.2 %scatter_fusion.4 = bf16[32,32768]{0,1:T(8,128)(2,1)} fusion(bf16[32,32768]{0,1:T(8,128)(2,1)} %scatter_fusion.3, s32[4096]{0:T(1024)S(1)} %copy-done.38, bf16[4096,32]{1,0:T(8,128)(2,1)S(1)} %bitcast.397), kind=kCustom, calls=%fused_computation.5 | custom fusion | bytes 802816
  499.6 19.6 %scatter_fusion.5 = bf16[32,32768]{0,1:T(8,128)(2,1)} fusion(bf16[32,32768]{0,1:T(8,128)(2,1)} %scatter_fusion.4, s32[4096]{0:T(1024)S(1)} %copy-done.39, bf16[4096,32]{1,0:T(8,128)(2,1)S(1)} %bitcast.396), kind=kCustom, calls=%fused_computation.6 | custom fusion | bytes 802816
  519.2 19.2 %scatter_fusion.6 = bf16[32,32768]{0,1:T(8,128)(2,1)} fusion(bf16[32,32768]{0,1:T(8,128)(2,1)} %scatter_fusion.5, s32[4096]{0:T(1024)S(1)} %copy-done.37, bf16[4096,32]{1,0:T(8,128)(2,1)S(1)} %bitcast.395), kind=kCustom, calls=%fused_computation.7 | custom fusion | bytes 802816
  538.3 6.9 %copy.702 = bf16[32,4,64,128]{3,0,2,1:T(8,128)(2,1)S(1)} copy(bf16[32,4,64,128]{0,3,2,1:T(8,128)(2,1)} %bitcast.393) | data formatting | bytes 4194304 | tf_op jit(solution)/shard_map/scatter | solution.py:235
  550.3 6.5 %fusion.213 = f32[4,64,128,4]{2,3,1,0:T(4,128)} fusion(bf16[32,4,64,128]{0,3,2,1:T(8,128)(2,1)} %bitcast.394, bf16[32,4,3,3,3]{0,1,4,3,2:T(4,128)(2,1)S(1)} %copy-done.41), kind=kOutput, calls=%fused_computation.196 | convolution fusion | flops 8388608 | bytes 2622464 | tf_op jit(solution)/shard_map/oc,oxyz->cxyz/dot_general | solution.py:250
  556.8 5.7 collective-permute-done.7
  590.7 6.0 copy.706
  596.7 6.0 copy.708
  602.7 9.5 %maximum_maximum_fusion = (bf16[32,6,66,129]{3,0,2,1:T(8,128)(2,1)S(1)}, bf16[32,6,66,129]{3,0,2,1:T(8,128)(2,1)S(1)}) fusion(bf16[32,6,1,128]{3,0,2,1:T(8,128)(2,1)S(1)} %collective-permute-done.9, bf16[32,1,64,128]{3,0,2,1:T(8,128)(2,1)S(1)} %collective-permute-done.7, bf16[32,4,64,128]{3,0,2,1:T(8,128)(2,1)S(1)} %copy.702, ...), kind=kLoop, calls=%fused_computation.8 | loop fusion | flops 39232512 | bytes 9833472 | tf_op jit(solution)/shard_map/concatenate | solution.py:20
  (354 shorter events, 344.5 us)
Async XLA Ops:
  0.6 62.4 %copy-start.36 = (bf16[32,2,32,64]{3,2,1,0:T(8,128)(2,1)S(1)}, bf16[32,2,32,64]{3,2,1,0:T(8,128)(2,1)}, u32[]{:S(2)}) copy-start(bf16[32,2,32,64]{3,2,1,0:T(8,128)(2,1)} %param.7) | copy-start | bytes 786436
  1.6 8.4 %collective-permute-start.1 = (bf16[4,1,64,128]{3,2,1,0:T(8,128)(2,1)S(1)}, bf16[4,1,64,128]{3,2,1,0:T(8,128)(2,1)S(1)}, u32[]{:S(2)}, u32[]{:S(2)}) collective-permute-start(bf16[4,1,64,128]{3,2,1,0:T(8,128)(2,1)S(1)} %get-tuple-element.60), channel_id=1, source_target_pairs={{8,0},{16,8},{24,16},{32,24},{40,32},{48,40},{56,48},{64,56},{72,6... | collective-permute-start | bytes 196616 | tf_op jit(solution)/shard_map/ppermute | solution.py:24
  2.3 6.7 %collective-permute-start = (bf16[4,1,64,128]{3,2,1,0:T(8,128)(2,1)S(1)}, bf16[4,1,64,128]{3,2,1,0:T(8,128)(2,1)S(1)}, u32[]{:S(2)}, u32[]{:S(2)}) collective-permute-start(bf16[4,1,64,128]{3,2,1,0:T(8,128)(2,1)S(1)} %get-tuple-element.61), channel_id=1, source_target_pairs={{0,8},{8,16},{16,24},{24,32},{32,40},{40,48},{48,56},{56,64},{64,7... | collective-permute-start | bytes 196616 | tf_op jit(solution)/shard_map/ppermute | solution.py:22
  10.1 45.5 %collective-permute-start.2 = (bf16[4,6,1,128]{3,2,1,0:T(2,128)(2,1)S(1)}, bf16[4,6,1,128]{3,2,1,0:T(2,128)(2,1)S(1)}, u32[]{:S(2)}, u32[]{:S(2)}) collective-permute-start(bf16[4,6,1,128]{3,2,1,0:T(2,128)(2,1)S(1)} %get-tuple-element.58), channel_id=1, source_target_pairs={{0,2},{2,4},{4,6},{6,0},{1,3},{3,5},{5,7},{7,1},{8,10},{10,12},{12... | collective-permute-start | bytes 18440 | tf_op jit(solution)/shard_map/ppermute | solution.py:22
  11.5 44.1 %collective-permute-start.3 = (bf16[4,6,1,128]{3,2,1,0:T(2,128)(2,1)S(1)}, bf16[4,6,1,128]{3,2,1,0:T(2,128)(2,1)S(1)}, u32[]{:S(2)}, u32[]{:S(2)}) collective-permute-start(bf16[4,6,1,128]{3,2,1,0:T(2,128)(2,1)S(1)} %get-tuple-element.59), channel_id=1, source_target_pairs={{2,0},{4,2},{6,4},{0,6},{3,1},{5,3},{7,5},{1,7},{10,8},{12,10},{14... | collective-permute-start | bytes 18440 | tf_op jit(solution)/shard_map/ppermute | solution.py:24
  57.9 61.2 %collective-permute-start.4 = (bf16[4,6,66,1]{3,2,1,0:T(8,128)(2,1)}, bf16[4,6,66,1]{3,2,1,0:T(8,128)(2,1)}, u32[]{:S(2)}, u32[]{:S(2)}) collective-permute-start(bf16[4,6,66,1]{3,2,1,0:T(8,128)(2,1)} %get-tuple-element.56), channel_id=1, source_target_pairs={{0,1},{1,0},{2,3},{3,2},{4,5},{5,4},{6,7},{7,6},{8,9},{9,8},{10,11... | collective-permute-start | bytes 9512 | tf_op jit(solution)/shard_map/ppermute | solution.py:22
  59.5 59.6 %collective-permute-start.5 = (bf16[4,6,66,1]{3,2,1,0:T(8,128)(2,1)S(1)}, bf16[4,6,66,1]{3,2,1,0:T(8,128)(2,1)}, u32[]{:S(2)}, u32[]{:S(2)}) collective-permute-start(bf16[4,6,66,1]{3,2,1,0:T(8,128)(2,1)S(1)} %get-tuple-element.57), channel_id=1, source_target_pairs={{1,0},{0,1},{3,2},{2,3},{5,4},{4,5},{7,6},{6,7},{9,8},{8,9},{11,10... | collective-permute-start | bytes 9512 | tf_op jit(solution)/shard_map/ppermute | solution.py:24
  81.2 182.5 %copy-start.5 = (bf16[4,1,4096]{2,1,0:T(2,128)(2,1)}, bf16[4,1,4096]{2,1,0:T(2,128)(2,1)S(1)}, u32[]{:S(2)}) copy-start(bf16[4,1,4096]{2,1,0:T(2,128)(2,1)S(1)} %reshape.413) | copy-start | bytes 98308
  81.3 182.4 %copy-start.7 = (bf16[4,1,4096]{2,1,0:T(2,128)(2,1)}, bf16[4,1,4096]{2,1,0:T(2,128)(2,1)S(1)}, u32[]{:S(2)}) copy-start(bf16[4,1,4096]{2,1,0:T(2,128)(2,1)S(1)} %reshape.412) | copy-start | bytes 98308
  81.5 182.2 %copy-start.9 = (bf16[4,1,4096]{2,1,0:T(2,128)(2,1)}, bf16[4,1,4096]{2,1,0:T(2,128)(2,1)S(1)}, u32[]{:S(2)}) copy-start(bf16[4,1,4096]{2,1,0:T(2,128)(2,1)S(1)} %reshape.410) | copy-start | bytes 98308
  81.6 182.1 %copy-start.11 = (bf16[4,1,4096]{2,1,0:T(2,128)(2,1)}, bf16[4,1,4096]{2,1,0:T(2,128)(2,1)S(1)}, u32[]{:S(2)}) copy-start(bf16[4,1,4096]{2,1,0:T(2,128)(2,1)S(1)} %reshape.409) | copy-start | bytes 98308
  115.9 161.0 %copy-start.13 = (bf16[4,1,4096]{2,1,0:T(2,128)(2,1)}, bf16[4,1,4096]{2,1,0:T(2,128)(2,1)S(1)}, u32[]{:S(2)}) copy-start(bf16[4,1,4096]{2,1,0:T(2,128)(2,1)S(1)} %reshape.425) | copy-start | bytes 98308
  116.0 160.9 %copy-start.14 = (bf16[4,1,4096]{2,1,0:T(2,128)(2,1)}, bf16[4,1,4096]{2,1,0:T(2,128)(2,1)S(1)}, u32[]{:S(2)}) copy-start(bf16[4,1,4096]{2,1,0:T(2,128)(2,1)S(1)} %reshape.424) | copy-start | bytes 98308
  116.1 160.8 %copy-start.15 = (bf16[4,1,4096]{2,1,0:T(2,128)(2,1)}, bf16[4,1,4096]{2,1,0:T(2,128)(2,1)S(1)}, u32[]{:S(2)}) copy-start(bf16[4,1,4096]{2,1,0:T(2,128)(2,1)S(1)} %reshape.416) | copy-start | bytes 98308
  116.2 160.7 %copy-start.16 = (bf16[4,1,4096]{2,1,0:T(2,128)(2,1)}, bf16[4,1,4096]{2,1,0:T(2,128)(2,1)S(1)}, u32[]{:S(2)}) copy-start(bf16[4,1,4096]{2,1,0:T(2,128)(2,1)S(1)} %reshape.415) | copy-start | bytes 98308
  220.3 30.3 %copy-start.23 = (bf16[4,1,4096]{2,1,0:T(2,128)(2,1)S(1)}, bf16[4,1,4096]{2,1,0:T(2,128)(2,1)}, u32[]{:S(2)}) copy-start(bf16[4,1,4096]{2,1,0:T(2,128)(2,1)} %reshape.461) | copy-start | bytes 98308
  220.3 30.3 %copy-start.24 = (bf16[4,1,4096]{2,1,0:T(2,128)(2,1)S(1)}, bf16[4,1,4096]{2,1,0:T(2,128)(2,1)}, u32[]{:S(2)}) copy-start(bf16[4,1,4096]{2,1,0:T(2,128)(2,1)} %reshape.460) | copy-start | bytes 98308
  300.3 26.0 %copy-start.44 = (f32[128]{0:T(128)S(1)}, f32[128]{0:T(128)}, u32[]{:S(2)}) copy-start(f32[128]{0:T(128)} %pad.58.clone) | copy-start | bytes 1540
  545.3 11.6 %collective-permute-start.6 = (bf16[32,1,64,128]{3,0,2,1:T(8,128)(2,1)S(1)}, bf16[32,1,64,128]{3,0,2,1:T(8,128)(2,1)S(1)}, u32[]{:S(2)}, u32[]{:S(2)}) collective-permute-start(bf16[32,1,64,128]{3,0,2,1:T(8,128)(2,1)S(1)} %get-tuple-element.46), channel_id=1, source_target_pairs={{0,8},{8,16},{16,24},{24,32},{32,40},{40,48},{48,56},{56,64},{64,7... | collective-permute-start | bytes 1572872 | tf_op jit(solution)/shard_map/ppermute | solution.py:22
  550.2 12.4 %collective-permute-start.7 = (bf16[32,1,64,128]{3,0,2,1:T(8,128)(2,1)S(1)}, bf16[32,1,64,128]{3,0,2,1:T(8,128)(2,1)S(1)}, u32[]{:S(2)}, u32[]{:S(2)}) collective-permute-start(bf16[32,1,64,128]{3,0,2,1:T(8,128)(2,1)S(1)} %get-tuple-element.47), channel_id=1, source_target_pairs={{8,0},{16,8},{24,16},{32,24},{40,32},{48,40},{56,48},{64,56},{72,6... | collective-permute-start | bytes 1572872 | tf_op jit(solution)/shard_map/ppermute | solution.py:24
  562.5 5.1 collective-permute-start.8
  562.8 4.8 collective-permute-start.9
  582.0 14.7 %collective-permute-start.11 = (bf16[32,6,66,1]{2,0,3,1:T(8,128)(2,1)S(1)}, bf16[32,6,66,1]{2,0,3,1:T(8,128)(2,1)S(1)}, u32[]{:S(2)}, u32[]{:S(2)}) collective-permute-start(bf16[32,6,66,1]{2,0,3,1:T(8,128)(2,1)S(1)} %copy.707), channel_id=1, source_target_pairs={{1,0},{0,1},{3,2},{2,3},{5,4},{4,5},{7,6},{6,7},{9,8},{8,9},{11,10... | collective-permute-start | bytes 76040 | tf_op jit(solution)/shard_map/ppermute | solution.py:24
  582.1 8.6 %collective-permute-start.10 = (bf16[32,6,66,1]{2,0,3,1:T(8,128)(2,1)S(1)}, bf16[32,6,66,1]{2,0,3,1:T(8,128)(2,1)S(1)}, u32[]{:S(2)}, u32[]{:S(2)}) collective-permute-start(bf16[32,6,66,1]{2,0,3,1:T(8,128)(2,1)S(1)} %copy.705), channel_id=1, source_target_pairs={{0,1},{1,0},{2,3},{3,2},{4,5},{5,4},{6,7},{7,6},{8,9},{9,8},{10,11... | collective-permute-start | bytes 76040 | tf_op jit(solution)/shard_map/ppermute | solution.py:22
  (33 other events, 329.5 us)

commit v3 on v1

--- a/solution.py
+++ b/solution.py
@@ -119,6 +119,104 @@
     return leak_slope + (1.0 - leak_slope) * jax.nn.sigmoid(soft_scale * preact)
 
 
+def forward_kernel(rows, w_ref, b_ref, q_ref, u_ref, p_ref, cot_ref,
+                   pooled_ref, delta_ref, wg_ref, bg_ref, wg_acc, bg_acc):
+    step = pl.program_id(0)
+    plane = p_ref.shape[-1] // 2
+    chunk = 4 * rows
+
+    @pl.when(step == 0)
+    def _():
+        wg_acc[...] = jnp.zeros_like(wg_acc)
+        bg_acc[...] = jnp.zeros_like(bg_acc)
+
+    weight = w_ref[...]
+    bias = b_ref[...]
+
+    @pl.loop(0, plane // chunk)
+    def _(j):
+        cot = cot_ref[:, pl.ds(pl.multiple_of(j * rows, rows), rows)]
+        up_lo = jnp.dot(cot, u_ref[0], preferred_element_type=jnp.float32) * 0.125
+        up_hi = jnp.dot(cot, u_ref[1], preferred_element_type=jnp.float32) * 0.125
+        spread = jnp.concatenate([up_lo, up_lo, up_hi, up_hi], axis=1)
+        total = None
+        for base in (0, plane):
+            cols = pl.ds(pl.multiple_of(base + j * chunk, chunk), chunk)
+            patch = p_ref[:, cols]
+            preact = jnp.dot(weight, patch, preferred_element_type=jnp.float32) + bias
+            scaled = soft_scale * preact
+            e = jnp.exp(-jnp.abs(scaled))
+            softplus = jnp.maximum(scaled, 0.0) + jnp.log1p(e)
+            activated = leak_slope * preact + (1.0 - leak_slope) / soft_scale * softplus
+            total = activated if total is None else total + activated
+            sigmoid = jnp.where(scaled >= 0.0, 1.0, e) / (1.0 + e)
+            slope = leak_slope + (1.0 - leak_slope) * sigmoid
+            delta = (slope * spread).astype(jnp.bfloat16)
+            delta_ref[:, cols] = delta
+            wg_acc[...] += lax.dot_general(
+                delta, patch, (((1,), (1,)), ((), ())), preferred_element_type=jnp.float32
+            )
+            bg_acc[...] += jnp.sum(delta.astype(jnp.float32), axis=1, keepdims=True)
+        pair_lo = total[:, 0:rows] + total[:, rows : 2 * rows]
+        pair_hi = total[:, 2 * rows : 3 * rows] + total[:, 3 * rows : 4 * rows]
+        pooled = jnp.dot(
+            pair_lo, q_ref[0], preferred_element_type=jnp.float32, precision=lax.Precision.HIGHEST
+        ) + jnp.dot(
+            pair_hi, q_ref[1], preferred_element_type=jnp.float32, precision=lax.Precision.HIGHEST
+        )
+        pooled_ref[:, pl.ds(pl.multiple_of(j * rows, rows), rows)] = (pooled * 0.125).astype(
+            pooled_ref.dtype
+        )
+
+    @pl.when(step == pl.num_programs(0) - 1)
+    def _():
+        wg_ref[...] = wg_acc[...]
+        bg_ref[...] = bg_acc[...]
+
+
+def forward(weight_mat, bias, patches, cot, rows, pairs):
+    taps, lanes = patches.shape
+    chan_out = weight_mat.shape[0]
+    half = rows // 2
+    z = jnp.arange(rows)
+    k = jnp.arange(rows)
+    pool = jnp.stack(
+        [(k[None, :] == z[:, None] // 2), (k[None, :] == half + z[:, None] // 2)]
+    ).astype(jnp.float32)
+    spread = jnp.stack(
+        [(z[None, :] // 2 == k[:, None]), (z[None, :] // 2 + half == k[:, None])]
+    ).astype(jnp.bfloat16)
+    full = lambda shape: pl.BlockSpec(shape, lambda p: (0,) * len(shape))
+    return pl.pallas_call(
+        lambda *refs: forward_kernel(rows, *refs),
+        grid=(pairs,),
+        out_shape=(
+            jax.ShapeDtypeStruct(cot.shape, jnp.bfloat16),
+            jax.ShapeDtypeStruct((chan_out, lanes), jnp.bfloat16),
+            jax.ShapeDtypeStruct((chan_out, taps), jnp.float32),
+            jax.ShapeDtypeStruct((chan_out, 1), jnp.float32),
+        ),
+        in_specs=[
+            full((chan_out, taps)),
+            full((chan_out, 1)),
+            full((2, rows, rows)),
+            full((2, rows, rows)),
+            pl.BlockSpec((taps, lanes // pairs), lambda p: (0, p)),
+            pl.BlockSpec((chan_out, cot.shape[1] // pairs), lambda p: (0, p)),
+        ],
+        out_specs=(
+            pl.BlockSpec((chan_out, cot.shape[1] // pairs), lambda p: (0, p)),
+            pl.BlockSpec((chan_out, lanes // pairs), lambda p: (0, p)),
+            full((chan_out, taps)),
+            full((chan_out, 1)),
+        ),
+        scratch_shapes=[
+            pltpu.VMEM((chan_out, taps), jnp.float32),
+            pltpu.VMEM((chan_out, 1), jnp.float32),
+        ],
+    )(weight_mat, bias, pool, spread, patches, cot)
+
+
 def on_device(cells, weight, bias, cotangent):
     chan_in, cells_x, cells_y, cells_z = cells.shape
     chan_out = weight.shape[0]
@@ -136,30 +234,18 @@
         ],
         axis=1,
     )
-    patches = patches.reshape(chan_in * 27, cells_x, cells_y, cells_z)
+    patches = patches.reshape(chan_in * 27, cells_x * cells_y * cells_z)
     weight_mat = weight.reshape(chan_out, chan_in * 27)
-    preact = (
-        jnp.einsum("ok,kxyz->oxyz", weight_mat, patches, preferred_element_type=jnp.float32)
-        + bias[:, None, None, None]
-    )
-    activated = activate(preact)
-    pooled = (
-        activated.reshape(chan_out, cells_x // 2, 2, cells_y // 2, 2, cells_z // 2, 2)
-        .mean(axis=(2, 4, 6))
-        .astype(jnp.bfloat16)
-    )
-    spread = jnp.broadcast_to(
-        cotangent.astype(jnp.float32)[:, :, None, :, None, :, None],
-        (chan_out, cells_x // 2, 2, cells_y // 2, 2, cells_z // 2, 2),
-    )
-    spread = spread.reshape(chan_out, cells_x, cells_y, cells_z)
-    delta = (slope_of(preact) * spread * 0.125).astype(jnp.bfloat16)
-    weight_local = jnp.einsum("oxyz,kxyz->ok", delta, patches, preferred_element_type=jnp.float32)
-    bias_local = jnp.sum(delta, axis=(1, 2, 3), dtype=jnp.float32)
+    cot = cotangent.reshape(chan_out, -1)
+    pooled, delta, weight_local, bias_local = forward(
+        weight_mat, bias.reshape(chan_out, 1), patches, cot, cells_z, cells_x // 2
+    )
+    pooled = pooled.reshape(cotangent.shape)
+    delta = delta.reshape(chan_out, cells_x, cells_y, cells_z)
     taps = chan_in * 27
     width = -(-(taps + 1) // 128) * 128
     partial = jnp.concatenate(
-        [weight_local, bias_local[:, None], jnp.zeros((chan_out, width - taps - 1), jnp.float32)],
+        [weight_local, bias_local, jnp.zeros((chan_out, width - taps - 1), jnp.float32)],
         axis=1,
     )
     sizes = tuple(lax.axis_size(a) for a in AXES)

time: 192 us -> 199 us (1.036)
  the two profiles are of different devices: /device:TPU:0 before, /device:TPU:7 now
where the time goes in v3:
time: 199 us; the launch traced here: 196 us
  local copies, waits for them, and re-layouts  65.1 us (33%)
  Pallas kernels  45 us (23%)
  starting transfers between devices  28.8 us (14%)
  matrix products  24.4 us (12%)
  waiting for transfers between devices  19.9 us (10%)
  other arithmetic  11.6 us (6%)
    pallas_call x1, Pallas kernels, forward(): pl.pallas_call(lambda *refs: forward_kernel(rows, *refs), grid=(pairs,),...  25.6 us
    dot_general x27, matrix products, on_device(): jnp.einsum('oc,oxyz->cxyz', weight[:, :, 2 - sa, 2 - sb, 2 - se], window,...  24.4 us
    ppermute x6, starting transfers between devices, extended(): lax.ppermute(head, axis, [((i + 1) % count, i) for i in range(count)])  19.8 us
    pallas_call x1, Pallas kernels, allreduce(): pl.pallas_call(lambda *refs: allreduce_kernel(sizes, *refs), out_shape=ja...  19.3 us
    reshape x1, local copies, waits for them, and re-layouts, on_device(): patches = patches.reshape(chan_in * 27, cells_x * cells_y * cells_z)  11.7 us
    unnamed x62, local copies, waits for them, and re-layouts  11.1 us
    ppermute x6, waiting for transfers between devices, extended(): lax.ppermute(tail, axis, [(i, (i + 1) % count) for i in range(count)])  11 us
    concatenate x4, other arithmetic, extended(): jnp.concatenate([lax.ppermute(tail, axis, [(i, (i + 1) % count) for i in...  9.26 us
  transfers between devices with their start and end apart: 12, of which 5 were waited for; matrix products, arithmetic and copies ran while one was open for 16% of the time, Pallas kernels for 10%

profile of v3, /device:TPU:7, one launch (start us, length us, event | category | flops | bytes accessed | tf_op | source)
XLA Modules:
  0.0 196.0 jit_solution(10731736579184885968)
XLA Ops:
  2.3 4.7 %collective-permute-start = (bf16[4,1,64,128]{3,2,1,0:T(8,128)(2,1)S(1)}, bf16[4,1,64,128]{3,2,1,0:T(8,128)(2,1)S(1)}, u32[]{:S(2)}, u32[]{:S(2)}) collective-permute-start(bf16[4,1,64,128]{3,2,1,0:T(8,128)(2,1)S(1)} %get-tuple-element.39), channel_id=1, source_target_pairs={{0,8},{8,16},{16,24},{24,32},{32,40},{40,48},{48,56},{56,64},{64,7... | collective-permute-start | bytes 196616 | tf_op jit(solution)/shard_map/ppermute | solution.py:22
  9.4 1.4 collective-permute-start.2
  10.8 1.5 collective-permute-start.3
  13.7 1.7 collective-permute-start.5
  19.4 2.2 %reshape.230.refs_5_ = bf16[32,4096]{1,0:T(8,128)(2,1)} reshape(bf16[32,2,32,64]{3,2,1,0:T(8,128)(2,1)} %param.7) | data formatting | bytes 524288 | tf_op jit(solution)/shard_map/reshape | solution.py:239
  21.7 4.5 %collective-permute-done.5 = bf16[4,6,66,1]{3,2,1,0:T(8,128)(2,1)S(1)} collective-permute-done((bf16[4,6,66,1]{3,2,1,0:T(8,128)(2,1)S(1)}, bf16[4,6,66,1]{3,2,1,0:T(8,128)(2,1)S(1)}, u32[]{:S(2)}, u32[]{:S(2)}) %collective-permute-start.5) | collective-permute-done | bytes 3200 | tf_op jit(solution)/shard_map/ppermute | solution.py:24
  26.1 8.8 %collective-permute-done.4 = bf16[4,6,66,1]{3,2,1,0:T(8,128)(2,1)S(1)} collective-permute-done((bf16[4,6,66,1]{3,2,1,0:T(8,128)(2,1)S(1)}, bf16[4,6,66,1]{3,2,1,0:T(8,128)(2,1)S(1)}, u32[]{:S(2)}, u32[]{:S(2)}) %collective-permute-start.4) | collective-permute-done | bytes 3200 | tf_op jit(solution)/shard_map/ppermute | solution.py:22
  40.0 4.8 %copy.33 = bf16[4,27,4,64,128]{4,3,2,1,0:T(8,128)(2,1)} copy(bf16[4,27,4,64,128]{4,3,2,0,1:T(8,128)(2,1)S(1)} %fusion.165) | data formatting | bytes 14155776 | tf_op jit(solution)/shard_map/stack | solution.py:230
  44.8 11.7 %reshape.229.refs_4_ = bf16[108,32768]{1,0:T(8,128)(2,1)} reshape(bf16[4,27,4,64,128]{4,3,2,1,0:T(8,128)(2,1)} %copy.33) | data formatting | bytes 14155776 | tf_op jit(solution)/shard_map/reshape | solution.py:237
  56.5 25.6 %shard_map.75 = (bf16[32,4096]{1,0:T(8,128)(2,1)}, bf16[32,32768]{1,0:T(8,128)(2,1)}, f32[32,108]{1,0:T(8,128)}, f32[32,1]{1,0:T(8,128)}) custom-call(bf16[32,108]{1,0:T(8,128)(2,1)} %copy.34.refs_0_, f32[32,1]{1,0:T(8,128)} %copy.35.refs_1_, f32[2,128,128]{2,1,0:T(8,128)} %get-tuple-element.44.refs_2_, bf16[2,128,128]{2,1,0:T(8,128)(2,1)} %get-tuple-element.45.refs_3_, ...), custom_call_target="tpu_custom_call" | custom-call | tf_op jit(solution)/shard_map/pallas_call | solution.py:190
  82.2 2.1 %copy.76 = bf16[4,8,256,128]{3,2,1,0:T(8,128)(2,1)S(1)} copy(bf16[4,8,256,128]{3,1,2,0:T(8,128)(2,1)} %bitcast.353) | data formatting | bytes 4194304
  89.9 19.3 %shard_map.76 = f32[32,128]{1,0:T(8,128)} custom-call(f32[32,128]{1,0:T(8,128)} %maximum_maximum_fusion.2.refs_0_), custom_call_target="tpu_custom_call" | custom-call | tf_op jit(solution)/shard_map/pallas_call | solution.py:90
  112.1 12.6 %collective-permute-start.7 = (bf16[32,1,64,128]{3,0,2,1:T(8,128)(2,1)S(1)}, bf16[32,1,64,128]{3,0,2,1:T(8,128)(2,1)S(1)}, u32[]{:S(2)}, u32[]{:S(2)}) collective-permute-start(bf16[32,1,64,128]{3,0,2,1:T(8,128)(2,1)S(1)} %get-tuple-element.30), channel_id=1, source_target_pairs={{8,0},{16,8},{24,16},{32,24},{40,32},{48,40},{56,48},{64,56},{72,6... | collective-permute-start | bytes 1572872 | tf_op jit(solution)/shard_map/ppermute | solution.py:24
  124.8 2.7 %fusion.204 = f32[4,64,128,4]{2,3,1,0:T(4,128)} fusion(bf16[32,4,3,3,3]{0,1,4,3,2:T(4,128)(2,1)} %param.5, bf16[32,4,64,128]{3,2,1,0:T(8,128)(2,1)S(1)} %bitcast.351), kind=kOutput, calls=%fused_computation.190 | convolution fusion | flops 8388608 | bytes 2622464 | tf_op jit(solution)/shard_map/oc,oxyz->cxyz/dot_general | solution.py:259
  127.5 1.4 slice_reduce_fusion
  128.9 1.5 constant_dynamic-update-slice_fusion.4
  130.4 4.4 %collective-permute-done.7 = bf16[32,1,64,128]{3,0,2,1:T(8,128)(2,1)S(1)} collective-permute-done((bf16[32,1,64,128]{3,0,2,1:T(8,128)(2,1)S(1)}, bf16[32,1,64,128]{3,0,2,1:T(8,128)(2,1)S(1)}, u32[]{:S(2)}, u32[]{:S(2)}) %collective-permute-start.7) | collective-permute-done | bytes 524320 | tf_op jit(solution)/shard_map/ppermute | solution.py:24
  135.3 2.4 %collective-permute-start.9 = (bf16[32,6,1,128]{3,0,2,1:T(8,128)(2,1)S(1)}, bf16[32,6,1,128]{3,0,2,1:T(8,128)(2,1)S(1)}, u32[]{:S(2)}, u32[]{:S(2)}) collective-permute-start(bf16[32,6,1,128]{3,0,2,1:T(8,128)(2,1)S(1)} %get-tuple-element.29), channel_id=1, source_target_pairs={{2,0},{4,2},{6,4},{0,6},{3,1},{5,3},{7,5},{1,7},{10,8},{12,10},{14... | collective-permute-start | bytes 147464 | tf_op jit(solution)/shard_map/ppermute | solution.py:24
  140.5 4.2 %fusion.255 = (bf16[32,6,66,1]{3,0,2,1:T(8,128)(2,1)}, bf16[32,6,66,1]{3,0,2,1:T(8,128)(2,1)}) fusion(bf16[32,6,66,128]{3,0,2,1:T(8,128)(2,1)S(1)} %pad_maximum_fusion.1), kind=kLoop, calls=%fused_computation.245 | loop fusion | bytes 101376 | tf_op jit(solution)/shard_map/slice | solution.py:19
  144.7 4.9 %copy.40 = bf16[32,6,66,1]{2,0,3,1:T(8,128)(2,1)S(1)} copy(bf16[32,6,66,1]{3,0,2,1:T(8,128)(2,1)} %get-tuple-element.26) | data formatting | bytes 50688 | tf_op jit(solution)/shard_map/slice | solution.py:19
  149.6 4.8 %copy.42 = bf16[32,6,66,1]{2,0,3,1:T(8,128)(2,1)S(1)} copy(bf16[32,6,66,1]{3,0,2,1:T(8,128)(2,1)} %get-tuple-element.27) | data formatting | bytes 50688 | tf_op jit(solution)/shard_map/slice | solution.py:18
  163.1 6.0 %copy.41 = bf16[32,6,66,1]{3,0,2,1:T(8,128)(2,1)} copy(bf16[32,6,66,1]{2,0,3,1:T(8,128)(2,1)S(1)} %collective-permute-done.10) | data formatting | bytes 50688 | tf_op jit(solution)/shard_map/ppermute | solution.py:22
  169.2 6.0 %copy.43 = bf16[32,6,66,1]{3,0,2,1:T(8,128)(2,1)} copy(bf16[32,6,66,1]{2,0,3,1:T(8,128)(2,1)S(1)} %collective-permute-done.11) | data formatting | bytes 50688 | tf_op jit(solution)/shard_map/ppermute | solution.py:24
  175.2 7.6 %maximum_maximum_fusion = (bf16[32,6,66,129]{3,0,2,1:T(8,128)(2,1)S(1)}, bf16[32,6,66,129]{3,0,2,1:T(8,128)(2,1)S(1)}) fusion(bf16[32,6,1,128]{3,0,2,1:T(8,128)(2,1)S(1)} %collective-permute-done.9, bf16[32,6,64,128]{3,0,2,1:T(8,128)(2,1)S(1)} %copy-done.1, bf16[32,6,1,128]{3,0,2,1:T(8,128)(2,1)S(1)} %collective-permute-done.8, ...), kind=kLoop, calls=%fused_computation | loop fusion | flops 26155008 | bytes 9833472 | tf_op jit(solution)/shard_map/concatenate | solution.py:20
  (135 shorter events, 47.7 us)
Async XLA Ops:
  0.6 35.9 %copy-start.2 = (bf16[4,4,64,128]{3,2,1,0:T(8,128)(2,1)S(1)}, bf16[4,4,64,128]{3,2,1,0:T(8,128)(2,1)}, u32[]{:S(2)}) copy-start(bf16[4,4,64,128]{3,2,1,0:T(8,128)(2,1)} %param.4) | copy-start | bytes 786436
  1.6 7.8 %collective-permute-start.1 = (bf16[4,1,64,128]{3,2,1,0:T(8,128)(2,1)S(1)}, bf16[4,1,64,128]{3,2,1,0:T(8,128)(2,1)S(1)}, u32[]{:S(2)}, u32[]{:S(2)}) collective-permute-start(bf16[4,1,64,128]{3,2,1,0:T(8,128)(2,1)S(1)} %get-tuple-element.38), channel_id=1, source_target_pairs={{8,0},{16,8},{24,16},{32,24},{40,32},{48,40},{56,48},{64,56},{72,6... | collective-permute-start | bytes 196616 | tf_op jit(solution)/shard_map/ppermute | solution.py:24
  2.3 6.0 %collective-permute-start = (bf16[4,1,64,128]{3,2,1,0:T(8,128)(2,1)S(1)}, bf16[4,1,64,128]{3,2,1,0:T(8,128)(2,1)S(1)}, u32[]{:S(2)}, u32[]{:S(2)}) collective-permute-start(bf16[4,1,64,128]{3,2,1,0:T(8,128)(2,1)S(1)} %get-tuple-element.39), channel_id=1, source_target_pairs={{0,8},{8,16},{16,24},{24,32},{32,40},{40,48},{48,56},{56,64},{64,7... | collective-permute-start | bytes 196616 | tf_op jit(solution)/shard_map/ppermute | solution.py:22
  9.4 3.9 %collective-permute-start.2 = (bf16[4,6,1,128]{3,2,1,0:T(2,128)(2,1)S(1)}, bf16[4,6,1,128]{3,2,1,0:T(2,128)(2,1)S(1)}, u32[]{:S(2)}, u32[]{:S(2)}) collective-permute-start(bf16[4,6,1,128]{3,2,1,0:T(2,128)(2,1)S(1)} %get-tuple-element.36), channel_id=1, source_target_pairs={{0,2},{2,4},{4,6},{6,0},{1,3},{3,5},{5,7},{7,1},{8,10},{10,12},{12... | collective-permute-start | bytes 18440 | tf_op jit(solution)/shard_map/ppermute | solution.py:22
  10.8 2.5 %collective-permute-start.3 = (bf16[4,6,1,128]{3,2,1,0:T(2,128)(2,1)S(1)}, bf16[4,6,1,128]{3,2,1,0:T(2,128)(2,1)S(1)}, u32[]{:S(2)}, u32[]{:S(2)}) collective-permute-start(bf16[4,6,1,128]{3,2,1,0:T(2,128)(2,1)S(1)} %get-tuple-element.37), channel_id=1, source_target_pairs={{2,0},{4,2},{6,4},{0,6},{3,1},{5,3},{7,5},{1,7},{10,8},{12,10},{14... | collective-permute-start | bytes 18440 | tf_op jit(solution)/shard_map/ppermute | solution.py:24
  13.7 12.4 %collective-permute-start.5 = (bf16[4,6,66,1]{3,2,1,0:T(8,128)(2,1)S(1)}, bf16[4,6,66,1]{3,2,1,0:T(8,128)(2,1)S(1)}, u32[]{:S(2)}, u32[]{:S(2)}) collective-permute-start(bf16[4,6,66,1]{3,2,1,0:T(8,128)(2,1)S(1)} %get-tuple-element.32), channel_id=1, source_target_pairs={{1,0},{0,1},{3,2},{2,3},{5,4},{4,5},{7,6},{6,7},{9,8},{8,9},{11,10... | collective-permute-start | bytes 9512 | tf_op jit(solution)/shard_map/ppermute | solution.py:24
  15.4 19.6 %collective-permute-start.4 = (bf16[4,6,66,1]{3,2,1,0:T(8,128)(2,1)S(1)}, bf16[4,6,66,1]{3,2,1,0:T(8,128)(2,1)S(1)}, u32[]{:S(2)}, u32[]{:S(2)}) collective-permute-start(bf16[4,6,66,1]{3,2,1,0:T(8,128)(2,1)S(1)} %get-tuple-element.33), channel_id=1, source_target_pairs={{0,1},{1,0},{2,3},{3,2},{4,5},{5,4},{6,7},{7,6},{8,9},{9,8},{10,11... | collective-permute-start | bytes 9512 | tf_op jit(solution)/shard_map/ppermute | solution.py:22
  82.1 7.1 %copy-start.16 = (f32[32,108]{1,0:T(8,128)S(1)}, f32[32,108]{1,0:T(8,128)}, u32[]{:S(2)}) copy-start(f32[32,108]{1,0:T(8,128)} %get-tuple-element.9) | copy-start | bytes 41476
  82.2 7.1 %copy-start.17 = (f32[32,1]{1,0:T(8,128)S(1)}, f32[32,1]{1,0:T(8,128)}, u32[]{:S(2)}) copy-start(f32[32,1]{1,0:T(8,128)} %get-tuple-element.10) | copy-start | bytes 388
  82.2 28.6 %copy-start.14 = (bf16[32,4096]{1,0:T(8,128)(2,1)S(1)}, bf16[32,4096]{1,0:T(8,128)(2,1)}, u32[]{:S(2)}) copy-start(bf16[32,4096]{1,0:T(8,128)(2,1)} %get-tuple-element.8) | copy-start | bytes 786436
  87.9 41.0 %collective-permute-start.6 = (bf16[32,1,64,128]{3,0,2,1:T(8,128)(2,1)}, bf16[32,1,64,128]{3,0,2,1:T(8,128)(2,1)S(1)}, u32[]{:S(2)}, u32[]{:S(2)}) collective-permute-start(bf16[32,1,64,128]{3,0,2,1:T(8,128)(2,1)} %get-tuple-element.31), channel_id=1, source_target_pairs={{0,8},{8,16},{16,24},{24,32},{32,40},{40,48},{48,56},{56,64},{64,7... | collective-permute-start | bytes 1572872 | tf_op jit(solution)/shard_map/ppermute | solution.py:22
  110.1 27.6 %copy-start.15 = (bf16[32,4,3,3,3]{0,1,4,3,2:T(4,128)(2,1)S(1)}, bf16[32,4,3,3,3]{0,1,4,3,2:T(4,128)(2,1)}, u32[]{:S(2)}) copy-start(bf16[32,4,3,3,3]{0,1,4,3,2:T(4,128)(2,1)} %param.5) | copy-start | bytes 20740
  112.1 25.6 %copy-start.4 = (bf16[32,4,64,128]{3,0,2,1:T(8,128)(2,1)S(1)}, bf16[32,4,64,128]{3,0,2,1:T(8,128)(2,1)}, u32[]{:S(2)}) copy-start(bf16[32,4,64,128]{3,0,2,1:T(8,128)(2,1)} %copy-done.3) | copy-start | bytes 6291460
  112.1 22.7 %collective-permute-start.7 = (bf16[32,1,64,128]{3,0,2,1:T(8,128)(2,1)S(1)}, bf16[32,1,64,128]{3,0,2,1:T(8,128)(2,1)S(1)}, u32[]{:S(2)}, u32[]{:S(2)}) collective-permute-start(bf16[32,1,64,128]{3,0,2,1:T(8,128)(2,1)S(1)} %get-tuple-element.30), channel_id=1, source_target_pairs={{8,0},{16,8},{24,16},{32,24},{40,32},{48,40},{56,48},{64,56},{72,6... | collective-permute-start | bytes 1572872 | tf_op jit(solution)/shard_map/ppermute | solution.py:24
  134.9 5.2 %copy-start = (bf16[32,6,64,128]{3,0,2,1:T(8,128)(2,1)}, bf16[32,6,64,128]{3,0,2,1:T(8,128)(2,1)S(1)}, u32[]{:S(2)}) copy-start(bf16[32,6,64,128]{3,0,2,1:T(8,128)(2,1)S(1)} %constant_dynamic-update-slice_fusion.3) | copy-start | bytes 9437188
  135.0 5.1 %collective-permute-start.8 = (bf16[32,6,1,128]{3,0,2,1:T(8,128)(2,1)S(1)}, bf16[32,6,1,128]{3,0,2,1:T(8,128)(2,1)S(1)}, u32[]{:S(2)}, u32[]{:S(2)}) collective-permute-start(bf16[32,6,1,128]{3,0,2,1:T(8,128)(2,1)S(1)} %get-tuple-element.28), channel_id=1, source_target_pairs={{0,2},{2,4},{4,6},{6,0},{1,3},{3,5},{5,7},{7,1},{8,10},{10,12},{12... | collective-permute-start | bytes 147464 | tf_op jit(solution)/shard_map/ppermute | solution.py:22
  135.3 4.8 %collective-permute-start.9 = (bf16[32,6,1,128]{3,0,2,1:T(8,128)(2,1)S(1)}, bf16[32,6,1,128]{3,0,2,1:T(8,128)(2,1)S(1)}, u32[]{:S(2)}, u32[]{:S(2)}) collective-permute-start(bf16[32,6,1,128]{3,0,2,1:T(8,128)(2,1)S(1)} %get-tuple-element.29), channel_id=1, source_target_pairs={{2,0},{4,2},{6,4},{0,6},{3,1},{5,3},{7,5},{1,7},{10,8},{12,10},{14... | collective-permute-start | bytes 147464 | tf_op jit(solution)/shard_map/ppermute | solution.py:24
  144.7 11.2 %copy-start.1 = (bf16[32,6,64,128]{3,0,2,1:T(8,128)(2,1)S(1)}, bf16[32,6,64,128]{3,0,2,1:T(8,128)(2,1)}, u32[]{:S(2)}) copy-start(bf16[32,6,64,128]{3,0,2,1:T(8,128)(2,1)} %copy-done) | copy-start | bytes 9437188
  154.4 14.8 %collective-permute-start.11 = (bf16[32,6,66,1]{2,0,3,1:T(8,128)(2,1)S(1)}, bf16[32,6,66,1]{2,0,3,1:T(8,128)(2,1)S(1)}, u32[]{:S(2)}, u32[]{:S(2)}) collective-permute-start(bf16[32,6,66,1]{2,0,3,1:T(8,128)(2,1)S(1)} %copy.42), channel_id=1, source_target_pairs={{1,0},{0,1},{3,2},{2,3},{5,4},{4,5},{7,6},{6,7},{9,8},{8,9},{11,10... | collective-permute-start | bytes 76040 | tf_op jit(solution)/shard_map/ppermute | solution.py:24
  155.2 8.0 %collective-permute-start.10 = (bf16[32,6,66,1]{2,0,3,1:T(8,128)(2,1)S(1)}, bf16[32,6,66,1]{2,0,3,1:T(8,128)(2,1)S(1)}, u32[]{:S(2)}, u32[]{:S(2)}) collective-permute-start(bf16[32,6,66,1]{2,0,3,1:T(8,128)(2,1)S(1)} %copy.40), channel_id=1, source_target_pairs={{0,1},{1,0},{2,3},{3,2},{4,5},{5,4},{6,7},{7,6},{8,9},{9,8},{10,11... | collective-permute-start | bytes 76040 | tf_op jit(solution)/shard_map/ppermute | solution.py:22
  188.4 4.2 %copy-start.7 = (f32[4,64,128,4]{2,3,1,0:T(4,128)S(1)}, f32[4,64,128,4]{2,3,1,0:T(4,128)}, u32[]{:S(2)}) copy-start(f32[4,64,128,4]{2,3,1,0:T(4,128)} %fusion) | copy-start | bytes 1572868
  188.4 4.2 %copy-start.11 = (f32[4,64,128,4]{2,3,1,0:T(4,128)S(1)}, f32[4,64,128,4]{2,3,1,0:T(4,128)}, u32[]{:S(2)}) copy-start(f32[4,64,128,4]{2,3,1,0:T(4,128)} %fusion.150) | copy-start | bytes 1572868
  188.4 4.2 %copy-start.12 = (f32[4,64,128,4]{2,3,1,0:T(4,128)S(1)}, f32[4,64,128,4]{2,3,1,0:T(4,128)}, u32[]{:S(2)}) copy-start(f32[4,64,128,4]{2,3,1,0:T(4,128)} %fusion.151) | copy-start | bytes 1572868
  188.4 4.2 %copy-start.13 = (f32[4,64,128,4]{2,3,1,0:T(4,128)S(1)}, f32[4,64,128,4]{2,3,1,0:T(4,128)}, u32[]{:S(2)}) copy-start(f32[4,64,128,4]{2,3,1,0:T(4,128)} %fusion.152) | copy-start | bytes 1572868
  (6 other events, 12.9 us)

commit v4 on v3

--- a/solution.py
+++ b/solution.py
@@ -122,8 +122,7 @@
 def forward_kernel(rows, w_ref, b_ref, q_ref, u_ref, p_ref, cot_ref,
                    pooled_ref, delta_ref, wg_ref, bg_ref, wg_acc, bg_acc):
     step = pl.program_id(0)
-    plane = p_ref.shape[-1] // 2
-    chunk = 4 * rows
+    plane = p_ref.shape[0] // 2
 
     @pl.when(step == 0)
     def _():
@@ -133,36 +132,43 @@
     weight = w_ref[...]
     bias = b_ref[...]
 
-    @pl.loop(0, plane // chunk)
+    @pl.loop(0, plane // 4)
     def _(j):
         cot = cot_ref[:, pl.ds(pl.multiple_of(j * rows, rows), rows)]
-        up_lo = jnp.dot(cot, u_ref[0], preferred_element_type=jnp.float32) * 0.125
-        up_hi = jnp.dot(cot, u_ref[1], preferred_element_type=jnp.float32) * 0.125
-        spread = jnp.concatenate([up_lo, up_lo, up_hi, up_hi], axis=1)
-        total = None
+        ups = (
+            jnp.dot(cot, u_ref[0], preferred_element_type=jnp.float32) * 0.125,
+            jnp.dot(cot, u_ref[1], preferred_element_type=jnp.float32) * 0.125,
+        )
+        totals = [None, None]
+        wg = None
+        bg = None
         for base in (0, plane):
-            cols = pl.ds(pl.multiple_of(base + j * chunk, chunk), chunk)
-            patch = p_ref[:, cols]
-            preact = jnp.dot(weight, patch, preferred_element_type=jnp.float32) + bias
-            scaled = soft_scale * preact
-            e = jnp.exp(-jnp.abs(scaled))
-            softplus = jnp.maximum(scaled, 0.0) + jnp.log1p(e)
-            activated = leak_slope * preact + (1.0 - leak_slope) / soft_scale * softplus
-            total = activated if total is None else total + activated
-            sigmoid = jnp.where(scaled >= 0.0, 1.0, e) / (1.0 + e)
-            slope = leak_slope + (1.0 - leak_slope) * sigmoid
-            delta = (slope * spread).astype(jnp.bfloat16)
-            delta_ref[:, cols] = delta
-            wg_acc[...] += lax.dot_general(
-                delta, patch, (((1,), (1,)), ((), ())), preferred_element_type=jnp.float32
-            )
-            bg_acc[...] += jnp.sum(delta.astype(jnp.float32), axis=1, keepdims=True)
-        pair_lo = total[:, 0:rows] + total[:, rows : 2 * rows]
-        pair_hi = total[:, 2 * rows : 3 * rows] + total[:, 3 * rows : 4 * rows]
+            for r in range(4):
+                row = base + j * 4 + r
+                patch = p_ref[row]
+                preact = jnp.dot(weight, patch, preferred_element_type=jnp.float32) + bias
+                scaled = soft_scale * preact
+                e = jnp.exp(-jnp.abs(scaled))
+                softplus = jnp.maximum(scaled, 0.0) + jnp.log1p(e)
+                activated = leak_slope * preact + (1.0 - leak_slope) / soft_scale * softplus
+                half = r // 2
+                totals[half] = activated if totals[half] is None else totals[half] + activated
+                sigmoid = jnp.where(scaled >= 0.0, 1.0, e) / (1.0 + e)
+                slope = leak_slope + (1.0 - leak_slope) * sigmoid
+                delta = (slope * ups[half]).astype(jnp.bfloat16)
+                delta_ref[row] = delta
+                term = lax.dot_general(
+                    delta, patch, (((1,), (1,)), ((), ())), preferred_element_type=jnp.float32
+                )
+                wg = term if wg is None else wg + term
+                part = delta.astype(jnp.float32)
+                bg = part if bg is None else bg + part
+        wg_acc[...] += wg
+        bg_acc[...] += jnp.sum(bg, axis=1, keepdims=True)
         pooled = jnp.dot(
-            pair_lo, q_ref[0], preferred_element_type=jnp.float32, precision=lax.Precision.HIGHEST
+            totals[0], q_ref[0], preferred_element_type=jnp.float32, precision=lax.Precision.HIGHEST
         ) + jnp.dot(
-            pair_hi, q_ref[1], preferred_element_type=jnp.float32, precision=lax.Precision.HIGHEST
+            totals[1], q_ref[1], preferred_element_type=jnp.float32, precision=lax.Precision.HIGHEST
         )
         pooled_ref[:, pl.ds(pl.multiple_of(j * rows, rows), rows)] = (pooled * 0.125).astype(
             pooled_ref.dtype
@@ -174,8 +180,8 @@
         bg_ref[...] = bg_acc[...]
 
 
-def forward(weight_mat, bias, patches, cot, rows, pairs):
-    taps, lanes = patches.shape
+def forward(weight_mat, bias, patches, cot, pairs):
+    lines, taps, rows = patches.shape
     chan_out = weight_mat.shape[0]
     half = rows // 2
     z = jnp.arange(rows)
@@ -187,12 +193,13 @@
         [(z[None, :] // 2 == k[:, None]), (z[None, :] // 2 + half == k[:, None])]
     ).astype(jnp.bfloat16)
     full = lambda shape: pl.BlockSpec(shape, lambda p: (0,) * len(shape))
+    block = lines // pairs
     return pl.pallas_call(
         lambda *refs: forward_kernel(rows, *refs),
         grid=(pairs,),
         out_shape=(
             jax.ShapeDtypeStruct(cot.shape, jnp.bfloat16),
-            jax.ShapeDtypeStruct((chan_out, lanes), jnp.bfloat16),
+            jax.ShapeDtypeStruct((lines, chan_out, rows), jnp.bfloat16),
             jax.ShapeDtypeStruct((chan_out, taps), jnp.float32),
             jax.ShapeDtypeStruct((chan_out, 1), jnp.float32),
         ),
@@ -201,12 +208,12 @@
             full((chan_out, 1)),
             full((2, rows, rows)),
             full((2, rows, rows)),
-            pl.BlockSpec((taps, lanes // pairs), lambda p: (0, p)),
+            pl.BlockSpec((block, taps, rows), lambda p: (p, 0, 0)),
             pl.BlockSpec((chan_out, cot.shape[1] // pairs), lambda p: (0, p)),
         ],
         out_specs=(
             pl.BlockSpec((chan_out, cot.shape[1] // pairs), lambda p: (0, p)),
-            pl.BlockSpec((chan_out, lanes // pairs), lambda p: (0, p)),
+            pl.BlockSpec((block, chan_out, rows), lambda p: (p, 0, 0)),
             full((chan_out, taps)),
             full((chan_out, 1)),
         ),
@@ -229,19 +236,21 @@
     widened = extended(cells, (("gx", 1), ("gy", 2), ("gz", 3)), 1)
     patches = jnp.stack(
         [
-            widened[:, sa : sa + cells_x, sb : sb + cells_y, se : se + cells_z]
+            jnp.transpose(
+                widened[:, sa : sa + cells_x, sb : sb + cells_y, se : se + cells_z], (1, 2, 0, 3)
+            )
             for sa, sb, se in stencil
         ],
-        axis=1,
-    )
-    patches = patches.reshape(chan_in * 27, cells_x * cells_y * cells_z)
+        axis=3,
+    )
+    patches = patches.reshape(cells_x * cells_y, chan_in * 27, cells_z)
     weight_mat = weight.reshape(chan_out, chan_in * 27)
     cot = cotangent.reshape(chan_out, -1)
     pooled, delta, weight_local, bias_local = forward(
-        weight_mat, bias.reshape(chan_out, 1), patches, cot, cells_z, cells_x // 2
+        weight_mat, bias.reshape(chan_out, 1), patches, cot, cells_x // 2
     )
     pooled = pooled.reshape(cotangent.shape)
-    delta = delta.reshape(chan_out, cells_x, cells_y, cells_z)
+    delta = jnp.transpose(delta.reshape(cells_x, cells_y, chan_out, cells_z), (2, 0, 1, 3))
     taps = chan_in * 27
     width = -(-(taps + 1) // 128) * 128
     partial = jnp.concatenate(

time: 199 us -> 174 us (0.87)
  the two profiles are of different devices: /device:TPU:7 before, /device:TPU:6 now
where the time goes in v4:
time: 174 us; the launch traced here: 171 us
  local copies, waits for them, and re-layouts  51.9 us (30%)
  Pallas kernels  47.5 us (27%)
  matrix products  24.3 us (14%)
  starting transfers between devices  17.2 us (10%)
  other arithmetic  14.5 us (8%)
  waiting for transfers between devices  13.9 us (8%)
    pallas_call x1, Pallas kernels, allreduce(): pl.pallas_call(lambda *refs: allreduce_kernel(sizes, *refs), out_shape=ja...  25.4 us
    dot_general x27, matrix products, on_device(): jnp.einsum('oc,oxyz->cxyz', weight[:, :, 2 - sa, 2 - sb, 2 - se], window,...  24.3 us
    pallas_call x1, Pallas kernels, forward(): pl.pallas_call(lambda *refs: forward_kernel(rows, *refs), grid=(pairs,),...  22.1 us
    concatenate x4, other arithmetic, extended(): jnp.concatenate([lax.ppermute(tail, axis, [(i, (i + 1) % count) for i in...  11.5 us
    slice x4, local copies, waits for them, and re-layouts, extended(): lax.slice_in_dim(cells, cells.shape[dim] - width, cells.shape[dim], axis=...  11.3 us
    ppermute x6, waiting for transfers between devices, extended(): lax.ppermute(head, axis, [((i + 1) % count, i) for i in range(count)])  9.86 us
    ppermute x6, starting transfers between devices, extended(): lax.ppermute(tail, axis, [(i, (i + 1) % count) for i in range(count)])  9.4 us
    ppermute x6, starting transfers between devices, extended(): lax.ppermute(head, axis, [((i + 1) % count, i) for i in range(count)])  7.85 us
  transfers between devices with their start and end apart: 12, of which 5 were waited for; matrix products, arithmetic and copies ran while one was open for 21% of the time, Pallas kernels for 15%

profile of v4, /device:TPU:6, one launch (start us, length us, event | category | flops | bytes accessed | tf_op | source)
XLA Modules:
  0.0 170.7 jit_solution(15184310970186280123)
XLA Ops:
  1.7 1.7 %collective-permute-start.1 = (bf16[4,1,64,128]{3,2,1,0:T(8,128)(2,1)S(1)}, bf16[4,1,64,128]{3,2,1,0:T(8,128)(2,1)S(1)}, u32[]{:S(2)}, u32[]{:S(2)}) collective-permute-start(bf16[4,1,64,128]{3,2,1,0:T(8,128)(2,1)S(1)} %get-tuple-element.38), channel_id=1, source_target_pairs={{8,0},{16,8},{24,16},{32,24},{40,32},{48,40},{56,48},{64,56},{72,6... | collective-permute-start | bytes 196616 | tf_op jit(solution)/shard_map/ppermute | solution.py:24
  3.5 1.8 %collective-permute-done = bf16[4,1,64,128]{3,2,1,0:T(8,128)(2,1)S(1)} collective-permute-done((bf16[4,1,64,128]{3,2,1,0:T(8,128)(2,1)S(1)}, bf16[4,1,64,128]{3,2,1,0:T(8,128)(2,1)S(1)}, u32[]{:S(2)}, u32[]{:S(2)}) %collective-permute-start) | collective-permute-done | bytes 65568 | tf_op jit(solution)/shard_map/ppermute | solution.py:22
  6.4 1.6 collective-permute-start.2
  8.0 1.7 collective-permute-start.3
  9.8 1.6 collective-permute-done.2
  12.1 2.0 %collective-permute-start.4 = (bf16[4,6,66,1]{3,2,1,0:T(8,128)(2,1)S(1)}, bf16[4,6,66,1]{3,2,1,0:T(8,128)(2,1)S(1)}, u32[]{:S(2)}, u32[]{:S(2)}) collective-permute-start(bf16[4,6,66,1]{3,2,1,0:T(8,128)(2,1)S(1)} %get-tuple-element.33), channel_id=1, source_target_pairs={{0,1},{1,0},{2,3},{3,2},{4,5},{5,4},{6,7},{7,6},{8,9},{9,8},{10,11... | collective-permute-start | bytes 9512 | tf_op jit(solution)/shard_map/ppermute | solution.py:22
  15.3 2.2 %reshape.230.refs_5_ = bf16[32,4096]{1,0:T(8,128)(2,1)} reshape(bf16[32,2,32,64]{3,2,1,0:T(8,128)(2,1)} %param.7) | data formatting | bytes 524288 | tf_op jit(solution)/shard_map/reshape | solution.py:248
  21.1 9.5 %collective-permute-done.5 = bf16[4,6,66,1]{3,2,1,0:T(8,128)(2,1)S(1)} collective-permute-done((bf16[4,6,66,1]{3,2,1,0:T(8,128)(2,1)S(1)}, bf16[4,6,66,1]{3,2,1,0:T(8,128)(2,1)S(1)}, u32[]{:S(2)}, u32[]{:S(2)}) %collective-permute-start.5) | collective-permute-done | bytes 3200 | tf_op jit(solution)/shard_map/ppermute | solution.py:24
  35.6 7.6 %copy.69.refs_4_ = bf16[256,108,128]{2,1,0:T(8,128)(2,1)} copy(bf16[256,108,128]{2,0,1:T(8,128)(2,1)S(1)} %bitcast.463) | data formatting | bytes 14155776 | tf_op jit(solution)/shard_map/reshape | solution.py:246
  43.2 22.1 %shard_map.75 = (bf16[32,4096]{1,0:T(8,128)(2,1)}, bf16[256,32,128]{2,1,0:T(8,128)(2,1)}, f32[32,108]{1,0:T(8,128)}, f32[32,1]{1,0:T(8,128)}) custom-call(bf16[32,108]{1,0:T(8,128)(2,1)} %copy.67.refs_0_, f32[32,1]{1,0:T(8,128)} %copy.68.refs_1_, f32[2,128,128]{2,1,0:T(8,128)} %get-tuple-element.44.refs_2_, bf16[2,128,128]{2,1,0:T(8,128)(2,1)} %get-tuple-element.45.refs_3_, ...), custom_call_target="tpu_custom_call" | custom-call | tf_op jit(solution)/shard_map/pallas_call | solution.py:197
  65.3 2.4 %fusion.249 = (bf16[32,1,64,128]{3,0,2,1:T(8,128)(2,1)}, bf16[32,1,64,128]{3,0,2,1:T(8,128)(2,1)}) fusion(bf16[32,4,64,128]{3,0,2,1:T(8,128)(2,1)} %bitcast.450), kind=kLoop, calls=%fused_computation.239 | loop fusion | bytes 2097152 | tf_op jit(solution)/shard_map/slice | solution.py:19
  67.7 4.0 %collective-permute-start.6 = (bf16[32,1,64,128]{3,0,2,1:T(8,128)(2,1)}, bf16[32,1,64,128]{3,0,2,1:T(8,128)(2,1)S(1)}, u32[]{:S(2)}, u32[]{:S(2)}) collective-permute-start(bf16[32,1,64,128]{3,0,2,1:T(8,128)(2,1)} %get-tuple-element.30), channel_id=1, source_target_pairs={{0,8},{8,16},{16,24},{24,32},{32,40},{40,48},{48,56},{56,64},{64,7... | collective-permute-start | bytes 1572872 | tf_op jit(solution)/shard_map/ppermute | solution.py:22
  71.8 1.4 maximum_maximum_fusion.3.refs_0_
  73.2 25.4 %shard_map.76 = f32[32,128]{1,0:T(8,128)} custom-call(f32[32,128]{1,0:T(8,128)} %maximum_maximum_fusion.3.refs_0_), custom_call_target="tpu_custom_call" | custom-call | tf_op jit(solution)/shard_map/pallas_call | solution.py:90
  100.1 2.3 %reshape.231 = bf16[32,2,32,64]{3,2,1,0:T(8,128)(2,1)} reshape(bf16[32,4096]{1,0:T(8,128)(2,1)} %get-tuple-element.8) | data formatting | bytes 524288 | tf_op jit(solution)/shard_map/reshape | solution.py:252
  102.4 1.4 slice_reduce_fusion
  103.8 2.8 %fusion.201 = f32[4,64,128,4]{2,3,1,0:T(4,128)} fusion(bf16[32,4,64,128]{3,0,2,1:T(8,128)(2,1)} %bitcast.451, bf16[32,4,3,3,3]{0,1,4,3,2:T(4,128)(2,1)S(1)} %copy-done.11), kind=kOutput, calls=%fused_computation.187 | convolution fusion | flops 8388608 | bytes 2622464 | tf_op jit(solution)/shard_map/oc,oxyz->cxyz/dot_general | solution.py:268
  107.4 2.6 %collective-permute-start.9 = (bf16[32,6,1,128]{3,0,2,1:T(8,128)(2,1)S(1)}, bf16[32,6,1,128]{3,0,2,1:T(8,128)(2,1)S(1)}, u32[]{:S(2)}, u32[]{:S(2)}) collective-permute-start(bf16[32,6,1,128]{3,0,2,1:T(8,128)(2,1)S(1)} %get-tuple-element.29), channel_id=1, source_target_pairs={{2,0},{4,2},{6,4},{0,6},{3,1},{5,3},{7,5},{1,7},{10,8},{12,10},{14... | collective-permute-start | bytes 147464 | tf_op jit(solution)/shard_map/ppermute | solution.py:24
  113.0 4.1 %fusion.248 = (bf16[32,6,66,1]{3,0,2,1:T(8,128)(2,1)}, bf16[32,6,66,1]{3,0,2,1:T(8,128)(2,1)}) fusion(bf16[32,6,66,128]{3,0,2,1:T(8,128)(2,1)S(1)} %pad_maximum_fusion.1), kind=kLoop, calls=%fused_computation.238 | loop fusion | bytes 101376 | tf_op jit(solution)/shard_map/slice | solution.py:19
  117.1 4.8 %copy.71 = bf16[32,6,66,1]{2,0,3,1:T(8,128)(2,1)S(1)} copy(bf16[32,6,66,1]{3,0,2,1:T(8,128)(2,1)} %get-tuple-element.26) | data formatting | bytes 50688 | tf_op jit(solution)/shard_map/slice | solution.py:19
  122.8 4.8 %copy.73 = bf16[32,6,66,1]{2,0,3,1:T(8,128)(2,1)S(1)} copy(bf16[32,6,66,1]{3,0,2,1:T(8,128)(2,1)} %get-tuple-element.27) | data formatting | bytes 50688 | tf_op jit(solution)/shard_map/slice | solution.py:18
  135.9 6.0 %copy.72 = bf16[32,6,66,1]{3,0,2,1:T(8,128)(2,1)} copy(bf16[32,6,66,1]{2,0,3,1:T(8,128)(2,1)S(1)} %collective-permute-done.10) | data formatting | bytes 50688 | tf_op jit(solution)/shard_map/ppermute | solution.py:22
  141.8 6.0 %copy.74 = bf16[32,6,66,1]{3,0,2,1:T(8,128)(2,1)} copy(bf16[32,6,66,1]{2,0,3,1:T(8,128)(2,1)S(1)} %collective-permute-done.11) | data formatting | bytes 50688 | tf_op jit(solution)/shard_map/ppermute | solution.py:24
  147.8 9.5 %maximum_maximum_fusion = (bf16[32,6,66,129]{3,0,2,1:T(8,128)(2,1)S(1)}, bf16[32,6,66,129]{3,0,2,1:T(8,128)(2,1)S(1)}) fusion(bf16[32,6,1,128]{3,0,2,1:T(8,128)(2,1)S(1)} %collective-permute-done.9, bf16[32,1,64,128]{3,0,2,1:T(8,128)(2,1)S(1)} %collective-permute-done.7, bf16[32,4,64,128]{3,0,2,1:T(8,128)(2,1)S(1)} %bitcast.462, ...), kind=kLoop, calls=%fused_computation | loop fusion | flops 39232512 | bytes 9833472 | tf_op jit(solution)/shard_map/concatenate | solution.py:20
  (117 shorter events, 40.3 us)
Async XLA Ops:
  0.6 31.5 %copy-start.1 = (bf16[4,4,64,128]{3,2,1,0:T(8,128)(2,1)S(1)}, bf16[4,4,64,128]{3,2,1,0:T(8,128)(2,1)}, u32[]{:S(2)}) copy-start(bf16[4,4,64,128]{3,2,1,0:T(8,128)(2,1)} %param.4) | copy-start | bytes 786436
  1.6 3.8 %collective-permute-start = (bf16[4,1,64,128]{3,2,1,0:T(8,128)(2,1)S(1)}, bf16[4,1,64,128]{3,2,1,0:T(8,128)(2,1)S(1)}, u32[]{:S(2)}, u32[]{:S(2)}) collective-permute-start(bf16[4,1,64,128]{3,2,1,0:T(8,128)(2,1)S(1)} %get-tuple-element.39), channel_id=1, source_target_pairs={{0,8},{8,16},{16,24},{24,32},{32,40},{40,48},{48,56},{56,64},{64,7... | collective-permute-start | bytes 196616 | tf_op jit(solution)/shard_map/ppermute | solution.py:22
  1.7 4.7 %collective-permute-start.1 = (bf16[4,1,64,128]{3,2,1,0:T(8,128)(2,1)S(1)}, bf16[4,1,64,128]{3,2,1,0:T(8,128)(2,1)S(1)}, u32[]{:S(2)}, u32[]{:S(2)}) collective-permute-start(bf16[4,1,64,128]{3,2,1,0:T(8,128)(2,1)S(1)} %get-tuple-element.38), channel_id=1, source_target_pairs={{8,0},{16,8},{24,16},{32,24},{40,32},{48,40},{56,48},{64,56},{72,6... | collective-permute-start | bytes 196616 | tf_op jit(solution)/shard_map/ppermute | solution.py:24
  6.4 5.0 %collective-permute-start.2 = (bf16[4,6,1,128]{3,2,1,0:T(2,128)(2,1)S(1)}, bf16[4,6,1,128]{3,2,1,0:T(2,128)(2,1)S(1)}, u32[]{:S(2)}, u32[]{:S(2)}) collective-permute-start(bf16[4,6,1,128]{3,2,1,0:T(2,128)(2,1)S(1)} %get-tuple-element.36), channel_id=1, source_target_pairs={{0,2},{2,4},{4,6},{6,0},{1,3},{3,5},{5,7},{7,1},{8,10},{10,12},{12... | collective-permute-start | bytes 18440 | tf_op jit(solution)/shard_map/ppermute | solution.py:22
  8.0 3.7 %collective-permute-start.3 = (bf16[4,6,1,128]{3,2,1,0:T(2,128)(2,1)S(1)}, bf16[4,6,1,128]{3,2,1,0:T(2,128)(2,1)S(1)}, u32[]{:S(2)}, u32[]{:S(2)}) collective-permute-start(bf16[4,6,1,128]{3,2,1,0:T(2,128)(2,1)S(1)} %get-tuple-element.37), channel_id=1, source_target_pairs={{2,0},{4,2},{6,4},{0,6},{3,1},{5,3},{7,5},{1,7},{10,8},{12,10},{14... | collective-permute-start | bytes 18440 | tf_op jit(solution)/shard_map/ppermute | solution.py:24
  12.1 9.0 %collective-permute-start.4 = (bf16[4,6,66,1]{3,2,1,0:T(8,128)(2,1)S(1)}, bf16[4,6,66,1]{3,2,1,0:T(8,128)(2,1)S(1)}, u32[]{:S(2)}, u32[]{:S(2)}) collective-permute-start(bf16[4,6,66,1]{3,2,1,0:T(8,128)(2,1)S(1)} %get-tuple-element.33), channel_id=1, source_target_pairs={{0,1},{1,0},{2,3},{3,2},{4,5},{5,4},{6,7},{7,6},{8,9},{9,8},{10,11... | collective-permute-start | bytes 9512 | tf_op jit(solution)/shard_map/ppermute | solution.py:22
  14.1 16.5 %collective-permute-start.5 = (bf16[4,6,66,1]{3,2,1,0:T(8,128)(2,1)S(1)}, bf16[4,6,66,1]{3,2,1,0:T(8,128)(2,1)S(1)}, u32[]{:S(2)}, u32[]{:S(2)}) collective-permute-start(bf16[4,6,66,1]{3,2,1,0:T(8,128)(2,1)S(1)} %get-tuple-element.32), channel_id=1, source_target_pairs={{1,0},{0,1},{3,2},{2,3},{5,4},{4,5},{7,6},{6,7},{9,8},{8,9},{11,10... | collective-permute-start | bytes 9512 | tf_op jit(solution)/shard_map/ppermute | solution.py:24
  43.2 60.6 %copy-start.11 = (bf16[32,4,3,3,3]{0,1,4,3,2:T(4,128)(2,1)S(1)}, bf16[32,4,3,3,3]{0,1,4,3,2:T(4,128)(2,1)}, u32[]{:S(2)}) copy-start(bf16[32,4,3,3,3]{0,1,4,3,2:T(4,128)(2,1)} %param.5) | copy-start | bytes 20740
  65.3 41.3 %copy-start = (bf16[256,32,128]{2,1,0:T(8,128)(2,1)S(1)}, bf16[256,32,128]{2,1,0:T(8,128)(2,1)}, u32[]{:S(2)}) copy-start(bf16[256,32,128]{2,1,0:T(8,128)(2,1)} %get-tuple-element.11) | copy-start | bytes 6291460
  67.7 38.9 %collective-permute-start.6 = (bf16[32,1,64,128]{3,0,2,1:T(8,128)(2,1)}, bf16[32,1,64,128]{3,0,2,1:T(8,128)(2,1)S(1)}, u32[]{:S(2)}, u32[]{:S(2)}) collective-permute-start(bf16[32,1,64,128]{3,0,2,1:T(8,128)(2,1)} %get-tuple-element.30), channel_id=1, source_target_pairs={{0,8},{8,16},{16,24},{24,32},{32,40},{40,48},{48,56},{56,64},{64,7... | collective-permute-start | bytes 1572872 | tf_op jit(solution)/shard_map/ppermute | solution.py:22
  71.7 34.9 %collective-permute-start.7 = (bf16[32,1,64,128]{3,0,2,1:T(8,128)(2,1)}, bf16[32,1,64,128]{3,0,2,1:T(8,128)(2,1)S(1)}, u32[]{:S(2)}, u32[]{:S(2)}) collective-permute-start(bf16[32,1,64,128]{3,0,2,1:T(8,128)(2,1)} %get-tuple-element.31), channel_id=1, source_target_pairs={{8,0},{16,8},{24,16},{32,24},{40,32},{48,40},{56,48},{64,56},{72,6... | collective-permute-start | bytes 1572872 | tf_op jit(solution)/shard_map/ppermute | solution.py:24
  106.6 5.7 %collective-permute-start.8 = (bf16[32,6,1,128]{3,0,2,1:T(8,128)(2,1)S(1)}, bf16[32,6,1,128]{3,0,2,1:T(8,128)(2,1)S(1)}, u32[]{:S(2)}, u32[]{:S(2)}) collective-permute-start(bf16[32,6,1,128]{3,0,2,1:T(8,128)(2,1)S(1)} %get-tuple-element.28), channel_id=1, source_target_pairs={{0,2},{2,4},{4,6},{6,0},{1,3},{3,5},{5,7},{7,1},{8,10},{10,12},{12... | collective-permute-start | bytes 147464 | tf_op jit(solution)/shard_map/ppermute | solution.py:22
  107.4 4.9 %collective-permute-start.9 = (bf16[32,6,1,128]{3,0,2,1:T(8,128)(2,1)S(1)}, bf16[32,6,1,128]{3,0,2,1:T(8,128)(2,1)S(1)}, u32[]{:S(2)}, u32[]{:S(2)}) collective-permute-start(bf16[32,6,1,128]{3,0,2,1:T(8,128)(2,1)S(1)} %get-tuple-element.29), channel_id=1, source_target_pairs={{2,0},{4,2},{6,4},{0,6},{3,1},{5,3},{7,5},{1,7},{10,8},{12,10},{14... | collective-permute-start | bytes 147464 | tf_op jit(solution)/shard_map/ppermute | solution.py:24
  121.8 14.0 %collective-permute-start.10 = (bf16[32,6,66,1]{2,0,3,1:T(8,128)(2,1)S(1)}, bf16[32,6,66,1]{2,0,3,1:T(8,128)(2,1)S(1)}, u32[]{:S(2)}, u32[]{:S(2)}) collective-permute-start(bf16[32,6,66,1]{2,0,3,1:T(8,128)(2,1)S(1)} %copy.71), channel_id=1, source_target_pairs={{0,1},{1,0},{2,3},{3,2},{4,5},{5,4},{6,7},{7,6},{8,9},{9,8},{10,11... | collective-permute-start | bytes 76040 | tf_op jit(solution)/shard_map/ppermute | solution.py:22
  127.6 14.3 %collective-permute-start.11 = (bf16[32,6,66,1]{2,0,3,1:T(8,128)(2,1)S(1)}, bf16[32,6,66,1]{2,0,3,1:T(8,128)(2,1)S(1)}, u32[]{:S(2)}, u32[]{:S(2)}) collective-permute-start(bf16[32,6,66,1]{2,0,3,1:T(8,128)(2,1)S(1)} %copy.73), channel_id=1, source_target_pairs={{1,0},{0,1},{3,2},{2,3},{5,4},{4,5},{7,6},{6,7},{9,8},{8,9},{11,10... | collective-permute-start | bytes 76040 | tf_op jit(solution)/shard_map/ppermute | solution.py:24
  163.9 3.4 %copy-start.2 = (f32[4,64,128,4]{2,3,1,0:T(4,128)S(1)}, f32[4,64,128,4]{2,3,1,0:T(4,128)}, u32[]{:S(2)}) copy-start(f32[4,64,128,4]{2,3,1,0:T(4,128)} %fusion.201) | copy-start | bytes 1572868
  163.9 3.4 %copy-start.4 = (f32[4,64,128,4]{2,3,1,0:T(4,128)S(1)}, f32[4,64,128,4]{2,3,1,0:T(4,128)}, u32[]{:S(2)}) copy-start(f32[4,64,128,4]{2,3,1,0:T(4,128)} %fusion) | copy-start | bytes 1572868
  163.9 3.4 %copy-start.8 = (f32[4,64,128,4]{2,3,1,0:T(4,128)S(1)}, f32[4,64,128,4]{2,3,1,0:T(4,128)}, u32[]{:S(2)}) copy-start(f32[4,64,128,4]{2,3,1,0:T(4,128)} %fusion.216) | copy-start | bytes 1572868
  163.9 3.4 %copy-start.9 = (f32[4,64,128,4]{2,3,1,0:T(4,128)S(1)}, f32[4,64,128,4]{2,3,1,0:T(4,128)}, u32[]{:S(2)}) copy-start(f32[4,64,128,4]{2,3,1,0:T(4,128)} %fusion.209) | copy-start | bytes 1572868
  163.9 3.4 %copy-start.10 = (f32[4,64,128,4]{2,3,1,0:T(4,128)S(1)}, f32[4,64,128,4]{2,3,1,0:T(4,128)}, u32[]{:S(2)}) copy-start(f32[4,64,128,4]{2,3,1,0:T(4,128)} %fusion.205) | copy-start | bytes 1572868
  166.4 1.9 %copy-start.3 = (f32[4,4,64,128]{3,0,2,1:T(4,128)S(1)}, f32[4,4,64,128]{3,0,2,1:T(4,128)}, u32[]{:S(2)}) copy-start(f32[4,4,64,128]{3,0,2,1:T(4,128)} %fusion.77) | copy-start | bytes 1572868
  166.4 1.9 %copy-start.5 = (f32[4,64,128,4]{2,3,1,0:T(4,128)S(1)}, f32[4,64,128,4]{2,3,1,0:T(4,128)}, u32[]{:S(2)}) copy-start(f32[4,64,128,4]{2,3,1,0:T(4,128)} %fusion.197) | copy-start | bytes 1572868
  166.4 1.9 %copy-start.6 = (f32[4,4,64,128]{3,0,2,1:T(4,128)S(1)}, f32[4,4,64,128]{3,0,2,1:T(4,128)}, u32[]{:S(2)}) copy-start(f32[4,4,64,128]{3,0,2,1:T(4,128)} %convolution_bitcast_fusion.1) | copy-start | bytes 1572868
  166.4 1.9 %copy-start.7 = (f32[4,4,64,128]{3,0,2,1:T(4,128)S(1)}, f32[4,4,64,128]{3,0,2,1:T(4,128)}, u32[]{:S(2)}) copy-start(f32[4,4,64,128]{3,0,2,1:T(4,128)} %convolution_bitcast_fusion) | copy-start | bytes 1572868

commit v5 on v4

--- a/solution.py
+++ b/solution.py
@@ -119,20 +119,29 @@
     return leak_slope + (1.0 - leak_slope) * jax.nn.sigmoid(soft_scale * preact)
 
 
-def forward_kernel(rows, w_ref, b_ref, q_ref, u_ref, p_ref, cot_ref,
-                   pooled_ref, delta_ref, wg_ref, bg_ref, wg_acc, bg_acc):
+def forward_kernel(rows, wide_y, w_ref, b_ref, q_ref, u_ref, wt_ref, p_ref, cot_ref,
+                   pooled_ref, wg_ref, bg_ref, main_ref, lo_ref, hi_ref, wg_acc, bg_acc):
     step = pl.program_id(0)
     plane = p_ref.shape[0] // 2
+    lines = plane // 4
 
     @pl.when(step == 0)
     def _():
         wg_acc[...] = jnp.zeros_like(wg_acc)
         bg_acc[...] = jnp.zeros_like(bg_acc)
+        main_ref[...] = jnp.zeros_like(main_ref)
+        lo_ref[...] = jnp.zeros_like(lo_ref)
+        hi_ref[...] = jnp.zeros_like(hi_ref)
 
     weight = w_ref[...]
     bias = b_ref[...]
-
-    @pl.loop(0, plane // 4)
+    spread_w = wt_ref[...]
+    slots = spread_w.shape[0] // 27
+    lane = lax.broadcasted_iota(jnp.int32, (slots, rows), 1)
+    first = lane == 0
+    last = lane == rows - 1
+
+    @pl.loop(0, lines)
     def _(j):
         cot = cot_ref[:, pl.ds(pl.multiple_of(j * rows, rows), rows)]
         ups = (
@@ -142,7 +151,8 @@
         totals = [None, None]
         wg = None
         bg = None
-        for base in (0, plane):
+        for px, base in enumerate((0, plane)):
+            deltas = []
             for r in range(4):
                 row = base + j * 4 + r
                 patch = p_ref[row]
@@ -156,13 +166,32 @@
                 sigmoid = jnp.where(scaled >= 0.0, 1.0, e) / (1.0 + e)
                 slope = leak_slope + (1.0 - leak_slope) * sigmoid
                 delta = (slope * ups[half]).astype(jnp.bfloat16)
-                delta_ref[row] = delta
+                deltas.append(delta)
                 term = lax.dot_general(
                     delta, patch, (((1,), (1,)), ((), ())), preferred_element_type=jnp.float32
                 )
                 wg = term if wg is None else wg + term
                 part = delta.astype(jnp.float32)
                 bg = part if bg is None else bg + part
+            spread = jnp.dot(
+                spread_w, jnp.concatenate(deltas, axis=1), preferred_element_type=jnp.float32
+            )
+            x = step * 2 + px
+            for r in range(4):
+                y = j * 4 + r
+                for a in range(3):
+                    for b in range(3):
+                        at = (a * 3 + b) * 3 * slots
+                        cols = slice(r * rows, (r + 1) * rows)
+                        v0 = pltpu.roll(spread[at : at + slots, cols], rows - 1, 1)
+                        v1 = spread[at + slots : at + 2 * slots, cols]
+                        v2 = pltpu.roll(spread[at + 2 * slots : at + 3 * slots, cols], 1, 1)
+                        out = (x + a) * wide_y + (y + b)
+                        main_ref[out] += (
+                            jnp.where(last, 0.0, v0) + v1 + jnp.where(first, 0.0, v2)
+                        )
+                        lo_ref[out] += jnp.where(last, v0, 0.0)
+                        hi_ref[out] += jnp.where(first, v2, 0.0)
         wg_acc[...] += wg
         bg_acc[...] += jnp.sum(bg, axis=1, keepdims=True)
         pooled = jnp.dot(
@@ -180,9 +209,14 @@
         bg_ref[...] = bg_acc[...]
 
 
-def forward(weight_mat, bias, patches, cot, pairs):
+def forward(weight, bias, patches, cot, pairs, wide_x, wide_y):
     lines, taps, rows = patches.shape
-    chan_out = weight_mat.shape[0]
+    chan_out, chan_in = weight.shape[:2]
+    weight_mat = weight.reshape(chan_out, taps)
+    slots = 8
+    spread_w = jnp.transpose(weight, (2, 3, 4, 1, 0))
+    spread_w = jnp.pad(spread_w, ((0, 0), (0, 0), (0, 0), (0, slots - chan_in), (0, 0)))
+    spread_w = spread_w.reshape(27 * slots, chan_out)
     half = rows // 2
     z = jnp.arange(rows)
     k = jnp.arange(rows)
@@ -194,34 +228,60 @@
     ).astype(jnp.bfloat16)
     full = lambda shape: pl.BlockSpec(shape, lambda p: (0,) * len(shape))
     block = lines // pairs
+    acc_shape = (wide_x * wide_y, slots, rows)
     return pl.pallas_call(
-        lambda *refs: forward_kernel(rows, *refs),
+        lambda *refs: forward_kernel(rows, wide_y, *refs),
         grid=(pairs,),
         out_shape=(
             jax.ShapeDtypeStruct(cot.shape, jnp.bfloat16),
-            jax.ShapeDtypeStruct((lines, chan_out, rows), jnp.bfloat16),
             jax.ShapeDtypeStruct((chan_out, taps), jnp.float32),
             jax.ShapeDtypeStruct((chan_out, 1), jnp.float32),
+            jax.ShapeDtypeStruct(acc_shape, jnp.float32),
+            jax.ShapeDtypeStruct(acc_shape, jnp.float32),
+            jax.ShapeDtypeStruct(acc_shape, jnp.float32),
         ),
         in_specs=[
             full((chan_out, taps)),
             full((chan_out, 1)),
             full((2, rows, rows)),
             full((2, rows, rows)),
+            full((27 * slots, chan_out)),
             pl.BlockSpec((block, taps, rows), lambda p: (p, 0, 0)),
             pl.BlockSpec((chan_out, cot.shape[1] // pairs), lambda p: (0, p)),
         ],
         out_specs=(
             pl.BlockSpec((chan_out, cot.shape[1] // pairs), lambda p: (0, p)),
-            pl.BlockSpec((block, chan_out, rows), lambda p: (p, 0, 0)),
             full((chan_out, taps)),
             full((chan_out, 1)),
+            full(acc_shape),
+            full(acc_shape),
+            full(acc_shape),
         ),
         scratch_shapes=[
             pltpu.VMEM((chan_out, taps), jnp.float32),
             pltpu.VMEM((chan_out, 1), jnp.float32),
         ],
-    )(weight_mat, bias, pool, spread, patches, cot)
+    )(weight_mat, bias, pool, spread, spread_w, patches, cot)
+
+
+def fold_halo(main, axis, dim, width):
+    count = lax.axis_size(axis)
+    size = main.shape[dim]
+    head = lax.slice_in_dim(main, 0, width, axis=dim)
+    tail = lax.slice_in_dim(main, size - width, size, axis=dim)
+    from_left = lax.ppermute(tail, axis, [(i, (i + 1) % count) for i in range(count)])
+    from_right = lax.ppermute(head, axis, [((i + 1) % count, i) for i in range(count)])
+    inner = lax.slice_in_dim(main, width, size - width, axis=dim)
+    inner_size = size - 2 * width
+    start = [0] * main.ndim
+    inner = lax.dynamic_update_slice(
+        inner, lax.slice_in_dim(inner, 0, width, axis=dim) + from_left, start
+    )
+    start[dim] = inner_size - width
+    inner = lax.dynamic_update_slice(
+        inner, lax.slice_in_dim(inner, inner_size - width, inner_size, axis=dim) + from_right, start
+    )
+    return inner
 
 
 def on_device(cells, weight, bias, cotangent):
@@ -244,13 +304,12 @@
         axis=3,
     )
     patches = patches.reshape(cells_x * cells_y, chan_in * 27, cells_z)
-    weight_mat = weight.reshape(chan_out, chan_in * 27)
     cot = cotangent.reshape(chan_out, -1)
-    pooled, delta, weight_local, bias_local = forward(
-        weight_mat, bias.reshape(chan_out, 1), patches, cot, cells_x // 2
+    wide_x, wide_y = cells_x + 2, cells_y + 2
+    pooled, weight_local, bias_local, main, lo, hi = forward(
+        weight, bias.reshape(chan_out, 1), patches, cot, cells_x // 2, wide_x, wide_y
     )
     pooled = pooled.reshape(cotangent.shape)
-    delta = jnp.transpose(delta.reshape(cells_x, cells_y, chan_out, cells_z), (2, 0, 1, 3))
     taps = chan_in * 27
     width = -(-(taps + 1) // 128) * 128
     partial = jnp.concatenate(
@@ -261,16 +320,23 @@
     both = allreduce(partial, sizes)
     weight_grad = both[:, :taps].reshape(chan_out, chan_in, 3, 3, 3)
     bias_grad = both[:, taps]
-    delta_wide = extended(delta, (("gx", 1), ("gy", 2), ("gz", 3)), 1)
-    input_grad = jnp.zeros((chan_in, cells_x, cells_y, cells_z), jnp.float32)
-    for sa, sb, se in stencil:
-        window = delta_wide[:, sa : sa + cells_x, sb : sb + cells_y, se : se + cells_z]
-        input_grad = input_grad + jnp.einsum(
-            "oc,oxyz->cxyz",
-            weight[:, :, 2 - sa, 2 - sb, 2 - se],
-            window,
-            preferred_element_type=jnp.float32,
-        )
+    main = main.reshape(wide_x, wide_y, -1, cells_z)[:, :, :chan_in]
+    lo = lo.reshape(wide_x, wide_y, -1, cells_z)[:, :, :chan_in, cells_z - 1 :]
+    hi = hi.reshape(wide_x, wide_y, -1, cells_z)[:, :, :chan_in, :1]
+    count = lax.axis_size("gz")
+    from_left = lax.ppermute(hi, "gz", [(i, (i + 1) % count) for i in range(count)])
+    from_right = lax.ppermute(lo, "gz", [((i + 1) % count, i) for i in range(count)])
+    main = jnp.concatenate(
+        [
+            main[..., :1] + from_left,
+            main[..., 1 : cells_z - 1],
+            main[..., cells_z - 1 :] + from_right,
+        ],
+        axis=3,
+    )
+    main = fold_halo(main, "gy", 1, 1)
+    main = fold_halo(main, "gx", 0, 1)
+    input_grad = jnp.transpose(main, (2, 0, 1, 3))
     return (pooled, weight_grad, bias_grad, input_grad)
 
 

time: 174 us -> 142 us (0.82)
  the two profiles are of different devices: /device:TPU:6 before, /device:TPU:7 now
where the time goes in v5:
time: 142 us; the launch traced here: 141 us
  Pallas kernels  56.9 us (40%)
  local copies, waits for them, and re-layouts  36.3 us (26%)
  waiting for transfers between devices  21.9 us (15%)
  starting transfers between devices  19.9 us (14%)
  other arithmetic  5.09 us (4%)
    pallas_call x1, Pallas kernels, forward(): pl.pallas_call(lambda *refs: forward_kernel(rows, wide_y, *refs), grid=(p...  40.3 us
    pallas_call x1, Pallas kernels, allreduce(): pl.pallas_call(lambda *refs: allreduce_kernel(sizes, *refs), out_shape=ja...  16.5 us
    ppermute x3, waiting for transfers between devices, extended(): lax.ppermute(head, axis, [((i + 1) % count, i) for i in range(count)])  10 us
    unnamed x37, local copies, waits for them, and re-layouts  8.57 us
    reshape x1, local copies, waits for them, and re-layouts, on_device(): patches = patches.reshape(cells_x * cells_y, chan_in * 27, cells_z)  7.52 us
    ppermute x2, waiting for transfers between devices, fold_halo(): lax.ppermute(head, axis, [((i + 1) % count, i) for i in range(count)])  6.4 us
    ppermute x3, starting transfers between devices, extended(): lax.ppermute(tail, axis, [(i, (i + 1) % count) for i in range(count)])  6.32 us
    ppermute x2, starting transfers between devices, fold_halo(): lax.ppermute(tail, axis, [(i, (i + 1) % count) for i in range(count)])  5.7 us
  transfers between devices with their start and end apart: 12, of which 9 were waited for; matrix products, arithmetic and copies ran while one was open for 17% of the time, Pallas kernels for 12%

profile of v5, /device:TPU:7, one launch (start us, length us, event | category | flops | bytes accessed | tf_op | source)
XLA Modules:
  0.0 141.1 jit_solution(11518040007958045488)
XLA Ops:
  1.6 4.1 %collective-permute-start = (bf16[4,1,64,128]{3,2,1,0:T(8,128)(2,1)S(1)}, bf16[4,1,64,128]{3,2,1,0:T(8,128)(2,1)S(1)}, u32[]{:S(2)}, u32[]{:S(2)}) collective-permute-start(bf16[4,1,64,128]{3,2,1,0:T(8,128)(2,1)S(1)} %get-tuple-element.41), channel_id=1, source_target_pairs={{0,8},{8,16},{16,24},{24,32},{32,40},{40,48},{48,56},{56,64},{64,7... | collective-permute-start | bytes 196616 | tf_op jit(solution)/shard_map/ppermute | solution.py:22
  8.0 5.0 %collective-permute-done.1 = bf16[4,1,64,128]{3,2,1,0:T(8,128)(2,1)S(1)} collective-permute-done((bf16[4,1,64,128]{3,2,1,0:T(8,128)(2,1)S(1)}, bf16[4,1,64,128]{3,2,1,0:T(8,128)(2,1)S(1)}, u32[]{:S(2)}, u32[]{:S(2)}) %collective-permute-start.1) | collective-permute-done | bytes 65568 | tf_op jit(solution)/shard_map/ppermute | solution.py:24
  13.1 1.4 collective-permute-start.2
  14.4 1.5 %collective-permute-start.3 = (bf16[4,6,1,128]{3,2,1,0:T(2,128)(2,1)S(1)}, bf16[4,6,1,128]{3,2,1,0:T(2,128)(2,1)S(1)}, u32[]{:S(2)}, u32[]{:S(2)}) collective-permute-start(bf16[4,6,1,128]{3,2,1,0:T(2,128)(2,1)S(1)} %get-tuple-element.39), channel_id=1, source_target_pairs={{2,0},{4,2},{6,4},{0,6},{3,1},{5,3},{7,5},{1,7},{10,8},{12,10},{14... | collective-permute-start | bytes 18440 | tf_op jit(solution)/shard_map/ppermute | solution.py:24
  19.8 2.2 %reshape.240.refs_6_ = bf16[32,4096]{1,0:T(8,128)(2,1)} reshape(bf16[32,2,32,64]{3,2,1,0:T(8,128)(2,1)} %param.7) | data formatting | bytes 524288 | tf_op jit(solution)/shard_map/reshape | solution.py:307
  23.5 1.3 copy.76.refs_1_
  24.9 1.4 pad.4
  26.3 3.7 %collective-permute-done.4 = bf16[4,6,66,1]{3,2,1,0:T(8,128)(2,1)S(1)} collective-permute-done((bf16[4,6,66,1]{3,2,1,0:T(8,128)(2,1)S(1)}, bf16[4,6,66,1]{3,2,1,0:T(8,128)(2,1)S(1)}, u32[]{:S(2)}, u32[]{:S(2)}) %collective-permute-start.4) | collective-permute-done | bytes 3200 | tf_op jit(solution)/shard_map/ppermute | solution.py:22
  30.0 4.7 %collective-permute-done.5 = bf16[4,6,66,1]{3,2,1,0:T(8,128)(2,1)S(1)} collective-permute-done((bf16[4,6,66,1]{3,2,1,0:T(8,128)(2,1)S(1)}, bf16[4,6,66,1]{3,2,1,0:T(8,128)(2,1)S(1)}, u32[]{:S(2)}, u32[]{:S(2)}) %collective-permute-start.5) | collective-permute-done | bytes 3200 | tf_op jit(solution)/shard_map/ppermute | solution.py:24
  39.7 7.5 %copy.77.refs_5_ = bf16[256,108,128]{2,1,0:T(8,128)(2,1)} copy(bf16[256,108,128]{2,0,1:T(8,128)(2,1)S(1)} %bitcast.221) | data formatting | bytes 14155776 | tf_op jit(solution)/shard_map/reshape | solution.py:306
  47.3 40.3 %shard_map.75 = (bf16[32,4096]{1,0:T(8,128)(2,1)}, f32[32,108]{1,0:T(8,128)}, f32[32,1]{1,0:T(8,128)}, f32[396,8,128]{2,1,0:T(8,128)}, f32[396,8,128]{2,1,0:T(8,128)}, /*index=5*/f32[396,8,128]{2,1,0:T(8,128)}) custom-call(bf16[32,108]{1,0:T(8,128)(2,1)} %copy.75.refs_0_, f32[32,1]{1,0:T(8,128)} %copy.76.refs_1_, f32[2,128,128]{2,1,0:T(8,128)} %add_convert_fusion.refs_2_, ...), custom_call_target="tpu_custom_call" | custom-call | tf_op jit(solution)/shard_map/pallas_call | solution.py:232
  87.6 1.7 %slice.259 = f32[6,66,4,1]{3,2,1,0:T(4,128)S(1)} slice(f32[6,66,8,128]{3,2,1,0:T(8,128)} %bitcast.226), slice={[0:6], [0:66], [0:4], [0:1]} | slice | bytes 12672 | tf_op jit(solution)/shard_map/slice | solution.py:325
  89.6 1.7 %collective-permute-start.6 = (f32[6,66,4,1]{1,2,3,0:T(4,128)S(1)}, f32[6,66,4,1]{1,2,3,0:T(4,128)S(1)}, u32[]{:S(2)}, u32[]{:S(2)}) collective-permute-start(f32[6,66,4,1]{1,2,3,0:T(4,128)S(1)} %copy.88), channel_id=1, source_target_pairs={{0,1},{1,0},{2,3},{3,2},{4,5},{5,4},{6,7},{7,6},{8,9},{9,8},{10,11... | collective-permute-start | bytes 19016 | tf_op jit(solution)/shard_map/ppermute | solution.py:327
  91.3 1.9 %slice.262 = f32[6,66,4,1]{3,2,1,0:T(4,128)S(1)} slice(f32[6,66,8,128]{3,2,1,0:T(8,128)} %bitcast.225), slice={[0:6], [0:66], [0:4], [127:128]} | slice | bytes 12672 | tf_op jit(solution)/shard_map/slice | solution.py:324
  93.8 3.4 %fusion.40 = (f32[6,66,4,1]{3,2,1,0:T(4,128)}, f32[6,66,4,1]{3,2,1,0:T(4,128)S(1)}) fusion(f32[6,66,8,128]{3,2,1,0:T(8,128)} %bitcast.222), kind=kLoop, calls=%fused_computation.97 | loop fusion | bytes 25344 | tf_op jit(solution)/shard_map/slice | solution.py:331
  97.7 1.5 %copy.87 = f32[6,66,4,1]{1,2,3,0:T(4,128)S(1)} copy(f32[6,66,4,1]{3,2,1,0:T(4,128)} %get-tuple-element.30) | data formatting | bytes 12672
  100.7 1.4 collective-permute-start.8
  102.7 1.4 %collective-permute-start.9 = (f32[6,1,4,128]{3,1,0,2:T(1,128)S(1)}, f32[6,1,4,128]{3,1,0,2:T(1,128)S(1)}, u32[]{:S(2)}, u32[]{:S(2)}) collective-permute-start(f32[6,1,4,128]{3,1,0,2:T(1,128)S(1)} %get-tuple-element.28), channel_id=1, source_target_pairs={{2,0},{4,2},{6,4},{0,6},{3,1},{5,3},{7,5},{1,7},{10,8},{12,10},{14... | collective-permute-start | bytes 36872 | tf_op jit(solution)/shard_map/ppermute | solution.py:273
  105.4 4.3 %collective-permute-start.10 = (f32[1,64,4,128]{3,1,0,2:T(8,128)S(1)}, f32[1,64,4,128]{3,1,0,2:T(8,128)S(1)}, u32[]{:S(2)}, u32[]{:S(2)}) collective-permute-start(f32[1,64,4,128]{3,1,0,2:T(8,128)S(1)} %get-tuple-element.33), channel_id=1, source_target_pairs={{0,8},{8,16},{16,24},{24,32},{32,40},{40,48},{48,56},{56,64},{64,7... | collective-permute-start | bytes 393224 | tf_op jit(solution)/shard_map/ppermute | solution.py:272
  110.4 16.5 %shard_map.76 = f32[32,128]{1,0:T(8,128)} custom-call(f32[32,128]{1,0:T(8,128)} %maximum_maximum_fusion.1.refs_0_), custom_call_target="tpu_custom_call" | custom-call | tf_op jit(solution)/shard_map/pallas_call | solution.py:90
  128.5 2.3 %reshape.241 = bf16[32,2,32,64]{3,2,1,0:T(8,128)(2,1)} reshape(bf16[32,4096]{1,0:T(8,128)(2,1)} %get-tuple-element.10) | data formatting | bytes 524288 | tf_op jit(solution)/shard_map/reshape | solution.py:312
  130.8 1.4 %slice_reduce_fusion = f32[32]{0:T(128)} fusion(f32[32,128]{1,0:T(8,128)} %shard_map.76), kind=kLoop, calls=%fused_computation.87 | loop fusion | bytes 256 | tf_op jit(solution)/shard_map/slice | solution.py:322
  132.2 2.2 %collective-permute-start.11 = (f32[1,64,4,128]{3,1,0,2:T(8,128)S(1)}, f32[1,64,4,128]{3,1,0,2:T(8,128)S(1)}, u32[]{:S(2)}, u32[]{:S(2)}) collective-permute-start(f32[1,64,4,128]{3,1,0,2:T(8,128)S(1)} %get-tuple-element.32), channel_id=1, source_target_pairs={{8,0},{16,8},{24,16},{32,24},{40,32},{48,40},{56,48},{64,56},{72,6... | collective-permute-start | bytes 393224 | tf_op jit(solution)/shard_map/ppermute | solution.py:273
  134.4 5.8 %collective-permute-done.11 = f32[1,64,4,128]{3,1,0,2:T(8,128)S(1)} collective-permute-done((f32[1,64,4,128]{3,1,0,2:T(8,128)S(1)}, f32[1,64,4,128]{3,1,0,2:T(8,128)S(1)}, u32[]{:S(2)}, u32[]{:S(2)}) %collective-permute-start.11) | collective-permute-done | bytes 131104 | tf_op jit(solution)/shard_map/ppermute | solution.py:273
  (91 shorter events, 21.5 us)
Async XLA Ops:
  0.6 35.6 %copy-start = (bf16[4,4,64,128]{3,2,1,0:T(8,128)(2,1)S(1)}, bf16[4,4,64,128]{3,2,1,0:T(8,128)(2,1)}, u32[]{:S(2)}) copy-start(bf16[4,4,64,128]{3,2,1,0:T(8,128)(2,1)} %param.4) | copy-start | bytes 786436
  1.6 5.5 %collective-permute-start = (bf16[4,1,64,128]{3,2,1,0:T(8,128)(2,1)S(1)}, bf16[4,1,64,128]{3,2,1,0:T(8,128)(2,1)S(1)}, u32[]{:S(2)}, u32[]{:S(2)}) collective-permute-start(bf16[4,1,64,128]{3,2,1,0:T(8,128)(2,1)S(1)} %get-tuple-element.41), channel_id=1, source_target_pairs={{0,8},{8,16},{16,24},{24,32},{32,40},{40,48},{48,56},{56,64},{64,7... | collective-permute-start | bytes 196616 | tf_op jit(solution)/shard_map/ppermute | solution.py:22
  5.7 7.3 %collective-permute-start.1 = (bf16[4,1,64,128]{3,2,1,0:T(8,128)(2,1)S(1)}, bf16[4,1,64,128]{3,2,1,0:T(8,128)(2,1)S(1)}, u32[]{:S(2)}, u32[]{:S(2)}) collective-permute-start(bf16[4,1,64,128]{3,2,1,0:T(8,128)(2,1)S(1)} %get-tuple-element.40), channel_id=1, source_target_pairs={{8,0},{16,8},{24,16},{32,24},{40,32},{48,40},{56,48},{64,56},{72,6... | collective-permute-start | bytes 196616 | tf_op jit(solution)/shard_map/ppermute | solution.py:24
  13.1 3.9 %collective-permute-start.2 = (bf16[4,6,1,128]{3,2,1,0:T(2,128)(2,1)S(1)}, bf16[4,6,1,128]{3,2,1,0:T(2,128)(2,1)S(1)}, u32[]{:S(2)}, u32[]{:S(2)}) collective-permute-start(bf16[4,6,1,128]{3,2,1,0:T(2,128)(2,1)S(1)} %get-tuple-element.38), channel_id=1, source_target_pairs={{0,2},{2,4},{4,6},{6,0},{1,3},{3,5},{5,7},{7,1},{8,10},{10,12},{12... | collective-permute-start | bytes 18440 | tf_op jit(solution)/shard_map/ppermute | solution.py:22
  14.4 2.8 %collective-permute-start.3 = (bf16[4,6,1,128]{3,2,1,0:T(2,128)(2,1)S(1)}, bf16[4,6,1,128]{3,2,1,0:T(2,128)(2,1)S(1)}, u32[]{:S(2)}, u32[]{:S(2)}) collective-permute-start(bf16[4,6,1,128]{3,2,1,0:T(2,128)(2,1)S(1)} %get-tuple-element.39), channel_id=1, source_target_pairs={{2,0},{4,2},{6,4},{0,6},{3,1},{5,3},{7,5},{1,7},{10,8},{12,10},{14... | collective-permute-start | bytes 18440 | tf_op jit(solution)/shard_map/ppermute | solution.py:24
  17.6 12.3 %collective-permute-start.4 = (bf16[4,6,66,1]{3,2,1,0:T(8,128)(2,1)S(1)}, bf16[4,6,66,1]{3,2,1,0:T(8,128)(2,1)S(1)}, u32[]{:S(2)}, u32[]{:S(2)}) collective-permute-start(bf16[4,6,66,1]{3,2,1,0:T(8,128)(2,1)S(1)} %get-tuple-element.35), channel_id=1, source_target_pairs={{0,1},{1,0},{2,3},{3,2},{4,5},{5,4},{6,7},{7,6},{8,9},{9,8},{10,11... | collective-permute-start | bytes 9512 | tf_op jit(solution)/shard_map/ppermute | solution.py:22
  18.5 16.2 %collective-permute-start.5 = (bf16[4,6,66,1]{3,2,1,0:T(8,128)(2,1)S(1)}, bf16[4,6,66,1]{3,2,1,0:T(8,128)(2,1)S(1)}, u32[]{:S(2)}, u32[]{:S(2)}) collective-permute-start(bf16[4,6,66,1]{3,2,1,0:T(8,128)(2,1)S(1)} %get-tuple-element.34), channel_id=1, source_target_pairs={{1,0},{0,1},{3,2},{2,3},{5,4},{4,5},{7,6},{6,7},{9,8},{8,9},{11,10... | collective-permute-start | bytes 9512 | tf_op jit(solution)/shard_map/ppermute | solution.py:24
  87.6 9.6 %copy-start.1 = (f32[396,8,128]{2,1,0:T(8,128)S(1)}, f32[396,8,128]{2,1,0:T(8,128)}, u32[]{:S(2)}) copy-start(f32[396,8,128]{2,1,0:T(8,128)} %get-tuple-element.13) | copy-start | bytes 4866052
  89.6 10.0 %collective-permute-start.6 = (f32[6,66,4,1]{1,2,3,0:T(4,128)S(1)}, f32[6,66,4,1]{1,2,3,0:T(4,128)S(1)}, u32[]{:S(2)}, u32[]{:S(2)}) collective-permute-start(f32[6,66,4,1]{1,2,3,0:T(4,128)S(1)} %copy.88), channel_id=1, source_target_pairs={{0,1},{1,0},{2,3},{3,2},{4,5},{5,4},{6,7},{7,6},{8,9},{9,8},{10,11... | collective-permute-start | bytes 19016 | tf_op jit(solution)/shard_map/ppermute | solution.py:327
  93.5 6.5 %collective-permute-start.7 = (f32[6,66,4,1]{1,2,3,0:T(4,128)S(1)}, f32[6,66,4,1]{1,2,3,0:T(4,128)S(1)}, u32[]{:S(2)}, u32[]{:S(2)}) collective-permute-start(f32[6,66,4,1]{1,2,3,0:T(4,128)S(1)} %copy.91), channel_id=1, source_target_pairs={{1,0},{0,1},{3,2},{2,3},{5,4},{4,5},{7,6},{6,7},{9,8},{8,9},{11,10... | collective-permute-start | bytes 19016 | tf_op jit(solution)/shard_map/ppermute | solution.py:328
  99.5 10.2 %copy-start.3 = (f32[32,108]{1,0:T(8,128)S(1)}, f32[32,108]{1,0:T(8,128)}, u32[]{:S(2)}) copy-start(f32[32,108]{1,0:T(8,128)} %get-tuple-element.11) | copy-start | bytes 41476
  99.5 10.2 %copy-start.4 = (f32[32,1]{1,0:T(8,128)S(1)}, f32[32,1]{1,0:T(8,128)}, u32[]{:S(2)}) copy-start(f32[32,1]{1,0:T(8,128)} %get-tuple-element.12) | copy-start | bytes 388
  100.7 3.8 %collective-permute-start.8 = (f32[6,1,4,128]{3,1,0,2:T(1,128)S(1)}, f32[6,1,4,128]{3,1,0,2:T(1,128)S(1)}, u32[]{:S(2)}, u32[]{:S(2)}) collective-permute-start(f32[6,1,4,128]{3,1,0,2:T(1,128)S(1)} %get-tuple-element.29), channel_id=1, source_target_pairs={{0,2},{2,4},{4,6},{6,0},{1,3},{3,5},{5,7},{7,1},{8,10},{10,12},{12... | collective-permute-start | bytes 36872 | tf_op jit(solution)/shard_map/ppermute | solution.py:272
  102.7 2.6 %collective-permute-start.9 = (f32[6,1,4,128]{3,1,0,2:T(1,128)S(1)}, f32[6,1,4,128]{3,1,0,2:T(1,128)S(1)}, u32[]{:S(2)}, u32[]{:S(2)}) collective-permute-start(f32[6,1,4,128]{3,1,0,2:T(1,128)S(1)} %get-tuple-element.28), channel_id=1, source_target_pairs={{2,0},{4,2},{6,4},{0,6},{3,1},{5,3},{7,5},{1,7},{10,8},{12,10},{14... | collective-permute-start | bytes 36872 | tf_op jit(solution)/shard_map/ppermute | solution.py:273
  105.4 29.0 %collective-permute-start.10 = (f32[1,64,4,128]{3,1,0,2:T(8,128)S(1)}, f32[1,64,4,128]{3,1,0,2:T(8,128)S(1)}, u32[]{:S(2)}, u32[]{:S(2)}) collective-permute-start(f32[1,64,4,128]{3,1,0,2:T(8,128)S(1)} %get-tuple-element.33), channel_id=1, source_target_pairs={{0,8},{8,16},{16,24},{24,32},{32,40},{40,48},{48,56},{56,64},{64,7... | collective-permute-start | bytes 393224 | tf_op jit(solution)/shard_map/ppermute | solution.py:272
  132.2 8.1 %collective-permute-start.11 = (f32[1,64,4,128]{3,1,0,2:T(8,128)S(1)}, f32[1,64,4,128]{3,1,0,2:T(8,128)S(1)}, u32[]{:S(2)}, u32[]{:S(2)}) collective-permute-start(f32[1,64,4,128]{3,1,0,2:T(8,128)S(1)} %get-tuple-element.32), channel_id=1, source_target_pairs={{8,0},{16,8},{24,16},{32,24},{40,32},{48,40},{56,48},{64,56},{72,6... | collective-permute-start | bytes 393224 | tf_op jit(solution)/shard_map/ppermute | solution.py:273
  140.3 0.8 copy-start.2

commit v6 on v5

--- a/solution.py
+++ b/solution.py
@@ -120,7 +120,7 @@
 
 
 def forward_kernel(rows, wide_y, w_ref, b_ref, q_ref, u_ref, wt_ref, p_ref, cot_ref,
-                   pooled_ref, wg_ref, bg_ref, main_ref, lo_ref, hi_ref, wg_acc, bg_acc):
+                   pooled_ref, wg_ref, bg_ref, main_ref, edge_ref, wg_acc, bg_acc):
     step = pl.program_id(0)
     plane = p_ref.shape[0] // 2
     lines = plane // 4
@@ -130,8 +130,7 @@
         wg_acc[...] = jnp.zeros_like(wg_acc)
         bg_acc[...] = jnp.zeros_like(bg_acc)
         main_ref[...] = jnp.zeros_like(main_ref)
-        lo_ref[...] = jnp.zeros_like(lo_ref)
-        hi_ref[...] = jnp.zeros_like(hi_ref)
+        edge_ref[...] = jnp.zeros_like(edge_ref)
 
     weight = w_ref[...]
     bias = b_ref[...]
@@ -151,6 +150,7 @@
         totals = [None, None]
         wg = None
         bg = None
+        spreads = []
         for px, base in enumerate((0, plane)):
             deltas = []
             for r in range(4):
@@ -173,25 +173,36 @@
                 wg = term if wg is None else wg + term
                 part = delta.astype(jnp.float32)
                 bg = part if bg is None else bg + part
-            spread = jnp.dot(
-                spread_w, jnp.concatenate(deltas, axis=1), preferred_element_type=jnp.float32
+            spreads.append(
+                jnp.dot(
+                    spread_w, jnp.concatenate(deltas, axis=1), preferred_element_type=jnp.float32
+                )
             )
-            x = step * 2 + px
+        acc_main = {}
+        acc_edge = {}
+        for px in range(2):
             for r in range(4):
-                y = j * 4 + r
+                cols = slice(r * rows, (r + 1) * rows)
                 for a in range(3):
                     for b in range(3):
                         at = (a * 3 + b) * 3 * slots
-                        cols = slice(r * rows, (r + 1) * rows)
-                        v0 = pltpu.roll(spread[at : at + slots, cols], rows - 1, 1)
-                        v1 = spread[at + slots : at + 2 * slots, cols]
-                        v2 = pltpu.roll(spread[at + 2 * slots : at + 3 * slots, cols], 1, 1)
-                        out = (x + a) * wide_y + (y + b)
-                        main_ref[out] += (
-                            jnp.where(last, 0.0, v0) + v1 + jnp.where(first, 0.0, v2)
-                        )
-                        lo_ref[out] += jnp.where(last, v0, 0.0)
-                        hi_ref[out] += jnp.where(first, v2, 0.0)
+                        g = spreads[px]
+                        v0 = pltpu.roll(g[at : at + slots, cols], rows - 1, 1)
+                        v1 = g[at + slots : at + 2 * slots, cols]
+                        v2 = pltpu.roll(g[at + 2 * slots : at + 3 * slots, cols], 1, 1)
+                        inner = jnp.where(last, 0.0, v0) + v1 + jnp.where(first, 0.0, v2)
+                        edge = jnp.where(last, v0, 0.0) + jnp.where(first, v2, 0.0)
+                        key = (px + a, r + b)
+                        if key in acc_main:
+                            acc_main[key] = acc_main[key] + inner
+                            acc_edge[key] = acc_edge[key] + edge
+                        else:
+                            acc_main[key] = inner
+                            acc_edge[key] = edge
+        for (dx, dy), value in acc_main.items():
+            out = (step * 2 + dx) * wide_y + (j * 4 + dy)
+            main_ref[out] += value[: main_ref.shape[1]]
+            edge_ref[out] += acc_edge[dx, dy][: edge_ref.shape[1]]
         wg_acc[...] += wg
         bg_acc[...] += jnp.sum(bg, axis=1, keepdims=True)
         pooled = jnp.dot(
@@ -228,7 +239,7 @@
     ).astype(jnp.bfloat16)
     full = lambda shape: pl.BlockSpec(shape, lambda p: (0,) * len(shape))
     block = lines // pairs
-    acc_shape = (wide_x * wide_y, slots, rows)
+    acc_shape = (wide_x * wide_y, chan_in, rows)
     return pl.pallas_call(
         lambda *refs: forward_kernel(rows, wide_y, *refs),
         grid=(pairs,),
@@ -236,7 +247,6 @@
             jax.ShapeDtypeStruct(cot.shape, jnp.bfloat16),
             jax.ShapeDtypeStruct((chan_out, taps), jnp.float32),
             jax.ShapeDtypeStruct((chan_out, 1), jnp.float32),
-            jax.ShapeDtypeStruct(acc_shape, jnp.float32),
             jax.ShapeDtypeStruct(acc_shape, jnp.float32),
             jax.ShapeDtypeStruct(acc_shape, jnp.float32),
         ),
@@ -253,7 +263,6 @@
             pl.BlockSpec((chan_out, cot.shape[1] // pairs), lambda p: (0, p)),
             full((chan_out, taps)),
             full((chan_out, 1)),
-            full(acc_shape),
             full(acc_shape),
             full(acc_shape),
         ),
@@ -306,7 +315,7 @@
     patches = patches.reshape(cells_x * cells_y, chan_in * 27, cells_z)
     cot = cotangent.reshape(chan_out, -1)
     wide_x, wide_y = cells_x + 2, cells_y + 2
-    pooled, weight_local, bias_local, main, lo, hi = forward(
+    pooled, weight_local, bias_local, main, edge = forward(
         weight, bias.reshape(chan_out, 1), patches, cot, cells_x // 2, wide_x, wide_y
     )
     pooled = pooled.reshape(cotangent.shape)
@@ -320,9 +329,10 @@
     both = allreduce(partial, sizes)
     weight_grad = both[:, :taps].reshape(chan_out, chan_in, 3, 3, 3)
     bias_grad = both[:, taps]
-    main = main.reshape(wide_x, wide_y, -1, cells_z)[:, :, :chan_in]
-    lo = lo.reshape(wide_x, wide_y, -1, cells_z)[:, :, :chan_in, cells_z - 1 :]
-    hi = hi.reshape(wide_x, wide_y, -1, cells_z)[:, :, :chan_in, :1]
+    main = main.reshape(wide_x, wide_y, chan_in, cells_z)
+    edge = edge.reshape(wide_x, wide_y, chan_in, cells_z)
+    lo = edge[..., cells_z - 1 :]
+    hi = edge[..., :1]
     count = lax.axis_size("gz")
     from_left = lax.ppermute(hi, "gz", [(i, (i + 1) % count) for i in range(count)])
     from_right = lax.ppermute(lo, "gz", [((i + 1) % count, i) for i in range(count)])

time: 142 us -> 137 us (0.965)
  local copies, waits for them, and re-layouts: 36.3 us -> 32.1 us
    slice x2 -> x1, local copies, waits for them, and re-layouts: 3.55 us -> 1.94 us  [on_device(): hi = edge[..., :1]]
    slice x1, local copies, waits for them, and re-layouts: 3.35 us -> 1.92 us  [on_device(): main[..., :1] + from_left]
  transfers between devices with their start and end apart: 12 -> 12, of which waited for: 9 -> 9; matrix products, arithmetic and copies ran while one was open for 17% -> 14% of each run, Pallas kernels for 12% -> 12%
where the time goes in v6:
time: 137 us; the launch traced here: 136 us
  Pallas kernels  55.9 us (41%)
  local copies, waits for them, and re-layouts  32.1 us (23%)
  waiting for transfers between devices  21.9 us (16%)
  starting transfers between devices  19.9 us (15%)
  other arithmetic  5.08 us (4%)
    pallas_call x1, Pallas kernels, forward(): pl.pallas_call(lambda *refs: forward_kernel(rows, wide_y, *refs), grid=(p...  39.4 us
    pallas_call x1, Pallas kernels, allreduce(): pl.pallas_call(lambda *refs: allreduce_kernel(sizes, *refs), out_shape=ja...  16.5 us
    ppermute x3, waiting for transfers between devices, extended(): lax.ppermute(head, axis, [((i + 1) % count, i) for i in range(count)])  10 us
    reshape x1, local copies, waits for them, and re-layouts, on_device(): patches = patches.reshape(cells_x * cells_y, chan_in * 27, cells_z)  7.54 us
    unnamed x37, local copies, waits for them, and re-layouts  7.44 us
    ppermute x2, waiting for transfers between devices, fold_halo(): lax.ppermute(head, axis, [((i + 1) % count, i) for i in range(count)])  6.4 us
    ppermute x3, starting transfers between devices, extended(): lax.ppermute(tail, axis, [(i, (i + 1) % count) for i in range(count)])  6.32 us
    ppermute x2, starting transfers between devices, fold_halo(): lax.ppermute(tail, axis, [(i, (i + 1) % count) for i in range(count)])  5.7 us
  transfers between devices with their start and end apart: 12, of which 9 were waited for; matrix products, arithmetic and copies ran while one was open for 14% of the time, Pallas kernels for 12%

profile of v6, /device:TPU:7, one launch (start us, length us, event | category | flops | bytes accessed | tf_op | source)
XLA Modules:
  0.0 136.0 jit_solution(17693277695719057812)
XLA Ops:
  1.6 4.1 %collective-permute-start = (bf16[4,1,64,128]{3,2,1,0:T(8,128)(2,1)S(1)}, bf16[4,1,64,128]{3,2,1,0:T(8,128)(2,1)S(1)}, u32[]{:S(2)}, u32[]{:S(2)}) collective-permute-start(bf16[4,1,64,128]{3,2,1,0:T(8,128)(2,1)S(1)} %get-tuple-element.41), channel_id=1, source_target_pairs={{0,8},{8,16},{16,24},{24,32},{32,40},{40,48},{48,56},{56,64},{64,7... | collective-permute-start | bytes 196616 | tf_op jit(solution)/shard_map/ppermute | solution.py:22
  5.9 1.1 collective-permute-done
  8.0 5.0 %collective-permute-done.1 = bf16[4,1,64,128]{3,2,1,0:T(8,128)(2,1)S(1)} collective-permute-done((bf16[4,1,64,128]{3,2,1,0:T(8,128)(2,1)S(1)}, bf16[4,1,64,128]{3,2,1,0:T(8,128)(2,1)S(1)}, u32[]{:S(2)}, u32[]{:S(2)}) %collective-permute-start.1) | collective-permute-done | bytes 65568 | tf_op jit(solution)/shard_map/ppermute | solution.py:24
  13.1 1.4 %collective-permute-start.2 = (bf16[4,6,1,128]{3,2,1,0:T(2,128)(2,1)S(1)}, bf16[4,6,1,128]{3,2,1,0:T(2,128)(2,1)S(1)}, u32[]{:S(2)}, u32[]{:S(2)}) collective-permute-start(bf16[4,6,1,128]{3,2,1,0:T(2,128)(2,1)S(1)} %get-tuple-element.38), channel_id=1, source_target_pairs={{0,2},{2,4},{4,6},{6,0},{1,3},{3,5},{5,7},{7,1},{8,10},{10,12},{12... | collective-permute-start | bytes 18440 | tf_op jit(solution)/shard_map/ppermute | solution.py:22
  14.4 1.5 %collective-permute-start.3 = (bf16[4,6,1,128]{3,2,1,0:T(2,128)(2,1)S(1)}, bf16[4,6,1,128]{3,2,1,0:T(2,128)(2,1)S(1)}, u32[]{:S(2)}, u32[]{:S(2)}) collective-permute-start(bf16[4,6,1,128]{3,2,1,0:T(2,128)(2,1)S(1)} %get-tuple-element.39), channel_id=1, source_target_pairs={{2,0},{4,2},{6,4},{0,6},{3,1},{5,3},{7,5},{1,7},{10,8},{12,10},{14... | collective-permute-start | bytes 18440 | tf_op jit(solution)/shard_map/ppermute | solution.py:24
  19.8 2.2 %reshape.237.refs_6_ = bf16[32,4096]{1,0:T(8,128)(2,1)} reshape(bf16[32,2,32,64]{3,2,1,0:T(8,128)(2,1)} %param.7) | data formatting | bytes 524288 | tf_op jit(solution)/shard_map/reshape | solution.py:316
  23.5 1.3 copy.76.refs_1_
  24.9 1.4 %pad.4 = bf16[3,3,3,8,32]{4,3,2,1,0:T(8,128)(2,1)} pad(bf16[3,3,3,4,32]{4,3,2,1,0:T(4,128)(2,1)} %bitcast.227, bf16[]{:T(256)} %constant.43.clone.1), padding=0_0x0_0x0_0x0_4x0_0 | pad | bytes 20738 | tf_op jit(solution)/shard_map/jit(_pad)/pad | solution.py:229
  26.3 3.7 %collective-permute-done.4 = bf16[4,6,66,1]{3,2,1,0:T(8,128)(2,1)S(1)} collective-permute-done((bf16[4,6,66,1]{3,2,1,0:T(8,128)(2,1)S(1)}, bf16[4,6,66,1]{3,2,1,0:T(8,128)(2,1)S(1)}, u32[]{:S(2)}, u32[]{:S(2)}) %collective-permute-start.4) | collective-permute-done | bytes 3200 | tf_op jit(solution)/shard_map/ppermute | solution.py:22
  30.0 4.7 %collective-permute-done.5 = bf16[4,6,66,1]{3,2,1,0:T(8,128)(2,1)S(1)} collective-permute-done((bf16[4,6,66,1]{3,2,1,0:T(8,128)(2,1)S(1)}, bf16[4,6,66,1]{3,2,1,0:T(8,128)(2,1)S(1)}, u32[]{:S(2)}, u32[]{:S(2)}) %collective-permute-start.5) | collective-permute-done | bytes 3200 | tf_op jit(solution)/shard_map/ppermute | solution.py:24
  34.7 1.1 pad_maximum_fusion
  39.7 7.5 %copy.77.refs_5_ = bf16[256,108,128]{2,1,0:T(8,128)(2,1)} copy(bf16[256,108,128]{2,0,1:T(8,128)(2,1)S(1)} %bitcast.220) | data formatting | bytes 14155776 | tf_op jit(solution)/shard_map/reshape | solution.py:315
  47.3 39.4 %shard_map.75 = (bf16[32,4096]{1,0:T(8,128)(2,1)}, f32[32,108]{1,0:T(8,128)}, f32[32,1]{1,0:T(8,128)}, f32[396,4,128]{2,1,0:T(4,128)}, f32[396,4,128]{2,1,0:T(4,128)}) custom-call(bf16[32,108]{1,0:T(8,128)(2,1)} %copy.75.refs_0_, f32[32,1]{1,0:T(8,128)} %copy.76.refs_1_, f32[2,128,128]{2,1,0:T(8,128)} %add_convert_fusion.refs_2_, ...), custom_call_target="tpu_custom_call" | custom-call | tf_op jit(solution)/shard_map/pallas_call | solution.py:243
  86.6 1.9 %fusion.40 = (f32[6,66,4,1]{3,2,1,0:T(4,128)S(1)}, f32[6,66,4,1]{3,2,1,0:T(4,128)S(1)}) fusion(f32[6,66,4,128]{3,2,1,0:T(4,128)} %bitcast.223), kind=kLoop, calls=%fused_computation.97 | loop fusion | bytes 25344 | tf_op jit(solution)/shard_map/slice | solution.py:335
  88.9 1.7 %collective-permute-start.6 = (f32[6,66,4,1]{1,2,3,0:T(4,128)S(1)}, f32[6,66,4,1]{1,2,3,0:T(4,128)S(1)}, u32[]{:S(2)}, u32[]{:S(2)}) collective-permute-start(f32[6,66,4,1]{1,2,3,0:T(4,128)S(1)} %copy.88), channel_id=1, source_target_pairs={{0,1},{1,0},{2,3},{3,2},{4,5},{5,4},{6,7},{7,6},{8,9},{9,8},{10,11... | collective-permute-start | bytes 19016 | tf_op jit(solution)/shard_map/ppermute | solution.py:337
  91.3 1.9 %fusion.41 = (f32[6,66,4,1]{3,2,1,0:T(4,128)S(1)}, f32[6,66,4,1]{3,2,1,0:T(4,128)S(1)}) fusion(f32[6,66,4,128]{3,2,1,0:T(4,128)} %bitcast.221), kind=kLoop, calls=%fused_computation.98 | loop fusion | bytes 25344 | tf_op jit(solution)/shard_map/slice | solution.py:341
  95.6 1.4 %collective-permute-start.8 = (f32[6,1,4,128]{3,1,0,2:T(1,128)S(1)}, f32[6,1,4,128]{3,1,0,2:T(1,128)S(1)}, u32[]{:S(2)}, u32[]{:S(2)}) collective-permute-start(f32[6,1,4,128]{3,1,0,2:T(1,128)S(1)} %get-tuple-element.27), channel_id=1, source_target_pairs={{0,2},{2,4},{4,6},{6,0},{1,3},{3,5},{5,7},{7,1},{8,10},{10,12},{12... | collective-permute-start | bytes 36872 | tf_op jit(solution)/shard_map/ppermute | solution.py:281
  97.6 1.4 %collective-permute-start.9 = (f32[6,1,4,128]{3,1,0,2:T(1,128)S(1)}, f32[6,1,4,128]{3,1,0,2:T(1,128)S(1)}, u32[]{:S(2)}, u32[]{:S(2)}) collective-permute-start(f32[6,1,4,128]{3,1,0,2:T(1,128)S(1)} %get-tuple-element.26), channel_id=1, source_target_pairs={{2,0},{4,2},{6,4},{0,6},{3,1},{5,3},{7,5},{1,7},{10,8},{12,10},{14... | collective-permute-start | bytes 36872 | tf_op jit(solution)/shard_map/ppermute | solution.py:282
  100.3 4.3 %collective-permute-start.10 = (f32[1,64,4,128]{3,1,0,2:T(8,128)S(1)}, f32[1,64,4,128]{3,1,0,2:T(8,128)S(1)}, u32[]{:S(2)}, u32[]{:S(2)}) collective-permute-start(f32[1,64,4,128]{3,1,0,2:T(8,128)S(1)} %get-tuple-element.33), channel_id=1, source_target_pairs={{0,8},{8,16},{16,24},{24,32},{32,40},{40,48},{48,56},{56,64},{64,7... | collective-permute-start | bytes 393224 | tf_op jit(solution)/shard_map/ppermute | solution.py:281
  105.3 16.5 %shard_map.76 = f32[32,128]{1,0:T(8,128)} custom-call(f32[32,128]{1,0:T(8,128)} %maximum_maximum_fusion.1.refs_0_), custom_call_target="tpu_custom_call" | custom-call | tf_op jit(solution)/shard_map/pallas_call | solution.py:90
  123.4 2.3 %reshape.238 = bf16[32,2,32,64]{3,2,1,0:T(8,128)(2,1)} reshape(bf16[32,4096]{1,0:T(8,128)(2,1)} %get-tuple-element.9) | data formatting | bytes 524288 | tf_op jit(solution)/shard_map/reshape | solution.py:321
  125.6 1.4 %slice_reduce_fusion = f32[32]{0:T(128)} fusion(f32[32,128]{1,0:T(8,128)} %shard_map.76), kind=kLoop, calls=%fused_computation.87 | loop fusion | bytes 256 | tf_op jit(solution)/shard_map/slice | solution.py:331
  127.1 2.2 %collective-permute-start.11 = (f32[1,64,4,128]{3,1,0,2:T(8,128)S(1)}, f32[1,64,4,128]{3,1,0,2:T(8,128)S(1)}, u32[]{:S(2)}, u32[]{:S(2)}) collective-permute-start(f32[1,64,4,128]{3,1,0,2:T(8,128)S(1)} %get-tuple-element.32), channel_id=1, source_target_pairs={{8,0},{16,8},{24,16},{32,24},{40,32},{48,40},{56,48},{64,56},{72,6... | collective-permute-start | bytes 393224 | tf_op jit(solution)/shard_map/ppermute | solution.py:282
  129.3 5.8 %collective-permute-done.11 = f32[1,64,4,128]{3,1,0,2:T(8,128)S(1)} collective-permute-done((f32[1,64,4,128]{3,1,0,2:T(8,128)S(1)}, f32[1,64,4,128]{3,1,0,2:T(8,128)S(1)}, u32[]{:S(2)}, u32[]{:S(2)}) %collective-permute-start.11) | collective-permute-done | bytes 131104 | tf_op jit(solution)/shard_map/ppermute | solution.py:282
  (90 shorter events, 19.6 us)
Async XLA Ops:
  0.6 35.6 %copy-start.1 = (bf16[4,4,64,128]{3,2,1,0:T(8,128)(2,1)S(1)}, bf16[4,4,64,128]{3,2,1,0:T(8,128)(2,1)}, u32[]{:S(2)}) copy-start(bf16[4,4,64,128]{3,2,1,0:T(8,128)(2,1)} %param.4) | copy-start | bytes 786436
  1.6 5.5 %collective-permute-start = (bf16[4,1,64,128]{3,2,1,0:T(8,128)(2,1)S(1)}, bf16[4,1,64,128]{3,2,1,0:T(8,128)(2,1)S(1)}, u32[]{:S(2)}, u32[]{:S(2)}) collective-permute-start(bf16[4,1,64,128]{3,2,1,0:T(8,128)(2,1)S(1)} %get-tuple-element.41), channel_id=1, source_target_pairs={{0,8},{8,16},{16,24},{24,32},{32,40},{40,48},{48,56},{56,64},{64,7... | collective-permute-start | bytes 196616 | tf_op jit(solution)/shard_map/ppermute | solution.py:22
  5.7 7.3 %collective-permute-start.1 = (bf16[4,1,64,128]{3,2,1,0:T(8,128)(2,1)S(1)}, bf16[4,1,64,128]{3,2,1,0:T(8,128)(2,1)S(1)}, u32[]{:S(2)}, u32[]{:S(2)}) collective-permute-start(bf16[4,1,64,128]{3,2,1,0:T(8,128)(2,1)S(1)} %get-tuple-element.40), channel_id=1, source_target_pairs={{8,0},{16,8},{24,16},{32,24},{40,32},{48,40},{56,48},{64,56},{72,6... | collective-permute-start | bytes 196616 | tf_op jit(solution)/shard_map/ppermute | solution.py:24
  13.1 3.9 %collective-permute-start.2 = (bf16[4,6,1,128]{3,2,1,0:T(2,128)(2,1)S(1)}, bf16[4,6,1,128]{3,2,1,0:T(2,128)(2,1)S(1)}, u32[]{:S(2)}, u32[]{:S(2)}) collective-permute-start(bf16[4,6,1,128]{3,2,1,0:T(2,128)(2,1)S(1)} %get-tuple-element.38), channel_id=1, source_target_pairs={{0,2},{2,4},{4,6},{6,0},{1,3},{3,5},{5,7},{7,1},{8,10},{10,12},{12... | collective-permute-start | bytes 18440 | tf_op jit(solution)/shard_map/ppermute | solution.py:22
  14.4 2.8 %collective-permute-start.3 = (bf16[4,6,1,128]{3,2,1,0:T(2,128)(2,1)S(1)}, bf16[4,6,1,128]{3,2,1,0:T(2,128)(2,1)S(1)}, u32[]{:S(2)}, u32[]{:S(2)}) collective-permute-start(bf16[4,6,1,128]{3,2,1,0:T(2,128)(2,1)S(1)} %get-tuple-element.39), channel_id=1, source_target_pairs={{2,0},{4,2},{6,4},{0,6},{3,1},{5,3},{7,5},{1,7},{10,8},{12,10},{14... | collective-permute-start | bytes 18440 | tf_op jit(solution)/shard_map/ppermute | solution.py:24
  17.6 12.3 %collective-permute-start.4 = (bf16[4,6,66,1]{3,2,1,0:T(8,128)(2,1)S(1)}, bf16[4,6,66,1]{3,2,1,0:T(8,128)(2,1)S(1)}, u32[]{:S(2)}, u32[]{:S(2)}) collective-permute-start(bf16[4,6,66,1]{3,2,1,0:T(8,128)(2,1)S(1)} %get-tuple-element.35), channel_id=1, source_target_pairs={{0,1},{1,0},{2,3},{3,2},{4,5},{5,4},{6,7},{7,6},{8,9},{9,8},{10,11... | collective-permute-start | bytes 9512 | tf_op jit(solution)/shard_map/ppermute | solution.py:22
  18.5 16.2 %collective-permute-start.5 = (bf16[4,6,66,1]{3,2,1,0:T(8,128)(2,1)S(1)}, bf16[4,6,66,1]{3,2,1,0:T(8,128)(2,1)S(1)}, u32[]{:S(2)}, u32[]{:S(2)}) collective-permute-start(bf16[4,6,66,1]{3,2,1,0:T(8,128)(2,1)S(1)} %get-tuple-element.34), channel_id=1, source_target_pairs={{1,0},{0,1},{3,2},{2,3},{5,4},{4,5},{7,6},{6,7},{9,8},{8,9},{11,10... | collective-permute-start | bytes 9512 | tf_op jit(solution)/shard_map/ppermute | solution.py:24
  86.6 6.6 %copy-start = (f32[396,4,128]{2,1,0:T(4,128)S(1)}, f32[396,4,128]{2,1,0:T(4,128)}, u32[]{:S(2)}) copy-start(f32[396,4,128]{2,1,0:T(4,128)} %get-tuple-element.12) | copy-start | bytes 2433028
  88.9 5.6 %collective-permute-start.6 = (f32[6,66,4,1]{1,2,3,0:T(4,128)S(1)}, f32[6,66,4,1]{1,2,3,0:T(4,128)S(1)}, u32[]{:S(2)}, u32[]{:S(2)}) collective-permute-start(f32[6,66,4,1]{1,2,3,0:T(4,128)S(1)} %copy.88), channel_id=1, source_target_pairs={{0,1},{1,0},{2,3},{3,2},{4,5},{5,4},{6,7},{7,6},{8,9},{9,8},{10,11... | collective-permute-start | bytes 19016 | tf_op jit(solution)/shard_map/ppermute | solution.py:337
  91.0 4.0 %collective-permute-start.7 = (f32[6,66,4,1]{1,2,3,0:T(4,128)S(1)}, f32[6,66,4,1]{1,2,3,0:T(4,128)S(1)}, u32[]{:S(2)}, u32[]{:S(2)}) collective-permute-start(f32[6,66,4,1]{1,2,3,0:T(4,128)S(1)} %copy.91), channel_id=1, source_target_pairs={{1,0},{0,1},{3,2},{2,3},{5,4},{4,5},{7,6},{6,7},{9,8},{8,9},{11,10... | collective-permute-start | bytes 19016 | tf_op jit(solution)/shard_map/ppermute | solution.py:338
  94.4 10.2 %copy-start.3 = (f32[32,108]{1,0:T(8,128)S(1)}, f32[32,108]{1,0:T(8,128)}, u32[]{:S(2)}) copy-start(f32[32,108]{1,0:T(8,128)} %get-tuple-element.10) | copy-start | bytes 41476
  94.4 10.2 %copy-start.4 = (f32[32,1]{1,0:T(8,128)S(1)}, f32[32,1]{1,0:T(8,128)}, u32[]{:S(2)}) copy-start(f32[32,1]{1,0:T(8,128)} %get-tuple-element.11) | copy-start | bytes 388
  95.6 3.8 %collective-permute-start.8 = (f32[6,1,4,128]{3,1,0,2:T(1,128)S(1)}, f32[6,1,4,128]{3,1,0,2:T(1,128)S(1)}, u32[]{:S(2)}, u32[]{:S(2)}) collective-permute-start(f32[6,1,4,128]{3,1,0,2:T(1,128)S(1)} %get-tuple-element.27), channel_id=1, source_target_pairs={{0,2},{2,4},{4,6},{6,0},{1,3},{3,5},{5,7},{7,1},{8,10},{10,12},{12... | collective-permute-start | bytes 36872 | tf_op jit(solution)/shard_map/ppermute | solution.py:281
  97.6 2.6 %collective-permute-start.9 = (f32[6,1,4,128]{3,1,0,2:T(1,128)S(1)}, f32[6,1,4,128]{3,1,0,2:T(1,128)S(1)}, u32[]{:S(2)}, u32[]{:S(2)}) collective-permute-start(f32[6,1,4,128]{3,1,0,2:T(1,128)S(1)} %get-tuple-element.26), channel_id=1, source_target_pairs={{2,0},{4,2},{6,4},{0,6},{3,1},{5,3},{7,5},{1,7},{10,8},{12,10},{14... | collective-permute-start | bytes 36872 | tf_op jit(solution)/shard_map/ppermute | solution.py:282
  100.3 29.0 %collective-permute-start.10 = (f32[1,64,4,128]{3,1,0,2:T(8,128)S(1)}, f32[1,64,4,128]{3,1,0,2:T(8,128)S(1)}, u32[]{:S(2)}, u32[]{:S(2)}) collective-permute-start(f32[1,64,4,128]{3,1,0,2:T(8,128)S(1)} %get-tuple-element.33), channel_id=1, source_target_pairs={{0,8},{8,16},{16,24},{24,32},{32,40},{40,48},{48,56},{56,64},{64,7... | collective-permute-start | bytes 393224 | tf_op jit(solution)/shard_map/ppermute | solution.py:281
  127.1 8.1 %collective-permute-start.11 = (f32[1,64,4,128]{3,1,0,2:T(8,128)S(1)}, f32[1,64,4,128]{3,1,0,2:T(8,128)S(1)}, u32[]{:S(2)}, u32[]{:S(2)}) collective-permute-start(f32[1,64,4,128]{3,1,0,2:T(8,128)S(1)} %get-tuple-element.32), channel_id=1, source_target_pairs={{8,0},{16,8},{24,16},{32,24},{40,32},{48,40},{56,48},{64,56},{72,6... | collective-permute-start | bytes 393224 | tf_op jit(solution)/shard_map/ppermute | solution.py:282
  135.2 0.8 copy-start.2

commit v7 on v6

--- a/solution.py
+++ b/solution.py
@@ -12,17 +12,21 @@
 soft_scale = 10.0
 
 
+def shift(piece, axis, dim, step):
+    count = lax.axis_size(axis)
+    pairs = [(i, (i + step) % count) for i in range(count)]
+    if piece.shape[dim] == 1:
+        moved = lax.ppermute(jnp.squeeze(piece, dim), axis, pairs)
+        return jnp.expand_dims(moved, dim)
+    return lax.ppermute(piece, axis, pairs)
+
+
 def extended(cells, sides, width):
     for axis, dim in sides:
-        count = lax.axis_size(axis)
         head = lax.slice_in_dim(cells, 0, width, axis=dim)
         tail = lax.slice_in_dim(cells, cells.shape[dim] - width, cells.shape[dim], axis=dim)
         cells = jnp.concatenate(
-            [
-                lax.ppermute(tail, axis, [(i, (i + 1) % count) for i in range(count)]),
-                cells,
-                lax.ppermute(head, axis, [((i + 1) % count, i) for i in range(count)]),
-            ],
+            [shift(tail, axis, dim, 1), cells, shift(head, axis, dim, -1)],
             axis=dim,
         )
     return cells
@@ -274,12 +278,11 @@
 
 
 def fold_halo(main, axis, dim, width):
-    count = lax.axis_size(axis)
     size = main.shape[dim]
     head = lax.slice_in_dim(main, 0, width, axis=dim)
     tail = lax.slice_in_dim(main, size - width, size, axis=dim)
-    from_left = lax.ppermute(tail, axis, [(i, (i + 1) % count) for i in range(count)])
-    from_right = lax.ppermute(head, axis, [((i + 1) % count, i) for i in range(count)])
+    from_left = shift(tail, axis, dim, 1)
+    from_right = shift(head, axis, dim, -1)
     inner = lax.slice_in_dim(main, width, size - width, axis=dim)
     inner_size = size - 2 * width
     start = [0] * main.ndim
@@ -305,12 +308,11 @@
     widened = extended(cells, (("gx", 1), ("gy", 2), ("gz", 3)), 1)
     patches = jnp.stack(
         [
-            jnp.transpose(
-                widened[:, sa : sa + cells_x, sb : sb + cells_y, se : se + cells_z], (1, 2, 0, 3)
-            )
+            widened[c, sa : sa + cells_x, sb : sb + cells_y, se : se + cells_z]
+            for c in range(chan_in)
             for sa, sb, se in stencil
         ],
-        axis=3,
+        axis=2,
     )
     patches = patches.reshape(cells_x * cells_y, chan_in * 27, cells_z)
     cot = cotangent.reshape(chan_out, -1)
@@ -333,9 +335,8 @@
     edge = edge.reshape(wide_x, wide_y, chan_in, cells_z)
     lo = edge[..., cells_z - 1 :]
     hi = edge[..., :1]
-    count = lax.axis_size("gz")
-    from_left = lax.ppermute(hi, "gz", [(i, (i + 1) % count) for i in range(count)])
-    from_right = lax.ppermute(lo, "gz", [((i + 1) % count, i) for i in range(count)])
+    from_left = shift(hi, "gz", 3, 1)
+    from_right = shift(lo, "gz", 3, -1)
     main = jnp.concatenate(
         [
             main[..., :1] + from_left,

time: 137 us -> 267 us (1.95); the launches traced: 136 us -> 263 us
  local copies, waits for them, and re-layouts: 32.1 us -> 144 us
  other arithmetic: 5.08 us -> 29.2 us
  waiting for transfers between devices: 21.9 us -> 7.85 us
  starting transfers between devices: 19.9 us -> 24.7 us
    another operation x1 -> x109, local copies, waits for them, and re-layouts: 0.24 us -> 123 us  [on_device(): jnp.stack([widened[c, sa:sa + cells_x, sb:sb + cells_y, se:se + cells_z]...]
    concatenate x1, other arithmetic: 0.52 us -> 25.1 us  [on_device(): jnp.concatenate([main[..., :1] + from_left, main[..., 1:cells_z - 1], mai...]
    ppermute x12, waiting for transfers between devices: 21.9 us -> 7.85 us  [shift(): moved = lax.ppermute(jnp.squeeze(piece, dim), axis, pairs)]
    reshape x1 -> x0, local copies, waits for them, and re-layouts: 7.54 us -> none  [on_device(): patches = patches.reshape(cells_x * cells_y, chan_in * 27, cells_z)]
    ppermute x12, starting transfers between devices: 19.9 us -> 24.7 us  [shift(): moved = lax.ppermute(jnp.squeeze(piece, dim), axis, pairs)]
    unnamed x37 -> x38, local copies, waits for them, and re-layouts: 7.44 us -> 3.66 us
  transfers between devices with their start and end apart: 12 -> 12, of which waited for: 9 -> 3; matrix products, arithmetic and copies ran while one was open for 14% -> 22% of each run, Pallas kernels for 12% -> 6%
where the time goes in v7:
time: 267 us; the launch traced here: 263 us
  local copies, waits for them, and re-layouts  144 us (54%)
  Pallas kernels  55.5 us (21%)
  other arithmetic  29.2 us (11%)
  starting transfers between devices  24.7 us (9%)
  waiting for transfers between devices  7.85 us (3%)
    another operation x109, local copies, waits for them, and re-layouts, on_device(): jnp.stack([widened[c, sa:sa + cells_x, sb:sb + cells_y, se:se + cells_z]...  123 us
    pallas_call x1, Pallas kernels, forward(): pl.pallas_call(lambda *refs: forward_kernel(rows, wide_y, *refs), grid=(p...  39.3 us
    concatenate x1, other arithmetic, on_device(): jnp.concatenate([main[..., :1] + from_left, main[..., 1:cells_z - 1], mai...  25.1 us
    ppermute x12, starting transfers between devices, shift(): moved = lax.ppermute(jnp.squeeze(piece, dim), axis, pairs)  24.7 us
    pallas_call x1, Pallas kernels, allreduce(): pl.pallas_call(lambda *refs: allreduce_kernel(sizes, *refs), out_shape=ja...  16.2 us
    ppermute x12, waiting for transfers between devices, shift(): moved = lax.ppermute(jnp.squeeze(piece, dim), axis, pairs)  7.85 us
  transfers between devices with their start and end apart: 12, of which 3 were waited for; matrix products, arithmetic and copies ran while one was open for 22% of the time, Pallas kernels for 6%

profile of v7, /device:TPU:7, one launch (start us, length us, event | category | flops | bytes accessed | tf_op | source)
XLA Modules:
  0.0 262.8 jit_solution(17561895857338348647)
XLA Ops:
  0.7 0.9 slice_bitcast_fusion.4
  1.6 4.1 %collective-permute-start = (bf16[4,64,128]{2,1,0:T(8,128)(2,1)S(1)}, bf16[4,64,128]{2,1,0:T(8,128)(2,1)S(1)}, u32[]{:S(2)}, u32[]{:S(2)}) collective-permute-start(bf16[4,64,128]{2,1,0:T(8,128)(2,1)S(1)} %get-tuple-element.153), channel_id=1, source_target_pairs={{0,8},{8,16},{16,24},{24,32},{32,40},{40,48},{48,56},{56,64},{64,7... | collective-permute-start | bytes 196616 | tf_op jit(solution)/shard_map/ppermute | solution.py:19
  5.7 0.8 slice.572
  6.9 2.2 reshape.450.refs_6_
  10.6 1.3 copy.284.refs_1_
  14.0 1.4 collective-permute-start.2
  15.3 1.5 collective-permute-start.3
  21.4 1.0 collective-permute-start.5
  37.6 1.0 pad_maximum_fusion
  81.5 1.0 copy.201
  94.6 52.6 %stack.339.refs_5_ = bf16[256,108,128]{2,1,0:T(8,128)(2,1)} concatenate(bf16[256,1,128]{2,1,0:T(2,128)(2,1)} %copy.175, bf16[256,1,128]{2,1,0:T(2,128)(2,1)S(1)} %copy.176, bf16[256,1,128]{2,1,0:T(2,128)(2,1)} %copy.177, bf16[256,1,128]{2,1,0:T(2,128)(2,1)} %copy.178, bf16[256,1,128]{2,1,0:T(2,128)(2,1)S(1)} %copy.179, bf16[256,1,128]{2,1,0:T(2,128)(2,1)} %copy.180, ...), dimensions={1} | concatenate | bytes 14155776 | tf_op jit(solution)/shard_map/stack | solution.py:309
  147.1 39.3 %shard_map.75 = (bf16[32,4096]{1,0:T(8,128)(2,1)}, f32[32,108]{1,0:T(8,128)}, f32[32,1]{1,0:T(8,128)}, f32[396,4,128]{2,1,0:T(4,128)}, f32[396,4,128]{2,1,0:T(4,128)}) custom-call(bf16[32,108]{1,0:T(8,128)(2,1)} %copy.283.refs_0_, f32[32,1]{1,0:T(8,128)} %copy.284.refs_1_, f32[2,128,128]{2,1,0:T(8,128)} %add_convert_fusion.refs_2_, ...), custom_call_target="tpu_custom_call" | custom-call | tf_op jit(solution)/shard_map/pallas_call | solution.py:247
  186.5 1.9 fusion.8
  188.8 0.8 collective-permute-start.6
  192.4 1.0 collective-permute-done.7
  194.3 25.1 %pad_maximum_fusion.1 = f32[6,66,4,128]{3,2,0,1:T(4,128)S(1)} fusion(f32[6,66,4,1]{3,2,0,1:T(4,128)S(1)} %copy.292, f32[6,66,4,1]{3,2,0,1:T(4,128)S(1)} %copy.291, f32[6,66,4,128]{3,2,1,0:T(4,128)S(1)} %bitcast.173), kind=kLoop, calls=%fused_computation.2 | loop fusion | flops 405504 | bytes 1634688 | tf_op jit(solution)/shard_map/concatenate | solution.py:340
  219.5 2.7 %collective-permute-start.9 = (f32[6,4,128]{2,1,0:T(4,128)S(1)}, f32[6,4,128]{2,1,0:T(4,128)S(1)}, u32[]{:S(2)}, u32[]{:S(2)}) collective-permute-start(f32[6,4,128]{2,1,0:T(4,128)S(1)} %get-tuple-element.26), channel_id=1, source_target_pairs={{0,6},{2,0},{4,2},{6,4},{1,7},{3,1},{5,3},{7,5},{8,14},{10,8},{12,... | collective-permute-start | bytes 36872 | tf_op jit(solution)/shard_map/ppermute | solution.py:19
  223.2 9.6 %collective-permute-start.10 = (f32[64,4,128]{2,0,1:T(8,128)S(1)}, f32[64,4,128]{2,0,1:T(8,128)S(1)}, u32[]{:S(2)}, u32[]{:S(2)}) collective-permute-start(f32[64,4,128]{2,0,1:T(8,128)S(1)} %get-tuple-element.105), channel_id=1, source_target_pairs={{0,8},{8,16},{16,24},{24,32},{32,40},{40,48},{48,56},{56,64},{64,7... | collective-permute-start | bytes 393224 | tf_op jit(solution)/shard_map/ppermute | solution.py:19
  233.5 16.2 %shard_map.76 = f32[32,128]{1,0:T(8,128)} custom-call(f32[32,128]{1,0:T(8,128)} %maximum_maximum_fusion.2.refs_0_), custom_call_target="tpu_custom_call" | custom-call | tf_op jit(solution)/shard_map/pallas_call | solution.py:94
  249.6 0.8 copy.285
  251.1 1.3 reshape.451
  252.5 1.4 slice_reduce_fusion
  253.9 1.7 collective-permute-start.11
  255.7 6.3 %collective-permute-done.11 = f32[64,4,128]{2,0,1:T(8,128)S(1)} collective-permute-done((f32[64,4,128]{2,0,1:T(8,128)S(1)}, f32[64,4,128]{2,0,1:T(8,128)S(1)}, u32[]{:S(2)}, u32[]{:S(2)}) %collective-permute-start.11) | collective-permute-done | bytes 131104 | tf_op jit(solution)/shard_map/ppermute | solution.py:19
  (207 shorter events, 85.5 us)
Async XLA Ops:
  1.6 12.3 %collective-permute-start = (bf16[4,64,128]{2,1,0:T(8,128)(2,1)S(1)}, bf16[4,64,128]{2,1,0:T(8,128)(2,1)S(1)}, u32[]{:S(2)}, u32[]{:S(2)}) collective-permute-start(bf16[4,64,128]{2,1,0:T(8,128)(2,1)S(1)} %get-tuple-element.153), channel_id=1, source_target_pairs={{0,8},{8,16},{16,24},{24,32},{32,40},{40,48},{48,56},{56,64},{64,7... | collective-permute-start | bytes 196616 | tf_op jit(solution)/shard_map/ppermute | solution.py:19
  5.7 8.2 %collective-permute-start.1 = (bf16[4,64,128]{2,1,0:T(8,128)(2,1)S(1)}, bf16[4,64,128]{2,1,0:T(8,128)(2,1)S(1)}, u32[]{:S(2)}, u32[]{:S(2)}) collective-permute-start(bf16[4,64,128]{2,1,0:T(8,128)(2,1)S(1)} %get-tuple-element.154), channel_id=1, source_target_pairs={{0,120},{8,0},{16,8},{24,16},{32,24},{40,32},{48,40},{56,48},{64,5... | collective-permute-start | bytes 196616 | tf_op jit(solution)/shard_map/ppermute | solution.py:19
  14.0 5.5 %collective-permute-start.2 = (bf16[4,6,128]{2,0,1:T(4,128)(2,1)S(1)}, bf16[4,6,128]{2,0,1:T(4,128)(2,1)S(1)}, u32[]{:S(2)}, u32[]{:S(2)}) collective-permute-start(bf16[4,6,128]{2,0,1:T(4,128)(2,1)S(1)} %bitcast.306), channel_id=1, source_target_pairs={{0,2},{2,4},{4,6},{6,0},{1,3},{3,5},{5,7},{7,1},{8,10},{10,12},{12... | collective-permute-start | bytes 18440 | tf_op jit(solution)/shard_map/ppermute | solution.py:19
  15.3 4.1 %collective-permute-start.3 = (bf16[4,6,128]{2,0,1:T(4,128)(2,1)S(1)}, bf16[4,6,128]{2,0,1:T(4,128)(2,1)S(1)}, u32[]{:S(2)}, u32[]{:S(2)}) collective-permute-start(bf16[4,6,128]{2,0,1:T(4,128)(2,1)S(1)} %bitcast.308), channel_id=1, source_target_pairs={{0,6},{2,0},{4,2},{6,4},{1,7},{3,1},{5,3},{7,5},{8,14},{10,8},{12,... | collective-permute-start | bytes 18440 | tf_op jit(solution)/shard_map/ppermute | solution.py:19
  20.4 16.6 %collective-permute-start.4 = (bf16[4,6,66]{2,0,1:T(4,128)(2,1)S(1)}, bf16[4,6,66]{2,0,1:T(4,128)(2,1)S(1)}, u32[]{:S(2)}, u32[]{:S(2)}) collective-permute-start(bf16[4,6,66]{2,0,1:T(4,128)(2,1)S(1)} %bitcast.302), channel_id=1, source_target_pairs={{0,1},{1,0},{2,3},{3,2},{4,5},{5,4},{6,7},{7,6},{8,9},{9,8},{10,11... | collective-permute-start | bytes 9512 | tf_op jit(solution)/shard_map/ppermute | solution.py:19
  21.4 15.9 %collective-permute-start.5 = (bf16[4,6,66]{2,0,1:T(4,128)(2,1)S(1)}, bf16[4,6,66]{2,0,1:T(4,128)(2,1)S(1)}, u32[]{:S(2)}, u32[]{:S(2)}) collective-permute-start(bf16[4,6,66]{2,0,1:T(4,128)(2,1)S(1)} %bitcast.304), channel_id=1, source_target_pairs={{0,1},{1,0},{2,3},{3,2},{4,5},{5,4},{6,7},{7,6},{8,9},{9,8},{10,11... | collective-permute-start | bytes 9512 | tf_op jit(solution)/shard_map/ppermute | solution.py:19
  80.7 13.8 %copy-start.2 = (bf16[256,1,128]{2,1,0:T(2,128)(2,1)S(1)}, bf16[256,1,128]{2,1,0:T(2,128)(2,1)}, u32[]{:S(2)}) copy-start(bf16[256,1,128]{2,1,0:T(2,128)(2,1)} %copy.269) | copy-start | bytes 196612
  80.7 13.8 %copy-start.3 = (bf16[256,1,128]{2,1,0:T(2,128)(2,1)S(1)}, bf16[256,1,128]{2,1,0:T(2,128)(2,1)}, u32[]{:S(2)}) copy-start(bf16[256,1,128]{2,1,0:T(2,128)(2,1)} %copy.278) | copy-start | bytes 196612
  80.7 13.8 %copy-start.4 = (bf16[256,1,128]{2,1,0:T(2,128)(2,1)S(1)}, bf16[256,1,128]{2,1,0:T(2,128)(2,1)}, u32[]{:S(2)}) copy-start(bf16[256,1,128]{2,1,0:T(2,128)(2,1)} %copy.203) | copy-start | bytes 196612
  80.7 13.8 %copy-start.5 = (bf16[256,1,128]{2,1,0:T(2,128)(2,1)S(1)}, bf16[256,1,128]{2,1,0:T(2,128)(2,1)}, u32[]{:S(2)}) copy-start(bf16[256,1,128]{2,1,0:T(2,128)(2,1)} %copy.209) | copy-start | bytes 196612
  80.7 13.8 %copy-start.6 = (bf16[256,1,128]{2,1,0:T(2,128)(2,1)S(1)}, bf16[256,1,128]{2,1,0:T(2,128)(2,1)}, u32[]{:S(2)}) copy-start(bf16[256,1,128]{2,1,0:T(2,128)(2,1)} %copy.212) | copy-start | bytes 196612
  80.7 13.8 %copy-start.7 = (bf16[256,1,128]{2,1,0:T(2,128)(2,1)S(1)}, bf16[256,1,128]{2,1,0:T(2,128)(2,1)}, u32[]{:S(2)}) copy-start(bf16[256,1,128]{2,1,0:T(2,128)(2,1)} %copy.218) | copy-start | bytes 196612
  80.7 13.8 %copy-start.8 = (bf16[256,1,128]{2,1,0:T(2,128)(2,1)S(1)}, bf16[256,1,128]{2,1,0:T(2,128)(2,1)}, u32[]{:S(2)}) copy-start(bf16[256,1,128]{2,1,0:T(2,128)(2,1)} %copy.221) | copy-start | bytes 196612
  80.7 13.8 %copy-start.9 = (bf16[256,1,128]{2,1,0:T(2,128)(2,1)S(1)}, bf16[256,1,128]{2,1,0:T(2,128)(2,1)}, u32[]{:S(2)}) copy-start(bf16[256,1,128]{2,1,0:T(2,128)(2,1)} %copy.227) | copy-start | bytes 196612
  80.7 13.8 %copy-start.10 = (bf16[256,1,128]{2,1,0:T(2,128)(2,1)S(1)}, bf16[256,1,128]{2,1,0:T(2,128)(2,1)}, u32[]{:S(2)}) copy-start(bf16[256,1,128]{2,1,0:T(2,128)(2,1)} %copy.230) | copy-start | bytes 196612
  188.8 3.1 %collective-permute-start.6 = (f32[6,66,4]{1,2,0:T(4,128)S(1)}, f32[6,66,4]{1,2,0:T(4,128)S(1)}, u32[]{:S(2)}, u32[]{:S(2)}) collective-permute-start(f32[6,66,4]{1,2,0:T(4,128)S(1)} %bitcast.300), channel_id=1, source_target_pairs={{0,1},{1,0},{2,3},{3,2},{4,5},{5,4},{6,7},{7,6},{8,9},{9,8},{10,11... | collective-permute-start | bytes 19016 | tf_op jit(solution)/shard_map/ppermute | solution.py:19
  190.8 2.6 collective-permute-start.7
  194.0 28.3 %collective-permute-start.8 = (f32[6,4,128]{2,1,0:T(4,128)S(1)}, f32[6,4,128]{2,1,0:T(4,128)S(1)}, u32[]{:S(2)}, u32[]{:S(2)}) collective-permute-start(f32[6,4,128]{2,1,0:T(4,128)S(1)} %get-tuple-element.27), channel_id=1, source_target_pairs={{0,2},{2,4},{4,6},{6,0},{1,3},{3,5},{5,7},{7,1},{8,10},{10,12},{12... | collective-permute-start | bytes 36872 | tf_op jit(solution)/shard_map/ppermute | solution.py:19
  219.5 13.3 %copy-start.14 = (f32[32,108]{1,0:T(8,128)S(1)}, f32[32,108]{1,0:T(8,128)}, u32[]{:S(2)}) copy-start(f32[32,108]{1,0:T(8,128)} %get-tuple-element.10) | copy-start | bytes 41476
  219.5 13.3 %copy-start.15 = (f32[32,1]{1,0:T(8,128)S(1)}, f32[32,1]{1,0:T(8,128)}, u32[]{:S(2)}) copy-start(f32[32,1]{1,0:T(8,128)} %get-tuple-element.11) | copy-start | bytes 388
  219.5 3.6 %collective-permute-start.9 = (f32[6,4,128]{2,1,0:T(4,128)S(1)}, f32[6,4,128]{2,1,0:T(4,128)S(1)}, u32[]{:S(2)}, u32[]{:S(2)}) collective-permute-start(f32[6,4,128]{2,1,0:T(4,128)S(1)} %get-tuple-element.26), channel_id=1, source_target_pairs={{0,6},{2,0},{4,2},{6,4},{1,7},{3,1},{5,3},{7,5},{8,14},{10,8},{12,... | collective-permute-start | bytes 36872 | tf_op jit(solution)/shard_map/ppermute | solution.py:19
  222.4 28.7 %copy-start.12 = (bf16[32,4096]{1,0:T(8,128)(2,1)S(1)}, bf16[32,4096]{1,0:T(8,128)(2,1)}, u32[]{:S(2)}) copy-start(bf16[32,4096]{1,0:T(8,128)(2,1)} %get-tuple-element.9) | copy-start | bytes 786436
  223.2 32.4 %collective-permute-start.10 = (f32[64,4,128]{2,0,1:T(8,128)S(1)}, f32[64,4,128]{2,0,1:T(8,128)S(1)}, u32[]{:S(2)}, u32[]{:S(2)}) collective-permute-start(f32[64,4,128]{2,0,1:T(8,128)S(1)} %get-tuple-element.105), channel_id=1, source_target_pairs={{0,8},{8,16},{16,24},{24,32},{32,40},{40,48},{48,56},{56,64},{64,7... | collective-permute-start | bytes 393224 | tf_op jit(solution)/shard_map/ppermute | solution.py:19
  253.9 8.1 %collective-permute-start.11 = (f32[64,4,128]{2,0,1:T(8,128)S(1)}, f32[64,4,128]{2,0,1:T(8,128)S(1)}, u32[]{:S(2)}, u32[]{:S(2)}) collective-permute-start(f32[64,4,128]{2,0,1:T(8,128)S(1)} %get-tuple-element.104), channel_id=1, source_target_pairs={{0,120},{8,0},{16,8},{24,16},{32,24},{40,32},{48,40},{56,48},{64,5... | collective-permute-start | bytes 393224 | tf_op jit(solution)/shard_map/ppermute | solution.py:19
  (4 other events, 29.1 us)

commit v8 on v7

--- a/solution.py
+++ b/solution.py
@@ -308,11 +308,12 @@
     widened = extended(cells, (("gx", 1), ("gy", 2), ("gz", 3)), 1)
     patches = jnp.stack(
         [
-            widened[c, sa : sa + cells_x, sb : sb + cells_y, se : se + cells_z]
-            for c in range(chan_in)
+            jnp.transpose(
+                widened[:, sa : sa + cells_x, sb : sb + cells_y, se : se + cells_z], (1, 2, 0, 3)
+            )
             for sa, sb, se in stencil
         ],
-        axis=2,
+        axis=3,
     )
     patches = patches.reshape(cells_x * cells_y, chan_in * 27, cells_z)
     cot = cotangent.reshape(chan_out, -1)

time: 267 us -> 155 us (0.58); the launches traced: 263 us -> 155 us
  local copies, waits for them, and re-layouts: 144 us -> 31.3 us
  waiting for transfers between devices: 7.85 us -> 13.9 us
  starting transfers between devices: 24.7 us -> 20.1 us
  other arithmetic: 29.2 us -> 32 us
    another operation x109 -> x1, local copies, waits for them, and re-layouts: 123 us -> 0.25 us  [on_device(): jnp.stack([jnp.transpose(widened[:, sa:sa + cells_x, sb:sb + cells_y, se:...]
    reshape x0 -> x1, local copies, waits for them, and re-layouts: none -> 7.53 us  [on_device(): patches = patches.reshape(cells_x * cells_y, chan_in * 27, cells_z)]
    ppermute x12, waiting for transfers between devices: 7.85 us -> 13.9 us  [shift(): moved = lax.ppermute(jnp.squeeze(piece, dim), axis, pairs)]
    ppermute x12, starting transfers between devices: 24.7 us -> 20.1 us  [shift(): moved = lax.ppermute(jnp.squeeze(piece, dim), axis, pairs)]
    unnamed x38 -> x42, local copies, waits for them, and re-layouts: 3.66 us -> 6.84 us
    slice x7 -> x0, local copies, waits for them, and re-layouts: 2.68 us -> none  [on_device(): widened[c, sa:sa + cells_x, sb:sb + cells_y, se:se + cells_z]]
  transfers between devices with their start and end apart: 12 -> 12, of which waited for: 3 -> 6; matrix products, arithmetic and copies ran while one was open for 22% -> 28% of each run, Pallas kernels for 6% -> 11%
where the time goes in v8:
time: 155 us
  Pallas kernels  56.2 us (36%)
  other arithmetic  32 us (21%)
  local copies, waits for them, and re-layouts  31.3 us (20%)
  starting transfers between devices  20.1 us (13%)
  waiting for transfers between devices  13.9 us (9%)
    pallas_call x1, Pallas kernels, forward(): pl.pallas_call(lambda *refs: forward_kernel(rows, wide_y, *refs), grid=(p...  39.4 us
    concatenate x1, other arithmetic, on_device(): jnp.concatenate([main[..., :1] + from_left, main[..., 1:cells_z - 1], mai...  25.1 us
    ppermute x12, starting transfers between devices, shift(): moved = lax.ppermute(jnp.squeeze(piece, dim), axis, pairs)  20.1 us
    pallas_call x1, Pallas kernels, allreduce(): pl.pallas_call(lambda *refs: allreduce_kernel(sizes, *refs), out_shape=ja...  16.8 us
    ppermute x12, waiting for transfers between devices, shift(): moved = lax.ppermute(jnp.squeeze(piece, dim), axis, pairs)  13.9 us
    reshape x1, local copies, waits for them, and re-layouts, on_device(): patches = patches.reshape(cells_x * cells_y, chan_in * 27, cells_z)  7.53 us
    unnamed x42, local copies, waits for them, and re-layouts  6.84 us
    concatenate x3, other arithmetic, extended(): jnp.concatenate([shift(tail, axis, dim, 1), cells, shift(head, axis, dim,...  3.45 us
  transfers between devices with their start and end apart: 12, of which 6 were waited for; matrix products, arithmetic and copies ran while one was open for 28% of the time, Pallas kernels for 11%

profile of v8, /device:TPU:7, one launch (start us, length us, event | category | flops | bytes accessed | tf_op | source)
XLA Modules:
  0.0 154.7 jit_solution(1511970219733443042)
XLA Ops:
  1.6 4.1 %collective-permute-start = (bf16[4,64,128]{2,1,0:T(8,128)(2,1)S(1)}, bf16[4,64,128]{2,1,0:T(8,128)(2,1)S(1)}, u32[]{:S(2)}, u32[]{:S(2)}) collective-permute-start(bf16[4,64,128]{2,1,0:T(8,128)(2,1)S(1)} %get-tuple-element.46), channel_id=1, source_target_pairs={{0,8},{8,16},{16,24},{24,32},{32,40},{40,48},{48,56},{56,64},{64,7... | collective-permute-start | bytes 196616 | tf_op jit(solution)/shard_map/ppermute | solution.py:19
  7.0 6.0 %collective-permute-done.1 = bf16[4,64,128]{2,1,0:T(8,128)(2,1)S(1)} collective-permute-done((bf16[4,64,128]{2,1,0:T(8,128)(2,1)S(1)}, bf16[4,64,128]{2,1,0:T(8,128)(2,1)S(1)}, u32[]{:S(2)}, u32[]{:S(2)}) %collective-permute-start.1) | collective-permute-done | bytes 65568 | tf_op jit(solution)/shard_map/ppermute | solution.py:19
  13.9 1.4 collective-permute-start.2
  15.2 1.5 collective-permute-start.3
  17.4 2.2 %reshape.237.refs_6_ = bf16[32,4096]{1,0:T(8,128)(2,1)} reshape(bf16[32,2,32,64]{3,2,1,0:T(8,128)(2,1)} %param.7) | data formatting | bytes 524288 | tf_op jit(solution)/shard_map/reshape | solution.py:319
  21.1 1.3 copy.195.refs_1_
  22.4 1.4 pad.4
  23.9 1.2 pad_maximum_fusion.2
  27.6 1.3 pad_maximum_fusion.3
  29.7 1.0 pad_maximum_fusion
  34.4 7.5 %copy.196.refs_5_ = bf16[256,108,128]{2,1,0:T(8,128)(2,1)} copy(bf16[256,108,128]{2,0,1:T(8,128)(2,1)S(1)} %bitcast.278) | data formatting | bytes 14155776 | tf_op jit(solution)/shard_map/reshape | solution.py:318
  42.0 39.4 %shard_map.75 = (bf16[32,4096]{1,0:T(8,128)(2,1)}, f32[32,108]{1,0:T(8,128)}, f32[32,1]{1,0:T(8,128)}, f32[396,4,128]{2,1,0:T(4,128)}, f32[396,4,128]{2,1,0:T(4,128)}) custom-call(bf16[32,108]{1,0:T(8,128)(2,1)} %copy.194.refs_0_, f32[32,1]{1,0:T(8,128)} %copy.195.refs_1_, f32[2,128,128]{2,1,0:T(8,128)} %add_convert_fusion.refs_2_, ...), custom_call_target="tpu_custom_call" | custom-call | tf_op jit(solution)/shard_map/pallas_call | solution.py:247
  81.3 1.9 %fusion.32 = (f32[6,66,4,1]{3,2,1,0:T(4,128)S(1)}, f32[6,66,4,1]{3,2,1,0:T(4,128)S(1)}) fusion(f32[6,66,4,128]{3,2,1,0:T(4,128)} %bitcast.279), kind=kLoop, calls=%fused_computation.94 | loop fusion | bytes 25344 | tf_op jit(solution)/shard_map/slice | solution.py:338
  83.6 1.0 collective-permute-start.6
  84.6 1.9 %fusion.33 = (f32[6,66,4,1]{3,2,1,0:T(4,128)S(1)}, f32[6,66,4,1]{3,2,1,0:T(4,128)S(1)}) fusion(f32[6,66,4,128]{3,2,1,0:T(4,128)} %bitcast.274), kind=kLoop, calls=%fused_computation.95 | loop fusion | bytes 25344 | tf_op jit(solution)/shard_map/slice | solution.py:343
  88.9 1.0 collective-permute-done.7
  90.6 25.1 %pad_maximum_fusion.1 = f32[6,66,4,128]{3,2,0,1:T(4,128)S(1)} fusion(f32[6,66,4,1]{3,2,0,1:T(4,128)S(1)} %copy.204, f32[6,66,4,1]{3,2,0,1:T(4,128)S(1)} %copy.203, f32[6,66,4,128]{3,2,1,0:T(4,128)S(1)} %bitcast.276), kind=kLoop, calls=%fused_computation.2 | loop fusion | flops 405504 | bytes 1634688 | tf_op jit(solution)/shard_map/concatenate | solution.py:341
  115.7 2.7 %collective-permute-start.9 = (f32[6,4,128]{2,1,0:T(4,128)S(1)}, f32[6,4,128]{2,1,0:T(4,128)S(1)}, u32[]{:S(2)}, u32[]{:S(2)}) collective-permute-start(f32[6,4,128]{2,1,0:T(4,128)S(1)} %get-tuple-element.30), channel_id=1, source_target_pairs={{0,6},{2,0},{4,2},{6,4},{1,7},{3,1},{5,3},{7,5},{8,14},{10,8},{12,... | collective-permute-start | bytes 36872 | tf_op jit(solution)/shard_map/ppermute | solution.py:19
  119.4 4.5 %collective-permute-start.10 = (f32[64,4,128]{2,0,1:T(8,128)S(1)}, f32[64,4,128]{2,0,1:T(8,128)S(1)}, u32[]{:S(2)}, u32[]{:S(2)}) collective-permute-start(f32[64,4,128]{2,0,1:T(8,128)S(1)} %get-tuple-element.37), channel_id=1, source_target_pairs={{0,8},{8,16},{16,24},{24,32},{32,40},{40,48},{48,56},{56,64},{64,7... | collective-permute-start | bytes 393224 | tf_op jit(solution)/shard_map/ppermute | solution.py:19
  124.6 16.8 %shard_map.76 = f32[32,128]{1,0:T(8,128)} custom-call(f32[32,128]{1,0:T(8,128)} %maximum_maximum_fusion.2.refs_0_), custom_call_target="tpu_custom_call" | custom-call | tf_op jit(solution)/shard_map/pallas_call | solution.py:94
  143.0 1.3 reshape.238
  144.3 1.4 slice_reduce_fusion
  145.8 2.2 %collective-permute-start.11 = (f32[64,4,128]{2,0,1:T(8,128)S(1)}, f32[64,4,128]{2,0,1:T(8,128)S(1)}, u32[]{:S(2)}, u32[]{:S(2)}) collective-permute-start(f32[64,4,128]{2,0,1:T(8,128)S(1)} %get-tuple-element.36), channel_id=1, source_target_pairs={{0,120},{8,0},{16,8},{24,16},{32,24},{40,32},{48,40},{56,48},{64,5... | collective-permute-start | bytes 393224 | tf_op jit(solution)/shard_map/ppermute | solution.py:19
  148.0 5.8 %collective-permute-done.11 = f32[64,4,128]{2,0,1:T(8,128)S(1)} collective-permute-done((f32[64,4,128]{2,0,1:T(8,128)S(1)}, f32[64,4,128]{2,0,1:T(8,128)S(1)}, u32[]{:S(2)}, u32[]{:S(2)}) %collective-permute-start.11) | collective-permute-done | bytes 131104 | tf_op jit(solution)/shard_map/ppermute | solution.py:19
  (98 shorter events, 19.5 us)
Async XLA Ops:
  0.6 29.0 %copy-start.1 = (bf16[4,4,64,128]{3,2,1,0:T(8,128)(2,1)S(1)}, bf16[4,4,64,128]{3,2,1,0:T(8,128)(2,1)}, u32[]{:S(2)}) copy-start(bf16[4,4,64,128]{3,2,1,0:T(8,128)(2,1)} %param.4) | copy-start | bytes 786436
  1.6 5.5 %collective-permute-start = (bf16[4,64,128]{2,1,0:T(8,128)(2,1)S(1)}, bf16[4,64,128]{2,1,0:T(8,128)(2,1)S(1)}, u32[]{:S(2)}, u32[]{:S(2)}) collective-permute-start(bf16[4,64,128]{2,1,0:T(8,128)(2,1)S(1)} %get-tuple-element.46), channel_id=1, source_target_pairs={{0,8},{8,16},{16,24},{24,32},{32,40},{40,48},{48,56},{56,64},{64,7... | collective-permute-start | bytes 196616 | tf_op jit(solution)/shard_map/ppermute | solution.py:19
  5.7 7.3 %collective-permute-start.1 = (bf16[4,64,128]{2,1,0:T(8,128)(2,1)S(1)}, bf16[4,64,128]{2,1,0:T(8,128)(2,1)S(1)}, u32[]{:S(2)}, u32[]{:S(2)}) collective-permute-start(bf16[4,64,128]{2,1,0:T(8,128)(2,1)S(1)} %get-tuple-element.47), channel_id=1, source_target_pairs={{0,120},{8,0},{16,8},{24,16},{32,24},{40,32},{48,40},{56,48},{64,5... | collective-permute-start | bytes 196616 | tf_op jit(solution)/shard_map/ppermute | solution.py:19
  13.9 10.0 %collective-permute-start.2 = (bf16[4,6,128]{2,0,1:T(4,128)(2,1)S(1)}, bf16[4,6,128]{2,0,1:T(4,128)(2,1)S(1)}, u32[]{:S(2)}, u32[]{:S(2)}) collective-permute-start(bf16[4,6,128]{2,0,1:T(4,128)(2,1)S(1)} %bitcast.302), channel_id=1, source_target_pairs={{0,2},{2,4},{4,6},{6,0},{1,3},{3,5},{5,7},{7,1},{8,10},{10,12},{12... | collective-permute-start | bytes 18440 | tf_op jit(solution)/shard_map/ppermute | solution.py:19
  15.2 8.7 %collective-permute-start.3 = (bf16[4,6,128]{2,0,1:T(4,128)(2,1)S(1)}, bf16[4,6,128]{2,0,1:T(4,128)(2,1)S(1)}, u32[]{:S(2)}, u32[]{:S(2)}) collective-permute-start(bf16[4,6,128]{2,0,1:T(4,128)(2,1)S(1)} %bitcast.304), channel_id=1, source_target_pairs={{0,6},{2,0},{4,2},{6,4},{1,7},{3,1},{5,3},{7,5},{8,14},{10,8},{12,... | collective-permute-start | bytes 18440 | tf_op jit(solution)/shard_map/ppermute | solution.py:19
  25.6 3.3 %collective-permute-start.4 = (bf16[4,6,66]{2,0,1:T(4,128)(2,1)S(1)}, bf16[4,6,66]{2,0,1:T(4,128)(2,1)S(1)}, u32[]{:S(2)}, u32[]{:S(2)}) collective-permute-start(bf16[4,6,66]{2,0,1:T(4,128)(2,1)S(1)} %bitcast.298), channel_id=1, source_target_pairs={{0,1},{1,0},{2,3},{3,2},{4,5},{5,4},{6,7},{7,6},{8,9},{9,8},{10,11... | collective-permute-start | bytes 9512 | tf_op jit(solution)/shard_map/ppermute | solution.py:19
  26.6 2.7 %collective-permute-start.5 = (bf16[4,6,66]{2,0,1:T(4,128)(2,1)S(1)}, bf16[4,6,66]{2,0,1:T(4,128)(2,1)S(1)}, u32[]{:S(2)}, u32[]{:S(2)}) collective-permute-start(bf16[4,6,66]{2,0,1:T(4,128)(2,1)S(1)} %bitcast.300), channel_id=1, source_target_pairs={{0,1},{1,0},{2,3},{3,2},{4,5},{5,4},{6,7},{7,6},{8,9},{9,8},{10,11... | collective-permute-start | bytes 9512 | tf_op jit(solution)/shard_map/ppermute | solution.py:19
  81.3 9.0 %copy-start = (f32[396,4,128]{2,1,0:T(4,128)S(1)}, f32[396,4,128]{2,1,0:T(4,128)}, u32[]{:S(2)}) copy-start(f32[396,4,128]{2,1,0:T(4,128)} %get-tuple-element.12) | copy-start | bytes 2433028
  83.6 4.8 %collective-permute-start.6 = (f32[6,66,4]{1,2,0:T(4,128)S(1)}, f32[6,66,4]{1,2,0:T(4,128)S(1)}, u32[]{:S(2)}, u32[]{:S(2)}) collective-permute-start(f32[6,66,4]{1,2,0:T(4,128)S(1)} %bitcast.296), channel_id=1, source_target_pairs={{0,1},{1,0},{2,3},{3,2},{4,5},{5,4},{6,7},{7,6},{8,9},{9,8},{10,11... | collective-permute-start | bytes 19016 | tf_op jit(solution)/shard_map/ppermute | solution.py:19
  87.3 2.6 %collective-permute-start.7 = (f32[6,66,4]{1,2,0:T(4,128)S(1)}, f32[6,66,4]{1,2,0:T(4,128)S(1)}, u32[]{:S(2)}, u32[]{:S(2)}) collective-permute-start(f32[6,66,4]{1,2,0:T(4,128)S(1)} %bitcast.297), channel_id=1, source_target_pairs={{0,1},{1,0},{2,3},{3,2},{4,5},{5,4},{6,7},{7,6},{8,9},{9,8},{10,11... | collective-permute-start | bytes 19016 | tf_op jit(solution)/shard_map/ppermute | solution.py:19
  88.1 35.8 %copy-start.4 = (f32[32,108]{1,0:T(8,128)S(1)}, f32[32,108]{1,0:T(8,128)}, u32[]{:S(2)}) copy-start(f32[32,108]{1,0:T(8,128)} %get-tuple-element.10) | copy-start | bytes 41476
  88.1 35.8 %copy-start.5 = (f32[32,1]{1,0:T(8,128)S(1)}, f32[32,1]{1,0:T(8,128)}, u32[]{:S(2)}) copy-start(f32[32,1]{1,0:T(8,128)} %get-tuple-element.11) | copy-start | bytes 388
  88.4 54.5 %copy-start.3 = (bf16[32,4096]{1,0:T(8,128)(2,1)S(1)}, bf16[32,4096]{1,0:T(8,128)(2,1)}, u32[]{:S(2)}) copy-start(bf16[32,4096]{1,0:T(8,128)(2,1)} %get-tuple-element.9) | copy-start | bytes 786436
  90.5 28.0 %collective-permute-start.8 = (f32[6,4,128]{2,1,0:T(4,128)S(1)}, f32[6,4,128]{2,1,0:T(4,128)S(1)}, u32[]{:S(2)}, u32[]{:S(2)}) collective-permute-start(f32[6,4,128]{2,1,0:T(4,128)S(1)} %get-tuple-element.31), channel_id=1, source_target_pairs={{0,2},{2,4},{4,6},{6,0},{1,3},{3,5},{5,7},{7,1},{8,10},{10,12},{12... | collective-permute-start | bytes 36872 | tf_op jit(solution)/shard_map/ppermute | solution.py:19
  115.7 3.6 %collective-permute-start.9 = (f32[6,4,128]{2,1,0:T(4,128)S(1)}, f32[6,4,128]{2,1,0:T(4,128)S(1)}, u32[]{:S(2)}, u32[]{:S(2)}) collective-permute-start(f32[6,4,128]{2,1,0:T(4,128)S(1)} %get-tuple-element.30), channel_id=1, source_target_pairs={{0,6},{2,0},{4,2},{6,4},{1,7},{3,1},{5,3},{7,5},{8,14},{10,8},{12,... | collective-permute-start | bytes 36872 | tf_op jit(solution)/shard_map/ppermute | solution.py:19
  119.4 28.5 %collective-permute-start.10 = (f32[64,4,128]{2,0,1:T(8,128)S(1)}, f32[64,4,128]{2,0,1:T(8,128)S(1)}, u32[]{:S(2)}, u32[]{:S(2)}) collective-permute-start(f32[64,4,128]{2,0,1:T(8,128)S(1)} %get-tuple-element.37), channel_id=1, source_target_pairs={{0,8},{8,16},{16,24},{24,32},{32,40},{40,48},{48,56},{56,64},{64,7... | collective-permute-start | bytes 393224 | tf_op jit(solution)/shard_map/ppermute | solution.py:19
  145.8 8.1 %collective-permute-start.11 = (f32[64,4,128]{2,0,1:T(8,128)S(1)}, f32[64,4,128]{2,0,1:T(8,128)S(1)}, u32[]{:S(2)}, u32[]{:S(2)}) collective-permute-start(f32[64,4,128]{2,0,1:T(8,128)S(1)} %get-tuple-element.36), channel_id=1, source_target_pairs={{0,120},{8,0},{16,8},{24,16},{32,24},{40,32},{48,40},{56,48},{64,5... | collective-permute-start | bytes 393224 | tf_op jit(solution)/shard_map/ppermute | solution.py:19
  153.9 0.8 copy-start.2

commit v9 on v6

--- a/solution.py
+++ b/solution.py
@@ -28,39 +28,61 @@
     return cells
 
 
-def allreduce_kernel(sizes, x_ref, o_ref, slots_x, slots_y, slots_z, acc_x, acc_y,
-                     send_x, recv_x, send_y, recv_y, send_z, recv_z):
+def allreduce_kernel(sizes, x_ref, o_ref, slots_a, slots_b, acc_a, send_a, recv_a, send_b, recv_b):
     me = tuple(lax.axis_index(a) for a in AXES)
-    slots = (slots_x, slots_y, slots_z)
-    sends = (send_x, send_y, send_z)
-    recvs = (recv_x, recv_y, recv_z)
-    sources = (x_ref, acc_x, acc_y)
-    sinks = (acc_x, acc_y, o_ref)
-
-    def peer(axis, index):
-        return tuple(index if k == axis else me[k] for k in range(3))
+    groups = (
+        [(k,) for k in range(sizes[0])],
+        [(k, m) for k in range(sizes[1]) for m in range(sizes[2])],
+    )
+    places = ((0,), (1, 2))
+
+    def device(phase, member):
+        coords = list(me)
+        for axis, value in zip(places[phase], member):
+            coords[axis] = value
+        return tuple(coords)
+
+    def rank(phase):
+        out = 0
+        for axis in places[phase]:
+            out = out * sizes[axis] + me[axis]
+        return out
+
+    def member_of(phase, index):
+        out = []
+        for axis in reversed(places[phase]):
+            out.append(lax.rem(index, sizes[axis]))
+            index = index // sizes[axis]
+        return tuple(reversed(out))
 
     barrier = pltpu.get_barrier_semaphore()
     count = 0
-    for axis, n in enumerate(sizes):
+    for phase in range(2):
+        n = len(groups[phase])
         for d in range(1, n):
-            target = lax.rem(me[axis] + d, n)
-            pl.semaphore_signal(barrier, inc=1, device_id=peer(axis, target), device_id_type=MESH)
+            target = member_of(phase, lax.rem(rank(phase) + d, n))
+            pl.semaphore_signal(barrier, inc=1, device_id=device(phase, target), device_id_type=MESH)
             count += 1
     pl.semaphore_wait(barrier, count)
 
-    for axis, n in enumerate(sizes):
-        src, held, sink = sources[axis], slots[axis], sinks[axis]
-        mine = me[axis]
+    slots = (slots_a, slots_b)
+    sends = (send_a, send_b)
+    recvs = (recv_a, recv_b)
+    sources = (x_ref, acc_a)
+    sinks = (acc_a, o_ref)
+    for phase in range(2):
+        n = len(groups[phase])
+        src, held, sink = sources[phase], slots[phase], sinks[phase]
+        mine = rank(phase)
         copies = []
         for d in range(1, n):
-            target = lax.rem(mine + d, n)
+            target = member_of(phase, lax.rem(mine + d, n))
             copy = pltpu.make_async_remote_copy(
                 src_ref=src,
                 dst_ref=held.at[mine],
-                send_sem=sends[axis].at[d],
-                recv_sem=recvs[axis].at[mine],
-                device_id=peer(axis, target),
+                send_sem=sends[phase].at[d],
+                recv_sem=recvs[phase].at[mine],
+                device_id=device(phase, target),
                 device_id_type=MESH,
             )
             copy.start()
@@ -71,9 +93,9 @@
             incoming = pltpu.make_async_remote_copy(
                 src_ref=src,
                 dst_ref=held.at[origin],
-                send_sem=sends[axis].at[d],
-                recv_sem=recvs[axis].at[origin],
-                device_id=peer(axis, origin),
+                send_sem=sends[phase].at[d],
+                recv_sem=recvs[phase].at[origin],
+                device_id=device(phase, member_of(phase, origin)),
                 device_id_type=MESH,
             )
             incoming.wait_recv()
@@ -87,36 +109,23 @@
 
 def allreduce(x, sizes):
     shape = x.shape
+    first, second = sizes[0], sizes[1] * sizes[2]
     return pl.pallas_call(
         lambda *refs: allreduce_kernel(sizes, *refs),
         out_shape=jax.ShapeDtypeStruct(shape, jnp.float32),
         in_specs=[pl.BlockSpec(memory_space=pltpu.VMEM)],
         out_specs=pl.BlockSpec(memory_space=pltpu.VMEM),
         scratch_shapes=[
-            pltpu.VMEM((sizes[0],) + shape, jnp.float32),
-            pltpu.VMEM((sizes[1],) + shape, jnp.float32),
-            pltpu.VMEM((sizes[2],) + shape, jnp.float32),
+            pltpu.VMEM((first,) + shape, jnp.float32),
+            pltpu.VMEM((second,) + shape, jnp.float32),
             pltpu.VMEM(shape, jnp.float32),
-            pltpu.VMEM(shape, jnp.float32),
-            pltpu.SemaphoreType.DMA((sizes[0],)),
-            pltpu.SemaphoreType.DMA((sizes[0],)),
-            pltpu.SemaphoreType.DMA((sizes[1],)),
-            pltpu.SemaphoreType.DMA((sizes[1],)),
-            pltpu.SemaphoreType.DMA((sizes[2],)),
-            pltpu.SemaphoreType.DMA((sizes[2],)),
+            pltpu.SemaphoreType.DMA((first,)),
+            pltpu.SemaphoreType.DMA((first,)),
+            pltpu.SemaphoreType.DMA((second,)),
+            pltpu.SemaphoreType.DMA((second,)),
         ],
         compiler_params=pltpu.CompilerParams(collective_id=0, has_side_effects=True),
     )(x)
-
-
-def activate(preact):
-    return leak_slope * preact + (1.0 - leak_slope) / soft_scale * jax.nn.softplus(
-        soft_scale * preact
-    )
-
-
-def slope_of(preact):
-    return leak_slope + (1.0 - leak_slope) * jax.nn.sigmoid(soft_scale * preact)
 
 
 def forward_kernel(rows, wide_y, w_ref, b_ref, q_ref, u_ref, wt_ref, p_ref, cot_ref,

time: 137 us -> 135 us (0.985)
  transfers between devices with their start and end apart: 12 -> 12, of which waited for: 9 -> 9; matrix products, arithmetic and copies ran while one was open for 14% -> 15% of each run, Pallas kernels for 12% -> 11%
where the time goes in v9:
time: 135 us
  Pallas kernels  54.7 us (41%)
  local copies, waits for them, and re-layouts  32.1 us (24%)
  waiting for transfers between devices  22.7 us (17%)
  starting transfers between devices  19.2 us (14%)
  other arithmetic  5.08 us (4%)
    pallas_call x1, Pallas kernels, forward(): pl.pallas_call(lambda *refs: forward_kernel(rows, wide_y, *refs), grid=(p...  39.4 us
    pallas_call x1, Pallas kernels, allreduce(): pl.pallas_call(lambda *refs: allreduce_kernel(sizes, *refs), out_shape=ja...  15.4 us
    ppermute x3, waiting for transfers between devices, extended(): lax.ppermute(head, axis, [((i + 1) % count, i) for i in range(count)])  10 us
    reshape x1, local copies, waits for them, and re-layouts, on_device(): patches = patches.reshape(cells_x * cells_y, chan_in * 27, cells_z)  7.54 us
    unnamed x37, local copies, waits for them, and re-layouts  7.44 us
    ppermute x2, waiting for transfers between devices, fold_halo(): lax.ppermute(head, axis, [((i + 1) % count, i) for i in range(count)])  7.15 us
    ppermute x3, starting transfers between devices, extended(): lax.ppermute(tail, axis, [(i, (i + 1) % count) for i in range(count)])  6.32 us
    ppermute x2, starting transfers between devices, fold_halo(): lax.ppermute(tail, axis, [(i, (i + 1) % count) for i in range(count)])  5.7 us
  transfers between devices with their start and end apart: 12, of which 9 were waited for; matrix products, arithmetic and copies ran while one was open for 15% of the time, Pallas kernels for 11%

profile of v9, /device:TPU:7, one launch (start us, length us, event | category | flops | bytes accessed | tf_op | source)
XLA Modules:
  0.0 134.8 jit_solution(16525146672759092641)
XLA Ops:
  1.6 4.1 %collective-permute-start = (bf16[4,1,64,128]{3,2,1,0:T(8,128)(2,1)S(1)}, bf16[4,1,64,128]{3,2,1,0:T(8,128)(2,1)S(1)}, u32[]{:S(2)}, u32[]{:S(2)}) collective-permute-start(bf16[4,1,64,128]{3,2,1,0:T(8,128)(2,1)S(1)} %get-tuple-element.41), channel_id=1, source_target_pairs={{0,8},{8,16},{16,24},{24,32},{32,40},{40,48},{48,56},{56,64},{64,7... | collective-permute-start | bytes 196616 | tf_op jit(solution)/shard_map/ppermute | solution.py:22
  5.9 1.1 collective-permute-done
  8.0 5.0 %collective-permute-done.1 = bf16[4,1,64,128]{3,2,1,0:T(8,128)(2,1)S(1)} collective-permute-done((bf16[4,1,64,128]{3,2,1,0:T(8,128)(2,1)S(1)}, bf16[4,1,64,128]{3,2,1,0:T(8,128)(2,1)S(1)}, u32[]{:S(2)}, u32[]{:S(2)}) %collective-permute-start.1) | collective-permute-done | bytes 65568 | tf_op jit(solution)/shard_map/ppermute | solution.py:24
  13.1 1.4 %collective-permute-start.2 = (bf16[4,6,1,128]{3,2,1,0:T(2,128)(2,1)S(1)}, bf16[4,6,1,128]{3,2,1,0:T(2,128)(2,1)S(1)}, u32[]{:S(2)}, u32[]{:S(2)}) collective-permute-start(bf16[4,6,1,128]{3,2,1,0:T(2,128)(2,1)S(1)} %get-tuple-element.38), channel_id=1, source_target_pairs={{0,2},{2,4},{4,6},{6,0},{1,3},{3,5},{5,7},{7,1},{8,10},{10,12},{12... | collective-permute-start | bytes 18440 | tf_op jit(solution)/shard_map/ppermute | solution.py:22
  14.4 1.5 %collective-permute-start.3 = (bf16[4,6,1,128]{3,2,1,0:T(2,128)(2,1)S(1)}, bf16[4,6,1,128]{3,2,1,0:T(2,128)(2,1)S(1)}, u32[]{:S(2)}, u32[]{:S(2)}) collective-permute-start(bf16[4,6,1,128]{3,2,1,0:T(2,128)(2,1)S(1)} %get-tuple-element.39), channel_id=1, source_target_pairs={{2,0},{4,2},{6,4},{0,6},{3,1},{5,3},{7,5},{1,7},{10,8},{12,10},{14... | collective-permute-start | bytes 18440 | tf_op jit(solution)/shard_map/ppermute | solution.py:24
  19.8 2.2 %reshape.237.refs_6_ = bf16[32,4096]{1,0:T(8,128)(2,1)} reshape(bf16[32,2,32,64]{3,2,1,0:T(8,128)(2,1)} %param.7) | data formatting | bytes 524288 | tf_op jit(solution)/shard_map/reshape | solution.py:325
  23.5 1.3 copy.76.refs_1_
  24.9 1.4 %pad.4 = bf16[3,3,3,8,32]{4,3,2,1,0:T(8,128)(2,1)} pad(bf16[3,3,3,4,32]{4,3,2,1,0:T(4,128)(2,1)} %bitcast.227, bf16[]{:T(256)} %constant.43.clone.1), padding=0_0x0_0x0_0x0_4x0_0 | pad | bytes 20738 | tf_op jit(solution)/shard_map/jit(_pad)/pad | solution.py:238
  26.3 3.7 %collective-permute-done.4 = bf16[4,6,66,1]{3,2,1,0:T(8,128)(2,1)S(1)} collective-permute-done((bf16[4,6,66,1]{3,2,1,0:T(8,128)(2,1)S(1)}, bf16[4,6,66,1]{3,2,1,0:T(8,128)(2,1)S(1)}, u32[]{:S(2)}, u32[]{:S(2)}) %collective-permute-start.4) | collective-permute-done | bytes 3200 | tf_op jit(solution)/shard_map/ppermute | solution.py:22
  30.0 4.7 %collective-permute-done.5 = bf16[4,6,66,1]{3,2,1,0:T(8,128)(2,1)S(1)} collective-permute-done((bf16[4,6,66,1]{3,2,1,0:T(8,128)(2,1)S(1)}, bf16[4,6,66,1]{3,2,1,0:T(8,128)(2,1)S(1)}, u32[]{:S(2)}, u32[]{:S(2)}) %collective-permute-start.5) | collective-permute-done | bytes 3200 | tf_op jit(solution)/shard_map/ppermute | solution.py:24
  34.7 1.1 pad_maximum_fusion
  39.7 7.5 %copy.77.refs_5_ = bf16[256,108,128]{2,1,0:T(8,128)(2,1)} copy(bf16[256,108,128]{2,0,1:T(8,128)(2,1)S(1)} %bitcast.220) | data formatting | bytes 14155776 | tf_op jit(solution)/shard_map/reshape | solution.py:324
  47.3 39.4 %shard_map.75 = (bf16[32,4096]{1,0:T(8,128)(2,1)}, f32[32,108]{1,0:T(8,128)}, f32[32,1]{1,0:T(8,128)}, f32[396,4,128]{2,1,0:T(4,128)}, f32[396,4,128]{2,1,0:T(4,128)}) custom-call(bf16[32,108]{1,0:T(8,128)(2,1)} %copy.75.refs_0_, f32[32,1]{1,0:T(8,128)} %copy.76.refs_1_, f32[2,128,128]{2,1,0:T(8,128)} %add_convert_fusion.refs_2_, ...), custom_call_target="tpu_custom_call" | custom-call | tf_op jit(solution)/shard_map/pallas_call | solution.py:252
  86.6 1.9 %fusion.40 = (f32[6,66,4,1]{3,2,1,0:T(4,128)S(1)}, f32[6,66,4,1]{3,2,1,0:T(4,128)S(1)}) fusion(f32[6,66,4,128]{3,2,1,0:T(4,128)} %bitcast.223), kind=kLoop, calls=%fused_computation.97 | loop fusion | bytes 25344 | tf_op jit(solution)/shard_map/slice | solution.py:344
  88.9 1.7 %collective-permute-start.6 = (f32[6,66,4,1]{1,2,3,0:T(4,128)S(1)}, f32[6,66,4,1]{1,2,3,0:T(4,128)S(1)}, u32[]{:S(2)}, u32[]{:S(2)}) collective-permute-start(f32[6,66,4,1]{1,2,3,0:T(4,128)S(1)} %copy.88), channel_id=1, source_target_pairs={{0,1},{1,0},{2,3},{3,2},{4,5},{5,4},{6,7},{7,6},{8,9},{9,8},{10,11... | collective-permute-start | bytes 19016 | tf_op jit(solution)/shard_map/ppermute | solution.py:346
  91.3 1.9 %fusion.41 = (f32[6,66,4,1]{3,2,1,0:T(4,128)S(1)}, f32[6,66,4,1]{3,2,1,0:T(4,128)S(1)}) fusion(f32[6,66,4,128]{3,2,1,0:T(4,128)} %bitcast.221), kind=kLoop, calls=%fused_computation.98 | loop fusion | bytes 25344 | tf_op jit(solution)/shard_map/slice | solution.py:350
  95.6 1.4 %collective-permute-start.8 = (f32[6,1,4,128]{3,1,0,2:T(1,128)S(1)}, f32[6,1,4,128]{3,1,0,2:T(1,128)S(1)}, u32[]{:S(2)}, u32[]{:S(2)}) collective-permute-start(f32[6,1,4,128]{3,1,0,2:T(1,128)S(1)} %get-tuple-element.27), channel_id=1, source_target_pairs={{0,2},{2,4},{4,6},{6,0},{1,3},{3,5},{5,7},{7,1},{8,10},{10,12},{12... | collective-permute-start | bytes 36872 | tf_op jit(solution)/shard_map/ppermute | solution.py:290
  97.6 1.4 %collective-permute-start.9 = (f32[6,1,4,128]{3,1,0,2:T(1,128)S(1)}, f32[6,1,4,128]{3,1,0,2:T(1,128)S(1)}, u32[]{:S(2)}, u32[]{:S(2)}) collective-permute-start(f32[6,1,4,128]{3,1,0,2:T(1,128)S(1)} %get-tuple-element.26), channel_id=1, source_target_pairs={{2,0},{4,2},{6,4},{0,6},{3,1},{5,3},{7,5},{1,7},{10,8},{12,10},{14... | collective-permute-start | bytes 36872 | tf_op jit(solution)/shard_map/ppermute | solution.py:291
  100.3 4.3 %collective-permute-start.10 = (f32[1,64,4,128]{3,1,0,2:T(8,128)S(1)}, f32[1,64,4,128]{3,1,0,2:T(8,128)S(1)}, u32[]{:S(2)}, u32[]{:S(2)}) collective-permute-start(f32[1,64,4,128]{3,1,0,2:T(8,128)S(1)} %get-tuple-element.33), channel_id=1, source_target_pairs={{0,8},{8,16},{16,24},{24,32},{32,40},{40,48},{48,56},{56,64},{64,7... | collective-permute-start | bytes 393224 | tf_op jit(solution)/shard_map/ppermute | solution.py:290
  105.3 15.4 %shard_map.76 = f32[32,128]{1,0:T(8,128)} custom-call(f32[32,128]{1,0:T(8,128)} %maximum_maximum_fusion.1.refs_0_), custom_call_target="tpu_custom_call" | custom-call | tf_op jit(solution)/shard_map/pallas_call | solution.py:113
  122.2 2.3 %reshape.238 = bf16[32,2,32,64]{3,2,1,0:T(8,128)(2,1)} reshape(bf16[32,4096]{1,0:T(8,128)(2,1)} %get-tuple-element.9) | data formatting | bytes 524288 | tf_op jit(solution)/shard_map/reshape | solution.py:330
  124.5 1.4 %slice_reduce_fusion = f32[32]{0:T(128)} fusion(f32[32,128]{1,0:T(8,128)} %shard_map.76), kind=kLoop, calls=%fused_computation.87 | loop fusion | bytes 256 | tf_op jit(solution)/shard_map/slice | solution.py:340
  125.9 1.5 %collective-permute-start.11 = (f32[1,64,4,128]{3,1,0,2:T(8,128)S(1)}, f32[1,64,4,128]{3,1,0,2:T(8,128)S(1)}, u32[]{:S(2)}, u32[]{:S(2)}) collective-permute-start(f32[1,64,4,128]{3,1,0,2:T(8,128)S(1)} %get-tuple-element.32), channel_id=1, source_target_pairs={{8,0},{16,8},{24,16},{32,24},{40,32},{48,40},{56,48},{64,56},{72,6... | collective-permute-start | bytes 393224 | tf_op jit(solution)/shard_map/ppermute | solution.py:291
  127.4 6.6 %collective-permute-done.11 = f32[1,64,4,128]{3,1,0,2:T(8,128)S(1)} collective-permute-done((f32[1,64,4,128]{3,1,0,2:T(8,128)S(1)}, f32[1,64,4,128]{3,1,0,2:T(8,128)S(1)}, u32[]{:S(2)}, u32[]{:S(2)}) %collective-permute-start.11) | collective-permute-done | bytes 131104 | tf_op jit(solution)/shard_map/ppermute | solution.py:291
  (90 shorter events, 19.6 us)
Async XLA Ops:
  0.6 35.6 %copy-start.1 = (bf16[4,4,64,128]{3,2,1,0:T(8,128)(2,1)S(1)}, bf16[4,4,64,128]{3,2,1,0:T(8,128)(2,1)}, u32[]{:S(2)}) copy-start(bf16[4,4,64,128]{3,2,1,0:T(8,128)(2,1)} %param.4) | copy-start | bytes 786436
  1.6 5.5 %collective-permute-start = (bf16[4,1,64,128]{3,2,1,0:T(8,128)(2,1)S(1)}, bf16[4,1,64,128]{3,2,1,0:T(8,128)(2,1)S(1)}, u32[]{:S(2)}, u32[]{:S(2)}) collective-permute-start(bf16[4,1,64,128]{3,2,1,0:T(8,128)(2,1)S(1)} %get-tuple-element.41), channel_id=1, source_target_pairs={{0,8},{8,16},{16,24},{24,32},{32,40},{40,48},{48,56},{56,64},{64,7... | collective-permute-start | bytes 196616 | tf_op jit(solution)/shard_map/ppermute | solution.py:22
  5.7 7.3 %collective-permute-start.1 = (bf16[4,1,64,128]{3,2,1,0:T(8,128)(2,1)S(1)}, bf16[4,1,64,128]{3,2,1,0:T(8,128)(2,1)S(1)}, u32[]{:S(2)}, u32[]{:S(2)}) collective-permute-start(bf16[4,1,64,128]{3,2,1,0:T(8,128)(2,1)S(1)} %get-tuple-element.40), channel_id=1, source_target_pairs={{8,0},{16,8},{24,16},{32,24},{40,32},{48,40},{56,48},{64,56},{72,6... | collective-permute-start | bytes 196616 | tf_op jit(solution)/shard_map/ppermute | solution.py:24
  13.1 3.9 %collective-permute-start.2 = (bf16[4,6,1,128]{3,2,1,0:T(2,128)(2,1)S(1)}, bf16[4,6,1,128]{3,2,1,0:T(2,128)(2,1)S(1)}, u32[]{:S(2)}, u32[]{:S(2)}) collective-permute-start(bf16[4,6,1,128]{3,2,1,0:T(2,128)(2,1)S(1)} %get-tuple-element.38), channel_id=1, source_target_pairs={{0,2},{2,4},{4,6},{6,0},{1,3},{3,5},{5,7},{7,1},{8,10},{10,12},{12... | collective-permute-start | bytes 18440 | tf_op jit(solution)/shard_map/ppermute | solution.py:22
  14.4 2.8 %collective-permute-start.3 = (bf16[4,6,1,128]{3,2,1,0:T(2,128)(2,1)S(1)}, bf16[4,6,1,128]{3,2,1,0:T(2,128)(2,1)S(1)}, u32[]{:S(2)}, u32[]{:S(2)}) collective-permute-start(bf16[4,6,1,128]{3,2,1,0:T(2,128)(2,1)S(1)} %get-tuple-element.39), channel_id=1, source_target_pairs={{2,0},{4,2},{6,4},{0,6},{3,1},{5,3},{7,5},{1,7},{10,8},{12,10},{14... | collective-permute-start | bytes 18440 | tf_op jit(solution)/shard_map/ppermute | solution.py:24
  17.6 12.3 %collective-permute-start.4 = (bf16[4,6,66,1]{3,2,1,0:T(8,128)(2,1)S(1)}, bf16[4,6,66,1]{3,2,1,0:T(8,128)(2,1)S(1)}, u32[]{:S(2)}, u32[]{:S(2)}) collective-permute-start(bf16[4,6,66,1]{3,2,1,0:T(8,128)(2,1)S(1)} %get-tuple-element.35), channel_id=1, source_target_pairs={{0,1},{1,0},{2,3},{3,2},{4,5},{5,4},{6,7},{7,6},{8,9},{9,8},{10,11... | collective-permute-start | bytes 9512 | tf_op jit(solution)/shard_map/ppermute | solution.py:22
  18.5 16.2 %collective-permute-start.5 = (bf16[4,6,66,1]{3,2,1,0:T(8,128)(2,1)S(1)}, bf16[4,6,66,1]{3,2,1,0:T(8,128)(2,1)S(1)}, u32[]{:S(2)}, u32[]{:S(2)}) collective-permute-start(bf16[4,6,66,1]{3,2,1,0:T(8,128)(2,1)S(1)} %get-tuple-element.34), channel_id=1, source_target_pairs={{1,0},{0,1},{3,2},{2,3},{5,4},{4,5},{7,6},{6,7},{9,8},{8,9},{11,10... | collective-permute-start | bytes 9512 | tf_op jit(solution)/shard_map/ppermute | solution.py:24
  86.6 6.6 %copy-start = (f32[396,4,128]{2,1,0:T(4,128)S(1)}, f32[396,4,128]{2,1,0:T(4,128)}, u32[]{:S(2)}) copy-start(f32[396,4,128]{2,1,0:T(4,128)} %get-tuple-element.12) | copy-start | bytes 2433028
  88.9 5.6 %collective-permute-start.6 = (f32[6,66,4,1]{1,2,3,0:T(4,128)S(1)}, f32[6,66,4,1]{1,2,3,0:T(4,128)S(1)}, u32[]{:S(2)}, u32[]{:S(2)}) collective-permute-start(f32[6,66,4,1]{1,2,3,0:T(4,128)S(1)} %copy.88), channel_id=1, source_target_pairs={{0,1},{1,0},{2,3},{3,2},{4,5},{5,4},{6,7},{7,6},{8,9},{9,8},{10,11... | collective-permute-start | bytes 19016 | tf_op jit(solution)/shard_map/ppermute | solution.py:346
  91.0 4.0 %collective-permute-start.7 = (f32[6,66,4,1]{1,2,3,0:T(4,128)S(1)}, f32[6,66,4,1]{1,2,3,0:T(4,128)S(1)}, u32[]{:S(2)}, u32[]{:S(2)}) collective-permute-start(f32[6,66,4,1]{1,2,3,0:T(4,128)S(1)} %copy.91), channel_id=1, source_target_pairs={{1,0},{0,1},{3,2},{2,3},{5,4},{4,5},{7,6},{6,7},{9,8},{8,9},{11,10... | collective-permute-start | bytes 19016 | tf_op jit(solution)/shard_map/ppermute | solution.py:347
  94.4 10.2 %copy-start.3 = (f32[32,108]{1,0:T(8,128)S(1)}, f32[32,108]{1,0:T(8,128)}, u32[]{:S(2)}) copy-start(f32[32,108]{1,0:T(8,128)} %get-tuple-element.10) | copy-start | bytes 41476
  94.4 10.2 %copy-start.4 = (f32[32,1]{1,0:T(8,128)S(1)}, f32[32,1]{1,0:T(8,128)}, u32[]{:S(2)}) copy-start(f32[32,1]{1,0:T(8,128)} %get-tuple-element.11) | copy-start | bytes 388
  95.6 3.8 %collective-permute-start.8 = (f32[6,1,4,128]{3,1,0,2:T(1,128)S(1)}, f32[6,1,4,128]{3,1,0,2:T(1,128)S(1)}, u32[]{:S(2)}, u32[]{:S(2)}) collective-permute-start(f32[6,1,4,128]{3,1,0,2:T(1,128)S(1)} %get-tuple-element.27), channel_id=1, source_target_pairs={{0,2},{2,4},{4,6},{6,0},{1,3},{3,5},{5,7},{7,1},{8,10},{10,12},{12... | collective-permute-start | bytes 36872 | tf_op jit(solution)/shard_map/ppermute | solution.py:290
  97.6 2.6 %collective-permute-start.9 = (f32[6,1,4,128]{3,1,0,2:T(1,128)S(1)}, f32[6,1,4,128]{3,1,0,2:T(1,128)S(1)}, u32[]{:S(2)}, u32[]{:S(2)}) collective-permute-start(f32[6,1,4,128]{3,1,0,2:T(1,128)S(1)} %get-tuple-element.26), channel_id=1, source_target_pairs={{2,0},{4,2},{6,4},{0,6},{3,1},{5,3},{7,5},{1,7},{10,8},{12,10},{14... | collective-permute-start | bytes 36872 | tf_op jit(solution)/shard_map/ppermute | solution.py:291
  100.3 27.1 %collective-permute-start.10 = (f32[1,64,4,128]{3,1,0,2:T(8,128)S(1)}, f32[1,64,4,128]{3,1,0,2:T(8,128)S(1)}, u32[]{:S(2)}, u32[]{:S(2)}) collective-permute-start(f32[1,64,4,128]{3,1,0,2:T(8,128)S(1)} %get-tuple-element.33), channel_id=1, source_target_pairs={{0,8},{8,16},{16,24},{24,32},{32,40},{40,48},{48,56},{56,64},{64,7... | collective-permute-start | bytes 393224 | tf_op jit(solution)/shard_map/ppermute | solution.py:290
  125.9 8.1 %collective-permute-start.11 = (f32[1,64,4,128]{3,1,0,2:T(8,128)S(1)}, f32[1,64,4,128]{3,1,0,2:T(8,128)S(1)}, u32[]{:S(2)}, u32[]{:S(2)}) collective-permute-start(f32[1,64,4,128]{3,1,0,2:T(8,128)S(1)} %get-tuple-element.32), channel_id=1, source_target_pairs={{8,0},{16,8},{24,16},{32,24},{40,32},{48,40},{56,48},{64,56},{72,6... | collective-permute-start | bytes 393224 | tf_op jit(solution)/shard_map/ppermute | solution.py:291
  134.0 0.8 copy-start.2

commit v10 on v9

--- a/solution.py
+++ b/solution.py
@@ -156,37 +156,34 @@
             jnp.dot(cot, u_ref[0], preferred_element_type=jnp.float32) * 0.125,
             jnp.dot(cot, u_ref[1], preferred_element_type=jnp.float32) * 0.125,
         )
+        spread4 = jnp.concatenate([ups[0], ups[0], ups[1], ups[1]], axis=1)
         totals = [None, None]
         wg = None
         bg = None
         spreads = []
         for px, base in enumerate((0, plane)):
-            deltas = []
-            for r in range(4):
-                row = base + j * 4 + r
-                patch = p_ref[row]
-                preact = jnp.dot(weight, patch, preferred_element_type=jnp.float32) + bias
-                scaled = soft_scale * preact
-                e = jnp.exp(-jnp.abs(scaled))
-                softplus = jnp.maximum(scaled, 0.0) + jnp.log1p(e)
-                activated = leak_slope * preact + (1.0 - leak_slope) / soft_scale * softplus
-                half = r // 2
-                totals[half] = activated if totals[half] is None else totals[half] + activated
-                sigmoid = jnp.where(scaled >= 0.0, 1.0, e) / (1.0 + e)
-                slope = leak_slope + (1.0 - leak_slope) * sigmoid
-                delta = (slope * ups[half]).astype(jnp.bfloat16)
-                deltas.append(delta)
-                term = lax.dot_general(
-                    delta, patch, (((1,), (1,)), ((), ())), preferred_element_type=jnp.float32
+            patch = jnp.concatenate([p_ref[base + j * 4 + r] for r in range(4)], axis=1)
+            preact = jnp.dot(weight, patch, preferred_element_type=jnp.float32) + bias
+            scaled = soft_scale * preact
+            e = jnp.exp(-jnp.abs(scaled))
+            softplus = jnp.maximum(scaled, 0.0) + jnp.log1p(e)
+            activated = leak_slope * preact + (1.0 - leak_slope) / soft_scale * softplus
+            for half in range(2):
+                pair = (
+                    activated[:, 2 * half * rows : (2 * half + 1) * rows]
+                    + activated[:, (2 * half + 1) * rows : (2 * half + 2) * rows]
                 )
-                wg = term if wg is None else wg + term
-                part = delta.astype(jnp.float32)
-                bg = part if bg is None else bg + part
-            spreads.append(
-                jnp.dot(
-                    spread_w, jnp.concatenate(deltas, axis=1), preferred_element_type=jnp.float32
-                )
+                totals[half] = pair if totals[half] is None else totals[half] + pair
+            sigmoid = jnp.where(scaled >= 0.0, 1.0, e) / (1.0 + e)
+            slope = leak_slope + (1.0 - leak_slope) * sigmoid
+            delta = (slope * spread4).astype(jnp.bfloat16)
+            term = lax.dot_general(
+                delta, patch, (((1,), (1,)), ((), ())), preferred_element_type=jnp.float32
             )
+            wg = term if wg is None else wg + term
+            part = delta.astype(jnp.float32)
+            bg = part if bg is None else bg + part
+            spreads.append(jnp.dot(spread_w, delta, preferred_element_type=jnp.float32))
         acc_main = {}
         acc_edge = {}
         for px in range(2):

time: 135 us -> 127 us (0.941)
  Pallas kernels: 54.7 us -> 46.5 us
    pallas_call x1, Pallas kernels: 39.4 us -> 31.2 us  [forward(): pl.pallas_call(lambda *refs: forward_kernel(rows, wide_y, *refs), grid=(p...]
  transfers between devices with their start and end apart: 12 -> 12, of which waited for: 9 -> 9; matrix products, arithmetic and copies ran while one was open for 15% -> 16% of each run, Pallas kernels for 11% -> 12%
where the time goes in v10:
time: 127 us
  Pallas kernels  46.5 us (37%)
  local copies, waits for them, and re-layouts  32.1 us (25%)
  waiting for transfers between devices  22.7 us (18%)
  starting transfers between devices  19.2 us (15%)
  other arithmetic  5.08 us (4%)
    pallas_call x1, Pallas kernels, forward(): pl.pallas_call(lambda *refs: forward_kernel(rows, wide_y, *refs), grid=(p...  31.2 us
    pallas_call x1, Pallas kernels, allreduce(): pl.pallas_call(lambda *refs: allreduce_kernel(sizes, *refs), out_shape=ja...  15.4 us
    ppermute x3, waiting for transfers between devices, extended(): lax.ppermute(head, axis, [((i + 1) % count, i) for i in range(count)])  10 us
    reshape x1, local copies, waits for them, and re-layouts, on_device(): patches = patches.reshape(cells_x * cells_y, chan_in * 27, cells_z)  7.54 us
    unnamed x37, local copies, waits for them, and re-layouts  7.44 us
    ppermute x2, waiting for transfers between devices, fold_halo(): lax.ppermute(head, axis, [((i + 1) % count, i) for i in range(count)])  7.15 us
    ppermute x3, starting transfers between devices, extended(): lax.ppermute(tail, axis, [(i, (i + 1) % count) for i in range(count)])  6.32 us
    ppermute x2, starting transfers between devices, fold_halo(): lax.ppermute(tail, axis, [(i, (i + 1) % count) for i in range(count)])  5.7 us
  transfers between devices with their start and end apart: 12, of which 9 were waited for; matrix products, arithmetic and copies ran while one was open for 16% of the time, Pallas kernels for 12%

profile of v10, /device:TPU:7, one launch (start us, length us, event | category | flops | bytes accessed | tf_op | source)
XLA Modules:
  0.0 126.6 jit_solution(17328922820716548508)
XLA Ops:
  1.6 4.1 %collective-permute-start = (bf16[4,1,64,128]{3,2,1,0:T(8,128)(2,1)S(1)}, bf16[4,1,64,128]{3,2,1,0:T(8,128)(2,1)S(1)}, u32[]{:S(2)}, u32[]{:S(2)}) collective-permute-start(bf16[4,1,64,128]{3,2,1,0:T(8,128)(2,1)S(1)} %get-tuple-element.41), channel_id=1, source_target_pairs={{0,8},{8,16},{16,24},{24,32},{32,40},{40,48},{48,56},{56,64},{64,7... | collective-permute-start | bytes 196616 | tf_op jit(solution)/shard_map/ppermute | solution.py:22
  5.9 1.1 collective-permute-done
  8.0 5.0 %collective-permute-done.1 = bf16[4,1,64,128]{3,2,1,0:T(8,128)(2,1)S(1)} collective-permute-done((bf16[4,1,64,128]{3,2,1,0:T(8,128)(2,1)S(1)}, bf16[4,1,64,128]{3,2,1,0:T(8,128)(2,1)S(1)}, u32[]{:S(2)}, u32[]{:S(2)}) %collective-permute-start.1) | collective-permute-done | bytes 65568 | tf_op jit(solution)/shard_map/ppermute | solution.py:24
  13.1 1.4 %collective-permute-start.2 = (bf16[4,6,1,128]{3,2,1,0:T(2,128)(2,1)S(1)}, bf16[4,6,1,128]{3,2,1,0:T(2,128)(2,1)S(1)}, u32[]{:S(2)}, u32[]{:S(2)}) collective-permute-start(bf16[4,6,1,128]{3,2,1,0:T(2,128)(2,1)S(1)} %get-tuple-element.38), channel_id=1, source_target_pairs={{0,2},{2,4},{4,6},{6,0},{1,3},{3,5},{5,7},{7,1},{8,10},{10,12},{12... | collective-permute-start | bytes 18440 | tf_op jit(solution)/shard_map/ppermute | solution.py:22
  14.4 1.5 %collective-permute-start.3 = (bf16[4,6,1,128]{3,2,1,0:T(2,128)(2,1)S(1)}, bf16[4,6,1,128]{3,2,1,0:T(2,128)(2,1)S(1)}, u32[]{:S(2)}, u32[]{:S(2)}) collective-permute-start(bf16[4,6,1,128]{3,2,1,0:T(2,128)(2,1)S(1)} %get-tuple-element.39), channel_id=1, source_target_pairs={{2,0},{4,2},{6,4},{0,6},{3,1},{5,3},{7,5},{1,7},{10,8},{12,10},{14... | collective-permute-start | bytes 18440 | tf_op jit(solution)/shard_map/ppermute | solution.py:24
  19.8 2.2 %reshape.237.refs_6_ = bf16[32,4096]{1,0:T(8,128)(2,1)} reshape(bf16[32,2,32,64]{3,2,1,0:T(8,128)(2,1)} %param.7) | data formatting | bytes 524288 | tf_op jit(solution)/shard_map/reshape | solution.py:322
  23.5 1.3 %copy.76.refs_1_ = f32[32,1]{1,0:T(8,128)} copy(f32[32,1]{0,1:T(1,128)} %bitcast.228) | data formatting | bytes 256 | tf_op jit(solution)/shard_map/reshape | solution.py:325
  24.9 1.4 %pad.4 = bf16[3,3,3,8,32]{4,3,2,1,0:T(8,128)(2,1)} pad(bf16[3,3,3,4,32]{4,3,2,1,0:T(4,128)(2,1)} %bitcast.227, bf16[]{:T(256)} %constant.43.clone.1), padding=0_0x0_0x0_0x0_4x0_0 | pad | bytes 20738 | tf_op jit(solution)/shard_map/jit(_pad)/pad | solution.py:235
  26.3 3.7 %collective-permute-done.4 = bf16[4,6,66,1]{3,2,1,0:T(8,128)(2,1)S(1)} collective-permute-done((bf16[4,6,66,1]{3,2,1,0:T(8,128)(2,1)S(1)}, bf16[4,6,66,1]{3,2,1,0:T(8,128)(2,1)S(1)}, u32[]{:S(2)}, u32[]{:S(2)}) %collective-permute-start.4) | collective-permute-done | bytes 3200 | tf_op jit(solution)/shard_map/ppermute | solution.py:22
  30.0 4.7 %collective-permute-done.5 = bf16[4,6,66,1]{3,2,1,0:T(8,128)(2,1)S(1)} collective-permute-done((bf16[4,6,66,1]{3,2,1,0:T(8,128)(2,1)S(1)}, bf16[4,6,66,1]{3,2,1,0:T(8,128)(2,1)S(1)}, u32[]{:S(2)}, u32[]{:S(2)}) %collective-permute-start.5) | collective-permute-done | bytes 3200 | tf_op jit(solution)/shard_map/ppermute | solution.py:24
  34.7 1.1 pad_maximum_fusion
  39.7 7.5 %copy.77.refs_5_ = bf16[256,108,128]{2,1,0:T(8,128)(2,1)} copy(bf16[256,108,128]{2,0,1:T(8,128)(2,1)S(1)} %bitcast.220) | data formatting | bytes 14155776 | tf_op jit(solution)/shard_map/reshape | solution.py:321
  47.3 31.2 %shard_map.75 = (bf16[32,4096]{1,0:T(8,128)(2,1)}, f32[32,108]{1,0:T(8,128)}, f32[32,1]{1,0:T(8,128)}, f32[396,4,128]{2,1,0:T(4,128)}, f32[396,4,128]{2,1,0:T(4,128)}) custom-call(bf16[32,108]{1,0:T(8,128)(2,1)} %copy.75.refs_0_, f32[32,1]{1,0:T(8,128)} %copy.76.refs_1_, f32[2,128,128]{2,1,0:T(8,128)} %add_convert_fusion.refs_2_, ...), custom_call_target="tpu_custom_call" | custom-call | tf_op jit(solution)/shard_map/pallas_call | solution.py:249
  78.5 1.9 %fusion.40 = (f32[6,66,4,1]{3,2,1,0:T(4,128)S(1)}, f32[6,66,4,1]{3,2,1,0:T(4,128)S(1)}) fusion(f32[6,66,4,128]{3,2,1,0:T(4,128)} %bitcast.223), kind=kLoop, calls=%fused_computation.97 | loop fusion | bytes 25344 | tf_op jit(solution)/shard_map/slice | solution.py:341
  80.8 1.7 %collective-permute-start.6 = (f32[6,66,4,1]{1,2,3,0:T(4,128)S(1)}, f32[6,66,4,1]{1,2,3,0:T(4,128)S(1)}, u32[]{:S(2)}, u32[]{:S(2)}) collective-permute-start(f32[6,66,4,1]{1,2,3,0:T(4,128)S(1)} %copy.88), channel_id=1, source_target_pairs={{0,1},{1,0},{2,3},{3,2},{4,5},{5,4},{6,7},{7,6},{8,9},{9,8},{10,11... | collective-permute-start | bytes 19016 | tf_op jit(solution)/shard_map/ppermute | solution.py:343
  83.1 1.9 %fusion.41 = (f32[6,66,4,1]{3,2,1,0:T(4,128)S(1)}, f32[6,66,4,1]{3,2,1,0:T(4,128)S(1)}) fusion(f32[6,66,4,128]{3,2,1,0:T(4,128)} %bitcast.221), kind=kLoop, calls=%fused_computation.98 | loop fusion | bytes 25344 | tf_op jit(solution)/shard_map/slice | solution.py:347
  87.4 1.4 %collective-permute-start.8 = (f32[6,1,4,128]{3,1,0,2:T(1,128)S(1)}, f32[6,1,4,128]{3,1,0,2:T(1,128)S(1)}, u32[]{:S(2)}, u32[]{:S(2)}) collective-permute-start(f32[6,1,4,128]{3,1,0,2:T(1,128)S(1)} %get-tuple-element.27), channel_id=1, source_target_pairs={{0,2},{2,4},{4,6},{6,0},{1,3},{3,5},{5,7},{7,1},{8,10},{10,12},{12... | collective-permute-start | bytes 36872 | tf_op jit(solution)/shard_map/ppermute | solution.py:287
  89.4 1.4 %collective-permute-start.9 = (f32[6,1,4,128]{3,1,0,2:T(1,128)S(1)}, f32[6,1,4,128]{3,1,0,2:T(1,128)S(1)}, u32[]{:S(2)}, u32[]{:S(2)}) collective-permute-start(f32[6,1,4,128]{3,1,0,2:T(1,128)S(1)} %get-tuple-element.26), channel_id=1, source_target_pairs={{2,0},{4,2},{6,4},{0,6},{3,1},{5,3},{7,5},{1,7},{10,8},{12,10},{14... | collective-permute-start | bytes 36872 | tf_op jit(solution)/shard_map/ppermute | solution.py:288
  92.1 4.3 %collective-permute-start.10 = (f32[1,64,4,128]{3,1,0,2:T(8,128)S(1)}, f32[1,64,4,128]{3,1,0,2:T(8,128)S(1)}, u32[]{:S(2)}, u32[]{:S(2)}) collective-permute-start(f32[1,64,4,128]{3,1,0,2:T(8,128)S(1)} %get-tuple-element.33), channel_id=1, source_target_pairs={{0,8},{8,16},{16,24},{24,32},{32,40},{40,48},{48,56},{56,64},{64,7... | collective-permute-start | bytes 393224 | tf_op jit(solution)/shard_map/ppermute | solution.py:287
  97.2 15.4 %shard_map.76 = f32[32,128]{1,0:T(8,128)} custom-call(f32[32,128]{1,0:T(8,128)} %maximum_maximum_fusion.1.refs_0_), custom_call_target="tpu_custom_call" | custom-call | tf_op jit(solution)/shard_map/pallas_call | solution.py:113
  114.0 2.3 %reshape.238 = bf16[32,2,32,64]{3,2,1,0:T(8,128)(2,1)} reshape(bf16[32,4096]{1,0:T(8,128)(2,1)} %get-tuple-element.9) | data formatting | bytes 524288 | tf_op jit(solution)/shard_map/reshape | solution.py:327
  116.3 1.4 %slice_reduce_fusion = f32[32]{0:T(128)} fusion(f32[32,128]{1,0:T(8,128)} %shard_map.76), kind=kLoop, calls=%fused_computation.87 | loop fusion | bytes 256 | tf_op jit(solution)/shard_map/slice | solution.py:337
  117.7 1.5 %collective-permute-start.11 = (f32[1,64,4,128]{3,1,0,2:T(8,128)S(1)}, f32[1,64,4,128]{3,1,0,2:T(8,128)S(1)}, u32[]{:S(2)}, u32[]{:S(2)}) collective-permute-start(f32[1,64,4,128]{3,1,0,2:T(8,128)S(1)} %get-tuple-element.32), channel_id=1, source_target_pairs={{8,0},{16,8},{24,16},{32,24},{40,32},{48,40},{56,48},{64,56},{72,6... | collective-permute-start | bytes 393224 | tf_op jit(solution)/shard_map/ppermute | solution.py:288
  119.2 6.6 %collective-permute-done.11 = f32[1,64,4,128]{3,1,0,2:T(8,128)S(1)} collective-permute-done((f32[1,64,4,128]{3,1,0,2:T(8,128)S(1)}, f32[1,64,4,128]{3,1,0,2:T(8,128)S(1)}, u32[]{:S(2)}, u32[]{:S(2)}) %collective-permute-start.11) | collective-permute-done | bytes 131104 | tf_op jit(solution)/shard_map/ppermute | solution.py:288
  (90 shorter events, 19.6 us)
Async XLA Ops:
  0.6 35.6 %copy-start.1 = (bf16[4,4,64,128]{3,2,1,0:T(8,128)(2,1)S(1)}, bf16[4,4,64,128]{3,2,1,0:T(8,128)(2,1)}, u32[]{:S(2)}) copy-start(bf16[4,4,64,128]{3,2,1,0:T(8,128)(2,1)} %param.4) | copy-start | bytes 786436
  1.6 5.5 %collective-permute-start = (bf16[4,1,64,128]{3,2,1,0:T(8,128)(2,1)S(1)}, bf16[4,1,64,128]{3,2,1,0:T(8,128)(2,1)S(1)}, u32[]{:S(2)}, u32[]{:S(2)}) collective-permute-start(bf16[4,1,64,128]{3,2,1,0:T(8,128)(2,1)S(1)} %get-tuple-element.41), channel_id=1, source_target_pairs={{0,8},{8,16},{16,24},{24,32},{32,40},{40,48},{48,56},{56,64},{64,7... | collective-permute-start | bytes 196616 | tf_op jit(solution)/shard_map/ppermute | solution.py:22
  5.7 7.3 %collective-permute-start.1 = (bf16[4,1,64,128]{3,2,1,0:T(8,128)(2,1)S(1)}, bf16[4,1,64,128]{3,2,1,0:T(8,128)(2,1)S(1)}, u32[]{:S(2)}, u32[]{:S(2)}) collective-permute-start(bf16[4,1,64,128]{3,2,1,0:T(8,128)(2,1)S(1)} %get-tuple-element.40), channel_id=1, source_target_pairs={{8,0},{16,8},{24,16},{32,24},{40,32},{48,40},{56,48},{64,56},{72,6... | collective-permute-start | bytes 196616 | tf_op jit(solution)/shard_map/ppermute | solution.py:24
  13.1 3.9 %collective-permute-start.2 = (bf16[4,6,1,128]{3,2,1,0:T(2,128)(2,1)S(1)}, bf16[4,6,1,128]{3,2,1,0:T(2,128)(2,1)S(1)}, u32[]{:S(2)}, u32[]{:S(2)}) collective-permute-start(bf16[4,6,1,128]{3,2,1,0:T(2,128)(2,1)S(1)} %get-tuple-element.38), channel_id=1, source_target_pairs={{0,2},{2,4},{4,6},{6,0},{1,3},{3,5},{5,7},{7,1},{8,10},{10,12},{12... | collective-permute-start | bytes 18440 | tf_op jit(solution)/shard_map/ppermute | solution.py:22
  14.4 2.8 %collective-permute-start.3 = (bf16[4,6,1,128]{3,2,1,0:T(2,128)(2,1)S(1)}, bf16[4,6,1,128]{3,2,1,0:T(2,128)(2,1)S(1)}, u32[]{:S(2)}, u32[]{:S(2)}) collective-permute-start(bf16[4,6,1,128]{3,2,1,0:T(2,128)(2,1)S(1)} %get-tuple-element.39), channel_id=1, source_target_pairs={{2,0},{4,2},{6,4},{0,6},{3,1},{5,3},{7,5},{1,7},{10,8},{12,10},{14... | collective-permute-start | bytes 18440 | tf_op jit(solution)/shard_map/ppermute | solution.py:24
  17.6 12.3 %collective-permute-start.4 = (bf16[4,6,66,1]{3,2,1,0:T(8,128)(2,1)S(1)}, bf16[4,6,66,1]{3,2,1,0:T(8,128)(2,1)S(1)}, u32[]{:S(2)}, u32[]{:S(2)}) collective-permute-start(bf16[4,6,66,1]{3,2,1,0:T(8,128)(2,1)S(1)} %get-tuple-element.35), channel_id=1, source_target_pairs={{0,1},{1,0},{2,3},{3,2},{4,5},{5,4},{6,7},{7,6},{8,9},{9,8},{10,11... | collective-permute-start | bytes 9512 | tf_op jit(solution)/shard_map/ppermute | solution.py:22
  18.5 16.2 %collective-permute-start.5 = (bf16[4,6,66,1]{3,2,1,0:T(8,128)(2,1)S(1)}, bf16[4,6,66,1]{3,2,1,0:T(8,128)(2,1)S(1)}, u32[]{:S(2)}, u32[]{:S(2)}) collective-permute-start(bf16[4,6,66,1]{3,2,1,0:T(8,128)(2,1)S(1)} %get-tuple-element.34), channel_id=1, source_target_pairs={{1,0},{0,1},{3,2},{2,3},{5,4},{4,5},{7,6},{6,7},{9,8},{8,9},{11,10... | collective-permute-start | bytes 9512 | tf_op jit(solution)/shard_map/ppermute | solution.py:24
  78.5 6.6 %copy-start = (f32[396,4,128]{2,1,0:T(4,128)S(1)}, f32[396,4,128]{2,1,0:T(4,128)}, u32[]{:S(2)}) copy-start(f32[396,4,128]{2,1,0:T(4,128)} %get-tuple-element.12) | copy-start | bytes 2433028
  80.8 5.6 %collective-permute-start.6 = (f32[6,66,4,1]{1,2,3,0:T(4,128)S(1)}, f32[6,66,4,1]{1,2,3,0:T(4,128)S(1)}, u32[]{:S(2)}, u32[]{:S(2)}) collective-permute-start(f32[6,66,4,1]{1,2,3,0:T(4,128)S(1)} %copy.88), channel_id=1, source_target_pairs={{0,1},{1,0},{2,3},{3,2},{4,5},{5,4},{6,7},{7,6},{8,9},{9,8},{10,11... | collective-permute-start | bytes 19016 | tf_op jit(solution)/shard_map/ppermute | solution.py:343
  82.8 4.0 %collective-permute-start.7 = (f32[6,66,4,1]{1,2,3,0:T(4,128)S(1)}, f32[6,66,4,1]{1,2,3,0:T(4,128)S(1)}, u32[]{:S(2)}, u32[]{:S(2)}) collective-permute-start(f32[6,66,4,1]{1,2,3,0:T(4,128)S(1)} %copy.91), channel_id=1, source_target_pairs={{1,0},{0,1},{3,2},{2,3},{5,4},{4,5},{7,6},{6,7},{9,8},{8,9},{11,10... | collective-permute-start | bytes 19016 | tf_op jit(solution)/shard_map/ppermute | solution.py:344
  86.2 10.2 %copy-start.3 = (f32[32,108]{1,0:T(8,128)S(1)}, f32[32,108]{1,0:T(8,128)}, u32[]{:S(2)}) copy-start(f32[32,108]{1,0:T(8,128)} %get-tuple-element.10) | copy-start | bytes 41476
  86.2 10.2 %copy-start.4 = (f32[32,1]{1,0:T(8,128)S(1)}, f32[32,1]{1,0:T(8,128)}, u32[]{:S(2)}) copy-start(f32[32,1]{1,0:T(8,128)} %get-tuple-element.11) | copy-start | bytes 388
  87.4 3.8 %collective-permute-start.8 = (f32[6,1,4,128]{3,1,0,2:T(1,128)S(1)}, f32[6,1,4,128]{3,1,0,2:T(1,128)S(1)}, u32[]{:S(2)}, u32[]{:S(2)}) collective-permute-start(f32[6,1,4,128]{3,1,0,2:T(1,128)S(1)} %get-tuple-element.27), channel_id=1, source_target_pairs={{0,2},{2,4},{4,6},{6,0},{1,3},{3,5},{5,7},{7,1},{8,10},{10,12},{12... | collective-permute-start | bytes 36872 | tf_op jit(solution)/shard_map/ppermute | solution.py:287
  89.4 2.6 %collective-permute-start.9 = (f32[6,1,4,128]{3,1,0,2:T(1,128)S(1)}, f32[6,1,4,128]{3,1,0,2:T(1,128)S(1)}, u32[]{:S(2)}, u32[]{:S(2)}) collective-permute-start(f32[6,1,4,128]{3,1,0,2:T(1,128)S(1)} %get-tuple-element.26), channel_id=1, source_target_pairs={{2,0},{4,2},{6,4},{0,6},{3,1},{5,3},{7,5},{1,7},{10,8},{12,10},{14... | collective-permute-start | bytes 36872 | tf_op jit(solution)/shard_map/ppermute | solution.py:288
  92.1 27.1 %collective-permute-start.10 = (f32[1,64,4,128]{3,1,0,2:T(8,128)S(1)}, f32[1,64,4,128]{3,1,0,2:T(8,128)S(1)}, u32[]{:S(2)}, u32[]{:S(2)}) collective-permute-start(f32[1,64,4,128]{3,1,0,2:T(8,128)S(1)} %get-tuple-element.33), channel_id=1, source_target_pairs={{0,8},{8,16},{16,24},{24,32},{32,40},{40,48},{48,56},{56,64},{64,7... | collective-permute-start | bytes 393224 | tf_op jit(solution)/shard_map/ppermute | solution.py:287
  117.7 8.1 %collective-permute-start.11 = (f32[1,64,4,128]{3,1,0,2:T(8,128)S(1)}, f32[1,64,4,128]{3,1,0,2:T(8,128)S(1)}, u32[]{:S(2)}, u32[]{:S(2)}) collective-permute-start(f32[1,64,4,128]{3,1,0,2:T(8,128)S(1)} %get-tuple-element.32), channel_id=1, source_target_pairs={{8,0},{16,8},{24,16},{32,24},{40,32},{48,40},{56,48},{64,56},{72,6... | collective-permute-start | bytes 393224 | tf_op jit(solution)/shard_map/ppermute | solution.py:288
  125.9 0.8 copy-start.2

commit v11 on v10

--- a/solution.py
+++ b/solution.py
@@ -26,6 +26,54 @@
             axis=dim,
         )
     return cells
+
+
+def extended_all(cells):
+    names = AXES
+    sizes = [lax.axis_size(a) for a in names]
+    dims = (1, 2, 3)
+
+    def part(piece, dim, d):
+        n = piece.shape[dim]
+        if d < 0:
+            return lax.slice_in_dim(piece, n - 1, n, axis=dim)
+        if d > 0:
+            return lax.slice_in_dim(piece, 0, 1, axis=dim)
+        return piece
+
+    def linear(ix, iy, iz):
+        return (ix * sizes[1] + iy) * sizes[2] + iz
+
+    blocks = {}
+    for dx in (-1, 0, 1):
+        for dy in (-1, 0, 1):
+            for dz in (-1, 0, 1):
+                piece = part(part(part(cells, 1, dx), 2, dy), 3, dz)
+                if (dx, dy, dz) != (0, 0, 0):
+                    pairs = [
+                        (
+                            linear(ix, iy, iz),
+                            linear((ix - dx) % sizes[0], (iy - dy) % sizes[1], (iz - dz) % sizes[2]),
+                        )
+                        for ix in range(sizes[0])
+                        for iy in range(sizes[1])
+                        for iz in range(sizes[2])
+                    ]
+                    piece = lax.ppermute(piece, names, pairs)
+                blocks[dx, dy, dz] = piece
+    return jnp.concatenate(
+        [
+            jnp.concatenate(
+                [
+                    jnp.concatenate([blocks[dx, dy, dz] for dz in (-1, 0, 1)], axis=3)
+                    for dy in (-1, 0, 1)
+                ],
+                axis=2,
+            )
+            for dx in (-1, 0, 1)
+        ],
+        axis=1,
+    )
 
 
 def allreduce_kernel(sizes, x_ref, o_ref, slots_a, slots_b, acc_a, send_a, recv_a, send_b, recv_b):
@@ -308,7 +356,7 @@
         for shift_b in range(3)
         for shift_e in range(3)
     ]
-    widened = extended(cells, (("gx", 1), ("gy", 2), ("gz", 3)), 1)
+    widened = extended_all(cells)
     patches = jnp.stack(
         [
             jnp.transpose(

time: 127 us -> 180 us (1.42)
  starting transfers between devices: 19.2 us -> 56.9 us
  waiting for transfers between devices: 22.7 us -> 34.9 us
  other arithmetic: 5.08 us -> 7.17 us
    ppermute x6 -> x26, starting transfers between devices: 8.57 us -> 48.7 us  [extended_all(): piece = lax.ppermute(piece, names, pairs)]
    ppermute x6 -> x26, waiting for transfers between devices: 15.1 us -> 27.4 us  [extended_all(): piece = lax.ppermute(piece, names, pairs)]
    slice x3 -> x7, local copies, waits for them, and re-layouts: 1.14 us -> 4.92 us  [the longest x6 4.91 us: part(): return lax.slice_in_dim(piece, n - 1, n, axis=dim)]
    ppermute x2, starting transfers between devices: 5.7 us -> 2.69 us  [fold_halo(): lax.ppermute(tail, axis, [(i, (i + 1) % count) for i in range(count)])]
    concatenate x2 -> x3, other arithmetic: 1.24 us -> 3.63 us  [the longest x2 2.87 us: extended_all(): jnp.concatenate([jnp.concatenate([jnp.concatenate([blocks[dx, dy, dz] for...]
    unnamed x37 -> x47, local copies, waits for them, and re-layouts: 7.44 us -> 7.23 us
  transfers between devices with their start and end apart: 12 -> 32, of which waited for: 9 -> 14; matrix products, arithmetic and copies ran while one was open for 16% -> 13% of each run, Pallas kernels for 12% -> 9%
where the time goes in v11:
time: 180 us; the launch traced here: 179 us
  starting transfers between devices  56.9 us (32%)
  Pallas kernels  47.1 us (26%)
  waiting for transfers between devices  34.9 us (19%)
  local copies, waits for them, and re-layouts  31.8 us (18%)
  other arithmetic  7.17 us (4%)
    ppermute x26, starting transfers between devices, extended_all(): piece = lax.ppermute(piece, names, pairs)  48.7 us
    pallas_call x1, Pallas kernels, forward(): pl.pallas_call(lambda *refs: forward_kernel(rows, wide_y, *refs), grid=(p...  31.2 us
    ppermute x26, waiting for transfers between devices, extended_all(): piece = lax.ppermute(piece, names, pairs)  27.4 us
    pallas_call x1, Pallas kernels, allreduce(): pl.pallas_call(lambda *refs: allreduce_kernel(sizes, *refs), out_shape=ja...  15.9 us
    reshape x1, local copies, waits for them, and re-layouts, on_device(): patches = patches.reshape(cells_x * cells_y, chan_in * 27, cells_z)  7.48 us
    unnamed x47, local copies, waits for them, and re-layouts  7.23 us
    ppermute x2, waiting for transfers between devices, fold_halo(): lax.ppermute(head, axis, [((i + 1) % count, i) for i in range(count)])  7.13 us
    slice x6, local copies, waits for them, and re-layouts, part(): return lax.slice_in_dim(piece, n - 1, n, axis=dim)  4.91 us
  transfers between devices with their start and end apart: 32, of which 14 were waited for; matrix products, arithmetic and copies ran while one was open for 13% of the time, Pallas kernels for 9%

profile of v11, /device:TPU:7, one launch (start us, length us, event | category | flops | bytes accessed | tf_op | source)
XLA Modules:
  0.0 179.0 jit_solution(17202044267576050655)
XLA Ops:
  1.6 5.3 %collective-permute-start = (bf16[4,1,1,1]{3,2,1,0:T(2,128)(2,1)S(1)}, bf16[4,1,1,1]{3,2,1,0:T(2,128)(2,1)S(1)}, u32[]{:S(2)}, u32[]{:S(2)}) collective-permute-start(bf16[4,1,1,1]{3,2,1,0:T(2,128)(2,1)S(1)} %get-tuple-element.42), channel_id=1, source_target_pairs={{0,11},{1,10},{2,13},{3,12},{4,15},{5,14},{6,9},{7,8},{8,19},{9,18... | collective-permute-start | bytes 32 | tf_op jit(solution)/shard_map/ppermute | solution.py:62
  20.8 4.4 %collective-permute-done.2 = bf16[4,1,1,1]{3,2,1,0:T(2,128)(2,1)S(1)} collective-permute-done((bf16[4,1,1,1]{3,2,1,0:T(2,128)(2,1)S(1)}, bf16[4,1,1,1]{3,2,1,0:T(2,128)(2,1)S(1)}, u32[]{:S(2)}, u32[]{:S(2)}) %collective-permute-start.2) | collective-permute-done | bytes 40 | tf_op jit(solution)/shard_map/ppermute | solution.py:62
  25.2 3.5 %collective-permute-start.6 = (bf16[4,1,1,1]{3,2,1,0:T(2,128)(2,1)S(1)}, bf16[4,1,1,1]{3,2,1,0:T(2,128)(2,1)S(1)}, u32[]{:S(2)}, u32[]{:S(2)}) collective-permute-start(bf16[4,1,1,1]{3,2,1,0:T(2,128)(2,1)S(1)} %get-tuple-element.40), channel_id=1, source_target_pairs={{0,15},{1,14},{2,9},{3,8},{4,11},{5,10},{6,13},{7,12},{8,23},{9,22... | collective-permute-start | bytes 32 | tf_op jit(solution)/shard_map/ppermute | solution.py:62
  29.4 7.7 %collective-permute-start.8 = (bf16[4,1,1,1]{3,2,1,0:T(2,128)(2,1)S(1)}, bf16[4,1,1,1]{3,2,1,0:T(2,128)(2,1)S(1)}, u32[]{:S(2)}, u32[]{:S(2)}) collective-permute-start(bf16[4,1,1,1]{3,2,1,0:T(2,128)(2,1)S(1)} %get-tuple-element.39), channel_id=1, source_target_pairs={{0,15},{1,14},{2,9},{3,8},{4,11},{5,10},{6,13},{7,12},{8,23},{9,22... | collective-permute-start | bytes 32 | tf_op jit(solution)/shard_map/ppermute | solution.py:62
  37.9 4.6 %collective-permute-done.11 = bf16[4,4,1,1]{3,2,1,0:T(2,128)(2,1)S(1)} collective-permute-done((bf16[4,4,1,1]{3,2,1,0:T(2,128)(2,1)S(1)}, bf16[4,4,1,1]{3,2,1,0:T(2,128)(2,1)S(1)}, u32[]{:S(2)}, u32[]{:S(2)}) %collective-permute-start.11) | collective-permute-done | bytes 64 | tf_op jit(solution)/shard_map/ppermute | solution.py:62
  42.5 3.4 %collective-permute-done.14 = bf16[4,4,1,1]{3,2,1,0:T(2,128)(2,1)S(1)} collective-permute-done((bf16[4,4,1,1]{3,2,1,0:T(2,128)(2,1)S(1)}, bf16[4,4,1,1]{3,2,1,0:T(2,128)(2,1)S(1)}, u32[]{:S(2)}, u32[]{:S(2)}) %collective-permute-start.14) | collective-permute-done | bytes 64 | tf_op jit(solution)/shard_map/ppermute | solution.py:62
  47.3 2.0 %collective-permute-done.16 = bf16[4,4,1,1]{3,2,1,0:T(2,128)(2,1)S(1)} collective-permute-done((bf16[4,4,1,1]{3,2,1,0:T(2,128)(2,1)S(1)}, bf16[4,4,1,1]{3,2,1,0:T(2,128)(2,1)S(1)}, u32[]{:S(2)}, u32[]{:S(2)}) %collective-permute-start.16) | collective-permute-done | bytes 64 | tf_op jit(solution)/shard_map/ppermute | solution.py:62
  49.3 4.6 %collective-permute-done.9 = bf16[4,4,1,1]{3,2,1,0:T(2,128)(2,1)S(1)} collective-permute-done((bf16[4,4,1,1]{3,2,1,0:T(2,128)(2,1)S(1)}, bf16[4,4,1,1]{3,2,1,0:T(2,128)(2,1)S(1)}, u32[]{:S(2)}, u32[]{:S(2)}) %collective-permute-start.9) | collective-permute-done | bytes 64 | tf_op jit(solution)/shard_map/ppermute | solution.py:62
  53.9 10.7 %collective-permute-start.3 = (bf16[4,1,64,1]{3,2,1,0:T(8,128)(2,1)S(1)}, bf16[4,1,64,1]{3,2,1,0:T(8,128)(2,1)S(1)}, u32[]{:S(2)}, u32[]{:S(2)}) collective-permute-start(bf16[4,1,64,1]{3,2,1,0:T(8,128)(2,1)S(1)} %get-tuple-element.51), channel_id=1, source_target_pairs={{0,9},{1,8},{2,11},{3,10},{4,13},{5,12},{6,15},{7,14},{8,17},{9,16... | collective-permute-start | bytes 1544 | tf_op jit(solution)/shard_map/ppermute | solution.py:62
  68.6 2.4 %collective-permute-start.19 = (bf16[4,1,1,1]{3,2,1,0:T(2,128)(2,1)S(1)}, bf16[4,1,1,1]{3,2,1,0:T(2,128)(2,1)S(1)}, u32[]{:S(2)}, u32[]{:S(2)}) collective-permute-start(bf16[4,1,1,1]{3,2,1,0:T(2,128)(2,1)S(1)} %get-tuple-element.38), channel_id=1, source_target_pairs={{0,123},{1,122},{2,125},{3,124},{4,127},{5,126},{6,121},{7,120},{8... | collective-permute-start | bytes 32 | tf_op jit(solution)/shard_map/ppermute | solution.py:62
  71.0 2.6 %collective-permute-start.23 = (bf16[4,1,1,1]{3,2,1,0:T(2,128)(2,1)S(1)}, bf16[4,1,1,1]{3,2,1,0:T(2,128)(2,1)S(1)}, u32[]{:S(2)}, u32[]{:S(2)}) collective-permute-start(bf16[4,1,1,1]{3,2,1,0:T(2,128)(2,1)S(1)} %get-tuple-element.37), channel_id=1, source_target_pairs={{0,127},{1,126},{2,121},{3,120},{4,123},{5,122},{6,125},{7,124},{8... | collective-permute-start | bytes 32 | tf_op jit(solution)/shard_map/ppermute | solution.py:62
  73.6 3.5 %collective-permute-start.25 = (bf16[4,1,1,1]{3,2,1,0:T(2,128)(2,1)S(1)}, bf16[4,1,1,1]{3,2,1,0:T(2,128)(2,1)S(1)}, u32[]{:S(2)}, u32[]{:S(2)}) collective-permute-start(bf16[4,1,1,1]{3,2,1,0:T(2,128)(2,1)S(1)} %get-tuple-element.43), channel_id=1, source_target_pairs={{0,127},{1,126},{2,121},{3,120},{4,123},{5,122},{6,125},{7,124},{8... | collective-permute-start | bytes 32 | tf_op jit(solution)/shard_map/ppermute | solution.py:62
  83.8 2.2 %collective-permute-start.21 = (bf16[4,1,64,128]{3,2,1,0:T(8,128)(2,1)S(1)}, bf16[4,1,64,128]{3,2,1,0:T(8,128)(2,1)S(1)}, u32[]{:S(2)}, u32[]{:S(2)}) collective-permute-start(bf16[4,1,64,128]{3,2,1,0:T(8,128)(2,1)S(1)} %get-tuple-element.52), channel_id=1, source_target_pairs={{0,120},{1,121},{2,122},{3,123},{4,124},{5,125},{6,126},{7,127},{8... | collective-permute-start | bytes 196616 | tf_op jit(solution)/shard_map/ppermute | solution.py:62
  86.2 2.4 %collective-permute-done.22 = bf16[4,1,64,1]{3,2,1,0:T(8,128)(2,1)S(1)} collective-permute-done((bf16[4,1,64,1]{3,2,1,0:T(8,128)(2,1)S(1)}, bf16[4,1,64,1]{3,2,1,0:T(8,128)(2,1)S(1)}, u32[]{:S(2)}, u32[]{:S(2)}) %collective-permute-start.22) | collective-permute-done | bytes 544 | tf_op jit(solution)/shard_map/ppermute | solution.py:62
  88.6 1.8 %collective-permute-done.18 = bf16[4,1,1,128]{3,2,1,0:T(2,128)(2,1)S(1)} collective-permute-done((bf16[4,1,1,128]{3,2,1,0:T(2,128)(2,1)S(1)}, bf16[4,1,1,128]{3,2,1,0:T(2,128)(2,1)S(1)}, u32[]{:S(2)}, u32[]{:S(2)}) %collective-permute-start.18) | collective-permute-done | bytes 1056 | tf_op jit(solution)/shard_map/ppermute | solution.py:62
  90.5 1.7 collective-permute-done.21
  95.5 7.5 %copy.77.refs_5_ = bf16[256,108,128]{2,1,0:T(8,128)(2,1)} copy(bf16[256,108,128]{2,0,1:T(8,128)(2,1)S(1)} %bitcast.220) | data formatting | bytes 14155776 | tf_op jit(solution)/shard_map/reshape | solution.py:369
  103.0 31.2 %shard_map.75 = (bf16[32,4096]{1,0:T(8,128)(2,1)}, f32[32,108]{1,0:T(8,128)}, f32[32,1]{1,0:T(8,128)}, f32[396,4,128]{2,1,0:T(4,128)}, f32[396,4,128]{2,1,0:T(4,128)}) custom-call(bf16[32,108]{1,0:T(8,128)(2,1)} %copy.75.refs_0_, f32[32,1]{1,0:T(8,128)} %copy.76.refs_1_, f32[2,128,128]{2,1,0:T(8,128)} %add_convert_fusion.refs_2_, ...), custom_call_target="tpu_custom_call" | custom-call | tf_op jit(solution)/shard_map/pallas_call | solution.py:297
  134.2 2.0 %fusion.30 = (f32[6,66,4,1]{3,2,1,0:T(4,128)S(1)}, f32[6,66,4,1]{3,2,1,0:T(4,128)S(1)}) fusion(f32[6,66,4,128]{3,2,1,0:T(4,128)} %bitcast.223), kind=kLoop, calls=%fused_computation.81 | loop fusion | bytes 25344 | tf_op jit(solution)/shard_map/slice | solution.py:389
  142.3 2.7 %collective-permute-start.29 = (f32[6,1,4,128]{3,1,0,2:T(1,128)S(1)}, f32[6,1,4,128]{3,1,0,2:T(1,128)S(1)}, u32[]{:S(2)}, u32[]{:S(2)}) collective-permute-start(f32[6,1,4,128]{3,1,0,2:T(1,128)S(1)} %get-tuple-element.26), channel_id=1, source_target_pairs={{2,0},{4,2},{6,4},{0,6},{3,1},{5,3},{7,5},{1,7},{10,8},{12,10},{14... | collective-permute-start | bytes 36872 | tf_op jit(solution)/shard_map/ppermute | solution.py:336
  146.0 2.4 %collective-permute-start.30 = (f32[1,64,4,128]{3,1,0,2:T(8,128)S(1)}, f32[1,64,4,128]{3,1,0,2:T(8,128)S(1)}, u32[]{:S(2)}, u32[]{:S(2)}) collective-permute-start(f32[1,64,4,128]{3,1,0,2:T(8,128)S(1)} %get-tuple-element.33), channel_id=1, source_target_pairs={{0,8},{8,16},{16,24},{24,32},{32,40},{40,48},{48,56},{56,64},{64,7... | collective-permute-start | bytes 393224 | tf_op jit(solution)/shard_map/ppermute | solution.py:335
  149.1 15.9 %shard_map.76 = f32[32,128]{1,0:T(8,128)} custom-call(f32[32,128]{1,0:T(8,128)} %maximum_maximum_fusion.4.refs_0_), custom_call_target="tpu_custom_call" | custom-call | tf_op jit(solution)/shard_map/pallas_call | solution.py:161
  166.4 2.3 %reshape.238 = bf16[32,2,32,64]{3,2,1,0:T(8,128)(2,1)} reshape(bf16[32,4096]{1,0:T(8,128)(2,1)} %get-tuple-element.9) | data formatting | bytes 524288 | tf_op jit(solution)/shard_map/reshape | solution.py:375
  171.3 6.9 %collective-permute-done.31 = f32[1,64,4,128]{3,1,0,2:T(8,128)S(1)} collective-permute-done((f32[1,64,4,128]{3,1,0,2:T(8,128)S(1)}, f32[1,64,4,128]{3,1,0,2:T(8,128)S(1)}, u32[]{:S(2)}, u32[]{:S(2)}) %collective-permute-start.31) | collective-permute-done | bytes 131104 | tf_op jit(solution)/shard_map/ppermute | solution.py:336
  (138 shorter events, 44.3 us)
Async XLA Ops:
  1.6 18.4 %collective-permute-start = (bf16[4,1,1,1]{3,2,1,0:T(2,128)(2,1)S(1)}, bf16[4,1,1,1]{3,2,1,0:T(2,128)(2,1)S(1)}, u32[]{:S(2)}, u32[]{:S(2)}) collective-permute-start(bf16[4,1,1,1]{3,2,1,0:T(2,128)(2,1)S(1)} %get-tuple-element.42), channel_id=1, source_target_pairs={{0,11},{1,10},{2,13},{3,12},{4,15},{5,14},{6,9},{7,8},{8,19},{9,18... | collective-permute-start | bytes 32 | tf_op jit(solution)/shard_map/ppermute | solution.py:62
  8.1 56.4 %collective-permute-start.12 = (bf16[4,4,64,1]{3,2,1,0:T(8,128)(2,1)S(1)}, bf16[4,4,64,1]{3,2,1,0:T(8,128)(2,1)S(1)}, u32[]{:S(2)}, u32[]{:S(2)}) collective-permute-start(bf16[4,4,64,1]{3,2,1,0:T(8,128)(2,1)S(1)} %get-tuple-element.60), channel_id=1, source_target_pairs={{0,1},{1,0},{2,3},{3,2},{4,5},{5,4},{6,7},{7,6},{8,9},{9,8},{10,11... | collective-permute-start | bytes 6152 | tf_op jit(solution)/shard_map/ppermute | solution.py:62
  8.2 56.4 %collective-permute-start.13 = (bf16[4,4,64,1]{3,2,1,0:T(8,128)(2,1)S(1)}, bf16[4,4,64,1]{3,2,1,0:T(8,128)(2,1)S(1)}, u32[]{:S(2)}, u32[]{:S(2)}) collective-permute-start(bf16[4,4,64,1]{3,2,1,0:T(8,128)(2,1)S(1)} %get-tuple-element.61), channel_id=1, source_target_pairs={{0,1},{1,0},{2,3},{3,2},{4,5},{5,4},{6,7},{7,6},{8,9},{9,8},{10,11... | collective-permute-start | bytes 6152 | tf_op jit(solution)/shard_map/ppermute | solution.py:62
  10.5 54.2 %collective-permute-start.10 = (bf16[4,4,1,128]{3,2,1,0:T(2,128)(2,1)S(1)}, bf16[4,4,1,128]{3,2,1,0:T(2,128)(2,1)S(1)}, u32[]{:S(2)}, u32[]{:S(2)}) collective-permute-start(bf16[4,4,1,128]{3,2,1,0:T(2,128)(2,1)S(1)} %get-tuple-element.58), channel_id=1, source_target_pairs={{0,2},{1,3},{2,4},{3,5},{4,6},{5,7},{6,0},{7,1},{8,10},{9,11},{10,... | collective-permute-start | bytes 12296 | tf_op jit(solution)/shard_map/ppermute | solution.py:62
  11.8 53.6 %collective-permute-start.15 = (bf16[4,4,1,128]{3,2,1,0:T(2,128)(2,1)S(1)}, bf16[4,4,1,128]{3,2,1,0:T(2,128)(2,1)S(1)}, u32[]{:S(2)}, u32[]{:S(2)}) collective-permute-start(bf16[4,4,1,128]{3,2,1,0:T(2,128)(2,1)S(1)} %get-tuple-element.59), channel_id=1, source_target_pairs={{0,6},{1,7},{2,0},{3,1},{4,2},{5,3},{6,4},{7,5},{8,14},{9,15},{10,... | collective-permute-start | bytes 12296 | tf_op jit(solution)/shard_map/ppermute | solution.py:62
  20.1 5.1 %collective-permute-start.2 = (bf16[4,1,1,1]{3,2,1,0:T(2,128)(2,1)S(1)}, bf16[4,1,1,1]{3,2,1,0:T(2,128)(2,1)S(1)}, u32[]{:S(2)}, u32[]{:S(2)}) collective-permute-start(bf16[4,1,1,1]{3,2,1,0:T(2,128)(2,1)S(1)} %get-tuple-element.41), channel_id=1, source_target_pairs={{0,11},{1,10},{2,13},{3,12},{4,15},{5,14},{6,9},{7,8},{8,19},{9,18... | collective-permute-start | bytes 32 | tf_op jit(solution)/shard_map/ppermute | solution.py:62
  29.4 8.4 %collective-permute-start.8 = (bf16[4,1,1,1]{3,2,1,0:T(2,128)(2,1)S(1)}, bf16[4,1,1,1]{3,2,1,0:T(2,128)(2,1)S(1)}, u32[]{:S(2)}, u32[]{:S(2)}) collective-permute-start(bf16[4,1,1,1]{3,2,1,0:T(2,128)(2,1)S(1)} %get-tuple-element.39), channel_id=1, source_target_pairs={{0,15},{1,14},{2,9},{3,8},{4,11},{5,10},{6,13},{7,12},{8,23},{9,22... | collective-permute-start | bytes 32 | tf_op jit(solution)/shard_map/ppermute | solution.py:62
  37.9 4.6 %collective-permute-start.11 = (bf16[4,4,1,1]{3,2,1,0:T(2,128)(2,1)S(1)}, bf16[4,4,1,1]{3,2,1,0:T(2,128)(2,1)S(1)}, u32[]{:S(2)}, u32[]{:S(2)}) collective-permute-start(bf16[4,4,1,1]{3,2,1,0:T(2,128)(2,1)S(1)} %get-tuple-element.57), channel_id=1, source_target_pairs={{0,3},{1,2},{2,5},{3,4},{4,7},{5,6},{6,1},{7,0},{8,11},{9,10},{10,... | collective-permute-start | bytes 104 | tf_op jit(solution)/shard_map/ppermute | solution.py:62
  49.3 4.6 %collective-permute-start.9 = (bf16[4,4,1,1]{3,2,1,0:T(2,128)(2,1)S(1)}, bf16[4,4,1,1]{3,2,1,0:T(2,128)(2,1)S(1)}, u32[]{:S(2)}, u32[]{:S(2)}) collective-permute-start(bf16[4,4,1,1]{3,2,1,0:T(2,128)(2,1)S(1)} %get-tuple-element.54), channel_id=1, source_target_pairs={{0,3},{1,2},{2,5},{3,4},{4,7},{5,6},{6,1},{7,0},{8,11},{9,10},{10,... | collective-permute-start | bytes 104 | tf_op jit(solution)/shard_map/ppermute | solution.py:62
  53.9 12.3 %collective-permute-start.3 = (bf16[4,1,64,1]{3,2,1,0:T(8,128)(2,1)S(1)}, bf16[4,1,64,1]{3,2,1,0:T(8,128)(2,1)S(1)}, u32[]{:S(2)}, u32[]{:S(2)}) collective-permute-start(bf16[4,1,64,1]{3,2,1,0:T(8,128)(2,1)S(1)} %get-tuple-element.51), channel_id=1, source_target_pairs={{0,9},{1,8},{2,11},{3,10},{4,13},{5,12},{6,15},{7,14},{8,17},{9,16... | collective-permute-start | bytes 1544 | tf_op jit(solution)/shard_map/ppermute | solution.py:62
  64.6 6.4 %collective-permute-start.1 = (bf16[4,1,1,128]{3,2,1,0:T(2,128)(2,1)S(1)}, bf16[4,1,1,128]{3,2,1,0:T(2,128)(2,1)S(1)}, u32[]{:S(2)}, u32[]{:S(2)}) collective-permute-start(bf16[4,1,1,128]{3,2,1,0:T(2,128)(2,1)S(1)} %get-tuple-element.46), channel_id=1, source_target_pairs={{0,10},{1,11},{2,12},{3,13},{4,14},{5,15},{6,8},{7,9},{8,18},{9,19... | collective-permute-start | bytes 3080 | tf_op jit(solution)/shard_map/ppermute | solution.py:62
  64.7 8.9 %collective-permute-start.7 = (bf16[4,1,1,128]{3,2,1,0:T(2,128)(2,1)S(1)}, bf16[4,1,1,128]{3,2,1,0:T(2,128)(2,1)S(1)}, u32[]{:S(2)}, u32[]{:S(2)}) collective-permute-start(bf16[4,1,1,128]{3,2,1,0:T(2,128)(2,1)S(1)} %get-tuple-element.45), channel_id=1, source_target_pairs={{0,14},{1,15},{2,8},{3,9},{4,10},{5,11},{6,12},{7,13},{8,22},{9,23... | collective-permute-start | bytes 3080 | tf_op jit(solution)/shard_map/ppermute | solution.py:62
  65.4 11.7 %collective-permute-start.4 = (bf16[4,1,64,128]{3,2,1,0:T(8,128)(2,1)S(1)}, bf16[4,1,64,128]{3,2,1,0:T(8,128)(2,1)S(1)}, u32[]{:S(2)}, u32[]{:S(2)}) collective-permute-start(bf16[4,1,64,128]{3,2,1,0:T(8,128)(2,1)S(1)} %get-tuple-element.53), channel_id=1, source_target_pairs={{0,8},{1,9},{2,10},{3,11},{4,12},{5,13},{6,14},{7,15},{8,16},{9,17... | collective-permute-start | bytes 196616 | tf_op jit(solution)/shard_map/ppermute | solution.py:62
  66.2 15.4 %collective-permute-start.17 = (bf16[4,1,1,1]{3,2,1,0:T(2,128)(2,1)S(1)}, bf16[4,1,1,1]{3,2,1,0:T(2,128)(2,1)S(1)}, u32[]{:S(2)}, u32[]{:S(2)}) collective-permute-start(bf16[4,1,1,1]{3,2,1,0:T(2,128)(2,1)S(1)} %get-tuple-element.36), channel_id=1, source_target_pairs={{0,123},{1,122},{2,125},{3,124},{4,127},{5,126},{6,121},{7,120},{8... | collective-permute-start | bytes 32 | tf_op jit(solution)/shard_map/ppermute | solution.py:62
  68.6 13.1 %collective-permute-start.19 = (bf16[4,1,1,1]{3,2,1,0:T(2,128)(2,1)S(1)}, bf16[4,1,1,1]{3,2,1,0:T(2,128)(2,1)S(1)}, u32[]{:S(2)}, u32[]{:S(2)}) collective-permute-start(bf16[4,1,1,1]{3,2,1,0:T(2,128)(2,1)S(1)} %get-tuple-element.38), channel_id=1, source_target_pairs={{0,123},{1,122},{2,125},{3,124},{4,127},{5,126},{6,121},{7,120},{8... | collective-permute-start | bytes 32 | tf_op jit(solution)/shard_map/ppermute | solution.py:62
  71.0 11.2 %collective-permute-start.23 = (bf16[4,1,1,1]{3,2,1,0:T(2,128)(2,1)S(1)}, bf16[4,1,1,1]{3,2,1,0:T(2,128)(2,1)S(1)}, u32[]{:S(2)}, u32[]{:S(2)}) collective-permute-start(bf16[4,1,1,1]{3,2,1,0:T(2,128)(2,1)S(1)} %get-tuple-element.37), channel_id=1, source_target_pairs={{0,127},{1,126},{2,121},{3,120},{4,123},{5,122},{6,125},{7,124},{8... | collective-permute-start | bytes 32 | tf_op jit(solution)/shard_map/ppermute | solution.py:62
  73.6 10.2 %collective-permute-start.25 = (bf16[4,1,1,1]{3,2,1,0:T(2,128)(2,1)S(1)}, bf16[4,1,1,1]{3,2,1,0:T(2,128)(2,1)S(1)}, u32[]{:S(2)}, u32[]{:S(2)}) collective-permute-start(bf16[4,1,1,1]{3,2,1,0:T(2,128)(2,1)S(1)} %get-tuple-element.43), channel_id=1, source_target_pairs={{0,127},{1,126},{2,121},{3,120},{4,123},{5,122},{6,125},{7,124},{8... | collective-permute-start | bytes 32 | tf_op jit(solution)/shard_map/ppermute | solution.py:62
  77.1 9.1 %collective-permute-start.20 = (bf16[4,1,64,1]{3,2,1,0:T(8,128)(2,1)S(1)}, bf16[4,1,64,1]{3,2,1,0:T(8,128)(2,1)S(1)}, u32[]{:S(2)}, u32[]{:S(2)}) collective-permute-start(bf16[4,1,64,1]{3,2,1,0:T(8,128)(2,1)S(1)} %get-tuple-element.48), channel_id=1, source_target_pairs={{0,121},{1,120},{2,123},{3,122},{4,125},{5,124},{6,127},{7,126},{8... | collective-permute-start | bytes 1544 | tf_op jit(solution)/shard_map/ppermute | solution.py:62
  81.6 7.1 %collective-permute-start.22 = (bf16[4,1,64,1]{3,2,1,0:T(8,128)(2,1)S(1)}, bf16[4,1,64,1]{3,2,1,0:T(8,128)(2,1)S(1)}, u32[]{:S(2)}, u32[]{:S(2)}) collective-permute-start(bf16[4,1,64,1]{3,2,1,0:T(8,128)(2,1)S(1)} %get-tuple-element.49), channel_id=1, source_target_pairs={{0,121},{1,120},{2,123},{3,122},{4,125},{5,124},{6,127},{7,126},{8... | collective-permute-start | bytes 1544 | tf_op jit(solution)/shard_map/ppermute | solution.py:62
  81.6 8.8 %collective-permute-start.18 = (bf16[4,1,1,128]{3,2,1,0:T(2,128)(2,1)S(1)}, bf16[4,1,1,128]{3,2,1,0:T(2,128)(2,1)S(1)}, u32[]{:S(2)}, u32[]{:S(2)}) collective-permute-start(bf16[4,1,1,128]{3,2,1,0:T(2,128)(2,1)S(1)} %get-tuple-element.44), channel_id=1, source_target_pairs={{0,122},{1,123},{2,124},{3,125},{4,126},{5,127},{6,120},{7,121},{8... | collective-permute-start | bytes 3080 | tf_op jit(solution)/shard_map/ppermute | solution.py:62
  82.2 8.2 %collective-permute-start.24 = (bf16[4,1,1,128]{3,2,1,0:T(2,128)(2,1)S(1)}, bf16[4,1,1,128]{3,2,1,0:T(2,128)(2,1)S(1)}, u32[]{:S(2)}, u32[]{:S(2)}) collective-permute-start(bf16[4,1,1,128]{3,2,1,0:T(2,128)(2,1)S(1)} %get-tuple-element.47), channel_id=1, source_target_pairs={{0,126},{1,127},{2,120},{3,121},{4,122},{5,123},{6,124},{7,125},{8... | collective-permute-start | bytes 3080 | tf_op jit(solution)/shard_map/ppermute | solution.py:62
  83.8 8.3 %collective-permute-start.21 = (bf16[4,1,64,128]{3,2,1,0:T(8,128)(2,1)S(1)}, bf16[4,1,64,128]{3,2,1,0:T(8,128)(2,1)S(1)}, u32[]{:S(2)}, u32[]{:S(2)}) collective-permute-start(bf16[4,1,64,128]{3,2,1,0:T(8,128)(2,1)S(1)} %get-tuple-element.52), channel_id=1, source_target_pairs={{0,120},{1,121},{2,122},{3,123},{4,124},{5,125},{6,126},{7,127},{8... | collective-permute-start | bytes 196616 | tf_op jit(solution)/shard_map/ppermute | solution.py:62
  146.0 25.3 %collective-permute-start.30 = (f32[1,64,4,128]{3,1,0,2:T(8,128)S(1)}, f32[1,64,4,128]{3,1,0,2:T(8,128)S(1)}, u32[]{:S(2)}, u32[]{:S(2)}) collective-permute-start(f32[1,64,4,128]{3,1,0,2:T(8,128)S(1)} %get-tuple-element.33), channel_id=1, source_target_pairs={{0,8},{8,16},{16,24},{24,32},{32,40},{40,48},{48,56},{56,64},{64,7... | collective-permute-start | bytes 393224 | tf_op jit(solution)/shard_map/ppermute | solution.py:335
  170.1 8.1 %collective-permute-start.31 = (f32[1,64,4,128]{3,1,0,2:T(8,128)S(1)}, f32[1,64,4,128]{3,1,0,2:T(8,128)S(1)}, u32[]{:S(2)}, u32[]{:S(2)}) collective-permute-start(f32[1,64,4,128]{3,1,0,2:T(8,128)S(1)} %get-tuple-element.32), channel_id=1, source_target_pairs={{8,0},{16,8},{24,16},{32,24},{40,32},{48,40},{56,48},{64,56},{72,6... | collective-permute-start | bytes 393224 | tf_op jit(solution)/shard_map/ppermute | solution.py:336
  (16 other events, 109.1 us)

commit v12 on v10

--- a/solution.py
+++ b/solution.py
@@ -149,34 +149,38 @@
     first = lane == 0
     last = lane == rows - 1
 
-    @pl.loop(0, lines)
+    group = 8
+    pooled_rows = group // 2
+    pieces = pooled_rows // 2
+
+    @pl.loop(0, plane // group)
     def _(j):
-        cot = cot_ref[:, pl.ds(pl.multiple_of(j * rows, rows), rows)]
-        ups = (
-            jnp.dot(cot, u_ref[0], preferred_element_type=jnp.float32) * 0.125,
-            jnp.dot(cot, u_ref[1], preferred_element_type=jnp.float32) * 0.125,
-        )
-        spread4 = jnp.concatenate([ups[0], ups[0], ups[1], ups[1]], axis=1)
-        totals = [None, None]
+        ups = []
+        for m in range(pieces):
+            cot = cot_ref[:, pl.ds(pl.multiple_of((j * pieces + m) * rows, rows), rows)]
+            ups.append(jnp.dot(cot, u_ref[0], preferred_element_type=jnp.float32) * 0.125)
+            ups.append(jnp.dot(cot, u_ref[1], preferred_element_type=jnp.float32) * 0.125)
+        spread_all = jnp.concatenate([ups[r // 2] for r in range(group)], axis=1)
+        totals = [None] * pooled_rows
         wg = None
         bg = None
         spreads = []
         for px, base in enumerate((0, plane)):
-            patch = jnp.concatenate([p_ref[base + j * 4 + r] for r in range(4)], axis=1)
+            patch = jnp.concatenate([p_ref[base + j * group + r] for r in range(group)], axis=1)
             preact = jnp.dot(weight, patch, preferred_element_type=jnp.float32) + bias
             scaled = soft_scale * preact
             e = jnp.exp(-jnp.abs(scaled))
             softplus = jnp.maximum(scaled, 0.0) + jnp.log1p(e)
             activated = leak_slope * preact + (1.0 - leak_slope) / soft_scale * softplus
-            for half in range(2):
+            for h in range(pooled_rows):
                 pair = (
-                    activated[:, 2 * half * rows : (2 * half + 1) * rows]
-                    + activated[:, (2 * half + 1) * rows : (2 * half + 2) * rows]
+                    activated[:, 2 * h * rows : (2 * h + 1) * rows]
+                    + activated[:, (2 * h + 1) * rows : (2 * h + 2) * rows]
                 )
-                totals[half] = pair if totals[half] is None else totals[half] + pair
+                totals[h] = pair if totals[h] is None else totals[h] + pair
             sigmoid = jnp.where(scaled >= 0.0, 1.0, e) / (1.0 + e)
             slope = leak_slope + (1.0 - leak_slope) * sigmoid
-            delta = (slope * spread4).astype(jnp.bfloat16)
+            delta = (slope * spread_all).astype(jnp.bfloat16)
             term = lax.dot_general(
                 delta, patch, (((1,), (1,)), ((), ())), preferred_element_type=jnp.float32
             )
@@ -187,7 +191,7 @@
         acc_main = {}
         acc_edge = {}
         for px in range(2):
-            for r in range(4):
+            for r in range(group):
                 cols = slice(r * rows, (r + 1) * rows)
                 for a in range(3):
                     for b in range(3):
@@ -206,19 +210,21 @@
                             acc_main[key] = inner
                             acc_edge[key] = edge
         for (dx, dy), value in acc_main.items():
-            out = (step * 2 + dx) * wide_y + (j * 4 + dy)
+            out = (step * 2 + dx) * wide_y + (j * group + dy)
             main_ref[out] += value[: main_ref.shape[1]]
             edge_ref[out] += acc_edge[dx, dy][: edge_ref.shape[1]]
         wg_acc[...] += wg
         bg_acc[...] += jnp.sum(bg, axis=1, keepdims=True)
-        pooled = jnp.dot(
-            totals[0], q_ref[0], preferred_element_type=jnp.float32, precision=lax.Precision.HIGHEST
-        ) + jnp.dot(
-            totals[1], q_ref[1], preferred_element_type=jnp.float32, precision=lax.Precision.HIGHEST
-        )
-        pooled_ref[:, pl.ds(pl.multiple_of(j * rows, rows), rows)] = (pooled * 0.125).astype(
-            pooled_ref.dtype
-        )
+        for m in range(pieces):
+            pooled = jnp.dot(
+                totals[2 * m], q_ref[0], preferred_element_type=jnp.float32,
+                precision=lax.Precision.HIGHEST,
+            ) + jnp.dot(
+                totals[2 * m + 1], q_ref[1], preferred_element_type=jnp.float32,
+                precision=lax.Precision.HIGHEST,
+            )
+            at = pl.multiple_of((j * pieces + m) * rows, rows)
+            pooled_ref[:, pl.ds(at, rows)] = (pooled * 0.125).astype(pooled_ref.dtype)
 
     @pl.when(step == pl.num_programs(0) - 1)
     def _():

time: 127 us -> 120 us (0.945)
  Pallas kernels: 46.5 us -> 39.6 us
    pallas_call x1, Pallas kernels: 31.2 us -> 24.2 us  [forward(): pl.pallas_call(lambda *refs: forward_kernel(rows, wide_y, *refs), grid=(p...]
  transfers between devices with their start and end apart: 12 -> 12, of which waited for: 9 -> 9; matrix products, arithmetic and copies ran while one was open for 16% -> 16% of each run, Pallas kernels for 12% -> 13%
where the time goes in v12:
time: 120 us
  Pallas kernels  39.6 us (33%)
  local copies, waits for them, and re-layouts  32.1 us (27%)
  waiting for transfers between devices  22.7 us (19%)
  starting transfers between devices  19.2 us (16%)
  other arithmetic  5.08 us (4%)
    pallas_call x1, Pallas kernels, forward(): pl.pallas_call(lambda *refs: forward_kernel(rows, wide_y, *refs), grid=(p...  24.2 us
    pallas_call x1, Pallas kernels, allreduce(): pl.pallas_call(lambda *refs: allreduce_kernel(sizes, *refs), out_shape=ja...  15.4 us
    ppermute x3, waiting for transfers between devices, extended(): lax.ppermute(head, axis, [((i + 1) % count, i) for i in range(count)])  10 us
    reshape x1, local copies, waits for them, and re-layouts, on_device(): patches = patches.reshape(cells_x * cells_y, chan_in * 27, cells_z)  7.54 us
    unnamed x37, local copies, waits for them, and re-layouts  7.44 us
    ppermute x2, waiting for transfers between devices, fold_halo(): lax.ppermute(head, axis, [((i + 1) % count, i) for i in range(count)])  7.14 us
    ppermute x3, starting transfers between devices, extended(): lax.ppermute(tail, axis, [(i, (i + 1) % count) for i in range(count)])  6.32 us
    ppermute x2, starting transfers between devices, fold_halo(): lax.ppermute(tail, axis, [(i, (i + 1) % count) for i in range(count)])  5.7 us
  transfers between devices with their start and end apart: 12, of which 9 were waited for; matrix products, arithmetic and copies ran while one was open for 16% of the time, Pallas kernels for 13%

profile of v12, /device:TPU:7, one launch (start us, length us, event | category | flops | bytes accessed | tf_op | source)
XLA Modules:
  0.0 119.7 jit_solution(17107152618450265248)
XLA Ops:
  1.6 4.1 %collective-permute-start = (bf16[4,1,64,128]{3,2,1,0:T(8,128)(2,1)S(1)}, bf16[4,1,64,128]{3,2,1,0:T(8,128)(2,1)S(1)}, u32[]{:S(2)}, u32[]{:S(2)}) collective-permute-start(bf16[4,1,64,128]{3,2,1,0:T(8,128)(2,1)S(1)} %get-tuple-element.41), channel_id=1, source_target_pairs={{0,8},{8,16},{16,24},{24,32},{32,40},{40,48},{48,56},{56,64},{64,7... | collective-permute-start | bytes 196616 | tf_op jit(solution)/shard_map/ppermute | solution.py:22
  5.9 1.1 collective-permute-done
  8.0 5.0 %collective-permute-done.1 = bf16[4,1,64,128]{3,2,1,0:T(8,128)(2,1)S(1)} collective-permute-done((bf16[4,1,64,128]{3,2,1,0:T(8,128)(2,1)S(1)}, bf16[4,1,64,128]{3,2,1,0:T(8,128)(2,1)S(1)}, u32[]{:S(2)}, u32[]{:S(2)}) %collective-permute-start.1) | collective-permute-done | bytes 65568 | tf_op jit(solution)/shard_map/ppermute | solution.py:24
  13.1 1.4 %collective-permute-start.2 = (bf16[4,6,1,128]{3,2,1,0:T(2,128)(2,1)S(1)}, bf16[4,6,1,128]{3,2,1,0:T(2,128)(2,1)S(1)}, u32[]{:S(2)}, u32[]{:S(2)}) collective-permute-start(bf16[4,6,1,128]{3,2,1,0:T(2,128)(2,1)S(1)} %get-tuple-element.38), channel_id=1, source_target_pairs={{0,2},{2,4},{4,6},{6,0},{1,3},{3,5},{5,7},{7,1},{8,10},{10,12},{12... | collective-permute-start | bytes 18440 | tf_op jit(solution)/shard_map/ppermute | solution.py:22
  14.4 1.5 %collective-permute-start.3 = (bf16[4,6,1,128]{3,2,1,0:T(2,128)(2,1)S(1)}, bf16[4,6,1,128]{3,2,1,0:T(2,128)(2,1)S(1)}, u32[]{:S(2)}, u32[]{:S(2)}) collective-permute-start(bf16[4,6,1,128]{3,2,1,0:T(2,128)(2,1)S(1)} %get-tuple-element.39), channel_id=1, source_target_pairs={{2,0},{4,2},{6,4},{0,6},{3,1},{5,3},{7,5},{1,7},{10,8},{12,10},{14... | collective-permute-start | bytes 18440 | tf_op jit(solution)/shard_map/ppermute | solution.py:24
  19.8 2.2 %reshape.237.refs_6_ = bf16[32,4096]{1,0:T(8,128)(2,1)} reshape(bf16[32,2,32,64]{3,2,1,0:T(8,128)(2,1)} %param.7) | data formatting | bytes 524288 | tf_op jit(solution)/shard_map/reshape | solution.py:328
  23.5 1.3 %copy.76.refs_1_ = f32[32,1]{1,0:T(8,128)} copy(f32[32,1]{0,1:T(1,128)} %bitcast.228) | data formatting | bytes 256 | tf_op jit(solution)/shard_map/reshape | solution.py:331
  24.9 1.4 %pad.4 = bf16[3,3,3,8,32]{4,3,2,1,0:T(8,128)(2,1)} pad(bf16[3,3,3,4,32]{4,3,2,1,0:T(4,128)(2,1)} %bitcast.227, bf16[]{:T(256)} %constant.43.clone.1), padding=0_0x0_0x0_0x0_4x0_0 | pad | bytes 20738 | tf_op jit(solution)/shard_map/jit(_pad)/pad | solution.py:241
  26.3 3.7 %collective-permute-done.4 = bf16[4,6,66,1]{3,2,1,0:T(8,128)(2,1)S(1)} collective-permute-done((bf16[4,6,66,1]{3,2,1,0:T(8,128)(2,1)S(1)}, bf16[4,6,66,1]{3,2,1,0:T(8,128)(2,1)S(1)}, u32[]{:S(2)}, u32[]{:S(2)}) %collective-permute-start.4) | collective-permute-done | bytes 3200 | tf_op jit(solution)/shard_map/ppermute | solution.py:22
  30.0 4.7 %collective-permute-done.5 = bf16[4,6,66,1]{3,2,1,0:T(8,128)(2,1)S(1)} collective-permute-done((bf16[4,6,66,1]{3,2,1,0:T(8,128)(2,1)S(1)}, bf16[4,6,66,1]{3,2,1,0:T(8,128)(2,1)S(1)}, u32[]{:S(2)}, u32[]{:S(2)}) %collective-permute-start.5) | collective-permute-done | bytes 3200 | tf_op jit(solution)/shard_map/ppermute | solution.py:24
  34.7 1.1 pad_maximum_fusion
  39.7 7.5 %copy.77.refs_5_ = bf16[256,108,128]{2,1,0:T(8,128)(2,1)} copy(bf16[256,108,128]{2,0,1:T(8,128)(2,1)S(1)} %bitcast.220) | data formatting | bytes 14155776 | tf_op jit(solution)/shard_map/reshape | solution.py:327
  47.3 24.2 %shard_map.75 = (bf16[32,4096]{1,0:T(8,128)(2,1)}, f32[32,108]{1,0:T(8,128)}, f32[32,1]{1,0:T(8,128)}, f32[396,4,128]{2,1,0:T(4,128)}, f32[396,4,128]{2,1,0:T(4,128)}) custom-call(bf16[32,108]{1,0:T(8,128)(2,1)} %copy.75.refs_0_, f32[32,1]{1,0:T(8,128)} %copy.76.refs_1_, f32[2,128,128]{2,1,0:T(8,128)} %add_convert_fusion.refs_2_, ...), custom_call_target="tpu_custom_call" | custom-call | tf_op jit(solution)/shard_map/pallas_call | solution.py:255
  71.5 1.9 %fusion.40 = (f32[6,66,4,1]{3,2,1,0:T(4,128)S(1)}, f32[6,66,4,1]{3,2,1,0:T(4,128)S(1)}) fusion(f32[6,66,4,128]{3,2,1,0:T(4,128)} %bitcast.223), kind=kLoop, calls=%fused_computation.97 | loop fusion | bytes 25344 | tf_op jit(solution)/shard_map/slice | solution.py:347
  73.8 1.9 %collective-permute-start.6 = (f32[6,66,4,1]{1,2,3,0:T(4,128)S(1)}, f32[6,66,4,1]{1,2,3,0:T(4,128)S(1)}, u32[]{:S(2)}, u32[]{:S(2)}) collective-permute-start(f32[6,66,4,1]{1,2,3,0:T(4,128)S(1)} %copy.88), channel_id=1, source_target_pairs={{0,1},{1,0},{2,3},{3,2},{4,5},{5,4},{6,7},{7,6},{8,9},{9,8},{10,11... | collective-permute-start | bytes 19016 | tf_op jit(solution)/shard_map/ppermute | solution.py:349
  76.1 1.9 %fusion.41 = (f32[6,66,4,1]{3,2,1,0:T(4,128)S(1)}, f32[6,66,4,1]{3,2,1,0:T(4,128)S(1)}) fusion(f32[6,66,4,128]{3,2,1,0:T(4,128)} %bitcast.221), kind=kLoop, calls=%fused_computation.98 | loop fusion | bytes 25344 | tf_op jit(solution)/shard_map/slice | solution.py:353
  80.4 1.4 %collective-permute-start.8 = (f32[6,1,4,128]{3,1,0,2:T(1,128)S(1)}, f32[6,1,4,128]{3,1,0,2:T(1,128)S(1)}, u32[]{:S(2)}, u32[]{:S(2)}) collective-permute-start(f32[6,1,4,128]{3,1,0,2:T(1,128)S(1)} %get-tuple-element.27), channel_id=1, source_target_pairs={{0,2},{2,4},{4,6},{6,0},{1,3},{3,5},{5,7},{7,1},{8,10},{10,12},{12... | collective-permute-start | bytes 36872 | tf_op jit(solution)/shard_map/ppermute | solution.py:293
  82.4 1.5 %collective-permute-start.9 = (f32[6,1,4,128]{3,1,0,2:T(1,128)S(1)}, f32[6,1,4,128]{3,1,0,2:T(1,128)S(1)}, u32[]{:S(2)}, u32[]{:S(2)}) collective-permute-start(f32[6,1,4,128]{3,1,0,2:T(1,128)S(1)} %get-tuple-element.26), channel_id=1, source_target_pairs={{2,0},{4,2},{6,4},{0,6},{3,1},{5,3},{7,5},{1,7},{10,8},{12,10},{14... | collective-permute-start | bytes 36872 | tf_op jit(solution)/shard_map/ppermute | solution.py:294
  85.2 4.3 %collective-permute-start.10 = (f32[1,64,4,128]{3,1,0,2:T(8,128)S(1)}, f32[1,64,4,128]{3,1,0,2:T(8,128)S(1)}, u32[]{:S(2)}, u32[]{:S(2)}) collective-permute-start(f32[1,64,4,128]{3,1,0,2:T(8,128)S(1)} %get-tuple-element.33), channel_id=1, source_target_pairs={{0,8},{8,16},{16,24},{24,32},{32,40},{40,48},{48,56},{56,64},{64,7... | collective-permute-start | bytes 393224 | tf_op jit(solution)/shard_map/ppermute | solution.py:293
  90.2 15.4 %shard_map.76 = f32[32,128]{1,0:T(8,128)} custom-call(f32[32,128]{1,0:T(8,128)} %maximum_maximum_fusion.1.refs_0_), custom_call_target="tpu_custom_call" | custom-call | tf_op jit(solution)/shard_map/pallas_call | solution.py:113
  107.0 2.3 %reshape.238 = bf16[32,2,32,64]{3,2,1,0:T(8,128)(2,1)} reshape(bf16[32,4096]{1,0:T(8,128)(2,1)} %get-tuple-element.9) | data formatting | bytes 524288 | tf_op jit(solution)/shard_map/reshape | solution.py:333
  109.3 1.4 %slice_reduce_fusion = f32[32]{0:T(128)} fusion(f32[32,128]{1,0:T(8,128)} %shard_map.76), kind=kLoop, calls=%fused_computation.87 | loop fusion | bytes 256 | tf_op jit(solution)/shard_map/slice | solution.py:343
  110.8 1.5 %collective-permute-start.11 = (f32[1,64,4,128]{3,1,0,2:T(8,128)S(1)}, f32[1,64,4,128]{3,1,0,2:T(8,128)S(1)}, u32[]{:S(2)}, u32[]{:S(2)}) collective-permute-start(f32[1,64,4,128]{3,1,0,2:T(8,128)S(1)} %get-tuple-element.32), channel_id=1, source_target_pairs={{8,0},{16,8},{24,16},{32,24},{40,32},{48,40},{56,48},{64,56},{72,6... | collective-permute-start | bytes 393224 | tf_op jit(solution)/shard_map/ppermute | solution.py:294
  112.3 6.6 %collective-permute-done.11 = f32[1,64,4,128]{3,1,0,2:T(8,128)S(1)} collective-permute-done((f32[1,64,4,128]{3,1,0,2:T(8,128)S(1)}, f32[1,64,4,128]{3,1,0,2:T(8,128)S(1)}, u32[]{:S(2)}, u32[]{:S(2)}) %collective-permute-start.11) | collective-permute-done | bytes 131104 | tf_op jit(solution)/shard_map/ppermute | solution.py:294
  (90 shorter events, 19.4 us)
Async XLA Ops:
  0.6 35.6 %copy-start.1 = (bf16[4,4,64,128]{3,2,1,0:T(8,128)(2,1)S(1)}, bf16[4,4,64,128]{3,2,1,0:T(8,128)(2,1)}, u32[]{:S(2)}) copy-start(bf16[4,4,64,128]{3,2,1,0:T(8,128)(2,1)} %param.4) | copy-start | bytes 786436
  1.6 5.5 %collective-permute-start = (bf16[4,1,64,128]{3,2,1,0:T(8,128)(2,1)S(1)}, bf16[4,1,64,128]{3,2,1,0:T(8,128)(2,1)S(1)}, u32[]{:S(2)}, u32[]{:S(2)}) collective-permute-start(bf16[4,1,64,128]{3,2,1,0:T(8,128)(2,1)S(1)} %get-tuple-element.41), channel_id=1, source_target_pairs={{0,8},{8,16},{16,24},{24,32},{32,40},{40,48},{48,56},{56,64},{64,7... | collective-permute-start | bytes 196616 | tf_op jit(solution)/shard_map/ppermute | solution.py:22
  5.7 7.3 %collective-permute-start.1 = (bf16[4,1,64,128]{3,2,1,0:T(8,128)(2,1)S(1)}, bf16[4,1,64,128]{3,2,1,0:T(8,128)(2,1)S(1)}, u32[]{:S(2)}, u32[]{:S(2)}) collective-permute-start(bf16[4,1,64,128]{3,2,1,0:T(8,128)(2,1)S(1)} %get-tuple-element.40), channel_id=1, source_target_pairs={{8,0},{16,8},{24,16},{32,24},{40,32},{48,40},{56,48},{64,56},{72,6... | collective-permute-start | bytes 196616 | tf_op jit(solution)/shard_map/ppermute | solution.py:24
  13.1 3.9 %collective-permute-start.2 = (bf16[4,6,1,128]{3,2,1,0:T(2,128)(2,1)S(1)}, bf16[4,6,1,128]{3,2,1,0:T(2,128)(2,1)S(1)}, u32[]{:S(2)}, u32[]{:S(2)}) collective-permute-start(bf16[4,6,1,128]{3,2,1,0:T(2,128)(2,1)S(1)} %get-tuple-element.38), channel_id=1, source_target_pairs={{0,2},{2,4},{4,6},{6,0},{1,3},{3,5},{5,7},{7,1},{8,10},{10,12},{12... | collective-permute-start | bytes 18440 | tf_op jit(solution)/shard_map/ppermute | solution.py:22
  14.4 2.8 %collective-permute-start.3 = (bf16[4,6,1,128]{3,2,1,0:T(2,128)(2,1)S(1)}, bf16[4,6,1,128]{3,2,1,0:T(2,128)(2,1)S(1)}, u32[]{:S(2)}, u32[]{:S(2)}) collective-permute-start(bf16[4,6,1,128]{3,2,1,0:T(2,128)(2,1)S(1)} %get-tuple-element.39), channel_id=1, source_target_pairs={{2,0},{4,2},{6,4},{0,6},{3,1},{5,3},{7,5},{1,7},{10,8},{12,10},{14... | collective-permute-start | bytes 18440 | tf_op jit(solution)/shard_map/ppermute | solution.py:24
  17.6 12.3 %collective-permute-start.4 = (bf16[4,6,66,1]{3,2,1,0:T(8,128)(2,1)S(1)}, bf16[4,6,66,1]{3,2,1,0:T(8,128)(2,1)S(1)}, u32[]{:S(2)}, u32[]{:S(2)}) collective-permute-start(bf16[4,6,66,1]{3,2,1,0:T(8,128)(2,1)S(1)} %get-tuple-element.35), channel_id=1, source_target_pairs={{0,1},{1,0},{2,3},{3,2},{4,5},{5,4},{6,7},{7,6},{8,9},{9,8},{10,11... | collective-permute-start | bytes 9512 | tf_op jit(solution)/shard_map/ppermute | solution.py:22
  18.5 16.2 %collective-permute-start.5 = (bf16[4,6,66,1]{3,2,1,0:T(8,128)(2,1)S(1)}, bf16[4,6,66,1]{3,2,1,0:T(8,128)(2,1)S(1)}, u32[]{:S(2)}, u32[]{:S(2)}) collective-permute-start(bf16[4,6,66,1]{3,2,1,0:T(8,128)(2,1)S(1)} %get-tuple-element.34), channel_id=1, source_target_pairs={{1,0},{0,1},{3,2},{2,3},{5,4},{4,5},{7,6},{6,7},{9,8},{8,9},{11,10... | collective-permute-start | bytes 9512 | tf_op jit(solution)/shard_map/ppermute | solution.py:24
  71.5 6.6 %copy-start = (f32[396,4,128]{2,1,0:T(4,128)S(1)}, f32[396,4,128]{2,1,0:T(4,128)}, u32[]{:S(2)}) copy-start(f32[396,4,128]{2,1,0:T(4,128)} %get-tuple-element.12) | copy-start | bytes 2433028
  73.8 5.6 %collective-permute-start.6 = (f32[6,66,4,1]{1,2,3,0:T(4,128)S(1)}, f32[6,66,4,1]{1,2,3,0:T(4,128)S(1)}, u32[]{:S(2)}, u32[]{:S(2)}) collective-permute-start(f32[6,66,4,1]{1,2,3,0:T(4,128)S(1)} %copy.88), channel_id=1, source_target_pairs={{0,1},{1,0},{2,3},{3,2},{4,5},{5,4},{6,7},{7,6},{8,9},{9,8},{10,11... | collective-permute-start | bytes 19016 | tf_op jit(solution)/shard_map/ppermute | solution.py:349
  76.1 3.8 %collective-permute-start.7 = (f32[6,66,4,1]{1,2,3,0:T(4,128)S(1)}, f32[6,66,4,1]{1,2,3,0:T(4,128)S(1)}, u32[]{:S(2)}, u32[]{:S(2)}) collective-permute-start(f32[6,66,4,1]{1,2,3,0:T(4,128)S(1)} %copy.91), channel_id=1, source_target_pairs={{1,0},{0,1},{3,2},{2,3},{5,4},{4,5},{7,6},{6,7},{9,8},{8,9},{11,10... | collective-permute-start | bytes 19016 | tf_op jit(solution)/shard_map/ppermute | solution.py:350
  79.3 10.2 %copy-start.3 = (f32[32,108]{1,0:T(8,128)S(1)}, f32[32,108]{1,0:T(8,128)}, u32[]{:S(2)}) copy-start(f32[32,108]{1,0:T(8,128)} %get-tuple-element.10) | copy-start | bytes 41476
  79.3 10.2 %copy-start.4 = (f32[32,1]{1,0:T(8,128)S(1)}, f32[32,1]{1,0:T(8,128)}, u32[]{:S(2)}) copy-start(f32[32,1]{1,0:T(8,128)} %get-tuple-element.11) | copy-start | bytes 388
  80.4 3.8 %collective-permute-start.8 = (f32[6,1,4,128]{3,1,0,2:T(1,128)S(1)}, f32[6,1,4,128]{3,1,0,2:T(1,128)S(1)}, u32[]{:S(2)}, u32[]{:S(2)}) collective-permute-start(f32[6,1,4,128]{3,1,0,2:T(1,128)S(1)} %get-tuple-element.27), channel_id=1, source_target_pairs={{0,2},{2,4},{4,6},{6,0},{1,3},{3,5},{5,7},{7,1},{8,10},{10,12},{12... | collective-permute-start | bytes 36872 | tf_op jit(solution)/shard_map/ppermute | solution.py:293
  82.4 2.6 %collective-permute-start.9 = (f32[6,1,4,128]{3,1,0,2:T(1,128)S(1)}, f32[6,1,4,128]{3,1,0,2:T(1,128)S(1)}, u32[]{:S(2)}, u32[]{:S(2)}) collective-permute-start(f32[6,1,4,128]{3,1,0,2:T(1,128)S(1)} %get-tuple-element.26), channel_id=1, source_target_pairs={{2,0},{4,2},{6,4},{0,6},{3,1},{5,3},{7,5},{1,7},{10,8},{12,10},{14... | collective-permute-start | bytes 36872 | tf_op jit(solution)/shard_map/ppermute | solution.py:294
  85.2 27.1 %collective-permute-start.10 = (f32[1,64,4,128]{3,1,0,2:T(8,128)S(1)}, f32[1,64,4,128]{3,1,0,2:T(8,128)S(1)}, u32[]{:S(2)}, u32[]{:S(2)}) collective-permute-start(f32[1,64,4,128]{3,1,0,2:T(8,128)S(1)} %get-tuple-element.33), channel_id=1, source_target_pairs={{0,8},{8,16},{16,24},{24,32},{32,40},{40,48},{48,56},{56,64},{64,7... | collective-permute-start | bytes 393224 | tf_op jit(solution)/shard_map/ppermute | solution.py:293
  110.8 8.1 %collective-permute-start.11 = (f32[1,64,4,128]{3,1,0,2:T(8,128)S(1)}, f32[1,64,4,128]{3,1,0,2:T(8,128)S(1)}, u32[]{:S(2)}, u32[]{:S(2)}) collective-permute-start(f32[1,64,4,128]{3,1,0,2:T(8,128)S(1)} %get-tuple-element.32), channel_id=1, source_target_pairs={{8,0},{16,8},{24,16},{32,24},{40,32},{48,40},{56,48},{64,56},{72,6... | collective-permute-start | bytes 393224 | tf_op jit(solution)/shard_map/ppermute | solution.py:294
  118.9 0.8 copy-start.2

commit v13 on v12

--- a/solution.py
+++ b/solution.py
@@ -149,7 +149,7 @@
     first = lane == 0
     last = lane == rows - 1
 
-    group = 8
+    group = 16
     pooled_rows = group // 2
     pieces = pooled_rows // 2
 

time: 120 us -> 117 us (0.975)
  Pallas kernels: 39.6 us -> 36.1 us
    pallas_call x1, Pallas kernels: 24.2 us -> 20.7 us  [forward(): pl.pallas_call(lambda *refs: forward_kernel(rows, wide_y, *refs), grid=(p...]
  transfers between devices with their start and end apart: 12 -> 12, of which waited for: 9 -> 9; matrix products, arithmetic and copies ran while one was open for 16% -> 17% of each run, Pallas kernels for 13% -> 13%
where the time goes in v13:
time: 117 us; the launch traced here: 116 us
  Pallas kernels  36.1 us (31%)
  local copies, waits for them, and re-layouts  32.1 us (27%)
  waiting for transfers between devices  22.7 us (19%)
  starting transfers between devices  19 us (16%)
  other arithmetic  5.08 us (4%)
    pallas_call x1, Pallas kernels, forward(): pl.pallas_call(lambda *refs: forward_kernel(rows, wide_y, *refs), grid=(p...  20.7 us
    pallas_call x1, Pallas kernels, allreduce(): pl.pallas_call(lambda *refs: allreduce_kernel(sizes, *refs), out_shape=ja...  15.3 us
    ppermute x3, waiting for transfers between devices, extended(): lax.ppermute(head, axis, [((i + 1) % count, i) for i in range(count)])  10 us
    reshape x1, local copies, waits for them, and re-layouts, on_device(): patches = patches.reshape(cells_x * cells_y, chan_in * 27, cells_z)  7.54 us
    unnamed x37, local copies, waits for them, and re-layouts  7.44 us
    ppermute x2, waiting for transfers between devices, fold_halo(): lax.ppermute(head, axis, [((i + 1) % count, i) for i in range(count)])  7.13 us
    ppermute x3, starting transfers between devices, extended(): lax.ppermute(tail, axis, [(i, (i + 1) % count) for i in range(count)])  6.32 us
    ppermute x2, starting transfers between devices, fold_halo(): lax.ppermute(tail, axis, [(i, (i + 1) % count) for i in range(count)])  5.69 us
  transfers between devices with their start and end apart: 12, of which 9 were waited for; matrix products, arithmetic and copies ran while one was open for 17% of the time, Pallas kernels for 13%

profile of v13, /device:TPU:7, one launch (start us, length us, event | category | flops | bytes accessed | tf_op | source)
XLA Modules:
  0.0 116.0 jit_solution(3945794534728804922)
XLA Ops:
  1.6 4.1 %collective-permute-start = (bf16[4,1,64,128]{3,2,1,0:T(8,128)(2,1)S(1)}, bf16[4,1,64,128]{3,2,1,0:T(8,128)(2,1)S(1)}, u32[]{:S(2)}, u32[]{:S(2)}) collective-permute-start(bf16[4,1,64,128]{3,2,1,0:T(8,128)(2,1)S(1)} %get-tuple-element.41), channel_id=1, source_target_pairs={{0,8},{8,16},{16,24},{24,32},{32,40},{40,48},{48,56},{56,64},{64,7... | collective-permute-start | bytes 196616 | tf_op jit(solution)/shard_map/ppermute | solution.py:22
  5.9 1.1 collective-permute-done
  8.0 5.0 %collective-permute-done.1 = bf16[4,1,64,128]{3,2,1,0:T(8,128)(2,1)S(1)} collective-permute-done((bf16[4,1,64,128]{3,2,1,0:T(8,128)(2,1)S(1)}, bf16[4,1,64,128]{3,2,1,0:T(8,128)(2,1)S(1)}, u32[]{:S(2)}, u32[]{:S(2)}) %collective-permute-start.1) | collective-permute-done | bytes 65568 | tf_op jit(solution)/shard_map/ppermute | solution.py:24
  13.1 1.4 %collective-permute-start.2 = (bf16[4,6,1,128]{3,2,1,0:T(2,128)(2,1)S(1)}, bf16[4,6,1,128]{3,2,1,0:T(2,128)(2,1)S(1)}, u32[]{:S(2)}, u32[]{:S(2)}) collective-permute-start(bf16[4,6,1,128]{3,2,1,0:T(2,128)(2,1)S(1)} %get-tuple-element.38), channel_id=1, source_target_pairs={{0,2},{2,4},{4,6},{6,0},{1,3},{3,5},{5,7},{7,1},{8,10},{10,12},{12... | collective-permute-start | bytes 18440 | tf_op jit(solution)/shard_map/ppermute | solution.py:22
  14.4 1.5 %collective-permute-start.3 = (bf16[4,6,1,128]{3,2,1,0:T(2,128)(2,1)S(1)}, bf16[4,6,1,128]{3,2,1,0:T(2,128)(2,1)S(1)}, u32[]{:S(2)}, u32[]{:S(2)}) collective-permute-start(bf16[4,6,1,128]{3,2,1,0:T(2,128)(2,1)S(1)} %get-tuple-element.39), channel_id=1, source_target_pairs={{2,0},{4,2},{6,4},{0,6},{3,1},{5,3},{7,5},{1,7},{10,8},{12,10},{14... | collective-permute-start | bytes 18440 | tf_op jit(solution)/shard_map/ppermute | solution.py:24
  19.8 2.2 %reshape.237.refs_6_ = bf16[32,4096]{1,0:T(8,128)(2,1)} reshape(bf16[32,2,32,64]{3,2,1,0:T(8,128)(2,1)} %param.7) | data formatting | bytes 524288 | tf_op jit(solution)/shard_map/reshape | solution.py:328
  23.5 1.3 %copy.76.refs_1_ = f32[32,1]{1,0:T(8,128)} copy(f32[32,1]{0,1:T(1,128)} %bitcast.228) | data formatting | bytes 256 | tf_op jit(solution)/shard_map/reshape | solution.py:331
  24.9 1.4 %pad.4 = bf16[3,3,3,8,32]{4,3,2,1,0:T(8,128)(2,1)} pad(bf16[3,3,3,4,32]{4,3,2,1,0:T(4,128)(2,1)} %bitcast.227, bf16[]{:T(256)} %constant.43.clone.1), padding=0_0x0_0x0_0x0_4x0_0 | pad | bytes 20738 | tf_op jit(solution)/shard_map/jit(_pad)/pad | solution.py:241
  26.3 3.7 %collective-permute-done.4 = bf16[4,6,66,1]{3,2,1,0:T(8,128)(2,1)S(1)} collective-permute-done((bf16[4,6,66,1]{3,2,1,0:T(8,128)(2,1)S(1)}, bf16[4,6,66,1]{3,2,1,0:T(8,128)(2,1)S(1)}, u32[]{:S(2)}, u32[]{:S(2)}) %collective-permute-start.4) | collective-permute-done | bytes 3200 | tf_op jit(solution)/shard_map/ppermute | solution.py:22
  30.0 4.7 %collective-permute-done.5 = bf16[4,6,66,1]{3,2,1,0:T(8,128)(2,1)S(1)} collective-permute-done((bf16[4,6,66,1]{3,2,1,0:T(8,128)(2,1)S(1)}, bf16[4,6,66,1]{3,2,1,0:T(8,128)(2,1)S(1)}, u32[]{:S(2)}, u32[]{:S(2)}) %collective-permute-start.5) | collective-permute-done | bytes 3200 | tf_op jit(solution)/shard_map/ppermute | solution.py:24
  34.7 1.1 pad_maximum_fusion
  39.7 7.5 %copy.77.refs_5_ = bf16[256,108,128]{2,1,0:T(8,128)(2,1)} copy(bf16[256,108,128]{2,0,1:T(8,128)(2,1)S(1)} %bitcast.220) | data formatting | bytes 14155776 | tf_op jit(solution)/shard_map/reshape | solution.py:327
  47.3 20.7 %shard_map.75 = (bf16[32,4096]{1,0:T(8,128)(2,1)}, f32[32,108]{1,0:T(8,128)}, f32[32,1]{1,0:T(8,128)}, f32[396,4,128]{2,1,0:T(4,128)}, f32[396,4,128]{2,1,0:T(4,128)}) custom-call(bf16[32,108]{1,0:T(8,128)(2,1)} %copy.75.refs_0_, f32[32,1]{1,0:T(8,128)} %copy.76.refs_1_, f32[2,128,128]{2,1,0:T(8,128)} %add_convert_fusion.refs_2_, ...), custom_call_target="tpu_custom_call" | custom-call | tf_op jit(solution)/shard_map/pallas_call | solution.py:255
  68.0 1.9 %fusion.40 = (f32[6,66,4,1]{3,2,1,0:T(4,128)S(1)}, f32[6,66,4,1]{3,2,1,0:T(4,128)S(1)}) fusion(f32[6,66,4,128]{3,2,1,0:T(4,128)} %bitcast.223), kind=kLoop, calls=%fused_computation.97 | loop fusion | bytes 25344 | tf_op jit(solution)/shard_map/slice | solution.py:347
  70.3 1.7 %collective-permute-start.6 = (f32[6,66,4,1]{1,2,3,0:T(4,128)S(1)}, f32[6,66,4,1]{1,2,3,0:T(4,128)S(1)}, u32[]{:S(2)}, u32[]{:S(2)}) collective-permute-start(f32[6,66,4,1]{1,2,3,0:T(4,128)S(1)} %copy.88), channel_id=1, source_target_pairs={{0,1},{1,0},{2,3},{3,2},{4,5},{5,4},{6,7},{7,6},{8,9},{9,8},{10,11... | collective-permute-start | bytes 19016 | tf_op jit(solution)/shard_map/ppermute | solution.py:349
  72.4 1.9 %fusion.41 = (f32[6,66,4,1]{3,2,1,0:T(4,128)S(1)}, f32[6,66,4,1]{3,2,1,0:T(4,128)S(1)}) fusion(f32[6,66,4,128]{3,2,1,0:T(4,128)} %bitcast.221), kind=kLoop, calls=%fused_computation.98 | loop fusion | bytes 25344 | tf_op jit(solution)/shard_map/slice | solution.py:353
  76.7 1.3 %collective-permute-start.8 = (f32[6,1,4,128]{3,1,0,2:T(1,128)S(1)}, f32[6,1,4,128]{3,1,0,2:T(1,128)S(1)}, u32[]{:S(2)}, u32[]{:S(2)}) collective-permute-start(f32[6,1,4,128]{3,1,0,2:T(1,128)S(1)} %get-tuple-element.27), channel_id=1, source_target_pairs={{0,2},{2,4},{4,6},{6,0},{1,3},{3,5},{5,7},{7,1},{8,10},{10,12},{12... | collective-permute-start | bytes 36872 | tf_op jit(solution)/shard_map/ppermute | solution.py:293
  78.7 1.5 %collective-permute-start.9 = (f32[6,1,4,128]{3,1,0,2:T(1,128)S(1)}, f32[6,1,4,128]{3,1,0,2:T(1,128)S(1)}, u32[]{:S(2)}, u32[]{:S(2)}) collective-permute-start(f32[6,1,4,128]{3,1,0,2:T(1,128)S(1)} %get-tuple-element.26), channel_id=1, source_target_pairs={{2,0},{4,2},{6,4},{0,6},{3,1},{5,3},{7,5},{1,7},{10,8},{12,10},{14... | collective-permute-start | bytes 36872 | tf_op jit(solution)/shard_map/ppermute | solution.py:294
  81.4 4.3 %collective-permute-start.10 = (f32[1,64,4,128]{3,1,0,2:T(8,128)S(1)}, f32[1,64,4,128]{3,1,0,2:T(8,128)S(1)}, u32[]{:S(2)}, u32[]{:S(2)}) collective-permute-start(f32[1,64,4,128]{3,1,0,2:T(8,128)S(1)} %get-tuple-element.33), channel_id=1, source_target_pairs={{0,8},{8,16},{16,24},{24,32},{32,40},{40,48},{48,56},{56,64},{64,7... | collective-permute-start | bytes 393224 | tf_op jit(solution)/shard_map/ppermute | solution.py:293
  86.5 15.3 %shard_map.76 = f32[32,128]{1,0:T(8,128)} custom-call(f32[32,128]{1,0:T(8,128)} %maximum_maximum_fusion.1.refs_0_), custom_call_target="tpu_custom_call" | custom-call | tf_op jit(solution)/shard_map/pallas_call | solution.py:113
  103.3 2.3 %reshape.238 = bf16[32,2,32,64]{3,2,1,0:T(8,128)(2,1)} reshape(bf16[32,4096]{1,0:T(8,128)(2,1)} %get-tuple-element.9) | data formatting | bytes 524288 | tf_op jit(solution)/shard_map/reshape | solution.py:333
  105.6 1.4 %slice_reduce_fusion = f32[32]{0:T(128)} fusion(f32[32,128]{1,0:T(8,128)} %shard_map.76), kind=kLoop, calls=%fused_computation.87 | loop fusion | bytes 256 | tf_op jit(solution)/shard_map/slice | solution.py:343
  107.0 1.5 %collective-permute-start.11 = (f32[1,64,4,128]{3,1,0,2:T(8,128)S(1)}, f32[1,64,4,128]{3,1,0,2:T(8,128)S(1)}, u32[]{:S(2)}, u32[]{:S(2)}) collective-permute-start(f32[1,64,4,128]{3,1,0,2:T(8,128)S(1)} %get-tuple-element.32), channel_id=1, source_target_pairs={{8,0},{16,8},{24,16},{32,24},{40,32},{48,40},{56,48},{64,56},{72,6... | collective-permute-start | bytes 393224 | tf_op jit(solution)/shard_map/ppermute | solution.py:294
  108.5 6.6 %collective-permute-done.11 = f32[1,64,4,128]{3,1,0,2:T(8,128)S(1)} collective-permute-done((f32[1,64,4,128]{3,1,0,2:T(8,128)S(1)}, f32[1,64,4,128]{3,1,0,2:T(8,128)S(1)}, u32[]{:S(2)}, u32[]{:S(2)}) %collective-permute-start.11) | collective-permute-done | bytes 131104 | tf_op jit(solution)/shard_map/ppermute | solution.py:294
  (90 shorter events, 19.4 us)
Async XLA Ops:
  0.6 35.6 %copy-start.1 = (bf16[4,4,64,128]{3,2,1,0:T(8,128)(2,1)S(1)}, bf16[4,4,64,128]{3,2,1,0:T(8,128)(2,1)}, u32[]{:S(2)}) copy-start(bf16[4,4,64,128]{3,2,1,0:T(8,128)(2,1)} %param.4) | copy-start | bytes 786436
  1.6 5.5 %collective-permute-start = (bf16[4,1,64,128]{3,2,1,0:T(8,128)(2,1)S(1)}, bf16[4,1,64,128]{3,2,1,0:T(8,128)(2,1)S(1)}, u32[]{:S(2)}, u32[]{:S(2)}) collective-permute-start(bf16[4,1,64,128]{3,2,1,0:T(8,128)(2,1)S(1)} %get-tuple-element.41), channel_id=1, source_target_pairs={{0,8},{8,16},{16,24},{24,32},{32,40},{40,48},{48,56},{56,64},{64,7... | collective-permute-start | bytes 196616 | tf_op jit(solution)/shard_map/ppermute | solution.py:22
  5.7 7.3 %collective-permute-start.1 = (bf16[4,1,64,128]{3,2,1,0:T(8,128)(2,1)S(1)}, bf16[4,1,64,128]{3,2,1,0:T(8,128)(2,1)S(1)}, u32[]{:S(2)}, u32[]{:S(2)}) collective-permute-start(bf16[4,1,64,128]{3,2,1,0:T(8,128)(2,1)S(1)} %get-tuple-element.40), channel_id=1, source_target_pairs={{8,0},{16,8},{24,16},{32,24},{40,32},{48,40},{56,48},{64,56},{72,6... | collective-permute-start | bytes 196616 | tf_op jit(solution)/shard_map/ppermute | solution.py:24
  13.1 3.9 %collective-permute-start.2 = (bf16[4,6,1,128]{3,2,1,0:T(2,128)(2,1)S(1)}, bf16[4,6,1,128]{3,2,1,0:T(2,128)(2,1)S(1)}, u32[]{:S(2)}, u32[]{:S(2)}) collective-permute-start(bf16[4,6,1,128]{3,2,1,0:T(2,128)(2,1)S(1)} %get-tuple-element.38), channel_id=1, source_target_pairs={{0,2},{2,4},{4,6},{6,0},{1,3},{3,5},{5,7},{7,1},{8,10},{10,12},{12... | collective-permute-start | bytes 18440 | tf_op jit(solution)/shard_map/ppermute | solution.py:22
  14.4 2.8 %collective-permute-start.3 = (bf16[4,6,1,128]{3,2,1,0:T(2,128)(2,1)S(1)}, bf16[4,6,1,128]{3,2,1,0:T(2,128)(2,1)S(1)}, u32[]{:S(2)}, u32[]{:S(2)}) collective-permute-start(bf16[4,6,1,128]{3,2,1,0:T(2,128)(2,1)S(1)} %get-tuple-element.39), channel_id=1, source_target_pairs={{2,0},{4,2},{6,4},{0,6},{3,1},{5,3},{7,5},{1,7},{10,8},{12,10},{14... | collective-permute-start | bytes 18440 | tf_op jit(solution)/shard_map/ppermute | solution.py:24
  17.6 12.3 %collective-permute-start.4 = (bf16[4,6,66,1]{3,2,1,0:T(8,128)(2,1)S(1)}, bf16[4,6,66,1]{3,2,1,0:T(8,128)(2,1)S(1)}, u32[]{:S(2)}, u32[]{:S(2)}) collective-permute-start(bf16[4,6,66,1]{3,2,1,0:T(8,128)(2,1)S(1)} %get-tuple-element.35), channel_id=1, source_target_pairs={{0,1},{1,0},{2,3},{3,2},{4,5},{5,4},{6,7},{7,6},{8,9},{9,8},{10,11... | collective-permute-start | bytes 9512 | tf_op jit(solution)/shard_map/ppermute | solution.py:22
  18.5 16.2 %collective-permute-start.5 = (bf16[4,6,66,1]{3,2,1,0:T(8,128)(2,1)S(1)}, bf16[4,6,66,1]{3,2,1,0:T(8,128)(2,1)S(1)}, u32[]{:S(2)}, u32[]{:S(2)}) collective-permute-start(bf16[4,6,66,1]{3,2,1,0:T(8,128)(2,1)S(1)} %get-tuple-element.34), channel_id=1, source_target_pairs={{1,0},{0,1},{3,2},{2,3},{5,4},{4,5},{7,6},{6,7},{9,8},{8,9},{11,10... | collective-permute-start | bytes 9512 | tf_op jit(solution)/shard_map/ppermute | solution.py:24
  68.0 6.3 %copy-start = (f32[396,4,128]{2,1,0:T(4,128)S(1)}, f32[396,4,128]{2,1,0:T(4,128)}, u32[]{:S(2)}) copy-start(f32[396,4,128]{2,1,0:T(4,128)} %get-tuple-element.12) | copy-start | bytes 2433028
  70.3 5.4 %collective-permute-start.6 = (f32[6,66,4,1]{1,2,3,0:T(4,128)S(1)}, f32[6,66,4,1]{1,2,3,0:T(4,128)S(1)}, u32[]{:S(2)}, u32[]{:S(2)}) collective-permute-start(f32[6,66,4,1]{1,2,3,0:T(4,128)S(1)} %copy.88), channel_id=1, source_target_pairs={{0,1},{1,0},{2,3},{3,2},{4,5},{5,4},{6,7},{7,6},{8,9},{9,8},{10,11... | collective-permute-start | bytes 19016 | tf_op jit(solution)/shard_map/ppermute | solution.py:349
  72.3 3.8 %collective-permute-start.7 = (f32[6,66,4,1]{1,2,3,0:T(4,128)S(1)}, f32[6,66,4,1]{1,2,3,0:T(4,128)S(1)}, u32[]{:S(2)}, u32[]{:S(2)}) collective-permute-start(f32[6,66,4,1]{1,2,3,0:T(4,128)S(1)} %copy.91), channel_id=1, source_target_pairs={{1,0},{0,1},{3,2},{2,3},{5,4},{4,5},{7,6},{6,7},{9,8},{8,9},{11,10... | collective-permute-start | bytes 19016 | tf_op jit(solution)/shard_map/ppermute | solution.py:350
  75.6 10.2 %copy-start.3 = (f32[32,108]{1,0:T(8,128)S(1)}, f32[32,108]{1,0:T(8,128)}, u32[]{:S(2)}) copy-start(f32[32,108]{1,0:T(8,128)} %get-tuple-element.10) | copy-start | bytes 41476
  75.6 10.2 %copy-start.4 = (f32[32,1]{1,0:T(8,128)S(1)}, f32[32,1]{1,0:T(8,128)}, u32[]{:S(2)}) copy-start(f32[32,1]{1,0:T(8,128)} %get-tuple-element.11) | copy-start | bytes 388
  76.7 3.8 %collective-permute-start.8 = (f32[6,1,4,128]{3,1,0,2:T(1,128)S(1)}, f32[6,1,4,128]{3,1,0,2:T(1,128)S(1)}, u32[]{:S(2)}, u32[]{:S(2)}) collective-permute-start(f32[6,1,4,128]{3,1,0,2:T(1,128)S(1)} %get-tuple-element.27), channel_id=1, source_target_pairs={{0,2},{2,4},{4,6},{6,0},{1,3},{3,5},{5,7},{7,1},{8,10},{10,12},{12... | collective-permute-start | bytes 36872 | tf_op jit(solution)/shard_map/ppermute | solution.py:293
  78.7 2.6 %collective-permute-start.9 = (f32[6,1,4,128]{3,1,0,2:T(1,128)S(1)}, f32[6,1,4,128]{3,1,0,2:T(1,128)S(1)}, u32[]{:S(2)}, u32[]{:S(2)}) collective-permute-start(f32[6,1,4,128]{3,1,0,2:T(1,128)S(1)} %get-tuple-element.26), channel_id=1, source_target_pairs={{2,0},{4,2},{6,4},{0,6},{3,1},{5,3},{7,5},{1,7},{10,8},{12,10},{14... | collective-permute-start | bytes 36872 | tf_op jit(solution)/shard_map/ppermute | solution.py:294
  81.4 27.1 %collective-permute-start.10 = (f32[1,64,4,128]{3,1,0,2:T(8,128)S(1)}, f32[1,64,4,128]{3,1,0,2:T(8,128)S(1)}, u32[]{:S(2)}, u32[]{:S(2)}) collective-permute-start(f32[1,64,4,128]{3,1,0,2:T(8,128)S(1)} %get-tuple-element.33), channel_id=1, source_target_pairs={{0,8},{8,16},{16,24},{24,32},{32,40},{40,48},{48,56},{56,64},{64,7... | collective-permute-start | bytes 393224 | tf_op jit(solution)/shard_map/ppermute | solution.py:293
  107.0 8.1 %collective-permute-start.11 = (f32[1,64,4,128]{3,1,0,2:T(8,128)S(1)}, f32[1,64,4,128]{3,1,0,2:T(8,128)S(1)}, u32[]{:S(2)}, u32[]{:S(2)}) collective-permute-start(f32[1,64,4,128]{3,1,0,2:T(8,128)S(1)} %get-tuple-element.32), channel_id=1, source_target_pairs={{8,0},{16,8},{24,16},{32,24},{40,32},{48,40},{56,48},{64,56},{72,6... | collective-permute-start | bytes 393224 | tf_op jit(solution)/shard_map/ppermute | solution.py:294
  115.2 0.8 copy-start.2

commit v14 on v13

--- a/solution.py
+++ b/solution.py
@@ -149,7 +149,7 @@
     first = lane == 0
     last = lane == rows - 1
 
-    group = 16
+    group = 32
     pooled_rows = group // 2
     pieces = pooled_rows // 2
 

time: 117 us -> 115 us (0.983)
  Pallas kernels: 36.1 us -> 34.5 us
    pallas_call x1, Pallas kernels: 20.7 us -> 19.2 us  [forward(): pl.pallas_call(lambda *refs: forward_kernel(rows, wide_y, *refs), grid=(p...]
where the time goes in v14:
time: 115 us; the launch traced here: 114 us
  Pallas kernels  34.5 us (30%)
  local copies, waits for them, and re-layouts  32.1 us (28%)
  waiting for transfers between devices  22.7 us (20%)
  starting transfers between devices  19 us (17%)
  other arithmetic  5.08 us (4%)
    pallas_call x1, Pallas kernels, forward(): pl.pallas_call(lambda *refs: forward_kernel(rows, wide_y, *refs), grid=(p...  19.2 us
    pallas_call x1, Pallas kernels, allreduce(): pl.pallas_call(lambda *refs: allreduce_kernel(sizes, *refs), out_shape=ja...  15.4 us
    ppermute x3, waiting for transfers between devices, extended(): lax.ppermute(head, axis, [((i + 1) % count, i) for i in range(count)])  10 us
    reshape x1, local copies, waits for them, and re-layouts, on_device(): patches = patches.reshape(cells_x * cells_y, chan_in * 27, cells_z)  7.54 us
    unnamed x37, local copies, waits for them, and re-layouts  7.44 us
    ppermute x2, waiting for transfers between devices, fold_halo(): lax.ppermute(head, axis, [((i + 1) % count, i) for i in range(count)])  7.12 us
    ppermute x3, starting transfers between devices, extended(): lax.ppermute(tail, axis, [(i, (i + 1) % count) for i in range(count)])  6.32 us
    ppermute x2, starting transfers between devices, fold_halo(): lax.ppermute(tail, axis, [(i, (i + 1) % count) for i in range(count)])  5.69 us
  transfers between devices with their start and end apart: 12, of which 9 were waited for; matrix products, arithmetic and copies ran while one was open for 17% of the time, Pallas kernels for 13%

profile of v14, /device:TPU:7, one launch (start us, length us, event | category | flops | bytes accessed | tf_op | source)
XLA Modules:
  0.0 114.4 jit_solution(14005056308086632848)
XLA Ops:
  1.6 4.1 %collective-permute-start = (bf16[4,1,64,128]{3,2,1,0:T(8,128)(2,1)S(1)}, bf16[4,1,64,128]{3,2,1,0:T(8,128)(2,1)S(1)}, u32[]{:S(2)}, u32[]{:S(2)}) collective-permute-start(bf16[4,1,64,128]{3,2,1,0:T(8,128)(2,1)S(1)} %get-tuple-element.41), channel_id=1, source_target_pairs={{0,8},{8,16},{16,24},{24,32},{32,40},{40,48},{48,56},{56,64},{64,7... | collective-permute-start | bytes 196616 | tf_op jit(solution)/shard_map/ppermute | solution.py:22
  5.9 1.1 collective-permute-done
  8.0 5.0 %collective-permute-done.1 = bf16[4,1,64,128]{3,2,1,0:T(8,128)(2,1)S(1)} collective-permute-done((bf16[4,1,64,128]{3,2,1,0:T(8,128)(2,1)S(1)}, bf16[4,1,64,128]{3,2,1,0:T(8,128)(2,1)S(1)}, u32[]{:S(2)}, u32[]{:S(2)}) %collective-permute-start.1) | collective-permute-done | bytes 65568 | tf_op jit(solution)/shard_map/ppermute | solution.py:24
  13.1 1.4 %collective-permute-start.2 = (bf16[4,6,1,128]{3,2,1,0:T(2,128)(2,1)S(1)}, bf16[4,6,1,128]{3,2,1,0:T(2,128)(2,1)S(1)}, u32[]{:S(2)}, u32[]{:S(2)}) collective-permute-start(bf16[4,6,1,128]{3,2,1,0:T(2,128)(2,1)S(1)} %get-tuple-element.38), channel_id=1, source_target_pairs={{0,2},{2,4},{4,6},{6,0},{1,3},{3,5},{5,7},{7,1},{8,10},{10,12},{12... | collective-permute-start | bytes 18440 | tf_op jit(solution)/shard_map/ppermute | solution.py:22
  14.4 1.5 %collective-permute-start.3 = (bf16[4,6,1,128]{3,2,1,0:T(2,128)(2,1)S(1)}, bf16[4,6,1,128]{3,2,1,0:T(2,128)(2,1)S(1)}, u32[]{:S(2)}, u32[]{:S(2)}) collective-permute-start(bf16[4,6,1,128]{3,2,1,0:T(2,128)(2,1)S(1)} %get-tuple-element.39), channel_id=1, source_target_pairs={{2,0},{4,2},{6,4},{0,6},{3,1},{5,3},{7,5},{1,7},{10,8},{12,10},{14... | collective-permute-start | bytes 18440 | tf_op jit(solution)/shard_map/ppermute | solution.py:24
  19.8 2.2 %reshape.237.refs_6_ = bf16[32,4096]{1,0:T(8,128)(2,1)} reshape(bf16[32,2,32,64]{3,2,1,0:T(8,128)(2,1)} %param.7) | data formatting | bytes 524288 | tf_op jit(solution)/shard_map/reshape | solution.py:328
  23.5 1.3 %copy.76.refs_1_ = f32[32,1]{1,0:T(8,128)} copy(f32[32,1]{0,1:T(1,128)} %bitcast.228) | data formatting | bytes 256 | tf_op jit(solution)/shard_map/reshape | solution.py:331
  24.9 1.4 %pad.4 = bf16[3,3,3,8,32]{4,3,2,1,0:T(8,128)(2,1)} pad(bf16[3,3,3,4,32]{4,3,2,1,0:T(4,128)(2,1)} %bitcast.227, bf16[]{:T(256)} %constant.43.clone.1), padding=0_0x0_0x0_0x0_4x0_0 | pad | bytes 20738 | tf_op jit(solution)/shard_map/jit(_pad)/pad | solution.py:241
  26.3 3.7 %collective-permute-done.4 = bf16[4,6,66,1]{3,2,1,0:T(8,128)(2,1)S(1)} collective-permute-done((bf16[4,6,66,1]{3,2,1,0:T(8,128)(2,1)S(1)}, bf16[4,6,66,1]{3,2,1,0:T(8,128)(2,1)S(1)}, u32[]{:S(2)}, u32[]{:S(2)}) %collective-permute-start.4) | collective-permute-done | bytes 3200 | tf_op jit(solution)/shard_map/ppermute | solution.py:22
  30.0 4.7 %collective-permute-done.5 = bf16[4,6,66,1]{3,2,1,0:T(8,128)(2,1)S(1)} collective-permute-done((bf16[4,6,66,1]{3,2,1,0:T(8,128)(2,1)S(1)}, bf16[4,6,66,1]{3,2,1,0:T(8,128)(2,1)S(1)}, u32[]{:S(2)}, u32[]{:S(2)}) %collective-permute-start.5) | collective-permute-done | bytes 3200 | tf_op jit(solution)/shard_map/ppermute | solution.py:24
  34.7 1.1 pad_maximum_fusion
  39.7 7.5 %copy.77.refs_5_ = bf16[256,108,128]{2,1,0:T(8,128)(2,1)} copy(bf16[256,108,128]{2,0,1:T(8,128)(2,1)S(1)} %bitcast.220) | data formatting | bytes 14155776 | tf_op jit(solution)/shard_map/reshape | solution.py:327
  47.3 19.2 %shard_map.75 = (bf16[32,4096]{1,0:T(8,128)(2,1)}, f32[32,108]{1,0:T(8,128)}, f32[32,1]{1,0:T(8,128)}, f32[396,4,128]{2,1,0:T(4,128)}, f32[396,4,128]{2,1,0:T(4,128)}) custom-call(bf16[32,108]{1,0:T(8,128)(2,1)} %copy.75.refs_0_, f32[32,1]{1,0:T(8,128)} %copy.76.refs_1_, f32[2,128,128]{2,1,0:T(8,128)} %add_convert_fusion.refs_2_, ...), custom_call_target="tpu_custom_call" | custom-call | tf_op jit(solution)/shard_map/pallas_call | solution.py:255
  66.4 1.9 %fusion.40 = (f32[6,66,4,1]{3,2,1,0:T(4,128)S(1)}, f32[6,66,4,1]{3,2,1,0:T(4,128)S(1)}) fusion(f32[6,66,4,128]{3,2,1,0:T(4,128)} %bitcast.223), kind=kLoop, calls=%fused_computation.97 | loop fusion | bytes 25344 | tf_op jit(solution)/shard_map/slice | solution.py:347
  68.7 1.7 %collective-permute-start.6 = (f32[6,66,4,1]{1,2,3,0:T(4,128)S(1)}, f32[6,66,4,1]{1,2,3,0:T(4,128)S(1)}, u32[]{:S(2)}, u32[]{:S(2)}) collective-permute-start(f32[6,66,4,1]{1,2,3,0:T(4,128)S(1)} %copy.88), channel_id=1, source_target_pairs={{0,1},{1,0},{2,3},{3,2},{4,5},{5,4},{6,7},{7,6},{8,9},{9,8},{10,11... | collective-permute-start | bytes 19016 | tf_op jit(solution)/shard_map/ppermute | solution.py:349
  70.9 1.9 %fusion.41 = (f32[6,66,4,1]{3,2,1,0:T(4,128)S(1)}, f32[6,66,4,1]{3,2,1,0:T(4,128)S(1)}) fusion(f32[6,66,4,128]{3,2,1,0:T(4,128)} %bitcast.221), kind=kLoop, calls=%fused_computation.98 | loop fusion | bytes 25344 | tf_op jit(solution)/shard_map/slice | solution.py:353
  75.2 1.3 %collective-permute-start.8 = (f32[6,1,4,128]{3,1,0,2:T(1,128)S(1)}, f32[6,1,4,128]{3,1,0,2:T(1,128)S(1)}, u32[]{:S(2)}, u32[]{:S(2)}) collective-permute-start(f32[6,1,4,128]{3,1,0,2:T(1,128)S(1)} %get-tuple-element.27), channel_id=1, source_target_pairs={{0,2},{2,4},{4,6},{6,0},{1,3},{3,5},{5,7},{7,1},{8,10},{10,12},{12... | collective-permute-start | bytes 36872 | tf_op jit(solution)/shard_map/ppermute | solution.py:293
  77.1 1.5 %collective-permute-start.9 = (f32[6,1,4,128]{3,1,0,2:T(1,128)S(1)}, f32[6,1,4,128]{3,1,0,2:T(1,128)S(1)}, u32[]{:S(2)}, u32[]{:S(2)}) collective-permute-start(f32[6,1,4,128]{3,1,0,2:T(1,128)S(1)} %get-tuple-element.26), channel_id=1, source_target_pairs={{2,0},{4,2},{6,4},{0,6},{3,1},{5,3},{7,5},{1,7},{10,8},{12,10},{14... | collective-permute-start | bytes 36872 | tf_op jit(solution)/shard_map/ppermute | solution.py:294
  79.9 4.3 %collective-permute-start.10 = (f32[1,64,4,128]{3,1,0,2:T(8,128)S(1)}, f32[1,64,4,128]{3,1,0,2:T(8,128)S(1)}, u32[]{:S(2)}, u32[]{:S(2)}) collective-permute-start(f32[1,64,4,128]{3,1,0,2:T(8,128)S(1)} %get-tuple-element.33), channel_id=1, source_target_pairs={{0,8},{8,16},{16,24},{24,32},{32,40},{40,48},{48,56},{56,64},{64,7... | collective-permute-start | bytes 393224 | tf_op jit(solution)/shard_map/ppermute | solution.py:293
  84.9 15.4 %shard_map.76 = f32[32,128]{1,0:T(8,128)} custom-call(f32[32,128]{1,0:T(8,128)} %maximum_maximum_fusion.1.refs_0_), custom_call_target="tpu_custom_call" | custom-call | tf_op jit(solution)/shard_map/pallas_call | solution.py:113
  101.8 2.3 %reshape.238 = bf16[32,2,32,64]{3,2,1,0:T(8,128)(2,1)} reshape(bf16[32,4096]{1,0:T(8,128)(2,1)} %get-tuple-element.9) | data formatting | bytes 524288 | tf_op jit(solution)/shard_map/reshape | solution.py:333
  104.0 1.4 %slice_reduce_fusion = f32[32]{0:T(128)} fusion(f32[32,128]{1,0:T(8,128)} %shard_map.76), kind=kLoop, calls=%fused_computation.87 | loop fusion | bytes 256 | tf_op jit(solution)/shard_map/slice | solution.py:343
  105.5 1.5 %collective-permute-start.11 = (f32[1,64,4,128]{3,1,0,2:T(8,128)S(1)}, f32[1,64,4,128]{3,1,0,2:T(8,128)S(1)}, u32[]{:S(2)}, u32[]{:S(2)}) collective-permute-start(f32[1,64,4,128]{3,1,0,2:T(8,128)S(1)} %get-tuple-element.32), channel_id=1, source_target_pairs={{8,0},{16,8},{24,16},{32,24},{40,32},{48,40},{56,48},{64,56},{72,6... | collective-permute-start | bytes 393224 | tf_op jit(solution)/shard_map/ppermute | solution.py:294
  107.0 6.6 %collective-permute-done.11 = f32[1,64,4,128]{3,1,0,2:T(8,128)S(1)} collective-permute-done((f32[1,64,4,128]{3,1,0,2:T(8,128)S(1)}, f32[1,64,4,128]{3,1,0,2:T(8,128)S(1)}, u32[]{:S(2)}, u32[]{:S(2)}) %collective-permute-start.11) | collective-permute-done | bytes 131104 | tf_op jit(solution)/shard_map/ppermute | solution.py:294
  (90 shorter events, 19.4 us)
Async XLA Ops:
  0.6 35.6 %copy-start.1 = (bf16[4,4,64,128]{3,2,1,0:T(8,128)(2,1)S(1)}, bf16[4,4,64,128]{3,2,1,0:T(8,128)(2,1)}, u32[]{:S(2)}) copy-start(bf16[4,4,64,128]{3,2,1,0:T(8,128)(2,1)} %param.4) | copy-start | bytes 786436
  1.6 5.5 %collective-permute-start = (bf16[4,1,64,128]{3,2,1,0:T(8,128)(2,1)S(1)}, bf16[4,1,64,128]{3,2,1,0:T(8,128)(2,1)S(1)}, u32[]{:S(2)}, u32[]{:S(2)}) collective-permute-start(bf16[4,1,64,128]{3,2,1,0:T(8,128)(2,1)S(1)} %get-tuple-element.41), channel_id=1, source_target_pairs={{0,8},{8,16},{16,24},{24,32},{32,40},{40,48},{48,56},{56,64},{64,7... | collective-permute-start | bytes 196616 | tf_op jit(solution)/shard_map/ppermute | solution.py:22
  5.7 7.3 %collective-permute-start.1 = (bf16[4,1,64,128]{3,2,1,0:T(8,128)(2,1)S(1)}, bf16[4,1,64,128]{3,2,1,0:T(8,128)(2,1)S(1)}, u32[]{:S(2)}, u32[]{:S(2)}) collective-permute-start(bf16[4,1,64,128]{3,2,1,0:T(8,128)(2,1)S(1)} %get-tuple-element.40), channel_id=1, source_target_pairs={{8,0},{16,8},{24,16},{32,24},{40,32},{48,40},{56,48},{64,56},{72,6... | collective-permute-start | bytes 196616 | tf_op jit(solution)/shard_map/ppermute | solution.py:24
  13.1 3.9 %collective-permute-start.2 = (bf16[4,6,1,128]{3,2,1,0:T(2,128)(2,1)S(1)}, bf16[4,6,1,128]{3,2,1,0:T(2,128)(2,1)S(1)}, u32[]{:S(2)}, u32[]{:S(2)}) collective-permute-start(bf16[4,6,1,128]{3,2,1,0:T(2,128)(2,1)S(1)} %get-tuple-element.38), channel_id=1, source_target_pairs={{0,2},{2,4},{4,6},{6,0},{1,3},{3,5},{5,7},{7,1},{8,10},{10,12},{12... | collective-permute-start | bytes 18440 | tf_op jit(solution)/shard_map/ppermute | solution.py:22
  14.4 2.8 %collective-permute-start.3 = (bf16[4,6,1,128]{3,2,1,0:T(2,128)(2,1)S(1)}, bf16[4,6,1,128]{3,2,1,0:T(2,128)(2,1)S(1)}, u32[]{:S(2)}, u32[]{:S(2)}) collective-permute-start(bf16[4,6,1,128]{3,2,1,0:T(2,128)(2,1)S(1)} %get-tuple-element.39), channel_id=1, source_target_pairs={{2,0},{4,2},{6,4},{0,6},{3,1},{5,3},{7,5},{1,7},{10,8},{12,10},{14... | collective-permute-start | bytes 18440 | tf_op jit(solution)/shard_map/ppermute | solution.py:24
  17.6 12.3 %collective-permute-start.4 = (bf16[4,6,66,1]{3,2,1,0:T(8,128)(2,1)S(1)}, bf16[4,6,66,1]{3,2,1,0:T(8,128)(2,1)S(1)}, u32[]{:S(2)}, u32[]{:S(2)}) collective-permute-start(bf16[4,6,66,1]{3,2,1,0:T(8,128)(2,1)S(1)} %get-tuple-element.35), channel_id=1, source_target_pairs={{0,1},{1,0},{2,3},{3,2},{4,5},{5,4},{6,7},{7,6},{8,9},{9,8},{10,11... | collective-permute-start | bytes 9512 | tf_op jit(solution)/shard_map/ppermute | solution.py:22
  18.5 16.2 %collective-permute-start.5 = (bf16[4,6,66,1]{3,2,1,0:T(8,128)(2,1)S(1)}, bf16[4,6,66,1]{3,2,1,0:T(8,128)(2,1)S(1)}, u32[]{:S(2)}, u32[]{:S(2)}) collective-permute-start(bf16[4,6,66,1]{3,2,1,0:T(8,128)(2,1)S(1)} %get-tuple-element.34), channel_id=1, source_target_pairs={{1,0},{0,1},{3,2},{2,3},{5,4},{4,5},{7,6},{6,7},{9,8},{8,9},{11,10... | collective-permute-start | bytes 9512 | tf_op jit(solution)/shard_map/ppermute | solution.py:24
  66.4 6.4 %copy-start = (f32[396,4,128]{2,1,0:T(4,128)S(1)}, f32[396,4,128]{2,1,0:T(4,128)}, u32[]{:S(2)}) copy-start(f32[396,4,128]{2,1,0:T(4,128)} %get-tuple-element.12) | copy-start | bytes 2433028
  68.7 5.4 %collective-permute-start.6 = (f32[6,66,4,1]{1,2,3,0:T(4,128)S(1)}, f32[6,66,4,1]{1,2,3,0:T(4,128)S(1)}, u32[]{:S(2)}, u32[]{:S(2)}) collective-permute-start(f32[6,66,4,1]{1,2,3,0:T(4,128)S(1)} %copy.88), channel_id=1, source_target_pairs={{0,1},{1,0},{2,3},{3,2},{4,5},{5,4},{6,7},{7,6},{8,9},{9,8},{10,11... | collective-permute-start | bytes 19016 | tf_op jit(solution)/shard_map/ppermute | solution.py:349
  70.8 3.8 %collective-permute-start.7 = (f32[6,66,4,1]{1,2,3,0:T(4,128)S(1)}, f32[6,66,4,1]{1,2,3,0:T(4,128)S(1)}, u32[]{:S(2)}, u32[]{:S(2)}) collective-permute-start(f32[6,66,4,1]{1,2,3,0:T(4,128)S(1)} %copy.91), channel_id=1, source_target_pairs={{1,0},{0,1},{3,2},{2,3},{5,4},{4,5},{7,6},{6,7},{9,8},{8,9},{11,10... | collective-permute-start | bytes 19016 | tf_op jit(solution)/shard_map/ppermute | solution.py:350
  74.0 10.2 %copy-start.3 = (f32[32,108]{1,0:T(8,128)S(1)}, f32[32,108]{1,0:T(8,128)}, u32[]{:S(2)}) copy-start(f32[32,108]{1,0:T(8,128)} %get-tuple-element.10) | copy-start | bytes 41476
  74.0 10.2 %copy-start.4 = (f32[32,1]{1,0:T(8,128)S(1)}, f32[32,1]{1,0:T(8,128)}, u32[]{:S(2)}) copy-start(f32[32,1]{1,0:T(8,128)} %get-tuple-element.11) | copy-start | bytes 388
  75.2 3.8 %collective-permute-start.8 = (f32[6,1,4,128]{3,1,0,2:T(1,128)S(1)}, f32[6,1,4,128]{3,1,0,2:T(1,128)S(1)}, u32[]{:S(2)}, u32[]{:S(2)}) collective-permute-start(f32[6,1,4,128]{3,1,0,2:T(1,128)S(1)} %get-tuple-element.27), channel_id=1, source_target_pairs={{0,2},{2,4},{4,6},{6,0},{1,3},{3,5},{5,7},{7,1},{8,10},{10,12},{12... | collective-permute-start | bytes 36872 | tf_op jit(solution)/shard_map/ppermute | solution.py:293
  77.1 2.6 %collective-permute-start.9 = (f32[6,1,4,128]{3,1,0,2:T(1,128)S(1)}, f32[6,1,4,128]{3,1,0,2:T(1,128)S(1)}, u32[]{:S(2)}, u32[]{:S(2)}) collective-permute-start(f32[6,1,4,128]{3,1,0,2:T(1,128)S(1)} %get-tuple-element.26), channel_id=1, source_target_pairs={{2,0},{4,2},{6,4},{0,6},{3,1},{5,3},{7,5},{1,7},{10,8},{12,10},{14... | collective-permute-start | bytes 36872 | tf_op jit(solution)/shard_map/ppermute | solution.py:294
  79.9 27.1 %collective-permute-start.10 = (f32[1,64,4,128]{3,1,0,2:T(8,128)S(1)}, f32[1,64,4,128]{3,1,0,2:T(8,128)S(1)}, u32[]{:S(2)}, u32[]{:S(2)}) collective-permute-start(f32[1,64,4,128]{3,1,0,2:T(8,128)S(1)} %get-tuple-element.33), channel_id=1, source_target_pairs={{0,8},{8,16},{16,24},{24,32},{32,40},{40,48},{48,56},{56,64},{64,7... | collective-permute-start | bytes 393224 | tf_op jit(solution)/shard_map/ppermute | solution.py:293
  105.5 8.1 %collective-permute-start.11 = (f32[1,64,4,128]{3,1,0,2:T(8,128)S(1)}, f32[1,64,4,128]{3,1,0,2:T(8,128)S(1)}, u32[]{:S(2)}, u32[]{:S(2)}) collective-permute-start(f32[1,64,4,128]{3,1,0,2:T(8,128)S(1)} %get-tuple-element.32), channel_id=1, source_target_pairs={{8,0},{16,8},{24,16},{32,24},{40,32},{48,40},{56,48},{64,56},{72,6... | collective-permute-start | bytes 393224 | tf_op jit(solution)/shard_map/ppermute | solution.py:294
  113.6 0.8 copy-start.2

commit v15 on v14

--- a/solution.py
+++ b/solution.py
@@ -235,7 +235,8 @@
 def forward(weight, bias, patches, cot, pairs, wide_x, wide_y):
     lines, taps, rows = patches.shape
     chan_out, chan_in = weight.shape[:2]
-    weight_mat = weight.reshape(chan_out, taps)
+    weight_mat = jnp.transpose(weight.reshape(chan_out, chan_in, 27), (0, 2, 1))
+    weight_mat = weight_mat.reshape(chan_out, taps)
     slots = 8
     spread_w = jnp.transpose(weight, (2, 3, 4, 1, 0))
     spread_w = jnp.pad(spread_w, ((0, 0), (0, 0), (0, 0), (0, slots - chan_in), (0, 0)))
@@ -315,22 +316,24 @@
         for shift_e in range(3)
     ]
     widened = extended(cells, (("gx", 1), ("gy", 2), ("gz", 3)), 1)
-    patches = jnp.stack(
+    patches = jnp.concatenate(
         [
             jnp.transpose(
                 widened[:, sa : sa + cells_x, sb : sb + cells_y, se : se + cells_z], (1, 2, 0, 3)
             )
             for sa, sb, se in stencil
         ],
-        axis=3,
-    )
-    patches = patches.reshape(cells_x * cells_y, chan_in * 27, cells_z)
+        axis=2,
+    )
+    patches = patches.reshape(cells_x * cells_y, 27 * chan_in, cells_z)
     cot = cotangent.reshape(chan_out, -1)
     wide_x, wide_y = cells_x + 2, cells_y + 2
     pooled, weight_local, bias_local, main, edge = forward(
         weight, bias.reshape(chan_out, 1), patches, cot, cells_x // 2, wide_x, wide_y
     )
     pooled = pooled.reshape(cotangent.shape)
+    weight_local = jnp.transpose(weight_local.reshape(chan_out, 27, chan_in), (0, 2, 1))
+    weight_local = weight_local.reshape(chan_out, -1)
     taps = chan_in * 27
     width = -(-(taps + 1) // 128) * 128
     partial = jnp.concatenate(

time: 115 us -> 115 us (level)
    concatenate x0 -> x2, local copies, waits for them, and re-layouts: none -> 7.78 us  [on_device(): jnp.concatenate([jnp.transpose(widened[:, sa:sa + cells_x, sb:sb + cells_...]
    reshape x3 -> x4, local copies, waits for them, and re-layouts: 8.25 us -> 1.56 us  [the longest x2 1.45 us: forward(): weight_mat = weight_mat.reshape(chan_out, taps)]
    unnamed x37 -> x36, local copies, waits for them, and re-layouts: 7.44 us -> 6.68 us
where the time goes in v15:
time: 115 us
  Pallas kernels  34.5 us (30%)
  local copies, waits for them, and re-layouts  32.4 us (28%)
  waiting for transfers between devices  22.7 us (20%)
  starting transfers between devices  19 us (17%)
  other arithmetic  5.1 us (4%)
    pallas_call x1, Pallas kernels, forward(): pl.pallas_call(lambda *refs: forward_kernel(rows, wide_y, *refs), grid=(p...  19.1 us
    pallas_call x1, Pallas kernels, allreduce(): pl.pallas_call(lambda *refs: allreduce_kernel(sizes, *refs), out_shape=ja...  15.3 us
    ppermute x3, waiting for transfers between devices, extended(): lax.ppermute(head, axis, [((i + 1) % count, i) for i in range(count)])  10 us
    concatenate x2, local copies, waits for them, and re-layouts, on_device(): jnp.concatenate([jnp.transpose(widened[:, sa:sa + cells_x, sb:sb + cells_...  7.78 us
    ppermute x2, waiting for transfers between devices, fold_halo(): lax.ppermute(head, axis, [((i + 1) % count, i) for i in range(count)])  7.14 us
    unnamed x36, local copies, waits for them, and re-layouts  6.68 us
    ppermute x3, starting transfers between devices, extended(): lax.ppermute(tail, axis, [(i, (i + 1) % count) for i in range(count)])  6.32 us
    ppermute x2, starting transfers between devices, fold_halo(): lax.ppermute(tail, axis, [(i, (i + 1) % count) for i in range(count)])  5.71 us
  transfers between devices with their start and end apart: 12, of which 9 were waited for; matrix products, arithmetic and copies ran while one was open for 17% of the time, Pallas kernels for 13%

profile of v15, /device:TPU:7, one launch (start us, length us, event | category | flops | bytes accessed | tf_op | source)
XLA Modules:
  0.0 114.8 jit_solution(2727913223422454358)
XLA Ops:
  1.6 4.1 %collective-permute-start = (bf16[4,1,64,128]{3,2,1,0:T(8,128)(2,1)S(1)}, bf16[4,1,64,128]{3,2,1,0:T(8,128)(2,1)S(1)}, u32[]{:S(2)}, u32[]{:S(2)}) collective-permute-start(bf16[4,1,64,128]{3,2,1,0:T(8,128)(2,1)S(1)} %get-tuple-element.41), channel_id=1, source_target_pairs={{0,8},{8,16},{16,24},{24,32},{32,40},{40,48},{48,56},{56,64},{64,7... | collective-permute-start | bytes 196616 | tf_op jit(solution)/shard_map/ppermute | solution.py:22
  5.9 1.1 collective-permute-done
  8.0 5.0 %collective-permute-done.1 = bf16[4,1,64,128]{3,2,1,0:T(8,128)(2,1)S(1)} collective-permute-done((bf16[4,1,64,128]{3,2,1,0:T(8,128)(2,1)S(1)}, bf16[4,1,64,128]{3,2,1,0:T(8,128)(2,1)S(1)}, u32[]{:S(2)}, u32[]{:S(2)}) %collective-permute-start.1) | collective-permute-done | bytes 65568 | tf_op jit(solution)/shard_map/ppermute | solution.py:24
  13.1 1.4 %collective-permute-start.2 = (bf16[4,6,1,128]{3,2,1,0:T(2,128)(2,1)S(1)}, bf16[4,6,1,128]{3,2,1,0:T(2,128)(2,1)S(1)}, u32[]{:S(2)}, u32[]{:S(2)}) collective-permute-start(bf16[4,6,1,128]{3,2,1,0:T(2,128)(2,1)S(1)} %get-tuple-element.38), channel_id=1, source_target_pairs={{0,2},{2,4},{4,6},{6,0},{1,3},{3,5},{5,7},{7,1},{8,10},{10,12},{12... | collective-permute-start | bytes 18440 | tf_op jit(solution)/shard_map/ppermute | solution.py:22
  14.4 1.5 %collective-permute-start.3 = (bf16[4,6,1,128]{3,2,1,0:T(2,128)(2,1)S(1)}, bf16[4,6,1,128]{3,2,1,0:T(2,128)(2,1)S(1)}, u32[]{:S(2)}, u32[]{:S(2)}) collective-permute-start(bf16[4,6,1,128]{3,2,1,0:T(2,128)(2,1)S(1)} %get-tuple-element.39), channel_id=1, source_target_pairs={{2,0},{4,2},{6,4},{0,6},{3,1},{5,3},{7,5},{1,7},{10,8},{12,10},{14... | collective-permute-start | bytes 18440 | tf_op jit(solution)/shard_map/ppermute | solution.py:24
  19.8 2.2 %reshape.247.refs_6_ = bf16[32,4096]{1,0:T(8,128)(2,1)} reshape(bf16[32,2,32,64]{3,2,1,0:T(8,128)(2,1)} %param.7) | data formatting | bytes 524288 | tf_op jit(solution)/shard_map/reshape | solution.py:329
  23.5 1.3 %copy.32.refs_1_ = f32[32,1]{1,0:T(8,128)} copy(f32[32,1]{0,1:T(1,128)} %bitcast.136) | data formatting | bytes 256 | tf_op jit(solution)/shard_map/reshape | solution.py:332
  24.8 1.4 %pad.4 = bf16[3,3,3,8,32]{4,3,2,1,0:T(8,128)(2,1)} pad(bf16[3,3,3,4,32]{4,3,2,1,0:T(4,128)(2,1)} %bitcast.135, bf16[]{:T(256)} %constant.43.clone.1), padding=0_0x0_0x0_0x0_4x0_0 | pad | bytes 20738 | tf_op jit(solution)/shard_map/jit(_pad)/pad | solution.py:242
  26.3 3.7 %collective-permute-done.4 = bf16[4,6,66,1]{3,2,1,0:T(8,128)(2,1)S(1)} collective-permute-done((bf16[4,6,66,1]{3,2,1,0:T(8,128)(2,1)S(1)}, bf16[4,6,66,1]{3,2,1,0:T(8,128)(2,1)S(1)}, u32[]{:S(2)}, u32[]{:S(2)}) %collective-permute-start.4) | collective-permute-done | bytes 3200 | tf_op jit(solution)/shard_map/ppermute | solution.py:22
  30.0 4.7 %collective-permute-done.5 = bf16[4,6,66,1]{3,2,1,0:T(8,128)(2,1)S(1)} collective-permute-done((bf16[4,6,66,1]{3,2,1,0:T(8,128)(2,1)S(1)}, bf16[4,6,66,1]{3,2,1,0:T(8,128)(2,1)S(1)}, u32[]{:S(2)}, u32[]{:S(2)}) %collective-permute-start.5) | collective-permute-done | bytes 3200 | tf_op jit(solution)/shard_map/ppermute | solution.py:24
  34.7 1.1 pad_maximum_fusion
  39.7 7.5 %copy.30 = bf16[4,64,108,128]{3,2,1,0:T(8,128)(2,1)} copy(bf16[4,64,108,128]{3,1,0,2:T(8,128)(2,1)S(1)} %fusion.12) | data formatting | bytes 14155776 | tf_op jit(solution)/shard_map/concatenate | solution.py:319
  47.3 19.1 %shard_map.75 = (bf16[32,4096]{1,0:T(8,128)(2,1)}, f32[32,108]{1,0:T(8,128)}, f32[32,1]{1,0:T(8,128)}, f32[396,4,128]{2,1,0:T(4,128)}, f32[396,4,128]{2,1,0:T(4,128)}) custom-call(bf16[32,108]{1,0:T(8,128)(2,1)} %copy.31.refs_0_, f32[32,1]{1,0:T(8,128)} %copy.32.refs_1_, f32[2,128,128]{2,1,0:T(8,128)} %add_convert_fusion.refs_2_, ...), custom_call_target="tpu_custom_call" | custom-call | tf_op jit(solution)/shard_map/pallas_call | solution.py:256
  66.4 1.9 %fusion.40 = (f32[6,66,4,1]{3,2,1,0:T(4,128)S(1)}, f32[6,66,4,1]{3,2,1,0:T(4,128)S(1)}) fusion(f32[6,66,4,128]{3,2,1,0:T(4,128)} %bitcast.129), kind=kLoop, calls=%fused_computation.97 | loop fusion | bytes 25344 | tf_op jit(solution)/shard_map/slice | solution.py:350
  68.7 1.7 %collective-permute-start.6 = (f32[6,66,4,1]{1,2,3,0:T(4,128)S(1)}, f32[6,66,4,1]{1,2,3,0:T(4,128)S(1)}, u32[]{:S(2)}, u32[]{:S(2)}) collective-permute-start(f32[6,66,4,1]{1,2,3,0:T(4,128)S(1)} %copy.45), channel_id=1, source_target_pairs={{0,1},{1,0},{2,3},{3,2},{4,5},{5,4},{6,7},{7,6},{8,9},{9,8},{10,11... | collective-permute-start | bytes 19016 | tf_op jit(solution)/shard_map/ppermute | solution.py:352
  70.9 1.9 %fusion.41 = (f32[6,66,4,1]{3,2,1,0:T(4,128)S(1)}, f32[6,66,4,1]{3,2,1,0:T(4,128)S(1)}) fusion(f32[6,66,4,128]{3,2,1,0:T(4,128)} %bitcast.127), kind=kLoop, calls=%fused_computation.98 | loop fusion | bytes 25344 | tf_op jit(solution)/shard_map/slice | solution.py:356
  75.5 1.4 %collective-permute-start.8 = (f32[6,1,4,128]{3,1,0,2:T(1,128)S(1)}, f32[6,1,4,128]{3,1,0,2:T(1,128)S(1)}, u32[]{:S(2)}, u32[]{:S(2)}) collective-permute-start(f32[6,1,4,128]{3,1,0,2:T(1,128)S(1)} %get-tuple-element.27), channel_id=1, source_target_pairs={{0,2},{2,4},{4,6},{6,0},{1,3},{3,5},{5,7},{7,1},{8,10},{10,12},{12... | collective-permute-start | bytes 36872 | tf_op jit(solution)/shard_map/ppermute | solution.py:294
  77.5 1.5 %collective-permute-start.9 = (f32[6,1,4,128]{3,1,0,2:T(1,128)S(1)}, f32[6,1,4,128]{3,1,0,2:T(1,128)S(1)}, u32[]{:S(2)}, u32[]{:S(2)}) collective-permute-start(f32[6,1,4,128]{3,1,0,2:T(1,128)S(1)} %get-tuple-element.26), channel_id=1, source_target_pairs={{2,0},{4,2},{6,4},{0,6},{3,1},{5,3},{7,5},{1,7},{10,8},{12,10},{14... | collective-permute-start | bytes 36872 | tf_op jit(solution)/shard_map/ppermute | solution.py:295
  80.2 4.4 %collective-permute-start.10 = (f32[1,64,4,128]{3,1,0,2:T(8,128)S(1)}, f32[1,64,4,128]{3,1,0,2:T(8,128)S(1)}, u32[]{:S(2)}, u32[]{:S(2)}) collective-permute-start(f32[1,64,4,128]{3,1,0,2:T(8,128)S(1)} %get-tuple-element.33), channel_id=1, source_target_pairs={{0,8},{8,16},{16,24},{24,32},{32,40},{40,48},{48,56},{56,64},{64,7... | collective-permute-start | bytes 393224 | tf_op jit(solution)/shard_map/ppermute | solution.py:294
  85.3 15.3 %shard_map.76 = f32[32,128]{1,0:T(8,128)} custom-call(f32[32,128]{1,0:T(8,128)} %maximum_maximum_fusion.1.refs_0_), custom_call_target="tpu_custom_call" | custom-call | tf_op jit(solution)/shard_map/pallas_call | solution.py:113
  102.1 2.3 %reshape.248 = bf16[32,2,32,64]{3,2,1,0:T(8,128)(2,1)} reshape(bf16[32,4096]{1,0:T(8,128)(2,1)} %get-tuple-element.9) | data formatting | bytes 524288 | tf_op jit(solution)/shard_map/reshape | solution.py:334
  104.4 1.4 %slice_reduce_fusion = f32[32]{0:T(128)} fusion(f32[32,128]{1,0:T(8,128)} %shard_map.76), kind=kLoop, calls=%fused_computation.87 | loop fusion | bytes 256 | tf_op jit(solution)/shard_map/slice | solution.py:346
  105.9 1.5 %collective-permute-start.11 = (f32[1,64,4,128]{3,1,0,2:T(8,128)S(1)}, f32[1,64,4,128]{3,1,0,2:T(8,128)S(1)}, u32[]{:S(2)}, u32[]{:S(2)}) collective-permute-start(f32[1,64,4,128]{3,1,0,2:T(8,128)S(1)} %get-tuple-element.32), channel_id=1, source_target_pairs={{8,0},{16,8},{24,16},{32,24},{40,32},{48,40},{56,48},{64,56},{72,6... | collective-permute-start | bytes 393224 | tf_op jit(solution)/shard_map/ppermute | solution.py:295
  107.3 6.6 %collective-permute-done.11 = f32[1,64,4,128]{3,1,0,2:T(8,128)S(1)} collective-permute-done((f32[1,64,4,128]{3,1,0,2:T(8,128)S(1)}, f32[1,64,4,128]{3,1,0,2:T(8,128)S(1)}, u32[]{:S(2)}, u32[]{:S(2)}) %collective-permute-start.11) | collective-permute-done | bytes 131104 | tf_op jit(solution)/shard_map/ppermute | solution.py:295
  (93 shorter events, 19.7 us)
Async XLA Ops:
  0.6 35.7 %copy-start.1 = (bf16[4,4,64,128]{3,2,1,0:T(8,128)(2,1)S(1)}, bf16[4,4,64,128]{3,2,1,0:T(8,128)(2,1)}, u32[]{:S(2)}) copy-start(bf16[4,4,64,128]{3,2,1,0:T(8,128)(2,1)} %param.4) | copy-start | bytes 786436
  1.6 5.5 %collective-permute-start = (bf16[4,1,64,128]{3,2,1,0:T(8,128)(2,1)S(1)}, bf16[4,1,64,128]{3,2,1,0:T(8,128)(2,1)S(1)}, u32[]{:S(2)}, u32[]{:S(2)}) collective-permute-start(bf16[4,1,64,128]{3,2,1,0:T(8,128)(2,1)S(1)} %get-tuple-element.41), channel_id=1, source_target_pairs={{0,8},{8,16},{16,24},{24,32},{32,40},{40,48},{48,56},{56,64},{64,7... | collective-permute-start | bytes 196616 | tf_op jit(solution)/shard_map/ppermute | solution.py:22
  5.7 7.3 %collective-permute-start.1 = (bf16[4,1,64,128]{3,2,1,0:T(8,128)(2,1)S(1)}, bf16[4,1,64,128]{3,2,1,0:T(8,128)(2,1)S(1)}, u32[]{:S(2)}, u32[]{:S(2)}) collective-permute-start(bf16[4,1,64,128]{3,2,1,0:T(8,128)(2,1)S(1)} %get-tuple-element.40), channel_id=1, source_target_pairs={{8,0},{16,8},{24,16},{32,24},{40,32},{48,40},{56,48},{64,56},{72,6... | collective-permute-start | bytes 196616 | tf_op jit(solution)/shard_map/ppermute | solution.py:24
  13.1 3.9 %collective-permute-start.2 = (bf16[4,6,1,128]{3,2,1,0:T(2,128)(2,1)S(1)}, bf16[4,6,1,128]{3,2,1,0:T(2,128)(2,1)S(1)}, u32[]{:S(2)}, u32[]{:S(2)}) collective-permute-start(bf16[4,6,1,128]{3,2,1,0:T(2,128)(2,1)S(1)} %get-tuple-element.38), channel_id=1, source_target_pairs={{0,2},{2,4},{4,6},{6,0},{1,3},{3,5},{5,7},{7,1},{8,10},{10,12},{12... | collective-permute-start | bytes 18440 | tf_op jit(solution)/shard_map/ppermute | solution.py:22
  14.4 2.8 %collective-permute-start.3 = (bf16[4,6,1,128]{3,2,1,0:T(2,128)(2,1)S(1)}, bf16[4,6,1,128]{3,2,1,0:T(2,128)(2,1)S(1)}, u32[]{:S(2)}, u32[]{:S(2)}) collective-permute-start(bf16[4,6,1,128]{3,2,1,0:T(2,128)(2,1)S(1)} %get-tuple-element.39), channel_id=1, source_target_pairs={{2,0},{4,2},{6,4},{0,6},{3,1},{5,3},{7,5},{1,7},{10,8},{12,10},{14... | collective-permute-start | bytes 18440 | tf_op jit(solution)/shard_map/ppermute | solution.py:24
  17.6 12.3 %collective-permute-start.4 = (bf16[4,6,66,1]{3,2,1,0:T(8,128)(2,1)S(1)}, bf16[4,6,66,1]{3,2,1,0:T(8,128)(2,1)S(1)}, u32[]{:S(2)}, u32[]{:S(2)}) collective-permute-start(bf16[4,6,66,1]{3,2,1,0:T(8,128)(2,1)S(1)} %get-tuple-element.35), channel_id=1, source_target_pairs={{0,1},{1,0},{2,3},{3,2},{4,5},{5,4},{6,7},{7,6},{8,9},{9,8},{10,11... | collective-permute-start | bytes 9512 | tf_op jit(solution)/shard_map/ppermute | solution.py:22
  18.5 16.2 %collective-permute-start.5 = (bf16[4,6,66,1]{3,2,1,0:T(8,128)(2,1)S(1)}, bf16[4,6,66,1]{3,2,1,0:T(8,128)(2,1)S(1)}, u32[]{:S(2)}, u32[]{:S(2)}) collective-permute-start(bf16[4,6,66,1]{3,2,1,0:T(8,128)(2,1)S(1)} %get-tuple-element.34), channel_id=1, source_target_pairs={{1,0},{0,1},{3,2},{2,3},{5,4},{4,5},{7,6},{6,7},{9,8},{8,9},{11,10... | collective-permute-start | bytes 9512 | tf_op jit(solution)/shard_map/ppermute | solution.py:24
  66.4 6.4 %copy-start = (f32[396,4,128]{2,1,0:T(4,128)S(1)}, f32[396,4,128]{2,1,0:T(4,128)}, u32[]{:S(2)}) copy-start(f32[396,4,128]{2,1,0:T(4,128)} %get-tuple-element.12) | copy-start | bytes 2433028
  66.4 7.7 %copy-start.4 = (f32[32,108]{1,0:T(8,128)S(1)}, f32[32,108]{1,0:T(8,128)}, u32[]{:S(2)}) copy-start(f32[32,108]{1,0:T(8,128)} %get-tuple-element.10) | copy-start | bytes 41476
  68.7 5.7 %collective-permute-start.6 = (f32[6,66,4,1]{1,2,3,0:T(4,128)S(1)}, f32[6,66,4,1]{1,2,3,0:T(4,128)S(1)}, u32[]{:S(2)}, u32[]{:S(2)}) collective-permute-start(f32[6,66,4,1]{1,2,3,0:T(4,128)S(1)} %copy.45), channel_id=1, source_target_pairs={{0,1},{1,0},{2,3},{3,2},{4,5},{5,4},{6,7},{7,6},{8,9},{9,8},{10,11... | collective-permute-start | bytes 19016 | tf_op jit(solution)/shard_map/ppermute | solution.py:352
  70.8 4.1 %collective-permute-start.7 = (f32[6,66,4,1]{1,2,3,0:T(4,128)S(1)}, f32[6,66,4,1]{1,2,3,0:T(4,128)S(1)}, u32[]{:S(2)}, u32[]{:S(2)}) collective-permute-start(f32[6,66,4,1]{1,2,3,0:T(4,128)S(1)} %copy.48), channel_id=1, source_target_pairs={{1,0},{0,1},{3,2},{2,3},{5,4},{4,5},{7,6},{6,7},{9,8},{8,9},{11,10... | collective-permute-start | bytes 19016 | tf_op jit(solution)/shard_map/ppermute | solution.py:353
  74.1 10.5 %copy-start.3 = (f32[32,1]{1,0:T(8,128)S(1)}, f32[32,1]{1,0:T(8,128)}, u32[]{:S(2)}) copy-start(f32[32,1]{1,0:T(8,128)} %get-tuple-element.11) | copy-start | bytes 388
  75.5 3.8 %collective-permute-start.8 = (f32[6,1,4,128]{3,1,0,2:T(1,128)S(1)}, f32[6,1,4,128]{3,1,0,2:T(1,128)S(1)}, u32[]{:S(2)}, u32[]{:S(2)}) collective-permute-start(f32[6,1,4,128]{3,1,0,2:T(1,128)S(1)} %get-tuple-element.27), channel_id=1, source_target_pairs={{0,2},{2,4},{4,6},{6,0},{1,3},{3,5},{5,7},{7,1},{8,10},{10,12},{12... | collective-permute-start | bytes 36872 | tf_op jit(solution)/shard_map/ppermute | solution.py:294
  77.5 2.6 %collective-permute-start.9 = (f32[6,1,4,128]{3,1,0,2:T(1,128)S(1)}, f32[6,1,4,128]{3,1,0,2:T(1,128)S(1)}, u32[]{:S(2)}, u32[]{:S(2)}) collective-permute-start(f32[6,1,4,128]{3,1,0,2:T(1,128)S(1)} %get-tuple-element.26), channel_id=1, source_target_pairs={{2,0},{4,2},{6,4},{0,6},{3,1},{5,3},{7,5},{1,7},{10,8},{12,10},{14... | collective-permute-start | bytes 36872 | tf_op jit(solution)/shard_map/ppermute | solution.py:295
  80.2 27.1 %collective-permute-start.10 = (f32[1,64,4,128]{3,1,0,2:T(8,128)S(1)}, f32[1,64,4,128]{3,1,0,2:T(8,128)S(1)}, u32[]{:S(2)}, u32[]{:S(2)}) collective-permute-start(f32[1,64,4,128]{3,1,0,2:T(8,128)S(1)} %get-tuple-element.33), channel_id=1, source_target_pairs={{0,8},{8,16},{16,24},{24,32},{32,40},{40,48},{48,56},{56,64},{64,7... | collective-permute-start | bytes 393224 | tf_op jit(solution)/shard_map/ppermute | solution.py:294
  105.9 8.1 %collective-permute-start.11 = (f32[1,64,4,128]{3,1,0,2:T(8,128)S(1)}, f32[1,64,4,128]{3,1,0,2:T(8,128)S(1)}, u32[]{:S(2)}, u32[]{:S(2)}) collective-permute-start(f32[1,64,4,128]{3,1,0,2:T(8,128)S(1)} %get-tuple-element.32), channel_id=1, source_target_pairs={{8,0},{16,8},{24,16},{32,24},{40,32},{48,40},{56,48},{64,56},{72,6... | collective-permute-start | bytes 393224 | tf_op jit(solution)/shard_map/ppermute | solution.py:295
  114.0 0.8 copy-start.2

commit v16 on v14

--- a/solution.py
+++ b/solution.py
@@ -149,7 +149,7 @@
     first = lane == 0
     last = lane == rows - 1
 
-    group = 32
+    group = 64
     pooled_rows = group // 2
     pieces = pooled_rows // 2
 

time: 115 us -> 115 us (level)
  no operation moved by 1% of the time
where the time goes in v16:
time: 115 us; the launch traced here: 114 us
  Pallas kernels  34.3 us (30%)
  local copies, waits for them, and re-layouts  32.1 us (28%)
  waiting for transfers between devices  22.7 us (20%)
  starting transfers between devices  19.2 us (17%)
  other arithmetic  5.08 us (4%)
    pallas_call x1, Pallas kernels, forward(): pl.pallas_call(lambda *refs: forward_kernel(rows, wide_y, *refs), grid=(p...  18.9 us
    pallas_call x1, Pallas kernels, allreduce(): pl.pallas_call(lambda *refs: allreduce_kernel(sizes, *refs), out_shape=ja...  15.4 us
    ppermute x3, waiting for transfers between devices, extended(): lax.ppermute(head, axis, [((i + 1) % count, i) for i in range(count)])  10 us
    reshape x1, local copies, waits for them, and re-layouts, on_device(): patches = patches.reshape(cells_x * cells_y, chan_in * 27, cells_z)  7.54 us
    unnamed x37, local copies, waits for them, and re-layouts  7.44 us
    ppermute x2, waiting for transfers between devices, fold_halo(): lax.ppermute(head, axis, [((i + 1) % count, i) for i in range(count)])  7.41 us
    ppermute x3, starting transfers between devices, extended(): lax.ppermute(tail, axis, [(i, (i + 1) % count) for i in range(count)])  6.32 us
    ppermute x2, starting transfers between devices, fold_halo(): lax.ppermute(tail, axis, [(i, (i + 1) % count) for i in range(count)])  5.7 us
  transfers between devices with their start and end apart: 12, of which 9 were waited for; matrix products, arithmetic and copies ran while one was open for 17% of the time, Pallas kernels for 13%

profile of v16, /device:TPU:7, one launch (start us, length us, event | category | flops | bytes accessed | tf_op | source)
XLA Modules:
  0.0 114.4 jit_solution(8440399551247196395)
XLA Ops:
  1.6 4.1 %collective-permute-start = (bf16[4,1,64,128]{3,2,1,0:T(8,128)(2,1)S(1)}, bf16[4,1,64,128]{3,2,1,0:T(8,128)(2,1)S(1)}, u32[]{:S(2)}, u32[]{:S(2)}) collective-permute-start(bf16[4,1,64,128]{3,2,1,0:T(8,128)(2,1)S(1)} %get-tuple-element.41), channel_id=1, source_target_pairs={{0,8},{8,16},{16,24},{24,32},{32,40},{40,48},{48,56},{56,64},{64,7... | collective-permute-start | bytes 196616 | tf_op jit(solution)/shard_map/ppermute | solution.py:22
  5.9 1.1 collective-permute-done
  8.0 5.0 %collective-permute-done.1 = bf16[4,1,64,128]{3,2,1,0:T(8,128)(2,1)S(1)} collective-permute-done((bf16[4,1,64,128]{3,2,1,0:T(8,128)(2,1)S(1)}, bf16[4,1,64,128]{3,2,1,0:T(8,128)(2,1)S(1)}, u32[]{:S(2)}, u32[]{:S(2)}) %collective-permute-start.1) | collective-permute-done | bytes 65568 | tf_op jit(solution)/shard_map/ppermute | solution.py:24
  13.1 1.4 %collective-permute-start.2 = (bf16[4,6,1,128]{3,2,1,0:T(2,128)(2,1)S(1)}, bf16[4,6,1,128]{3,2,1,0:T(2,128)(2,1)S(1)}, u32[]{:S(2)}, u32[]{:S(2)}) collective-permute-start(bf16[4,6,1,128]{3,2,1,0:T(2,128)(2,1)S(1)} %get-tuple-element.38), channel_id=1, source_target_pairs={{0,2},{2,4},{4,6},{6,0},{1,3},{3,5},{5,7},{7,1},{8,10},{10,12},{12... | collective-permute-start | bytes 18440 | tf_op jit(solution)/shard_map/ppermute | solution.py:22
  14.4 1.5 %collective-permute-start.3 = (bf16[4,6,1,128]{3,2,1,0:T(2,128)(2,1)S(1)}, bf16[4,6,1,128]{3,2,1,0:T(2,128)(2,1)S(1)}, u32[]{:S(2)}, u32[]{:S(2)}) collective-permute-start(bf16[4,6,1,128]{3,2,1,0:T(2,128)(2,1)S(1)} %get-tuple-element.39), channel_id=1, source_target_pairs={{2,0},{4,2},{6,4},{0,6},{3,1},{5,3},{7,5},{1,7},{10,8},{12,10},{14... | collective-permute-start | bytes 18440 | tf_op jit(solution)/shard_map/ppermute | solution.py:24
  19.8 2.2 %reshape.237.refs_6_ = bf16[32,4096]{1,0:T(8,128)(2,1)} reshape(bf16[32,2,32,64]{3,2,1,0:T(8,128)(2,1)} %param.7) | data formatting | bytes 524288 | tf_op jit(solution)/shard_map/reshape | solution.py:328
  23.5 1.3 %copy.76.refs_1_ = f32[32,1]{1,0:T(8,128)} copy(f32[32,1]{0,1:T(1,128)} %bitcast.228) | data formatting | bytes 256 | tf_op jit(solution)/shard_map/reshape | solution.py:331
  24.9 1.4 %pad.4 = bf16[3,3,3,8,32]{4,3,2,1,0:T(8,128)(2,1)} pad(bf16[3,3,3,4,32]{4,3,2,1,0:T(4,128)(2,1)} %bitcast.227, bf16[]{:T(256)} %constant.43.clone.1), padding=0_0x0_0x0_0x0_4x0_0 | pad | bytes 20738 | tf_op jit(solution)/shard_map/jit(_pad)/pad | solution.py:241
  26.3 3.7 %collective-permute-done.4 = bf16[4,6,66,1]{3,2,1,0:T(8,128)(2,1)S(1)} collective-permute-done((bf16[4,6,66,1]{3,2,1,0:T(8,128)(2,1)S(1)}, bf16[4,6,66,1]{3,2,1,0:T(8,128)(2,1)S(1)}, u32[]{:S(2)}, u32[]{:S(2)}) %collective-permute-start.4) | collective-permute-done | bytes 3200 | tf_op jit(solution)/shard_map/ppermute | solution.py:22
  30.0 4.7 %collective-permute-done.5 = bf16[4,6,66,1]{3,2,1,0:T(8,128)(2,1)S(1)} collective-permute-done((bf16[4,6,66,1]{3,2,1,0:T(8,128)(2,1)S(1)}, bf16[4,6,66,1]{3,2,1,0:T(8,128)(2,1)S(1)}, u32[]{:S(2)}, u32[]{:S(2)}) %collective-permute-start.5) | collective-permute-done | bytes 3200 | tf_op jit(solution)/shard_map/ppermute | solution.py:24
  34.7 1.1 pad_maximum_fusion
  39.7 7.5 %copy.77.refs_5_ = bf16[256,108,128]{2,1,0:T(8,128)(2,1)} copy(bf16[256,108,128]{2,0,1:T(8,128)(2,1)S(1)} %bitcast.220) | data formatting | bytes 14155776 | tf_op jit(solution)/shard_map/reshape | solution.py:327
  47.3 18.9 %shard_map.75 = (bf16[32,4096]{1,0:T(8,128)(2,1)}, f32[32,108]{1,0:T(8,128)}, f32[32,1]{1,0:T(8,128)}, f32[396,4,128]{2,1,0:T(4,128)}, f32[396,4,128]{2,1,0:T(4,128)}) custom-call(bf16[32,108]{1,0:T(8,128)(2,1)} %copy.75.refs_0_, f32[32,1]{1,0:T(8,128)} %copy.76.refs_1_, f32[2,128,128]{2,1,0:T(8,128)} %add_convert_fusion.refs_2_, ...), custom_call_target="tpu_custom_call" | custom-call | tf_op jit(solution)/shard_map/pallas_call | solution.py:255
  66.2 1.9 %fusion.40 = (f32[6,66,4,1]{3,2,1,0:T(4,128)S(1)}, f32[6,66,4,1]{3,2,1,0:T(4,128)S(1)}) fusion(f32[6,66,4,128]{3,2,1,0:T(4,128)} %bitcast.223), kind=kLoop, calls=%fused_computation.97 | loop fusion | bytes 25344 | tf_op jit(solution)/shard_map/slice | solution.py:347
  68.5 1.7 %collective-permute-start.6 = (f32[6,66,4,1]{1,2,3,0:T(4,128)S(1)}, f32[6,66,4,1]{1,2,3,0:T(4,128)S(1)}, u32[]{:S(2)}, u32[]{:S(2)}) collective-permute-start(f32[6,66,4,1]{1,2,3,0:T(4,128)S(1)} %copy.88), channel_id=1, source_target_pairs={{0,1},{1,0},{2,3},{3,2},{4,5},{5,4},{6,7},{7,6},{8,9},{9,8},{10,11... | collective-permute-start | bytes 19016 | tf_op jit(solution)/shard_map/ppermute | solution.py:349
  70.6 1.9 %fusion.41 = (f32[6,66,4,1]{3,2,1,0:T(4,128)S(1)}, f32[6,66,4,1]{3,2,1,0:T(4,128)S(1)}) fusion(f32[6,66,4,128]{3,2,1,0:T(4,128)} %bitcast.221), kind=kLoop, calls=%fused_computation.98 | loop fusion | bytes 25344 | tf_op jit(solution)/shard_map/slice | solution.py:353
  74.9 1.4 %collective-permute-start.8 = (f32[6,1,4,128]{3,1,0,2:T(1,128)S(1)}, f32[6,1,4,128]{3,1,0,2:T(1,128)S(1)}, u32[]{:S(2)}, u32[]{:S(2)}) collective-permute-start(f32[6,1,4,128]{3,1,0,2:T(1,128)S(1)} %get-tuple-element.27), channel_id=1, source_target_pairs={{0,2},{2,4},{4,6},{6,0},{1,3},{3,5},{5,7},{7,1},{8,10},{10,12},{12... | collective-permute-start | bytes 36872 | tf_op jit(solution)/shard_map/ppermute | solution.py:293
  76.9 1.7 %collective-permute-start.9 = (f32[6,1,4,128]{3,1,0,2:T(1,128)S(1)}, f32[6,1,4,128]{3,1,0,2:T(1,128)S(1)}, u32[]{:S(2)}, u32[]{:S(2)}) collective-permute-start(f32[6,1,4,128]{3,1,0,2:T(1,128)S(1)} %get-tuple-element.26), channel_id=1, source_target_pairs={{2,0},{4,2},{6,4},{0,6},{3,1},{5,3},{7,5},{1,7},{10,8},{12,10},{14... | collective-permute-start | bytes 36872 | tf_op jit(solution)/shard_map/ppermute | solution.py:294
  79.9 4.3 %collective-permute-start.10 = (f32[1,64,4,128]{3,1,0,2:T(8,128)S(1)}, f32[1,64,4,128]{3,1,0,2:T(8,128)S(1)}, u32[]{:S(2)}, u32[]{:S(2)}) collective-permute-start(f32[1,64,4,128]{3,1,0,2:T(8,128)S(1)} %get-tuple-element.33), channel_id=1, source_target_pairs={{0,8},{8,16},{16,24},{24,32},{32,40},{40,48},{48,56},{56,64},{64,7... | collective-permute-start | bytes 393224 | tf_op jit(solution)/shard_map/ppermute | solution.py:293
  85.0 15.4 %shard_map.76 = f32[32,128]{1,0:T(8,128)} custom-call(f32[32,128]{1,0:T(8,128)} %maximum_maximum_fusion.1.refs_0_), custom_call_target="tpu_custom_call" | custom-call | tf_op jit(solution)/shard_map/pallas_call | solution.py:113
  101.8 2.3 %reshape.238 = bf16[32,2,32,64]{3,2,1,0:T(8,128)(2,1)} reshape(bf16[32,4096]{1,0:T(8,128)(2,1)} %get-tuple-element.9) | data formatting | bytes 524288 | tf_op jit(solution)/shard_map/reshape | solution.py:333
  104.1 1.4 %slice_reduce_fusion = f32[32]{0:T(128)} fusion(f32[32,128]{1,0:T(8,128)} %shard_map.76), kind=kLoop, calls=%fused_computation.87 | loop fusion | bytes 256 | tf_op jit(solution)/shard_map/slice | solution.py:343
  105.5 1.5 %collective-permute-start.11 = (f32[1,64,4,128]{3,1,0,2:T(8,128)S(1)}, f32[1,64,4,128]{3,1,0,2:T(8,128)S(1)}, u32[]{:S(2)}, u32[]{:S(2)}) collective-permute-start(f32[1,64,4,128]{3,1,0,2:T(8,128)S(1)} %get-tuple-element.32), channel_id=1, source_target_pairs={{8,0},{16,8},{24,16},{32,24},{40,32},{48,40},{56,48},{64,56},{72,6... | collective-permute-start | bytes 393224 | tf_op jit(solution)/shard_map/ppermute | solution.py:294
  107.0 6.6 %collective-permute-done.11 = f32[1,64,4,128]{3,1,0,2:T(8,128)S(1)} collective-permute-done((f32[1,64,4,128]{3,1,0,2:T(8,128)S(1)}, f32[1,64,4,128]{3,1,0,2:T(8,128)S(1)}, u32[]{:S(2)}, u32[]{:S(2)}) %collective-permute-start.11) | collective-permute-done | bytes 131104 | tf_op jit(solution)/shard_map/ppermute | solution.py:294
  (90 shorter events, 19.4 us)
Async XLA Ops:
  0.6 35.6 %copy-start.1 = (bf16[4,4,64,128]{3,2,1,0:T(8,128)(2,1)S(1)}, bf16[4,4,64,128]{3,2,1,0:T(8,128)(2,1)}, u32[]{:S(2)}) copy-start(bf16[4,4,64,128]{3,2,1,0:T(8,128)(2,1)} %param.4) | copy-start | bytes 786436
  1.6 5.5 %collective-permute-start = (bf16[4,1,64,128]{3,2,1,0:T(8,128)(2,1)S(1)}, bf16[4,1,64,128]{3,2,1,0:T(8,128)(2,1)S(1)}, u32[]{:S(2)}, u32[]{:S(2)}) collective-permute-start(bf16[4,1,64,128]{3,2,1,0:T(8,128)(2,1)S(1)} %get-tuple-element.41), channel_id=1, source_target_pairs={{0,8},{8,16},{16,24},{24,32},{32,40},{40,48},{48,56},{56,64},{64,7... | collective-permute-start | bytes 196616 | tf_op jit(solution)/shard_map/ppermute | solution.py:22
  5.7 7.3 %collective-permute-start.1 = (bf16[4,1,64,128]{3,2,1,0:T(8,128)(2,1)S(1)}, bf16[4,1,64,128]{3,2,1,0:T(8,128)(2,1)S(1)}, u32[]{:S(2)}, u32[]{:S(2)}) collective-permute-start(bf16[4,1,64,128]{3,2,1,0:T(8,128)(2,1)S(1)} %get-tuple-element.40), channel_id=1, source_target_pairs={{8,0},{16,8},{24,16},{32,24},{40,32},{48,40},{56,48},{64,56},{72,6... | collective-permute-start | bytes 196616 | tf_op jit(solution)/shard_map/ppermute | solution.py:24
  13.1 3.9 %collective-permute-start.2 = (bf16[4,6,1,128]{3,2,1,0:T(2,128)(2,1)S(1)}, bf16[4,6,1,128]{3,2,1,0:T(2,128)(2,1)S(1)}, u32[]{:S(2)}, u32[]{:S(2)}) collective-permute-start(bf16[4,6,1,128]{3,2,1,0:T(2,128)(2,1)S(1)} %get-tuple-element.38), channel_id=1, source_target_pairs={{0,2},{2,4},{4,6},{6,0},{1,3},{3,5},{5,7},{7,1},{8,10},{10,12},{12... | collective-permute-start | bytes 18440 | tf_op jit(solution)/shard_map/ppermute | solution.py:22
  14.4 2.8 %collective-permute-start.3 = (bf16[4,6,1,128]{3,2,1,0:T(2,128)(2,1)S(1)}, bf16[4,6,1,128]{3,2,1,0:T(2,128)(2,1)S(1)}, u32[]{:S(2)}, u32[]{:S(2)}) collective-permute-start(bf16[4,6,1,128]{3,2,1,0:T(2,128)(2,1)S(1)} %get-tuple-element.39), channel_id=1, source_target_pairs={{2,0},{4,2},{6,4},{0,6},{3,1},{5,3},{7,5},{1,7},{10,8},{12,10},{14... | collective-permute-start | bytes 18440 | tf_op jit(solution)/shard_map/ppermute | solution.py:24
  17.6 12.3 %collective-permute-start.4 = (bf16[4,6,66,1]{3,2,1,0:T(8,128)(2,1)S(1)}, bf16[4,6,66,1]{3,2,1,0:T(8,128)(2,1)S(1)}, u32[]{:S(2)}, u32[]{:S(2)}) collective-permute-start(bf16[4,6,66,1]{3,2,1,0:T(8,128)(2,1)S(1)} %get-tuple-element.35), channel_id=1, source_target_pairs={{0,1},{1,0},{2,3},{3,2},{4,5},{5,4},{6,7},{7,6},{8,9},{9,8},{10,11... | collective-permute-start | bytes 9512 | tf_op jit(solution)/shard_map/ppermute | solution.py:22
  18.5 16.2 %collective-permute-start.5 = (bf16[4,6,66,1]{3,2,1,0:T(8,128)(2,1)S(1)}, bf16[4,6,66,1]{3,2,1,0:T(8,128)(2,1)S(1)}, u32[]{:S(2)}, u32[]{:S(2)}) collective-permute-start(bf16[4,6,66,1]{3,2,1,0:T(8,128)(2,1)S(1)} %get-tuple-element.34), channel_id=1, source_target_pairs={{1,0},{0,1},{3,2},{2,3},{5,4},{4,5},{7,6},{6,7},{9,8},{8,9},{11,10... | collective-permute-start | bytes 9512 | tf_op jit(solution)/shard_map/ppermute | solution.py:24
  66.2 6.3 %copy-start = (f32[396,4,128]{2,1,0:T(4,128)S(1)}, f32[396,4,128]{2,1,0:T(4,128)}, u32[]{:S(2)}) copy-start(f32[396,4,128]{2,1,0:T(4,128)} %get-tuple-element.12) | copy-start | bytes 2433028
  68.5 5.4 %collective-permute-start.6 = (f32[6,66,4,1]{1,2,3,0:T(4,128)S(1)}, f32[6,66,4,1]{1,2,3,0:T(4,128)S(1)}, u32[]{:S(2)}, u32[]{:S(2)}) collective-permute-start(f32[6,66,4,1]{1,2,3,0:T(4,128)S(1)} %copy.88), channel_id=1, source_target_pairs={{0,1},{1,0},{2,3},{3,2},{4,5},{5,4},{6,7},{7,6},{8,9},{9,8},{10,11... | collective-permute-start | bytes 19016 | tf_op jit(solution)/shard_map/ppermute | solution.py:349
  70.6 3.8 %collective-permute-start.7 = (f32[6,66,4,1]{1,2,3,0:T(4,128)S(1)}, f32[6,66,4,1]{1,2,3,0:T(4,128)S(1)}, u32[]{:S(2)}, u32[]{:S(2)}) collective-permute-start(f32[6,66,4,1]{1,2,3,0:T(4,128)S(1)} %copy.91), channel_id=1, source_target_pairs={{1,0},{0,1},{3,2},{2,3},{5,4},{4,5},{7,6},{6,7},{9,8},{8,9},{11,10... | collective-permute-start | bytes 19016 | tf_op jit(solution)/shard_map/ppermute | solution.py:350
  73.8 10.5 %copy-start.3 = (f32[32,108]{1,0:T(8,128)S(1)}, f32[32,108]{1,0:T(8,128)}, u32[]{:S(2)}) copy-start(f32[32,108]{1,0:T(8,128)} %get-tuple-element.10) | copy-start | bytes 41476
  73.8 10.5 %copy-start.4 = (f32[32,1]{1,0:T(8,128)S(1)}, f32[32,1]{1,0:T(8,128)}, u32[]{:S(2)}) copy-start(f32[32,1]{1,0:T(8,128)} %get-tuple-element.11) | copy-start | bytes 388
  74.9 3.8 %collective-permute-start.8 = (f32[6,1,4,128]{3,1,0,2:T(1,128)S(1)}, f32[6,1,4,128]{3,1,0,2:T(1,128)S(1)}, u32[]{:S(2)}, u32[]{:S(2)}) collective-permute-start(f32[6,1,4,128]{3,1,0,2:T(1,128)S(1)} %get-tuple-element.27), channel_id=1, source_target_pairs={{0,2},{2,4},{4,6},{6,0},{1,3},{3,5},{5,7},{7,1},{8,10},{10,12},{12... | collective-permute-start | bytes 36872 | tf_op jit(solution)/shard_map/ppermute | solution.py:293
  76.9 2.9 %collective-permute-start.9 = (f32[6,1,4,128]{3,1,0,2:T(1,128)S(1)}, f32[6,1,4,128]{3,1,0,2:T(1,128)S(1)}, u32[]{:S(2)}, u32[]{:S(2)}) collective-permute-start(f32[6,1,4,128]{3,1,0,2:T(1,128)S(1)} %get-tuple-element.26), channel_id=1, source_target_pairs={{2,0},{4,2},{6,4},{0,6},{3,1},{5,3},{7,5},{1,7},{10,8},{12,10},{14... | collective-permute-start | bytes 36872 | tf_op jit(solution)/shard_map/ppermute | solution.py:294
  79.9 27.1 %collective-permute-start.10 = (f32[1,64,4,128]{3,1,0,2:T(8,128)S(1)}, f32[1,64,4,128]{3,1,0,2:T(8,128)S(1)}, u32[]{:S(2)}, u32[]{:S(2)}) collective-permute-start(f32[1,64,4,128]{3,1,0,2:T(8,128)S(1)} %get-tuple-element.33), channel_id=1, source_target_pairs={{0,8},{8,16},{16,24},{24,32},{32,40},{40,48},{48,56},{56,64},{64,7... | collective-permute-start | bytes 393224 | tf_op jit(solution)/shard_map/ppermute | solution.py:293
  105.5 8.1 %collective-permute-start.11 = (f32[1,64,4,128]{3,1,0,2:T(8,128)S(1)}, f32[1,64,4,128]{3,1,0,2:T(8,128)S(1)}, u32[]{:S(2)}, u32[]{:S(2)}) collective-permute-start(f32[1,64,4,128]{3,1,0,2:T(8,128)S(1)} %get-tuple-element.32), channel_id=1, source_target_pairs={{8,0},{16,8},{24,16},{32,24},{40,32},{48,40},{56,48},{64,56},{72,6... | collective-permute-start | bytes 393224 | tf_op jit(solution)/shard_map/ppermute | solution.py:294
  113.6 0.8 copy-start.2

commit v17 on v14

--- a/solution.py
+++ b/solution.py
@@ -314,7 +314,7 @@
         for shift_b in range(3)
         for shift_e in range(3)
     ]
-    widened = extended(cells, (("gx", 1), ("gy", 2), ("gz", 3)), 1)
+    widened = extended(cells, (("gz", 3), ("gy", 2), ("gx", 1)), 1)
     patches = jnp.stack(
         [
             jnp.transpose(

time: 115 us -> 120 us (1.043)
  other arithmetic: 5.08 us -> 9.44 us
  starting transfers between devices: 19 us -> 17.1 us
  waiting for transfers between devices: 22.7 us -> 24.5 us
    ppermute x2, starting transfers between devices: 5.69 us -> 1.92 us  [fold_halo(): lax.ppermute(tail, axis, [(i, (i + 1) % count) for i in range(count)])]
    concatenate x2 -> x3, other arithmetic: 1.24 us -> 4.99 us  [extended(): jnp.concatenate([lax.ppermute(tail, axis, [(i, (i + 1) % count) for i in...]
    ppermute x3, starting transfers between devices: 6.32 us -> 8.14 us  [extended(): lax.ppermute(tail, axis, [(i, (i + 1) % count) for i in range(count)])]
    ppermute x3, waiting for transfers between devices: 10 us -> 11.7 us  [extended(): lax.ppermute(head, axis, [((i + 1) % count, i) for i in range(count)])]
    unnamed x37 -> x41, local copies, waits for them, and re-layouts: 7.44 us -> 7.97 us
  transfers between devices with their start and end apart: 12 -> 12, of which waited for: 9 -> 7; matrix products, arithmetic and copies ran while one was open for 17% -> 17% of each run, Pallas kernels for 13% -> 13%
where the time goes in v17:
time: 120 us
  Pallas kernels  34.9 us (29%)
  local copies, waits for them, and re-layouts  32.7 us (27%)
  waiting for transfers between devices  24.5 us (20%)
  starting transfers between devices  17.1 us (14%)
  other arithmetic  9.44 us (8%)
    pallas_call x1, Pallas kernels, forward(): pl.pallas_call(lambda *refs: forward_kernel(rows, wide_y, *refs), grid=(p...  19.2 us
    pallas_call x1, Pallas kernels, allreduce(): pl.pallas_call(lambda *refs: allreduce_kernel(sizes, *refs), out_shape=ja...  15.7 us
    ppermute x3, waiting for transfers between devices, extended(): lax.ppermute(head, axis, [((i + 1) % count, i) for i in range(count)])  11.7 us
    ppermute x3, starting transfers between devices, extended(): lax.ppermute(tail, axis, [(i, (i + 1) % count) for i in range(count)])  8.14 us
    unnamed x41, local copies, waits for them, and re-layouts  7.97 us
    reshape x1, local copies, waits for them, and re-layouts, on_device(): patches = patches.reshape(cells_x * cells_y, chan_in * 27, cells_z)  7.53 us
    ppermute x2, waiting for transfers between devices, fold_halo(): lax.ppermute(head, axis, [((i + 1) % count, i) for i in range(count)])  7.14 us
    ppermute x3, waiting for transfers between devices, extended(): lax.ppermute(tail, axis, [(i, (i + 1) % count) for i in range(count)])  5.26 us
  transfers between devices with their start and end apart: 12, of which 7 were waited for; matrix products, arithmetic and copies ran while one was open for 17% of the time, Pallas kernels for 13%

profile of v17, /device:TPU:7, one launch (start us, length us, event | category | flops | bytes accessed | tf_op | source)
XLA Modules:
  0.0 119.6 jit_solution(18357599726288765799)
XLA Ops:
  0.6 1.2 fusion.33
  1.8 1.7 %collective-permute-start = (bf16[4,4,64,1]{3,2,1,0:T(8,128)(2,1)S(1)}, bf16[4,4,64,1]{3,2,1,0:T(8,128)(2,1)S(1)}, u32[]{:S(2)}, u32[]{:S(2)}) collective-permute-start(bf16[4,4,64,1]{3,2,1,0:T(8,128)(2,1)S(1)} %get-tuple-element.42), channel_id=1, source_target_pairs={{0,1},{1,0},{2,3},{3,2},{4,5},{5,4},{6,7},{7,6},{8,9},{9,8},{10,11... | collective-permute-start | bytes 6152 | tf_op jit(solution)/shard_map/ppermute | solution.py:22
  4.5 5.0 %collective-permute-done = bf16[4,4,64,1]{3,2,1,0:T(8,128)(2,1)S(1)} collective-permute-done((bf16[4,4,64,1]{3,2,1,0:T(8,128)(2,1)S(1)}, bf16[4,4,64,1]{3,2,1,0:T(8,128)(2,1)S(1)}, u32[]{:S(2)}, u32[]{:S(2)}) %collective-permute-start) | collective-permute-done | bytes 2080 | tf_op jit(solution)/shard_map/ppermute | solution.py:22
  9.4 5.6 %collective-permute-done.1 = bf16[4,4,64,1]{3,2,1,0:T(8,128)(2,1)S(1)} collective-permute-done((bf16[4,4,64,1]{3,2,1,0:T(8,128)(2,1)S(1)}, bf16[4,4,64,1]{3,2,1,0:T(8,128)(2,1)S(1)}, u32[]{:S(2)}, u32[]{:S(2)}) %collective-permute-start.1) | collective-permute-done | bytes 2080 | tf_op jit(solution)/shard_map/ppermute | solution.py:24
  16.0 1.4 %collective-permute-start.2 = (bf16[4,4,1,130]{3,2,1,0:T(2,128)(2,1)S(1)}, bf16[4,4,1,130]{3,2,1,0:T(2,128)(2,1)S(1)}, u32[]{:S(2)}, u32[]{:S(2)}) collective-permute-start(bf16[4,4,1,130]{3,2,1,0:T(2,128)(2,1)S(1)} %get-tuple-element.40), channel_id=1, source_target_pairs={{0,2},{2,4},{4,6},{6,0},{1,3},{3,5},{5,7},{7,1},{8,10},{10,12},{12... | collective-permute-start | bytes 12488 | tf_op jit(solution)/shard_map/ppermute | solution.py:22
  17.3 1.5 %collective-permute-start.3 = (bf16[4,4,1,130]{3,2,1,0:T(2,128)(2,1)S(1)}, bf16[4,4,1,130]{3,2,1,0:T(2,128)(2,1)S(1)}, u32[]{:S(2)}, u32[]{:S(2)}) collective-permute-start(bf16[4,4,1,130]{3,2,1,0:T(2,128)(2,1)S(1)} %get-tuple-element.41), channel_id=1, source_target_pairs={{2,0},{4,2},{6,4},{0,6},{3,1},{5,3},{7,5},{1,7},{10,8},{12,10},{14... | collective-permute-start | bytes 12488 | tf_op jit(solution)/shard_map/ppermute | solution.py:24
  19.5 2.2 %reshape.237.refs_6_ = bf16[32,4096]{1,0:T(8,128)(2,1)} reshape(bf16[32,2,32,64]{3,2,1,0:T(8,128)(2,1)} %param.7) | data formatting | bytes 524288 | tf_op jit(solution)/shard_map/reshape | solution.py:328
  23.2 1.3 %copy.76.refs_1_ = f32[32,1]{1,0:T(8,128)} copy(f32[32,1]{0,1:T(1,128)} %bitcast.228) | data formatting | bytes 256 | tf_op jit(solution)/shard_map/reshape | solution.py:331
  24.5 1.4 %pad.4 = bf16[3,3,3,8,32]{4,3,2,1,0:T(8,128)(2,1)} pad(bf16[3,3,3,4,32]{4,3,2,1,0:T(4,128)(2,1)} %bitcast.227, bf16[]{:T(256)} %constant.43.clone.1), padding=0_0x0_0x0_0x0_4x0_0 | pad | bytes 20738 | tf_op jit(solution)/shard_map/jit(_pad)/pad | solution.py:241
  26.0 1.1 pad_maximum_fusion.5
  27.1 5.1 %collective-permute-start.4 = (bf16[4,1,66,130]{3,2,1,0:T(8,128)(2,1)S(1)}, bf16[4,1,66,130]{3,2,1,0:T(8,128)(2,1)S(1)}, u32[]{:S(2)}, u32[]{:S(2)}) collective-permute-start(bf16[4,1,66,130]{3,2,1,0:T(8,128)(2,1)S(1)} %get-tuple-element.31), channel_id=1, source_target_pairs={{0,8},{8,16},{16,24},{24,32},{32,40},{40,48},{48,56},{56,64},{64,7... | collective-permute-start | bytes 205928 | tf_op jit(solution)/shard_map/ppermute | solution.py:22
  32.2 1.8 %pad_maximum_fusion.2 = (bf16[4,4,65,130]{3,2,1,0:T(8,128)(2,1)S(1)}, bf16[4,4,65,130]{3,2,1,0:T(8,128)(2,1)S(1)}) fusion(bf16[4,4,1,130]{3,2,1,0:T(2,128)(2,1)S(1)} %collective-permute-done.3, bf16[4,4,64,1]{3,2,1,0:T(8,128)(2,1)S(1)} %collective-permute-done.1, bf16[4,4,64,128]{3,2,1,0:T(8,128)(2,1)} %param.4, ...), kind=kLoop, calls=%fused_computation.4 | loop fusion | flops 2163200 | bytes 815360 | tf_op jit(solution)/shard_map/concatenate | solution.py:20
  34.3 6.1 %collective-permute-done.5 = bf16[4,1,66,130]{3,2,1,0:T(8,128)(2,1)S(1)} collective-permute-done((bf16[4,1,66,130]{3,2,1,0:T(8,128)(2,1)S(1)}, bf16[4,1,66,130]{3,2,1,0:T(8,128)(2,1)S(1)}, u32[]{:S(2)}, u32[]{:S(2)}) %collective-permute-start.5) | collective-permute-done | bytes 68672 | tf_op jit(solution)/shard_map/ppermute | solution.py:24
  40.3 2.1 %pad_maximum_fusion.1 = (bf16[4,5,66,130]{3,2,1,0:T(8,128)(2,1)S(1)}, bf16[4,5,66,130]{3,2,1,0:T(8,128)(2,1)S(1)}) fusion(bf16[4,1,66,130]{3,2,1,0:T(8,128)(2,1)S(1)} %collective-permute-done.5, bf16[4,4,1,130]{3,2,1,0:T(2,128)(2,1)S(1)} %collective-permute-done.3, bf16[4,4,64,1]{3,2,1,0:T(8,128)(2,1)S(1)} %collective-permute-done.1, ...), kind=kLoop, calls=%fused_computation.2 | loop fusion | flops 4118400 | bytes 1098240 | tf_op jit(solution)/shard_map/concatenate | solution.py:20
  47.6 7.5 %copy.77.refs_5_ = bf16[256,108,128]{2,1,0:T(8,128)(2,1)} copy(bf16[256,108,128]{2,0,1:T(8,128)(2,1)S(1)} %bitcast.220) | data formatting | bytes 14155776 | tf_op jit(solution)/shard_map/reshape | solution.py:327
  55.2 19.2 %shard_map.75 = (bf16[32,4096]{1,0:T(8,128)(2,1)}, f32[32,108]{1,0:T(8,128)}, f32[32,1]{1,0:T(8,128)}, f32[396,4,128]{2,1,0:T(4,128)}, f32[396,4,128]{2,1,0:T(4,128)}) custom-call(bf16[32,108]{1,0:T(8,128)(2,1)} %copy.75.refs_0_, f32[32,1]{1,0:T(8,128)} %copy.76.refs_1_, f32[2,128,128]{2,1,0:T(8,128)} %add_convert_fusion.refs_2_, ...), custom_call_target="tpu_custom_call" | custom-call | tf_op jit(solution)/shard_map/pallas_call | solution.py:255
  74.3 1.9 %fusion.30 = (f32[6,66,4,1]{3,2,1,0:T(4,128)S(1)}, f32[6,66,4,1]{3,2,1,0:T(4,128)S(1)}) fusion(f32[6,66,4,128]{3,2,1,0:T(4,128)} %bitcast.223), kind=kLoop, calls=%fused_computation.89 | loop fusion | bytes 25344 | tf_op jit(solution)/shard_map/slice | solution.py:347
  78.6 1.9 %fusion.31 = (f32[6,66,4,1]{3,2,1,0:T(4,128)S(1)}, f32[6,66,4,1]{3,2,1,0:T(4,128)S(1)}) fusion(f32[6,66,4,128]{3,2,1,0:T(4,128)} %bitcast.221), kind=kLoop, calls=%fused_computation.90 | loop fusion | bytes 25344 | tf_op jit(solution)/shard_map/slice | solution.py:353
  83.6 2.7 %collective-permute-start.9 = (f32[6,1,4,128]{3,1,0,2:T(1,128)S(1)}, f32[6,1,4,128]{3,1,0,2:T(1,128)S(1)}, u32[]{:S(2)}, u32[]{:S(2)}) collective-permute-start(f32[6,1,4,128]{3,1,0,2:T(1,128)S(1)} %get-tuple-element.26), channel_id=1, source_target_pairs={{2,0},{4,2},{6,4},{0,6},{3,1},{5,3},{7,5},{1,7},{10,8},{12,10},{14... | collective-permute-start | bytes 36872 | tf_op jit(solution)/shard_map/ppermute | solution.py:294
  87.3 1.8 %collective-permute-start.10 = (f32[1,64,4,128]{3,1,0,2:T(8,128)S(1)}, f32[1,64,4,128]{3,1,0,2:T(8,128)S(1)}, u32[]{:S(2)}, u32[]{:S(2)}) collective-permute-start(f32[1,64,4,128]{3,1,0,2:T(8,128)S(1)} %get-tuple-element.37), channel_id=1, source_target_pairs={{0,8},{8,16},{16,24},{24,32},{32,40},{40,48},{48,56},{56,64},{64,7... | collective-permute-start | bytes 393224 | tf_op jit(solution)/shard_map/ppermute | solution.py:293
  89.7 15.7 %shard_map.76 = f32[32,128]{1,0:T(8,128)} custom-call(f32[32,128]{1,0:T(8,128)} %maximum_maximum_fusion.2.refs_0_), custom_call_target="tpu_custom_call" | custom-call | tf_op jit(solution)/shard_map/pallas_call | solution.py:113
  106.9 2.3 %reshape.238 = bf16[32,2,32,64]{3,2,1,0:T(8,128)(2,1)} reshape(bf16[32,4096]{1,0:T(8,128)(2,1)} %get-tuple-element.9) | data formatting | bytes 524288 | tf_op jit(solution)/shard_map/reshape | solution.py:333
  109.2 1.4 %slice_reduce_fusion = f32[32]{0:T(128)} fusion(f32[32,128]{1,0:T(8,128)} %shard_map.76), kind=kLoop, calls=%fused_computation.79 | loop fusion | bytes 256 | tf_op jit(solution)/shard_map/slice | solution.py:343
  111.8 6.9 %collective-permute-done.11 = f32[1,64,4,128]{3,1,0,2:T(8,128)S(1)} collective-permute-done((f32[1,64,4,128]{3,1,0,2:T(8,128)S(1)}, f32[1,64,4,128]{3,1,0,2:T(8,128)S(1)}, u32[]{:S(2)}, u32[]{:S(2)}) %collective-permute-start.11) | collective-permute-done | bytes 131104 | tf_op jit(solution)/shard_map/ppermute | solution.py:294
  (87 shorter events, 19.9 us)
Async XLA Ops:
  1.8 7.6 %collective-permute-start = (bf16[4,4,64,1]{3,2,1,0:T(8,128)(2,1)S(1)}, bf16[4,4,64,1]{3,2,1,0:T(8,128)(2,1)S(1)}, u32[]{:S(2)}, u32[]{:S(2)}) collective-permute-start(bf16[4,4,64,1]{3,2,1,0:T(8,128)(2,1)S(1)} %get-tuple-element.42), channel_id=1, source_target_pairs={{0,1},{1,0},{2,3},{3,2},{4,5},{5,4},{6,7},{7,6},{8,9},{9,8},{10,11... | collective-permute-start | bytes 6152 | tf_op jit(solution)/shard_map/ppermute | solution.py:22
  3.5 11.5 %collective-permute-start.1 = (bf16[4,4,64,1]{3,2,1,0:T(8,128)(2,1)S(1)}, bf16[4,4,64,1]{3,2,1,0:T(8,128)(2,1)S(1)}, u32[]{:S(2)}, u32[]{:S(2)}) collective-permute-start(bf16[4,4,64,1]{3,2,1,0:T(8,128)(2,1)S(1)} %get-tuple-element.43), channel_id=1, source_target_pairs={{1,0},{0,1},{3,2},{2,3},{5,4},{4,5},{7,6},{6,7},{9,8},{8,9},{11,10... | collective-permute-start | bytes 6152 | tf_op jit(solution)/shard_map/ppermute | solution.py:24
  3.8 40.9 %copy-start = (bf16[4,4,64,128]{3,2,1,0:T(8,128)(2,1)S(1)}, bf16[4,4,64,128]{3,2,1,0:T(8,128)(2,1)}, u32[]{:S(2)}) copy-start(bf16[4,4,64,128]{3,2,1,0:T(8,128)(2,1)} %param.4) | copy-start | bytes 786436
  16.0 10.0 %collective-permute-start.2 = (bf16[4,4,1,130]{3,2,1,0:T(2,128)(2,1)S(1)}, bf16[4,4,1,130]{3,2,1,0:T(2,128)(2,1)S(1)}, u32[]{:S(2)}, u32[]{:S(2)}) collective-permute-start(bf16[4,4,1,130]{3,2,1,0:T(2,128)(2,1)S(1)} %get-tuple-element.40), channel_id=1, source_target_pairs={{0,2},{2,4},{4,6},{6,0},{1,3},{3,5},{5,7},{7,1},{8,10},{10,12},{12... | collective-permute-start | bytes 12488 | tf_op jit(solution)/shard_map/ppermute | solution.py:22
  17.3 8.6 %collective-permute-start.3 = (bf16[4,4,1,130]{3,2,1,0:T(2,128)(2,1)S(1)}, bf16[4,4,1,130]{3,2,1,0:T(2,128)(2,1)S(1)}, u32[]{:S(2)}, u32[]{:S(2)}) collective-permute-start(bf16[4,4,1,130]{3,2,1,0:T(2,128)(2,1)S(1)} %get-tuple-element.41), channel_id=1, source_target_pairs={{2,0},{4,2},{6,4},{0,6},{3,1},{5,3},{7,5},{1,7},{10,8},{12,10},{14... | collective-permute-start | bytes 12488 | tf_op jit(solution)/shard_map/ppermute | solution.py:24
  27.1 7.2 %collective-permute-start.4 = (bf16[4,1,66,130]{3,2,1,0:T(8,128)(2,1)S(1)}, bf16[4,1,66,130]{3,2,1,0:T(8,128)(2,1)S(1)}, u32[]{:S(2)}, u32[]{:S(2)}) collective-permute-start(bf16[4,1,66,130]{3,2,1,0:T(8,128)(2,1)S(1)} %get-tuple-element.31), channel_id=1, source_target_pairs={{0,8},{8,16},{16,24},{24,32},{32,40},{40,48},{48,56},{56,64},{64,7... | collective-permute-start | bytes 205928 | tf_op jit(solution)/shard_map/ppermute | solution.py:22
  32.2 8.2 %collective-permute-start.5 = (bf16[4,1,66,130]{3,2,1,0:T(8,128)(2,1)S(1)}, bf16[4,1,66,130]{3,2,1,0:T(8,128)(2,1)S(1)}, u32[]{:S(2)}, u32[]{:S(2)}) collective-permute-start(bf16[4,1,66,130]{3,2,1,0:T(8,128)(2,1)S(1)} %get-tuple-element.30), channel_id=1, source_target_pairs={{8,0},{16,8},{24,16},{32,24},{40,32},{48,40},{56,48},{64,56},{72,6... | collective-permute-start | bytes 205928 | tf_op jit(solution)/shard_map/ppermute | solution.py:24
  74.3 6.2 %copy-start.1 = (f32[396,4,128]{2,1,0:T(4,128)S(1)}, f32[396,4,128]{2,1,0:T(4,128)}, u32[]{:S(2)}) copy-start(f32[396,4,128]{2,1,0:T(4,128)} %get-tuple-element.12) | copy-start | bytes 2433028
  76.6 5.2 %collective-permute-start.6 = (f32[6,66,4,1]{1,2,3,0:T(4,128)S(1)}, f32[6,66,4,1]{1,2,3,0:T(4,128)S(1)}, u32[]{:S(2)}, u32[]{:S(2)}) collective-permute-start(f32[6,66,4,1]{1,2,3,0:T(4,128)S(1)} %copy.88), channel_id=1, source_target_pairs={{0,1},{1,0},{2,3},{3,2},{4,5},{5,4},{6,7},{7,6},{8,9},{9,8},{10,11... | collective-permute-start | bytes 19016 | tf_op jit(solution)/shard_map/ppermute | solution.py:349
  77.8 4.5 %collective-permute-start.7 = (f32[6,66,4,1]{1,2,3,0:T(4,128)S(1)}, f32[6,66,4,1]{1,2,3,0:T(4,128)S(1)}, u32[]{:S(2)}, u32[]{:S(2)}) collective-permute-start(f32[6,66,4,1]{1,2,3,0:T(4,128)S(1)} %copy.91), channel_id=1, source_target_pairs={{1,0},{0,1},{3,2},{2,3},{5,4},{4,5},{7,6},{6,7},{9,8},{8,9},{11,10... | collective-permute-start | bytes 19016 | tf_op jit(solution)/shard_map/ppermute | solution.py:350
  81.7 7.4 %copy-start.3 = (f32[32,108]{1,0:T(8,128)S(1)}, f32[32,108]{1,0:T(8,128)}, u32[]{:S(2)}) copy-start(f32[32,108]{1,0:T(8,128)} %get-tuple-element.10) | copy-start | bytes 41476
  81.7 7.4 %copy-start.4 = (f32[32,1]{1,0:T(8,128)S(1)}, f32[32,1]{1,0:T(8,128)}, u32[]{:S(2)}) copy-start(f32[32,1]{1,0:T(8,128)} %get-tuple-element.11) | copy-start | bytes 388
  82.9 3.8 %collective-permute-start.8 = (f32[6,1,4,128]{3,1,0,2:T(1,128)S(1)}, f32[6,1,4,128]{3,1,0,2:T(1,128)S(1)}, u32[]{:S(2)}, u32[]{:S(2)}) collective-permute-start(f32[6,1,4,128]{3,1,0,2:T(1,128)S(1)} %get-tuple-element.27), channel_id=1, source_target_pairs={{0,2},{2,4},{4,6},{6,0},{1,3},{3,5},{5,7},{7,1},{8,10},{10,12},{12... | collective-permute-start | bytes 36872 | tf_op jit(solution)/shard_map/ppermute | solution.py:293
  83.6 3.5 %collective-permute-start.9 = (f32[6,1,4,128]{3,1,0,2:T(1,128)S(1)}, f32[6,1,4,128]{3,1,0,2:T(1,128)S(1)}, u32[]{:S(2)}, u32[]{:S(2)}) collective-permute-start(f32[6,1,4,128]{3,1,0,2:T(1,128)S(1)} %get-tuple-element.26), channel_id=1, source_target_pairs={{2,0},{4,2},{6,4},{0,6},{3,1},{5,3},{7,5},{1,7},{10,8},{12,10},{14... | collective-permute-start | bytes 36872 | tf_op jit(solution)/shard_map/ppermute | solution.py:294
  87.3 24.5 %collective-permute-start.10 = (f32[1,64,4,128]{3,1,0,2:T(8,128)S(1)}, f32[1,64,4,128]{3,1,0,2:T(8,128)S(1)}, u32[]{:S(2)}, u32[]{:S(2)}) collective-permute-start(f32[1,64,4,128]{3,1,0,2:T(8,128)S(1)} %get-tuple-element.37), channel_id=1, source_target_pairs={{0,8},{8,16},{16,24},{24,32},{32,40},{40,48},{48,56},{56,64},{64,7... | collective-permute-start | bytes 393224 | tf_op jit(solution)/shard_map/ppermute | solution.py:293
  110.6 8.1 %collective-permute-start.11 = (f32[1,64,4,128]{3,1,0,2:T(8,128)S(1)}, f32[1,64,4,128]{3,1,0,2:T(8,128)S(1)}, u32[]{:S(2)}, u32[]{:S(2)}) collective-permute-start(f32[1,64,4,128]{3,1,0,2:T(8,128)S(1)} %get-tuple-element.36), channel_id=1, source_target_pairs={{8,0},{16,8},{24,16},{32,24},{40,32},{48,40},{56,48},{64,56},{72,6... | collective-permute-start | bytes 393224 | tf_op jit(solution)/shard_map/ppermute | solution.py:294
  118.8 0.8 copy-start.2

commit v18 on v14

--- a/solution.py
+++ b/solution.py
@@ -216,13 +216,15 @@
         wg_acc[...] += wg
         bg_acc[...] += jnp.sum(bg, axis=1, keepdims=True)
         for m in range(pieces):
-            pooled = jnp.dot(
-                totals[2 * m], q_ref[0], preferred_element_type=jnp.float32,
-                precision=lax.Precision.HIGHEST,
-            ) + jnp.dot(
-                totals[2 * m + 1], q_ref[1], preferred_element_type=jnp.float32,
-                precision=lax.Precision.HIGHEST,
-            )
+            pooled = None
+            for half in range(2):
+                value = totals[2 * m + half]
+                high = value.astype(jnp.bfloat16)
+                low = (value - high.astype(jnp.float32)).astype(jnp.bfloat16)
+                both = jnp.concatenate([high, low], axis=0)
+                part = jnp.dot(both, q_ref[half], preferred_element_type=jnp.float32)
+                part = part[: value.shape[0]] + part[value.shape[0] :]
+                pooled = part if pooled is None else pooled + part
             at = pl.multiple_of((j * pieces + m) * rows, rows)
             pooled_ref[:, pl.ds(at, rows)] = (pooled * 0.125).astype(pooled_ref.dtype)
 
@@ -245,7 +247,7 @@
     k = jnp.arange(rows)
     pool = jnp.stack(
         [(k[None, :] == z[:, None] // 2), (k[None, :] == half + z[:, None] // 2)]
-    ).astype(jnp.float32)
+    ).astype(jnp.bfloat16)
     spread = jnp.stack(
         [(z[None, :] // 2 == k[:, None]), (z[None, :] // 2 + half == k[:, None])]
     ).astype(jnp.bfloat16)

time: 115 us -> 112 us (0.974)
  Pallas kernels: 34.5 us -> 31.7 us
    pallas_call x1, Pallas kernels: 19.2 us -> 16.4 us  [forward(): pl.pallas_call(lambda *refs: forward_kernel(rows, wide_y, *refs), grid=(p...]
  transfers between devices with their start and end apart: 12 -> 12, of which waited for: 9 -> 9; matrix products, arithmetic and copies ran while one was open for 17% -> 18% of each run, Pallas kernels for 13% -> 14%
where the time goes in v18:
time: 112 us
  local copies, waits for them, and re-layouts  32.1 us (29%)
  Pallas kernels  31.7 us (28%)
  waiting for transfers between devices  22.7 us (20%)
  starting transfers between devices  19 us (17%)
  other arithmetic  5.06 us (5%)
    pallas_call x1, Pallas kernels, forward(): pl.pallas_call(lambda *refs: forward_kernel(rows, wide_y, *refs), grid=(p...  16.4 us
    pallas_call x1, Pallas kernels, allreduce(): pl.pallas_call(lambda *refs: allreduce_kernel(sizes, *refs), out_shape=ja...  15.4 us
    ppermute x3, waiting for transfers between devices, extended(): lax.ppermute(head, axis, [((i + 1) % count, i) for i in range(count)])  10 us
    reshape x1, local copies, waits for them, and re-layouts, on_device(): patches = patches.reshape(cells_x * cells_y, chan_in * 27, cells_z)  7.54 us
    unnamed x37, local copies, waits for them, and re-layouts  7.44 us
    ppermute x2, waiting for transfers between devices, fold_halo(): lax.ppermute(head, axis, [((i + 1) % count, i) for i in range(count)])  7.15 us
    ppermute x3, starting transfers between devices, extended(): lax.ppermute(tail, axis, [(i, (i + 1) % count) for i in range(count)])  6.32 us
    ppermute x2, starting transfers between devices, fold_halo(): lax.ppermute(tail, axis, [(i, (i + 1) % count) for i in range(count)])  5.7 us
  transfers between devices with their start and end apart: 12, of which 9 were waited for; matrix products, arithmetic and copies ran while one was open for 18% of the time, Pallas kernels for 14%

profile of v18, /device:TPU:7, one launch (start us, length us, event | category | flops | bytes accessed | tf_op | source)
XLA Modules:
  0.0 111.6 jit_solution(3558384791078283938)
XLA Ops:
  1.6 4.1 %collective-permute-start = (bf16[4,1,64,128]{3,2,1,0:T(8,128)(2,1)S(1)}, bf16[4,1,64,128]{3,2,1,0:T(8,128)(2,1)S(1)}, u32[]{:S(2)}, u32[]{:S(2)}) collective-permute-start(bf16[4,1,64,128]{3,2,1,0:T(8,128)(2,1)S(1)} %get-tuple-element.41), channel_id=1, source_target_pairs={{0,8},{8,16},{16,24},{24,32},{32,40},{40,48},{48,56},{56,64},{64,7... | collective-permute-start | bytes 196616 | tf_op jit(solution)/shard_map/ppermute | solution.py:22
  5.9 1.1 %collective-permute-done = bf16[4,1,64,128]{3,2,1,0:T(8,128)(2,1)S(1)} collective-permute-done((bf16[4,1,64,128]{3,2,1,0:T(8,128)(2,1)S(1)}, bf16[4,1,64,128]{3,2,1,0:T(8,128)(2,1)S(1)}, u32[]{:S(2)}, u32[]{:S(2)}) %collective-permute-start) | collective-permute-done | bytes 65568 | tf_op jit(solution)/shard_map/ppermute | solution.py:22
  8.0 5.0 %collective-permute-done.1 = bf16[4,1,64,128]{3,2,1,0:T(8,128)(2,1)S(1)} collective-permute-done((bf16[4,1,64,128]{3,2,1,0:T(8,128)(2,1)S(1)}, bf16[4,1,64,128]{3,2,1,0:T(8,128)(2,1)S(1)}, u32[]{:S(2)}, u32[]{:S(2)}) %collective-permute-start.1) | collective-permute-done | bytes 65568 | tf_op jit(solution)/shard_map/ppermute | solution.py:24
  13.1 1.4 %collective-permute-start.2 = (bf16[4,6,1,128]{3,2,1,0:T(2,128)(2,1)S(1)}, bf16[4,6,1,128]{3,2,1,0:T(2,128)(2,1)S(1)}, u32[]{:S(2)}, u32[]{:S(2)}) collective-permute-start(bf16[4,6,1,128]{3,2,1,0:T(2,128)(2,1)S(1)} %get-tuple-element.38), channel_id=1, source_target_pairs={{0,2},{2,4},{4,6},{6,0},{1,3},{3,5},{5,7},{7,1},{8,10},{10,12},{12... | collective-permute-start | bytes 18440 | tf_op jit(solution)/shard_map/ppermute | solution.py:22
  14.4 1.5 %collective-permute-start.3 = (bf16[4,6,1,128]{3,2,1,0:T(2,128)(2,1)S(1)}, bf16[4,6,1,128]{3,2,1,0:T(2,128)(2,1)S(1)}, u32[]{:S(2)}, u32[]{:S(2)}) collective-permute-start(bf16[4,6,1,128]{3,2,1,0:T(2,128)(2,1)S(1)} %get-tuple-element.39), channel_id=1, source_target_pairs={{2,0},{4,2},{6,4},{0,6},{3,1},{5,3},{7,5},{1,7},{10,8},{12,10},{14... | collective-permute-start | bytes 18440 | tf_op jit(solution)/shard_map/ppermute | solution.py:24
  19.8 2.2 %reshape.237.refs_6_ = bf16[32,4096]{1,0:T(8,128)(2,1)} reshape(bf16[32,2,32,64]{3,2,1,0:T(8,128)(2,1)} %param.7) | data formatting | bytes 524288 | tf_op jit(solution)/shard_map/reshape | solution.py:330
  23.5 1.3 %copy.76.refs_1_ = f32[32,1]{1,0:T(8,128)} copy(f32[32,1]{0,1:T(1,128)} %bitcast.228) | data formatting | bytes 256 | tf_op jit(solution)/shard_map/reshape | solution.py:333
  24.9 1.4 %pad.4 = bf16[3,3,3,8,32]{4,3,2,1,0:T(8,128)(2,1)} pad(bf16[3,3,3,4,32]{4,3,2,1,0:T(4,128)(2,1)} %bitcast.227, bf16[]{:T(256)} %constant.43.clone.1), padding=0_0x0_0x0_0x0_4x0_0 | pad | bytes 20738 | tf_op jit(solution)/shard_map/jit(_pad)/pad | solution.py:243
  26.3 3.7 %collective-permute-done.4 = bf16[4,6,66,1]{3,2,1,0:T(8,128)(2,1)S(1)} collective-permute-done((bf16[4,6,66,1]{3,2,1,0:T(8,128)(2,1)S(1)}, bf16[4,6,66,1]{3,2,1,0:T(8,128)(2,1)S(1)}, u32[]{:S(2)}, u32[]{:S(2)}) %collective-permute-start.4) | collective-permute-done | bytes 3200 | tf_op jit(solution)/shard_map/ppermute | solution.py:22
  30.0 4.7 %collective-permute-done.5 = bf16[4,6,66,1]{3,2,1,0:T(8,128)(2,1)S(1)} collective-permute-done((bf16[4,6,66,1]{3,2,1,0:T(8,128)(2,1)S(1)}, bf16[4,6,66,1]{3,2,1,0:T(8,128)(2,1)S(1)}, u32[]{:S(2)}, u32[]{:S(2)}) %collective-permute-start.5) | collective-permute-done | bytes 3200 | tf_op jit(solution)/shard_map/ppermute | solution.py:24
  34.7 1.1 pad_maximum_fusion
  39.7 7.5 %copy.77.refs_5_ = bf16[256,108,128]{2,1,0:T(8,128)(2,1)} copy(bf16[256,108,128]{2,0,1:T(8,128)(2,1)S(1)} %bitcast.220) | data formatting | bytes 14155776 | tf_op jit(solution)/shard_map/reshape | solution.py:329
  47.3 16.4 %shard_map.75 = (bf16[32,4096]{1,0:T(8,128)(2,1)}, f32[32,108]{1,0:T(8,128)}, f32[32,1]{1,0:T(8,128)}, f32[396,4,128]{2,1,0:T(4,128)}, f32[396,4,128]{2,1,0:T(4,128)}) custom-call(bf16[32,108]{1,0:T(8,128)(2,1)} %copy.75.refs_0_, f32[32,1]{1,0:T(8,128)} %copy.76.refs_1_, bf16[2,128,128]{2,1,0:T(8,128)(2,1)} %add_convert_fusion.refs_2_, ...), custom_call_target="tpu_custom_call" | custom-call | tf_op jit(solution)/shard_map/pallas_call | solution.py:257
  63.6 1.9 %fusion.40 = (f32[6,66,4,1]{3,2,1,0:T(4,128)S(1)}, f32[6,66,4,1]{3,2,1,0:T(4,128)S(1)}) fusion(f32[6,66,4,128]{3,2,1,0:T(4,128)} %bitcast.223), kind=kLoop, calls=%fused_computation.97 | loop fusion | bytes 25344 | tf_op jit(solution)/shard_map/slice | solution.py:349
  65.9 1.7 %collective-permute-start.6 = (f32[6,66,4,1]{1,2,3,0:T(4,128)S(1)}, f32[6,66,4,1]{1,2,3,0:T(4,128)S(1)}, u32[]{:S(2)}, u32[]{:S(2)}) collective-permute-start(f32[6,66,4,1]{1,2,3,0:T(4,128)S(1)} %copy.88), channel_id=1, source_target_pairs={{0,1},{1,0},{2,3},{3,2},{4,5},{5,4},{6,7},{7,6},{8,9},{9,8},{10,11... | collective-permute-start | bytes 19016 | tf_op jit(solution)/shard_map/ppermute | solution.py:351
  68.1 1.9 %fusion.41 = (f32[6,66,4,1]{3,2,1,0:T(4,128)S(1)}, f32[6,66,4,1]{3,2,1,0:T(4,128)S(1)}) fusion(f32[6,66,4,128]{3,2,1,0:T(4,128)} %bitcast.221), kind=kLoop, calls=%fused_computation.98 | loop fusion | bytes 25344 | tf_op jit(solution)/shard_map/slice | solution.py:355
  72.4 1.4 %collective-permute-start.8 = (f32[6,1,4,128]{3,1,0,2:T(1,128)S(1)}, f32[6,1,4,128]{3,1,0,2:T(1,128)S(1)}, u32[]{:S(2)}, u32[]{:S(2)}) collective-permute-start(f32[6,1,4,128]{3,1,0,2:T(1,128)S(1)} %get-tuple-element.27), channel_id=1, source_target_pairs={{0,2},{2,4},{4,6},{6,0},{1,3},{3,5},{5,7},{7,1},{8,10},{10,12},{12... | collective-permute-start | bytes 36872 | tf_op jit(solution)/shard_map/ppermute | solution.py:295
  74.3 1.4 %collective-permute-start.9 = (f32[6,1,4,128]{3,1,0,2:T(1,128)S(1)}, f32[6,1,4,128]{3,1,0,2:T(1,128)S(1)}, u32[]{:S(2)}, u32[]{:S(2)}) collective-permute-start(f32[6,1,4,128]{3,1,0,2:T(1,128)S(1)} %get-tuple-element.26), channel_id=1, source_target_pairs={{2,0},{4,2},{6,4},{0,6},{3,1},{5,3},{7,5},{1,7},{10,8},{12,10},{14... | collective-permute-start | bytes 36872 | tf_op jit(solution)/shard_map/ppermute | solution.py:296
  77.1 4.3 %collective-permute-start.10 = (f32[1,64,4,128]{3,1,0,2:T(8,128)S(1)}, f32[1,64,4,128]{3,1,0,2:T(8,128)S(1)}, u32[]{:S(2)}, u32[]{:S(2)}) collective-permute-start(f32[1,64,4,128]{3,1,0,2:T(8,128)S(1)} %get-tuple-element.33), channel_id=1, source_target_pairs={{0,8},{8,16},{16,24},{24,32},{32,40},{40,48},{48,56},{56,64},{64,7... | collective-permute-start | bytes 393224 | tf_op jit(solution)/shard_map/ppermute | solution.py:295
  82.1 15.4 %shard_map.76 = f32[32,128]{1,0:T(8,128)} custom-call(f32[32,128]{1,0:T(8,128)} %maximum_maximum_fusion.1.refs_0_), custom_call_target="tpu_custom_call" | custom-call | tf_op jit(solution)/shard_map/pallas_call | solution.py:113
  99.0 2.3 %reshape.238 = bf16[32,2,32,64]{3,2,1,0:T(8,128)(2,1)} reshape(bf16[32,4096]{1,0:T(8,128)(2,1)} %get-tuple-element.9) | data formatting | bytes 524288 | tf_op jit(solution)/shard_map/reshape | solution.py:335
  101.2 1.4 %slice_reduce_fusion = f32[32]{0:T(128)} fusion(f32[32,128]{1,0:T(8,128)} %shard_map.76), kind=kLoop, calls=%fused_computation.87 | loop fusion | bytes 256 | tf_op jit(solution)/shard_map/slice | solution.py:345
  102.7 1.5 %collective-permute-start.11 = (f32[1,64,4,128]{3,1,0,2:T(8,128)S(1)}, f32[1,64,4,128]{3,1,0,2:T(8,128)S(1)}, u32[]{:S(2)}, u32[]{:S(2)}) collective-permute-start(f32[1,64,4,128]{3,1,0,2:T(8,128)S(1)} %get-tuple-element.32), channel_id=1, source_target_pairs={{8,0},{16,8},{24,16},{32,24},{40,32},{48,40},{56,48},{64,56},{72,6... | collective-permute-start | bytes 393224 | tf_op jit(solution)/shard_map/ppermute | solution.py:296
  104.2 6.6 %collective-permute-done.11 = f32[1,64,4,128]{3,1,0,2:T(8,128)S(1)} collective-permute-done((f32[1,64,4,128]{3,1,0,2:T(8,128)S(1)}, f32[1,64,4,128]{3,1,0,2:T(8,128)S(1)}, u32[]{:S(2)}, u32[]{:S(2)}) %collective-permute-start.11) | collective-permute-done | bytes 131104 | tf_op jit(solution)/shard_map/ppermute | solution.py:296
  (90 shorter events, 19.4 us)
Async XLA Ops:
  0.6 35.6 %copy-start.1 = (bf16[4,4,64,128]{3,2,1,0:T(8,128)(2,1)S(1)}, bf16[4,4,64,128]{3,2,1,0:T(8,128)(2,1)}, u32[]{:S(2)}) copy-start(bf16[4,4,64,128]{3,2,1,0:T(8,128)(2,1)} %param.4) | copy-start | bytes 786436
  1.6 5.5 %collective-permute-start = (bf16[4,1,64,128]{3,2,1,0:T(8,128)(2,1)S(1)}, bf16[4,1,64,128]{3,2,1,0:T(8,128)(2,1)S(1)}, u32[]{:S(2)}, u32[]{:S(2)}) collective-permute-start(bf16[4,1,64,128]{3,2,1,0:T(8,128)(2,1)S(1)} %get-tuple-element.41), channel_id=1, source_target_pairs={{0,8},{8,16},{16,24},{24,32},{32,40},{40,48},{48,56},{56,64},{64,7... | collective-permute-start | bytes 196616 | tf_op jit(solution)/shard_map/ppermute | solution.py:22
  5.7 7.3 %collective-permute-start.1 = (bf16[4,1,64,128]{3,2,1,0:T(8,128)(2,1)S(1)}, bf16[4,1,64,128]{3,2,1,0:T(8,128)(2,1)S(1)}, u32[]{:S(2)}, u32[]{:S(2)}) collective-permute-start(bf16[4,1,64,128]{3,2,1,0:T(8,128)(2,1)S(1)} %get-tuple-element.40), channel_id=1, source_target_pairs={{8,0},{16,8},{24,16},{32,24},{40,32},{48,40},{56,48},{64,56},{72,6... | collective-permute-start | bytes 196616 | tf_op jit(solution)/shard_map/ppermute | solution.py:24
  13.1 3.9 %collective-permute-start.2 = (bf16[4,6,1,128]{3,2,1,0:T(2,128)(2,1)S(1)}, bf16[4,6,1,128]{3,2,1,0:T(2,128)(2,1)S(1)}, u32[]{:S(2)}, u32[]{:S(2)}) collective-permute-start(bf16[4,6,1,128]{3,2,1,0:T(2,128)(2,1)S(1)} %get-tuple-element.38), channel_id=1, source_target_pairs={{0,2},{2,4},{4,6},{6,0},{1,3},{3,5},{5,7},{7,1},{8,10},{10,12},{12... | collective-permute-start | bytes 18440 | tf_op jit(solution)/shard_map/ppermute | solution.py:22
  14.4 2.8 %collective-permute-start.3 = (bf16[4,6,1,128]{3,2,1,0:T(2,128)(2,1)S(1)}, bf16[4,6,1,128]{3,2,1,0:T(2,128)(2,1)S(1)}, u32[]{:S(2)}, u32[]{:S(2)}) collective-permute-start(bf16[4,6,1,128]{3,2,1,0:T(2,128)(2,1)S(1)} %get-tuple-element.39), channel_id=1, source_target_pairs={{2,0},{4,2},{6,4},{0,6},{3,1},{5,3},{7,5},{1,7},{10,8},{12,10},{14... | collective-permute-start | bytes 18440 | tf_op jit(solution)/shard_map/ppermute | solution.py:24
  17.6 12.3 %collective-permute-start.4 = (bf16[4,6,66,1]{3,2,1,0:T(8,128)(2,1)S(1)}, bf16[4,6,66,1]{3,2,1,0:T(8,128)(2,1)S(1)}, u32[]{:S(2)}, u32[]{:S(2)}) collective-permute-start(bf16[4,6,66,1]{3,2,1,0:T(8,128)(2,1)S(1)} %get-tuple-element.35), channel_id=1, source_target_pairs={{0,1},{1,0},{2,3},{3,2},{4,5},{5,4},{6,7},{7,6},{8,9},{9,8},{10,11... | collective-permute-start | bytes 9512 | tf_op jit(solution)/shard_map/ppermute | solution.py:22
  18.5 16.2 %collective-permute-start.5 = (bf16[4,6,66,1]{3,2,1,0:T(8,128)(2,1)S(1)}, bf16[4,6,66,1]{3,2,1,0:T(8,128)(2,1)S(1)}, u32[]{:S(2)}, u32[]{:S(2)}) collective-permute-start(bf16[4,6,66,1]{3,2,1,0:T(8,128)(2,1)S(1)} %get-tuple-element.34), channel_id=1, source_target_pairs={{1,0},{0,1},{3,2},{2,3},{5,4},{4,5},{7,6},{6,7},{9,8},{8,9},{11,10... | collective-permute-start | bytes 9512 | tf_op jit(solution)/shard_map/ppermute | solution.py:24
  63.6 6.3 %copy-start = (f32[396,4,128]{2,1,0:T(4,128)S(1)}, f32[396,4,128]{2,1,0:T(4,128)}, u32[]{:S(2)}) copy-start(f32[396,4,128]{2,1,0:T(4,128)} %get-tuple-element.12) | copy-start | bytes 2433028
  65.9 5.4 %collective-permute-start.6 = (f32[6,66,4,1]{1,2,3,0:T(4,128)S(1)}, f32[6,66,4,1]{1,2,3,0:T(4,128)S(1)}, u32[]{:S(2)}, u32[]{:S(2)}) collective-permute-start(f32[6,66,4,1]{1,2,3,0:T(4,128)S(1)} %copy.88), channel_id=1, source_target_pairs={{0,1},{1,0},{2,3},{3,2},{4,5},{5,4},{6,7},{7,6},{8,9},{9,8},{10,11... | collective-permute-start | bytes 19016 | tf_op jit(solution)/shard_map/ppermute | solution.py:351
  68.0 3.8 %collective-permute-start.7 = (f32[6,66,4,1]{1,2,3,0:T(4,128)S(1)}, f32[6,66,4,1]{1,2,3,0:T(4,128)S(1)}, u32[]{:S(2)}, u32[]{:S(2)}) collective-permute-start(f32[6,66,4,1]{1,2,3,0:T(4,128)S(1)} %copy.91), channel_id=1, source_target_pairs={{1,0},{0,1},{3,2},{2,3},{5,4},{4,5},{7,6},{6,7},{9,8},{8,9},{11,10... | collective-permute-start | bytes 19016 | tf_op jit(solution)/shard_map/ppermute | solution.py:352
  71.2 10.2 %copy-start.3 = (f32[32,108]{1,0:T(8,128)S(1)}, f32[32,108]{1,0:T(8,128)}, u32[]{:S(2)}) copy-start(f32[32,108]{1,0:T(8,128)} %get-tuple-element.10) | copy-start | bytes 41476
  71.2 10.2 %copy-start.4 = (f32[32,1]{1,0:T(8,128)S(1)}, f32[32,1]{1,0:T(8,128)}, u32[]{:S(2)}) copy-start(f32[32,1]{1,0:T(8,128)} %get-tuple-element.11) | copy-start | bytes 388
  72.4 3.8 %collective-permute-start.8 = (f32[6,1,4,128]{3,1,0,2:T(1,128)S(1)}, f32[6,1,4,128]{3,1,0,2:T(1,128)S(1)}, u32[]{:S(2)}, u32[]{:S(2)}) collective-permute-start(f32[6,1,4,128]{3,1,0,2:T(1,128)S(1)} %get-tuple-element.27), channel_id=1, source_target_pairs={{0,2},{2,4},{4,6},{6,0},{1,3},{3,5},{5,7},{7,1},{8,10},{10,12},{12... | collective-permute-start | bytes 36872 | tf_op jit(solution)/shard_map/ppermute | solution.py:295
  74.3 2.6 %collective-permute-start.9 = (f32[6,1,4,128]{3,1,0,2:T(1,128)S(1)}, f32[6,1,4,128]{3,1,0,2:T(1,128)S(1)}, u32[]{:S(2)}, u32[]{:S(2)}) collective-permute-start(f32[6,1,4,128]{3,1,0,2:T(1,128)S(1)} %get-tuple-element.26), channel_id=1, source_target_pairs={{2,0},{4,2},{6,4},{0,6},{3,1},{5,3},{7,5},{1,7},{10,8},{12,10},{14... | collective-permute-start | bytes 36872 | tf_op jit(solution)/shard_map/ppermute | solution.py:296
  77.1 27.1 %collective-permute-start.10 = (f32[1,64,4,128]{3,1,0,2:T(8,128)S(1)}, f32[1,64,4,128]{3,1,0,2:T(8,128)S(1)}, u32[]{:S(2)}, u32[]{:S(2)}) collective-permute-start(f32[1,64,4,128]{3,1,0,2:T(8,128)S(1)} %get-tuple-element.33), channel_id=1, source_target_pairs={{0,8},{8,16},{16,24},{24,32},{32,40},{40,48},{48,56},{56,64},{64,7... | collective-permute-start | bytes 393224 | tf_op jit(solution)/shard_map/ppermute | solution.py:295
  102.7 8.1 %collective-permute-start.11 = (f32[1,64,4,128]{3,1,0,2:T(8,128)S(1)}, f32[1,64,4,128]{3,1,0,2:T(8,128)S(1)}, u32[]{:S(2)}, u32[]{:S(2)}) collective-permute-start(f32[1,64,4,128]{3,1,0,2:T(8,128)S(1)} %get-tuple-element.32), channel_id=1, source_target_pairs={{8,0},{16,8},{24,16},{32,24},{40,32},{48,40},{56,48},{64,56},{72,6... | collective-permute-start | bytes 393224 | tf_op jit(solution)/shard_map/ppermute | solution.py:296
  110.8 0.8 copy-start.2

commit v19 on v18

--- a/solution.py
+++ b/solution.py
@@ -182,7 +182,7 @@
             slope = leak_slope + (1.0 - leak_slope) * sigmoid
             delta = (slope * spread_all).astype(jnp.bfloat16)
             term = lax.dot_general(
-                delta, patch, (((1,), (1,)), ((), ())), preferred_element_type=jnp.float32
+                patch, delta, (((1,), (1,)), ((), ())), preferred_element_type=jnp.float32
             )
             wg = term if wg is None else wg + term
             part = delta.astype(jnp.float32)
@@ -259,7 +259,7 @@
         grid=(pairs,),
         out_shape=(
             jax.ShapeDtypeStruct(cot.shape, jnp.bfloat16),
-            jax.ShapeDtypeStruct((chan_out, taps), jnp.float32),
+            jax.ShapeDtypeStruct((taps, chan_out), jnp.float32),
             jax.ShapeDtypeStruct((chan_out, 1), jnp.float32),
             jax.ShapeDtypeStruct(acc_shape, jnp.float32),
             jax.ShapeDtypeStruct(acc_shape, jnp.float32),
@@ -275,13 +275,13 @@
         ],
         out_specs=(
             pl.BlockSpec((chan_out, cot.shape[1] // pairs), lambda p: (0, p)),
-            full((chan_out, taps)),
+            full((taps, chan_out)),
             full((chan_out, 1)),
             full(acc_shape),
             full(acc_shape),
         ),
         scratch_shapes=[
-            pltpu.VMEM((chan_out, taps), jnp.float32),
+            pltpu.VMEM((taps, chan_out), jnp.float32),
             pltpu.VMEM((chan_out, 1), jnp.float32),
         ],
     )(weight_mat, bias, pool, spread, spread_w, patches, cot)
@@ -333,6 +333,7 @@
         weight, bias.reshape(chan_out, 1), patches, cot, cells_x // 2, wide_x, wide_y
     )
     pooled = pooled.reshape(cotangent.shape)
+    weight_local = weight_local.T
     taps = chan_in * 27
     width = -(-(taps + 1) // 128) * 128
     partial = jnp.concatenate(

time: 112 us -> 113 us (level)
  no operation moved by 1% of the time
where the time goes in v19:
time: 113 us; the launch traced here: 112 us
  local copies, waits for them, and re-layouts  32.2 us (28%)
  Pallas kernels  32 us (28%)
  waiting for transfers between devices  22.7 us (20%)
  starting transfers between devices  19 us (17%)
  other arithmetic  5.07 us (4%)
    pallas_call x1, Pallas kernels, forward(): pl.pallas_call(lambda *refs: forward_kernel(rows, wide_y, *refs), grid=(p...  16.7 us
    pallas_call x1, Pallas kernels, allreduce(): pl.pallas_call(lambda *refs: allreduce_kernel(sizes, *refs), out_shape=ja...  15.4 us
    ppermute x3, waiting for transfers between devices, extended(): lax.ppermute(head, axis, [((i + 1) % count, i) for i in range(count)])  10 us
    reshape x1, local copies, waits for them, and re-layouts, on_device(): patches = patches.reshape(cells_x * cells_y, chan_in * 27, cells_z)  7.54 us
    unnamed x37, local copies, waits for them, and re-layouts  7.45 us
    ppermute x2, waiting for transfers between devices, fold_halo(): lax.ppermute(head, axis, [((i + 1) % count, i) for i in range(count)])  7.15 us
    ppermute x3, starting transfers between devices, extended(): lax.ppermute(tail, axis, [(i, (i + 1) % count) for i in range(count)])  6.32 us
    ppermute x2, starting transfers between devices, fold_halo(): lax.ppermute(tail, axis, [(i, (i + 1) % count) for i in range(count)])  5.7 us
  transfers between devices with their start and end apart: 12, of which 9 were waited for; matrix products, arithmetic and copies ran while one was open for 18% of the time, Pallas kernels for 14%

profile of v19, /device:TPU:7, one launch (start us, length us, event | category | flops | bytes accessed | tf_op | source)
XLA Modules:
  0.0 112.0 jit_solution(11507668651325231790)
XLA Ops:
  1.6 4.1 %collective-permute-start = (bf16[4,1,64,128]{3,2,1,0:T(8,128)(2,1)S(1)}, bf16[4,1,64,128]{3,2,1,0:T(8,128)(2,1)S(1)}, u32[]{:S(2)}, u32[]{:S(2)}) collective-permute-start(bf16[4,1,64,128]{3,2,1,0:T(8,128)(2,1)S(1)} %get-tuple-element.41), channel_id=1, source_target_pairs={{0,8},{8,16},{16,24},{24,32},{32,40},{40,48},{48,56},{56,64},{64,7... | collective-permute-start | bytes 196616 | tf_op jit(solution)/shard_map/ppermute | solution.py:22
  5.9 1.1 %collective-permute-done = bf16[4,1,64,128]{3,2,1,0:T(8,128)(2,1)S(1)} collective-permute-done((bf16[4,1,64,128]{3,2,1,0:T(8,128)(2,1)S(1)}, bf16[4,1,64,128]{3,2,1,0:T(8,128)(2,1)S(1)}, u32[]{:S(2)}, u32[]{:S(2)}) %collective-permute-start) | collective-permute-done | bytes 65568 | tf_op jit(solution)/shard_map/ppermute | solution.py:22
  8.0 5.0 %collective-permute-done.1 = bf16[4,1,64,128]{3,2,1,0:T(8,128)(2,1)S(1)} collective-permute-done((bf16[4,1,64,128]{3,2,1,0:T(8,128)(2,1)S(1)}, bf16[4,1,64,128]{3,2,1,0:T(8,128)(2,1)S(1)}, u32[]{:S(2)}, u32[]{:S(2)}) %collective-permute-start.1) | collective-permute-done | bytes 65568 | tf_op jit(solution)/shard_map/ppermute | solution.py:24
  13.1 1.4 %collective-permute-start.2 = (bf16[4,6,1,128]{3,2,1,0:T(2,128)(2,1)S(1)}, bf16[4,6,1,128]{3,2,1,0:T(2,128)(2,1)S(1)}, u32[]{:S(2)}, u32[]{:S(2)}) collective-permute-start(bf16[4,6,1,128]{3,2,1,0:T(2,128)(2,1)S(1)} %get-tuple-element.38), channel_id=1, source_target_pairs={{0,2},{2,4},{4,6},{6,0},{1,3},{3,5},{5,7},{7,1},{8,10},{10,12},{12... | collective-permute-start | bytes 18440 | tf_op jit(solution)/shard_map/ppermute | solution.py:22
  14.4 1.5 %collective-permute-start.3 = (bf16[4,6,1,128]{3,2,1,0:T(2,128)(2,1)S(1)}, bf16[4,6,1,128]{3,2,1,0:T(2,128)(2,1)S(1)}, u32[]{:S(2)}, u32[]{:S(2)}) collective-permute-start(bf16[4,6,1,128]{3,2,1,0:T(2,128)(2,1)S(1)} %get-tuple-element.39), channel_id=1, source_target_pairs={{2,0},{4,2},{6,4},{0,6},{3,1},{5,3},{7,5},{1,7},{10,8},{12,10},{14... | collective-permute-start | bytes 18440 | tf_op jit(solution)/shard_map/ppermute | solution.py:24
  19.8 2.2 %reshape.237.refs_6_ = bf16[32,4096]{1,0:T(8,128)(2,1)} reshape(bf16[32,2,32,64]{3,2,1,0:T(8,128)(2,1)} %param.7) | data formatting | bytes 524288 | tf_op jit(solution)/shard_map/reshape | solution.py:330
  23.5 1.3 %copy.78.refs_1_ = f32[32,1]{1,0:T(8,128)} copy(f32[32,1]{0,1:T(1,128)} %bitcast.230) | data formatting | bytes 256 | tf_op jit(solution)/shard_map/reshape | solution.py:333
  24.9 1.4 %pad.4 = bf16[3,3,3,8,32]{4,3,2,1,0:T(8,128)(2,1)} pad(bf16[3,3,3,4,32]{4,3,2,1,0:T(4,128)(2,1)} %bitcast.228, bf16[]{:T(256)} %constant.43.clone.1), padding=0_0x0_0x0_0x0_4x0_0 | pad | bytes 20738 | tf_op jit(solution)/shard_map/jit(_pad)/pad | solution.py:243
  26.3 3.6 %collective-permute-done.4 = bf16[4,6,66,1]{3,2,1,0:T(8,128)(2,1)S(1)} collective-permute-done((bf16[4,6,66,1]{3,2,1,0:T(8,128)(2,1)S(1)}, bf16[4,6,66,1]{3,2,1,0:T(8,128)(2,1)S(1)}, u32[]{:S(2)}, u32[]{:S(2)}) %collective-permute-start.4) | collective-permute-done | bytes 3200 | tf_op jit(solution)/shard_map/ppermute | solution.py:22
  30.0 4.7 %collective-permute-done.5 = bf16[4,6,66,1]{3,2,1,0:T(8,128)(2,1)S(1)} collective-permute-done((bf16[4,6,66,1]{3,2,1,0:T(8,128)(2,1)S(1)}, bf16[4,6,66,1]{3,2,1,0:T(8,128)(2,1)S(1)}, u32[]{:S(2)}, u32[]{:S(2)}) %collective-permute-start.5) | collective-permute-done | bytes 3200 | tf_op jit(solution)/shard_map/ppermute | solution.py:24
  34.7 1.1 pad_maximum_fusion
  39.7 7.5 %copy.79.refs_5_ = bf16[256,108,128]{2,1,0:T(8,128)(2,1)} copy(bf16[256,108,128]{2,0,1:T(8,128)(2,1)S(1)} %bitcast.221) | data formatting | bytes 14155776 | tf_op jit(solution)/shard_map/reshape | solution.py:329
  47.3 16.7 %shard_map.75 = (bf16[32,4096]{1,0:T(8,128)(2,1)}, f32[108,32]{1,0:T(8,128)}, f32[32,1]{1,0:T(8,128)}, f32[396,4,128]{2,1,0:T(4,128)}, f32[396,4,128]{2,1,0:T(4,128)}) custom-call(bf16[32,108]{1,0:T(8,128)(2,1)} %copy.77.refs_0_, f32[32,1]{1,0:T(8,128)} %copy.78.refs_1_, bf16[2,128,128]{2,1,0:T(8,128)(2,1)} %add_convert_fusion.refs_2_, ...), custom_call_target="tpu_custom_call" | custom-call | tf_op jit(solution)/shard_map/pallas_call | solution.py:257
  64.0 1.9 %fusion.40 = (f32[6,66,4,1]{3,2,1,0:T(4,128)S(1)}, f32[6,66,4,1]{3,2,1,0:T(4,128)S(1)}) fusion(f32[6,66,4,128]{3,2,1,0:T(4,128)} %bitcast.224), kind=kLoop, calls=%fused_computation.97 | loop fusion | bytes 25344 | tf_op jit(solution)/shard_map/slice | solution.py:350
  66.3 1.7 %collective-permute-start.6 = (f32[6,66,4,1]{1,2,3,0:T(4,128)S(1)}, f32[6,66,4,1]{1,2,3,0:T(4,128)S(1)}, u32[]{:S(2)}, u32[]{:S(2)}) collective-permute-start(f32[6,66,4,1]{1,2,3,0:T(4,128)S(1)} %copy.91), channel_id=1, source_target_pairs={{0,1},{1,0},{2,3},{3,2},{4,5},{5,4},{6,7},{7,6},{8,9},{9,8},{10,11... | collective-permute-start | bytes 19016 | tf_op jit(solution)/shard_map/ppermute | solution.py:352
  68.4 1.9 %fusion.41 = (f32[6,66,4,1]{3,2,1,0:T(4,128)S(1)}, f32[6,66,4,1]{3,2,1,0:T(4,128)S(1)}) fusion(f32[6,66,4,128]{3,2,1,0:T(4,128)} %bitcast.222), kind=kLoop, calls=%fused_computation.98 | loop fusion | bytes 25344 | tf_op jit(solution)/shard_map/slice | solution.py:356
  72.8 1.4 %collective-permute-start.8 = (f32[6,1,4,128]{3,1,0,2:T(1,128)S(1)}, f32[6,1,4,128]{3,1,0,2:T(1,128)S(1)}, u32[]{:S(2)}, u32[]{:S(2)}) collective-permute-start(f32[6,1,4,128]{3,1,0,2:T(1,128)S(1)} %get-tuple-element.27), channel_id=1, source_target_pairs={{0,2},{2,4},{4,6},{6,0},{1,3},{3,5},{5,7},{7,1},{8,10},{10,12},{12... | collective-permute-start | bytes 36872 | tf_op jit(solution)/shard_map/ppermute | solution.py:295
  74.7 1.4 %collective-permute-start.9 = (f32[6,1,4,128]{3,1,0,2:T(1,128)S(1)}, f32[6,1,4,128]{3,1,0,2:T(1,128)S(1)}, u32[]{:S(2)}, u32[]{:S(2)}) collective-permute-start(f32[6,1,4,128]{3,1,0,2:T(1,128)S(1)} %get-tuple-element.26), channel_id=1, source_target_pairs={{2,0},{4,2},{6,4},{0,6},{3,1},{5,3},{7,5},{1,7},{10,8},{12,10},{14... | collective-permute-start | bytes 36872 | tf_op jit(solution)/shard_map/ppermute | solution.py:296
  77.5 4.3 %collective-permute-start.10 = (f32[1,64,4,128]{3,1,0,2:T(8,128)S(1)}, f32[1,64,4,128]{3,1,0,2:T(8,128)S(1)}, u32[]{:S(2)}, u32[]{:S(2)}) collective-permute-start(f32[1,64,4,128]{3,1,0,2:T(8,128)S(1)} %get-tuple-element.33), channel_id=1, source_target_pairs={{0,8},{8,16},{16,24},{24,32},{32,40},{40,48},{48,56},{56,64},{64,7... | collective-permute-start | bytes 393224 | tf_op jit(solution)/shard_map/ppermute | solution.py:295
  82.5 15.4 %shard_map.76 = f32[32,128]{1,0:T(8,128)} custom-call(f32[32,128]{1,0:T(8,128)} %maximum_maximum_fusion.1.refs_0_), custom_call_target="tpu_custom_call" | custom-call | tf_op jit(solution)/shard_map/pallas_call | solution.py:113
  99.4 2.3 %reshape.238 = bf16[32,2,32,64]{3,2,1,0:T(8,128)(2,1)} reshape(bf16[32,4096]{1,0:T(8,128)(2,1)} %get-tuple-element.9) | data formatting | bytes 524288 | tf_op jit(solution)/shard_map/reshape | solution.py:335
  101.6 1.4 %slice_reduce_fusion = f32[32]{0:T(128)} fusion(f32[32,128]{1,0:T(8,128)} %shard_map.76), kind=kLoop, calls=%fused_computation.87 | loop fusion | bytes 256 | tf_op jit(solution)/shard_map/slice | solution.py:346
  103.1 1.5 %collective-permute-start.11 = (f32[1,64,4,128]{3,1,0,2:T(8,128)S(1)}, f32[1,64,4,128]{3,1,0,2:T(8,128)S(1)}, u32[]{:S(2)}, u32[]{:S(2)}) collective-permute-start(f32[1,64,4,128]{3,1,0,2:T(8,128)S(1)} %get-tuple-element.32), channel_id=1, source_target_pairs={{8,0},{16,8},{24,16},{32,24},{40,32},{48,40},{56,48},{64,56},{72,6... | collective-permute-start | bytes 393224 | tf_op jit(solution)/shard_map/ppermute | solution.py:296
  104.6 6.6 %collective-permute-done.11 = f32[1,64,4,128]{3,1,0,2:T(8,128)S(1)} collective-permute-done((f32[1,64,4,128]{3,1,0,2:T(8,128)S(1)}, f32[1,64,4,128]{3,1,0,2:T(8,128)S(1)}, u32[]{:S(2)}, u32[]{:S(2)}) %collective-permute-start.11) | collective-permute-done | bytes 131104 | tf_op jit(solution)/shard_map/ppermute | solution.py:296
  (91 shorter events, 19.5 us)
Async XLA Ops:
  0.6 35.6 %copy-start.1 = (bf16[4,4,64,128]{3,2,1,0:T(8,128)(2,1)S(1)}, bf16[4,4,64,128]{3,2,1,0:T(8,128)(2,1)}, u32[]{:S(2)}) copy-start(bf16[4,4,64,128]{3,2,1,0:T(8,128)(2,1)} %param.4) | copy-start | bytes 786436
  1.6 5.5 %collective-permute-start = (bf16[4,1,64,128]{3,2,1,0:T(8,128)(2,1)S(1)}, bf16[4,1,64,128]{3,2,1,0:T(8,128)(2,1)S(1)}, u32[]{:S(2)}, u32[]{:S(2)}) collective-permute-start(bf16[4,1,64,128]{3,2,1,0:T(8,128)(2,1)S(1)} %get-tuple-element.41), channel_id=1, source_target_pairs={{0,8},{8,16},{16,24},{24,32},{32,40},{40,48},{48,56},{56,64},{64,7... | collective-permute-start | bytes 196616 | tf_op jit(solution)/shard_map/ppermute | solution.py:22
  5.7 7.3 %collective-permute-start.1 = (bf16[4,1,64,128]{3,2,1,0:T(8,128)(2,1)S(1)}, bf16[4,1,64,128]{3,2,1,0:T(8,128)(2,1)S(1)}, u32[]{:S(2)}, u32[]{:S(2)}) collective-permute-start(bf16[4,1,64,128]{3,2,1,0:T(8,128)(2,1)S(1)} %get-tuple-element.40), channel_id=1, source_target_pairs={{8,0},{16,8},{24,16},{32,24},{40,32},{48,40},{56,48},{64,56},{72,6... | collective-permute-start | bytes 196616 | tf_op jit(solution)/shard_map/ppermute | solution.py:24
  13.1 3.9 %collective-permute-start.2 = (bf16[4,6,1,128]{3,2,1,0:T(2,128)(2,1)S(1)}, bf16[4,6,1,128]{3,2,1,0:T(2,128)(2,1)S(1)}, u32[]{:S(2)}, u32[]{:S(2)}) collective-permute-start(bf16[4,6,1,128]{3,2,1,0:T(2,128)(2,1)S(1)} %get-tuple-element.38), channel_id=1, source_target_pairs={{0,2},{2,4},{4,6},{6,0},{1,3},{3,5},{5,7},{7,1},{8,10},{10,12},{12... | collective-permute-start | bytes 18440 | tf_op jit(solution)/shard_map/ppermute | solution.py:22
  14.4 2.8 %collective-permute-start.3 = (bf16[4,6,1,128]{3,2,1,0:T(2,128)(2,1)S(1)}, bf16[4,6,1,128]{3,2,1,0:T(2,128)(2,1)S(1)}, u32[]{:S(2)}, u32[]{:S(2)}) collective-permute-start(bf16[4,6,1,128]{3,2,1,0:T(2,128)(2,1)S(1)} %get-tuple-element.39), channel_id=1, source_target_pairs={{2,0},{4,2},{6,4},{0,6},{3,1},{5,3},{7,5},{1,7},{10,8},{12,10},{14... | collective-permute-start | bytes 18440 | tf_op jit(solution)/shard_map/ppermute | solution.py:24
  17.6 12.3 %collective-permute-start.4 = (bf16[4,6,66,1]{3,2,1,0:T(8,128)(2,1)S(1)}, bf16[4,6,66,1]{3,2,1,0:T(8,128)(2,1)S(1)}, u32[]{:S(2)}, u32[]{:S(2)}) collective-permute-start(bf16[4,6,66,1]{3,2,1,0:T(8,128)(2,1)S(1)} %get-tuple-element.35), channel_id=1, source_target_pairs={{0,1},{1,0},{2,3},{3,2},{4,5},{5,4},{6,7},{7,6},{8,9},{9,8},{10,11... | collective-permute-start | bytes 9512 | tf_op jit(solution)/shard_map/ppermute | solution.py:22
  18.5 16.2 %collective-permute-start.5 = (bf16[4,6,66,1]{3,2,1,0:T(8,128)(2,1)S(1)}, bf16[4,6,66,1]{3,2,1,0:T(8,128)(2,1)S(1)}, u32[]{:S(2)}, u32[]{:S(2)}) collective-permute-start(bf16[4,6,66,1]{3,2,1,0:T(8,128)(2,1)S(1)} %get-tuple-element.34), channel_id=1, source_target_pairs={{1,0},{0,1},{3,2},{2,3},{5,4},{4,5},{7,6},{6,7},{9,8},{8,9},{11,10... | collective-permute-start | bytes 9512 | tf_op jit(solution)/shard_map/ppermute | solution.py:24
  64.0 6.3 %copy-start = (f32[396,4,128]{2,1,0:T(4,128)S(1)}, f32[396,4,128]{2,1,0:T(4,128)}, u32[]{:S(2)}) copy-start(f32[396,4,128]{2,1,0:T(4,128)} %get-tuple-element.12) | copy-start | bytes 2433028
  64.0 7.6 %copy-start.3 = (f32[108,32]{1,0:T(8,128)S(1)}, f32[108,32]{1,0:T(8,128)}, u32[]{:S(2)}) copy-start(f32[108,32]{1,0:T(8,128)} %get-tuple-element.10) | copy-start | bytes 41476
  66.3 5.4 %collective-permute-start.6 = (f32[6,66,4,1]{1,2,3,0:T(4,128)S(1)}, f32[6,66,4,1]{1,2,3,0:T(4,128)S(1)}, u32[]{:S(2)}, u32[]{:S(2)}) collective-permute-start(f32[6,66,4,1]{1,2,3,0:T(4,128)S(1)} %copy.91), channel_id=1, source_target_pairs={{0,1},{1,0},{2,3},{3,2},{4,5},{5,4},{6,7},{7,6},{8,9},{9,8},{10,11... | collective-permute-start | bytes 19016 | tf_op jit(solution)/shard_map/ppermute | solution.py:352
  68.3 3.8 %collective-permute-start.7 = (f32[6,66,4,1]{1,2,3,0:T(4,128)S(1)}, f32[6,66,4,1]{1,2,3,0:T(4,128)S(1)}, u32[]{:S(2)}, u32[]{:S(2)}) collective-permute-start(f32[6,66,4,1]{1,2,3,0:T(4,128)S(1)} %copy.94), channel_id=1, source_target_pairs={{1,0},{0,1},{3,2},{2,3},{5,4},{4,5},{7,6},{6,7},{9,8},{8,9},{11,10... | collective-permute-start | bytes 19016 | tf_op jit(solution)/shard_map/ppermute | solution.py:353
  71.5 10.3 %copy-start.4 = (f32[32,1]{1,0:T(8,128)S(1)}, f32[32,1]{1,0:T(8,128)}, u32[]{:S(2)}) copy-start(f32[32,1]{1,0:T(8,128)} %get-tuple-element.11) | copy-start | bytes 388
  72.8 3.8 %collective-permute-start.8 = (f32[6,1,4,128]{3,1,0,2:T(1,128)S(1)}, f32[6,1,4,128]{3,1,0,2:T(1,128)S(1)}, u32[]{:S(2)}, u32[]{:S(2)}) collective-permute-start(f32[6,1,4,128]{3,1,0,2:T(1,128)S(1)} %get-tuple-element.27), channel_id=1, source_target_pairs={{0,2},{2,4},{4,6},{6,0},{1,3},{3,5},{5,7},{7,1},{8,10},{10,12},{12... | collective-permute-start | bytes 36872 | tf_op jit(solution)/shard_map/ppermute | solution.py:295
  74.7 2.6 %collective-permute-start.9 = (f32[6,1,4,128]{3,1,0,2:T(1,128)S(1)}, f32[6,1,4,128]{3,1,0,2:T(1,128)S(1)}, u32[]{:S(2)}, u32[]{:S(2)}) collective-permute-start(f32[6,1,4,128]{3,1,0,2:T(1,128)S(1)} %get-tuple-element.26), channel_id=1, source_target_pairs={{2,0},{4,2},{6,4},{0,6},{3,1},{5,3},{7,5},{1,7},{10,8},{12,10},{14... | collective-permute-start | bytes 36872 | tf_op jit(solution)/shard_map/ppermute | solution.py:296
  77.5 27.1 %collective-permute-start.10 = (f32[1,64,4,128]{3,1,0,2:T(8,128)S(1)}, f32[1,64,4,128]{3,1,0,2:T(8,128)S(1)}, u32[]{:S(2)}, u32[]{:S(2)}) collective-permute-start(f32[1,64,4,128]{3,1,0,2:T(8,128)S(1)} %get-tuple-element.33), channel_id=1, source_target_pairs={{0,8},{8,16},{16,24},{24,32},{32,40},{40,48},{48,56},{56,64},{64,7... | collective-permute-start | bytes 393224 | tf_op jit(solution)/shard_map/ppermute | solution.py:295
  103.1 8.1 %collective-permute-start.11 = (f32[1,64,4,128]{3,1,0,2:T(8,128)S(1)}, f32[1,64,4,128]{3,1,0,2:T(8,128)S(1)}, u32[]{:S(2)}, u32[]{:S(2)}) collective-permute-start(f32[1,64,4,128]{3,1,0,2:T(8,128)S(1)} %get-tuple-element.32), channel_id=1, source_target_pairs={{8,0},{16,8},{24,16},{32,24},{40,32},{48,40},{56,48},{64,56},{72,6... | collective-permute-start | bytes 393224 | tf_op jit(solution)/shard_map/ppermute | solution.py:296
  111.2 0.8 copy-start.2

commit v20 on v18

--- a/solution.py
+++ b/solution.py
@@ -6,6 +6,7 @@
 from jax.sharding import PartitionSpec as P
 
 MESH = pl.DeviceIdType.MESH
+BLOCK_ROWS = 32
 AXES = ("gx", "gy", "gz")
 
 leak_slope = 0.3
@@ -128,7 +129,7 @@
     )(x)
 
 
-def forward_kernel(rows, wide_y, w_ref, b_ref, q_ref, u_ref, wt_ref, p_ref, cot_ref,
+def forward_kernel(rows, wide_y, w_ref, b_ref, q_ref, u_ref, wt_ref, ones_ref, p_ref, cot_ref,
                    pooled_ref, wg_ref, bg_ref, main_ref, edge_ref, wg_acc, bg_acc):
     step = pl.program_id(0)
     plane = p_ref.shape[0] // 2
@@ -149,7 +150,7 @@
     first = lane == 0
     last = lane == rows - 1
 
-    group = 32
+    group = BLOCK_ROWS
     pooled_rows = group // 2
     pieces = pooled_rows // 2
 
@@ -185,7 +186,7 @@
                 delta, patch, (((1,), (1,)), ((), ())), preferred_element_type=jnp.float32
             )
             wg = term if wg is None else wg + term
-            part = delta.astype(jnp.float32)
+            part = jnp.dot(delta, ones_ref[...], preferred_element_type=jnp.float32)
             bg = part if bg is None else bg + part
             spreads.append(jnp.dot(spread_w, delta, preferred_element_type=jnp.float32))
         acc_main = {}
@@ -214,7 +215,7 @@
             main_ref[out] += value[: main_ref.shape[1]]
             edge_ref[out] += acc_edge[dx, dy][: edge_ref.shape[1]]
         wg_acc[...] += wg
-        bg_acc[...] += jnp.sum(bg, axis=1, keepdims=True)
+        bg_acc[...] += bg[:, :1]
         for m in range(pieces):
             pooled = None
             for half in range(2):
@@ -270,6 +271,7 @@
             full((2, rows, rows)),
             full((2, rows, rows)),
             full((27 * slots, chan_out)),
+            full((BLOCK_ROWS * rows, rows)),
             pl.BlockSpec((block, taps, rows), lambda p: (p, 0, 0)),
             pl.BlockSpec((chan_out, cot.shape[1] // pairs), lambda p: (0, p)),
         ],
@@ -284,7 +286,8 @@
             pltpu.VMEM((chan_out, taps), jnp.float32),
             pltpu.VMEM((chan_out, 1), jnp.float32),
         ],
-    )(weight_mat, bias, pool, spread, spread_w, patches, cot)
+    )(weight_mat, bias, pool, spread, spread_w, jnp.ones((BLOCK_ROWS * rows, rows), jnp.bfloat16),
+      patches, cot)
 
 
 def fold_halo(main, axis, dim, width):

time: 112 us -> 115 us (1.027)
  Pallas kernels: 31.7 us -> 33 us
  local copies, waits for them, and re-layouts: 32.1 us -> 33.4 us
    pallas_call x1, Pallas kernels: 16.4 us -> 17.6 us  [forward(): pl.pallas_call(lambda *refs: forward_kernel(rows, wide_y, *refs), grid=(p...]
    broadcast_in_dim x0 -> x1, local copies, waits for them, and re-layouts: none -> 1.22 us  [forward(): jnp.ones((BLOCK_ROWS * rows, rows), jnp.bfloat16)]
  transfers between devices with their start and end apart: 12 -> 12, of which waited for: 9 -> 9; matrix products, arithmetic and copies ran while one was open for 18% -> 17% of each run, Pallas kernels for 14% -> 13%
where the time goes in v20:
time: 115 us; the launch traced here: 114 us
  local copies, waits for them, and re-layouts  33.4 us (29%)
  Pallas kernels  33 us (29%)
  waiting for transfers between devices  22.7 us (20%)
  starting transfers between devices  19 us (17%)
  other arithmetic  5.07 us (4%)
    pallas_call x1, Pallas kernels, forward(): pl.pallas_call(lambda *refs: forward_kernel(rows, wide_y, *refs), grid=(p...  17.6 us
    pallas_call x1, Pallas kernels, allreduce(): pl.pallas_call(lambda *refs: allreduce_kernel(sizes, *refs), out_shape=ja...  15.4 us
    ppermute x3, waiting for transfers between devices, extended(): lax.ppermute(head, axis, [((i + 1) % count, i) for i in range(count)])  10 us
    reshape x1, local copies, waits for them, and re-layouts, on_device(): patches = patches.reshape(cells_x * cells_y, chan_in * 27, cells_z)  7.54 us
    unnamed x37, local copies, waits for them, and re-layouts  7.44 us
    ppermute x2, waiting for transfers between devices, fold_halo(): lax.ppermute(head, axis, [((i + 1) % count, i) for i in range(count)])  7.15 us
    ppermute x3, starting transfers between devices, extended(): lax.ppermute(tail, axis, [(i, (i + 1) % count) for i in range(count)])  6.32 us
    ppermute x2, starting transfers between devices, fold_halo(): lax.ppermute(tail, axis, [(i, (i + 1) % count) for i in range(count)])  5.7 us
  transfers between devices with their start and end apart: 12, of which 9 were waited for; matrix products, arithmetic and copies ran while one was open for 17% of the time, Pallas kernels for 13%

profile of v20, /device:TPU:7, one launch (start us, length us, event | category | flops | bytes accessed | tf_op | source)
XLA Modules:
  0.0 114.2 jit_solution(11901817985028501351)
XLA Ops:
  1.6 4.1 %collective-permute-start = (bf16[4,1,64,128]{3,2,1,0:T(8,128)(2,1)S(1)}, bf16[4,1,64,128]{3,2,1,0:T(8,128)(2,1)S(1)}, u32[]{:S(2)}, u32[]{:S(2)}) collective-permute-start(bf16[4,1,64,128]{3,2,1,0:T(8,128)(2,1)S(1)} %get-tuple-element.41), channel_id=1, source_target_pairs={{0,8},{8,16},{16,24},{24,32},{32,40},{40,48},{48,56},{56,64},{64,7... | collective-permute-start | bytes 196616 | tf_op jit(solution)/shard_map/ppermute | solution.py:23
  5.9 1.1 collective-permute-done
  8.0 5.0 %collective-permute-done.1 = bf16[4,1,64,128]{3,2,1,0:T(8,128)(2,1)S(1)} collective-permute-done((bf16[4,1,64,128]{3,2,1,0:T(8,128)(2,1)S(1)}, bf16[4,1,64,128]{3,2,1,0:T(8,128)(2,1)S(1)}, u32[]{:S(2)}, u32[]{:S(2)}) %collective-permute-start.1) | collective-permute-done | bytes 65568 | tf_op jit(solution)/shard_map/ppermute | solution.py:25
  13.1 1.4 %collective-permute-start.2 = (bf16[4,6,1,128]{3,2,1,0:T(2,128)(2,1)S(1)}, bf16[4,6,1,128]{3,2,1,0:T(2,128)(2,1)S(1)}, u32[]{:S(2)}, u32[]{:S(2)}) collective-permute-start(bf16[4,6,1,128]{3,2,1,0:T(2,128)(2,1)S(1)} %get-tuple-element.38), channel_id=1, source_target_pairs={{0,2},{2,4},{4,6},{6,0},{1,3},{3,5},{5,7},{7,1},{8,10},{10,12},{12... | collective-permute-start | bytes 18440 | tf_op jit(solution)/shard_map/ppermute | solution.py:23
  14.4 1.5 %collective-permute-start.3 = (bf16[4,6,1,128]{3,2,1,0:T(2,128)(2,1)S(1)}, bf16[4,6,1,128]{3,2,1,0:T(2,128)(2,1)S(1)}, u32[]{:S(2)}, u32[]{:S(2)}) collective-permute-start(bf16[4,6,1,128]{3,2,1,0:T(2,128)(2,1)S(1)} %get-tuple-element.39), channel_id=1, source_target_pairs={{2,0},{4,2},{6,4},{0,6},{3,1},{5,3},{7,5},{1,7},{10,8},{12,10},{14... | collective-permute-start | bytes 18440 | tf_op jit(solution)/shard_map/ppermute | solution.py:25
  19.8 2.2 %reshape.237.refs_7_ = bf16[32,4096]{1,0:T(8,128)(2,1)} reshape(bf16[32,2,32,64]{3,2,1,0:T(8,128)(2,1)} %param.7) | data formatting | bytes 524288 | tf_op jit(solution)/shard_map/reshape | solution.py:333
  23.5 1.3 %copy.76.refs_1_ = f32[32,1]{1,0:T(8,128)} copy(f32[32,1]{0,1:T(1,128)} %bitcast.228) | data formatting | bytes 256 | tf_op jit(solution)/shard_map/reshape | solution.py:336
  24.9 1.4 %pad.4 = bf16[3,3,3,8,32]{4,3,2,1,0:T(8,128)(2,1)} pad(bf16[3,3,3,4,32]{4,3,2,1,0:T(4,128)(2,1)} %bitcast.227, bf16[]{:T(256)} %constant.44.clone.1), padding=0_0x0_0x0_0x0_4x0_0 | pad | bytes 20738 | tf_op jit(solution)/shard_map/jit(_pad)/pad | solution.py:244
  26.3 3.7 %collective-permute-done.4 = bf16[4,6,66,1]{3,2,1,0:T(8,128)(2,1)S(1)} collective-permute-done((bf16[4,6,66,1]{3,2,1,0:T(8,128)(2,1)S(1)}, bf16[4,6,66,1]{3,2,1,0:T(8,128)(2,1)S(1)}, u32[]{:S(2)}, u32[]{:S(2)}) %collective-permute-start.4) | collective-permute-done | bytes 3200 | tf_op jit(solution)/shard_map/ppermute | solution.py:23
  30.0 4.7 %collective-permute-done.5 = bf16[4,6,66,1]{3,2,1,0:T(8,128)(2,1)S(1)} collective-permute-done((bf16[4,6,66,1]{3,2,1,0:T(8,128)(2,1)S(1)}, bf16[4,6,66,1]{3,2,1,0:T(8,128)(2,1)S(1)}, u32[]{:S(2)}, u32[]{:S(2)}) %collective-permute-start.5) | collective-permute-done | bytes 3200 | tf_op jit(solution)/shard_map/ppermute | solution.py:25
  39.7 7.5 %copy.77.refs_6_ = bf16[256,108,128]{2,1,0:T(8,128)(2,1)} copy(bf16[256,108,128]{2,0,1:T(8,128)(2,1)S(1)} %bitcast.220) | data formatting | bytes 14155776 | tf_op jit(solution)/shard_map/reshape | solution.py:332
  47.3 1.2 %broadcast_in_dim.4.refs_5_ = bf16[4096,128]{1,0:T(8,128)(2,1)} broadcast(bf16[]{:T(256)} %constant.45.clone.1), dimensions={} | broadcast | bytes 1048578 | tf_op jit(solution)/shard_map/broadcast_in_dim | solution.py:289
  48.5 17.6 %shard_map.75 = (bf16[32,4096]{1,0:T(8,128)(2,1)}, f32[32,108]{1,0:T(8,128)}, f32[32,1]{1,0:T(8,128)}, f32[396,4,128]{2,1,0:T(4,128)}, f32[396,4,128]{2,1,0:T(4,128)}) custom-call(bf16[32,108]{1,0:T(8,128)(2,1)} %copy.75.refs_0_, f32[32,1]{1,0:T(8,128)} %copy.76.refs_1_, bf16[2,128,128]{2,1,0:T(8,128)(2,1)} %add_convert_fusion.refs_2_, ...), custom_call_target="tpu_custom_call" | custom-call | tf_op jit(solution)/shard_map/pallas_call | solution.py:258
  66.1 1.9 %fusion.40 = (f32[6,66,4,1]{3,2,1,0:T(4,128)S(1)}, f32[6,66,4,1]{3,2,1,0:T(4,128)S(1)}) fusion(f32[6,66,4,128]{3,2,1,0:T(4,128)} %bitcast.223), kind=kLoop, calls=%fused_computation.97 | loop fusion | bytes 25344 | tf_op jit(solution)/shard_map/slice | solution.py:352
  68.4 1.7 %collective-permute-start.6 = (f32[6,66,4,1]{1,2,3,0:T(4,128)S(1)}, f32[6,66,4,1]{1,2,3,0:T(4,128)S(1)}, u32[]{:S(2)}, u32[]{:S(2)}) collective-permute-start(f32[6,66,4,1]{1,2,3,0:T(4,128)S(1)} %copy.88), channel_id=1, source_target_pairs={{0,1},{1,0},{2,3},{3,2},{4,5},{5,4},{6,7},{7,6},{8,9},{9,8},{10,11... | collective-permute-start | bytes 19016 | tf_op jit(solution)/shard_map/ppermute | solution.py:354
  70.5 2.0 %fusion.41 = (f32[6,66,4,1]{3,2,1,0:T(4,128)S(1)}, f32[6,66,4,1]{3,2,1,0:T(4,128)S(1)}) fusion(f32[6,66,4,128]{3,2,1,0:T(4,128)} %bitcast.221), kind=kLoop, calls=%fused_computation.98 | loop fusion | bytes 25344 | tf_op jit(solution)/shard_map/slice | solution.py:358
  74.9 1.4 %collective-permute-start.8 = (f32[6,1,4,128]{3,1,0,2:T(1,128)S(1)}, f32[6,1,4,128]{3,1,0,2:T(1,128)S(1)}, u32[]{:S(2)}, u32[]{:S(2)}) collective-permute-start(f32[6,1,4,128]{3,1,0,2:T(1,128)S(1)} %get-tuple-element.27), channel_id=1, source_target_pairs={{0,2},{2,4},{4,6},{6,0},{1,3},{3,5},{5,7},{7,1},{8,10},{10,12},{12... | collective-permute-start | bytes 36872 | tf_op jit(solution)/shard_map/ppermute | solution.py:298
  76.9 1.4 %collective-permute-start.9 = (f32[6,1,4,128]{3,1,0,2:T(1,128)S(1)}, f32[6,1,4,128]{3,1,0,2:T(1,128)S(1)}, u32[]{:S(2)}, u32[]{:S(2)}) collective-permute-start(f32[6,1,4,128]{3,1,0,2:T(1,128)S(1)} %get-tuple-element.26), channel_id=1, source_target_pairs={{2,0},{4,2},{6,4},{0,6},{3,1},{5,3},{7,5},{1,7},{10,8},{12,10},{14... | collective-permute-start | bytes 36872 | tf_op jit(solution)/shard_map/ppermute | solution.py:299
  79.6 4.3 %collective-permute-start.10 = (f32[1,64,4,128]{3,1,0,2:T(8,128)S(1)}, f32[1,64,4,128]{3,1,0,2:T(8,128)S(1)}, u32[]{:S(2)}, u32[]{:S(2)}) collective-permute-start(f32[1,64,4,128]{3,1,0,2:T(8,128)S(1)} %get-tuple-element.33), channel_id=1, source_target_pairs={{0,8},{8,16},{16,24},{24,32},{32,40},{40,48},{48,56},{56,64},{64,7... | collective-permute-start | bytes 393224 | tf_op jit(solution)/shard_map/ppermute | solution.py:298
  84.7 15.4 %shard_map.76 = f32[32,128]{1,0:T(8,128)} custom-call(f32[32,128]{1,0:T(8,128)} %maximum_maximum_fusion.1.refs_0_), custom_call_target="tpu_custom_call" | custom-call | tf_op jit(solution)/shard_map/pallas_call | solution.py:114
  101.5 2.3 %reshape.238 = bf16[32,2,32,64]{3,2,1,0:T(8,128)(2,1)} reshape(bf16[32,4096]{1,0:T(8,128)(2,1)} %get-tuple-element.9) | data formatting | bytes 524288 | tf_op jit(solution)/shard_map/reshape | solution.py:338
  103.8 1.4 %slice_reduce_fusion = f32[32]{0:T(128)} fusion(f32[32,128]{1,0:T(8,128)} %shard_map.76), kind=kLoop, calls=%fused_computation.87 | loop fusion | bytes 256 | tf_op jit(solution)/shard_map/slice | solution.py:348
  105.2 1.5 %collective-permute-start.11 = (f32[1,64,4,128]{3,1,0,2:T(8,128)S(1)}, f32[1,64,4,128]{3,1,0,2:T(8,128)S(1)}, u32[]{:S(2)}, u32[]{:S(2)}) collective-permute-start(f32[1,64,4,128]{3,1,0,2:T(8,128)S(1)} %get-tuple-element.32), channel_id=1, source_target_pairs={{8,0},{16,8},{24,16},{32,24},{40,32},{48,40},{56,48},{64,56},{72,6... | collective-permute-start | bytes 393224 | tf_op jit(solution)/shard_map/ppermute | solution.py:299
  106.7 6.6 %collective-permute-done.11 = f32[1,64,4,128]{3,1,0,2:T(8,128)S(1)} collective-permute-done((f32[1,64,4,128]{3,1,0,2:T(8,128)S(1)}, f32[1,64,4,128]{3,1,0,2:T(8,128)S(1)}, u32[]{:S(2)}, u32[]{:S(2)}) %collective-permute-start.11) | collective-permute-done | bytes 131104 | tf_op jit(solution)/shard_map/ppermute | solution.py:299
  (91 shorter events, 20.4 us)
Async XLA Ops:
  0.6 35.6 %copy-start.1 = (bf16[4,4,64,128]{3,2,1,0:T(8,128)(2,1)S(1)}, bf16[4,4,64,128]{3,2,1,0:T(8,128)(2,1)}, u32[]{:S(2)}) copy-start(bf16[4,4,64,128]{3,2,1,0:T(8,128)(2,1)} %param.4) | copy-start | bytes 786436
  1.6 5.5 %collective-permute-start = (bf16[4,1,64,128]{3,2,1,0:T(8,128)(2,1)S(1)}, bf16[4,1,64,128]{3,2,1,0:T(8,128)(2,1)S(1)}, u32[]{:S(2)}, u32[]{:S(2)}) collective-permute-start(bf16[4,1,64,128]{3,2,1,0:T(8,128)(2,1)S(1)} %get-tuple-element.41), channel_id=1, source_target_pairs={{0,8},{8,16},{16,24},{24,32},{32,40},{40,48},{48,56},{56,64},{64,7... | collective-permute-start | bytes 196616 | tf_op jit(solution)/shard_map/ppermute | solution.py:23
  5.7 7.3 %collective-permute-start.1 = (bf16[4,1,64,128]{3,2,1,0:T(8,128)(2,1)S(1)}, bf16[4,1,64,128]{3,2,1,0:T(8,128)(2,1)S(1)}, u32[]{:S(2)}, u32[]{:S(2)}) collective-permute-start(bf16[4,1,64,128]{3,2,1,0:T(8,128)(2,1)S(1)} %get-tuple-element.40), channel_id=1, source_target_pairs={{8,0},{16,8},{24,16},{32,24},{40,32},{48,40},{56,48},{64,56},{72,6... | collective-permute-start | bytes 196616 | tf_op jit(solution)/shard_map/ppermute | solution.py:25
  13.1 3.9 %collective-permute-start.2 = (bf16[4,6,1,128]{3,2,1,0:T(2,128)(2,1)S(1)}, bf16[4,6,1,128]{3,2,1,0:T(2,128)(2,1)S(1)}, u32[]{:S(2)}, u32[]{:S(2)}) collective-permute-start(bf16[4,6,1,128]{3,2,1,0:T(2,128)(2,1)S(1)} %get-tuple-element.38), channel_id=1, source_target_pairs={{0,2},{2,4},{4,6},{6,0},{1,3},{3,5},{5,7},{7,1},{8,10},{10,12},{12... | collective-permute-start | bytes 18440 | tf_op jit(solution)/shard_map/ppermute | solution.py:23
  14.4 2.8 %collective-permute-start.3 = (bf16[4,6,1,128]{3,2,1,0:T(2,128)(2,1)S(1)}, bf16[4,6,1,128]{3,2,1,0:T(2,128)(2,1)S(1)}, u32[]{:S(2)}, u32[]{:S(2)}) collective-permute-start(bf16[4,6,1,128]{3,2,1,0:T(2,128)(2,1)S(1)} %get-tuple-element.39), channel_id=1, source_target_pairs={{2,0},{4,2},{6,4},{0,6},{3,1},{5,3},{7,5},{1,7},{10,8},{12,10},{14... | collective-permute-start | bytes 18440 | tf_op jit(solution)/shard_map/ppermute | solution.py:25
  17.6 12.3 %collective-permute-start.4 = (bf16[4,6,66,1]{3,2,1,0:T(8,128)(2,1)S(1)}, bf16[4,6,66,1]{3,2,1,0:T(8,128)(2,1)S(1)}, u32[]{:S(2)}, u32[]{:S(2)}) collective-permute-start(bf16[4,6,66,1]{3,2,1,0:T(8,128)(2,1)S(1)} %get-tuple-element.35), channel_id=1, source_target_pairs={{0,1},{1,0},{2,3},{3,2},{4,5},{5,4},{6,7},{7,6},{8,9},{9,8},{10,11... | collective-permute-start | bytes 9512 | tf_op jit(solution)/shard_map/ppermute | solution.py:23
  18.5 16.2 %collective-permute-start.5 = (bf16[4,6,66,1]{3,2,1,0:T(8,128)(2,1)S(1)}, bf16[4,6,66,1]{3,2,1,0:T(8,128)(2,1)S(1)}, u32[]{:S(2)}, u32[]{:S(2)}) collective-permute-start(bf16[4,6,66,1]{3,2,1,0:T(8,128)(2,1)S(1)} %get-tuple-element.34), channel_id=1, source_target_pairs={{1,0},{0,1},{3,2},{2,3},{5,4},{4,5},{7,6},{6,7},{9,8},{8,9},{11,10... | collective-permute-start | bytes 9512 | tf_op jit(solution)/shard_map/ppermute | solution.py:25
  66.1 6.4 %copy-start = (f32[396,4,128]{2,1,0:T(4,128)S(1)}, f32[396,4,128]{2,1,0:T(4,128)}, u32[]{:S(2)}) copy-start(f32[396,4,128]{2,1,0:T(4,128)} %get-tuple-element.12) | copy-start | bytes 2433028
  68.4 5.4 %collective-permute-start.6 = (f32[6,66,4,1]{1,2,3,0:T(4,128)S(1)}, f32[6,66,4,1]{1,2,3,0:T(4,128)S(1)}, u32[]{:S(2)}, u32[]{:S(2)}) collective-permute-start(f32[6,66,4,1]{1,2,3,0:T(4,128)S(1)} %copy.88), channel_id=1, source_target_pairs={{0,1},{1,0},{2,3},{3,2},{4,5},{5,4},{6,7},{7,6},{8,9},{9,8},{10,11... | collective-permute-start | bytes 19016 | tf_op jit(solution)/shard_map/ppermute | solution.py:354
  70.5 3.8 %collective-permute-start.7 = (f32[6,66,4,1]{1,2,3,0:T(4,128)S(1)}, f32[6,66,4,1]{1,2,3,0:T(4,128)S(1)}, u32[]{:S(2)}, u32[]{:S(2)}) collective-permute-start(f32[6,66,4,1]{1,2,3,0:T(4,128)S(1)} %copy.91), channel_id=1, source_target_pairs={{1,0},{0,1},{3,2},{2,3},{5,4},{4,5},{7,6},{6,7},{9,8},{8,9},{11,10... | collective-permute-start | bytes 19016 | tf_op jit(solution)/shard_map/ppermute | solution.py:355
  73.7 10.2 %copy-start.3 = (f32[32,108]{1,0:T(8,128)S(1)}, f32[32,108]{1,0:T(8,128)}, u32[]{:S(2)}) copy-start(f32[32,108]{1,0:T(8,128)} %get-tuple-element.10) | copy-start | bytes 41476
  73.7 10.2 %copy-start.4 = (f32[32,1]{1,0:T(8,128)S(1)}, f32[32,1]{1,0:T(8,128)}, u32[]{:S(2)}) copy-start(f32[32,1]{1,0:T(8,128)} %get-tuple-element.11) | copy-start | bytes 388
  74.9 3.8 %collective-permute-start.8 = (f32[6,1,4,128]{3,1,0,2:T(1,128)S(1)}, f32[6,1,4,128]{3,1,0,2:T(1,128)S(1)}, u32[]{:S(2)}, u32[]{:S(2)}) collective-permute-start(f32[6,1,4,128]{3,1,0,2:T(1,128)S(1)} %get-tuple-element.27), channel_id=1, source_target_pairs={{0,2},{2,4},{4,6},{6,0},{1,3},{3,5},{5,7},{7,1},{8,10},{10,12},{12... | collective-permute-start | bytes 36872 | tf_op jit(solution)/shard_map/ppermute | solution.py:298
  76.9 2.6 %collective-permute-start.9 = (f32[6,1,4,128]{3,1,0,2:T(1,128)S(1)}, f32[6,1,4,128]{3,1,0,2:T(1,128)S(1)}, u32[]{:S(2)}, u32[]{:S(2)}) collective-permute-start(f32[6,1,4,128]{3,1,0,2:T(1,128)S(1)} %get-tuple-element.26), channel_id=1, source_target_pairs={{2,0},{4,2},{6,4},{0,6},{3,1},{5,3},{7,5},{1,7},{10,8},{12,10},{14... | collective-permute-start | bytes 36872 | tf_op jit(solution)/shard_map/ppermute | solution.py:299
  79.6 27.1 %collective-permute-start.10 = (f32[1,64,4,128]{3,1,0,2:T(8,128)S(1)}, f32[1,64,4,128]{3,1,0,2:T(8,128)S(1)}, u32[]{:S(2)}, u32[]{:S(2)}) collective-permute-start(f32[1,64,4,128]{3,1,0,2:T(8,128)S(1)} %get-tuple-element.33), channel_id=1, source_target_pairs={{0,8},{8,16},{16,24},{24,32},{32,40},{40,48},{48,56},{56,64},{64,7... | collective-permute-start | bytes 393224 | tf_op jit(solution)/shard_map/ppermute | solution.py:298
  105.2 8.1 %collective-permute-start.11 = (f32[1,64,4,128]{3,1,0,2:T(8,128)S(1)}, f32[1,64,4,128]{3,1,0,2:T(8,128)S(1)}, u32[]{:S(2)}, u32[]{:S(2)}) collective-permute-start(f32[1,64,4,128]{3,1,0,2:T(8,128)S(1)} %get-tuple-element.32), channel_id=1, source_target_pairs={{8,0},{16,8},{24,16},{32,24},{40,32},{48,40},{56,48},{64,56},{72,6... | collective-permute-start | bytes 393224 | tf_op jit(solution)/shard_map/ppermute | solution.py:299
  113.4 0.8 copy-start.2

commit v21 on v14

--- a/solution.py
+++ b/solution.py
@@ -150,6 +150,8 @@
     last = lane == rows - 1
 
     group = 32
+    up_both = jnp.concatenate([u_ref[0], u_ref[1]], axis=1)
+    pool_both = jnp.concatenate([q_ref[0], q_ref[1]], axis=0)
     pooled_rows = group // 2
     pieces = pooled_rows // 2
 
@@ -158,8 +160,9 @@
         ups = []
         for m in range(pieces):
             cot = cot_ref[:, pl.ds(pl.multiple_of((j * pieces + m) * rows, rows), rows)]
-            ups.append(jnp.dot(cot, u_ref[0], preferred_element_type=jnp.float32) * 0.125)
-            ups.append(jnp.dot(cot, u_ref[1], preferred_element_type=jnp.float32) * 0.125)
+            up = jnp.dot(cot, up_both, preferred_element_type=jnp.float32) * 0.125
+            ups.append(up[:, :rows])
+            ups.append(up[:, rows:])
         spread_all = jnp.concatenate([ups[r // 2] for r in range(group)], axis=1)
         totals = [None] * pooled_rows
         wg = None
@@ -216,13 +219,13 @@
         wg_acc[...] += wg
         bg_acc[...] += jnp.sum(bg, axis=1, keepdims=True)
         for m in range(pieces):
-            pooled = jnp.dot(
-                totals[2 * m], q_ref[0], preferred_element_type=jnp.float32,
-                precision=lax.Precision.HIGHEST,
-            ) + jnp.dot(
-                totals[2 * m + 1], q_ref[1], preferred_element_type=jnp.float32,
-                precision=lax.Precision.HIGHEST,
-            )
+            value = jnp.concatenate([totals[2 * m], totals[2 * m + 1]], axis=1)
+            high = value.astype(jnp.bfloat16)
+            low = (value - high.astype(jnp.float32)).astype(jnp.bfloat16)
+            part = jnp.dot(
+                jnp.concatenate([high, low], axis=0), pool_both, preferred_element_type=jnp.float32
+            )
+            pooled = part[: value.shape[0]] + part[value.shape[0] :]
             at = pl.multiple_of((j * pieces + m) * rows, rows)
             pooled_ref[:, pl.ds(at, rows)] = (pooled * 0.125).astype(pooled_ref.dtype)
 
@@ -245,7 +248,7 @@
     k = jnp.arange(rows)
     pool = jnp.stack(
         [(k[None, :] == z[:, None] // 2), (k[None, :] == half + z[:, None] // 2)]
-    ).astype(jnp.float32)
+    ).astype(jnp.bfloat16)
     spread = jnp.stack(
         [(z[None, :] // 2 == k[:, None]), (z[None, :] // 2 + half == k[:, None])]
     ).astype(jnp.bfloat16)

time: 115 us -> 112 us (0.974)
  Pallas kernels: 34.5 us -> 31.7 us
    pallas_call x1, Pallas kernels: 19.2 us -> 16.3 us  [forward(): pl.pallas_call(lambda *refs: forward_kernel(rows, wide_y, *refs), grid=(p...]
  transfers between devices with their start and end apart: 12 -> 12, of which waited for: 9 -> 9; matrix products, arithmetic and copies ran while one was open for 17% -> 18% of each run, Pallas kernels for 13% -> 14%
where the time goes in v21:
time: 112 us
  local copies, waits for them, and re-layouts  32.1 us (29%)
  Pallas kernels  31.7 us (28%)
  waiting for transfers between devices  22.7 us (20%)
  starting transfers between devices  18.9 us (17%)
  other arithmetic  5.06 us (5%)
    pallas_call x1, Pallas kernels, forward(): pl.pallas_call(lambda *refs: forward_kernel(rows, wide_y, *refs), grid=(p...  16.3 us
    pallas_call x1, Pallas kernels, allreduce(): pl.pallas_call(lambda *refs: allreduce_kernel(sizes, *refs), out_shape=ja...  15.4 us
    ppermute x3, waiting for transfers between devices, extended(): lax.ppermute(head, axis, [((i + 1) % count, i) for i in range(count)])  10 us
    reshape x1, local copies, waits for them, and re-layouts, on_device(): patches = patches.reshape(cells_x * cells_y, chan_in * 27, cells_z)  7.54 us
    unnamed x37, local copies, waits for them, and re-layouts  7.44 us
    ppermute x2, waiting for transfers between devices, fold_halo(): lax.ppermute(head, axis, [((i + 1) % count, i) for i in range(count)])  7.16 us
    ppermute x3, starting transfers between devices, extended(): lax.ppermute(tail, axis, [(i, (i + 1) % count) for i in range(count)])  6.32 us
    ppermute x2, starting transfers between devices, fold_halo(): lax.ppermute(tail, axis, [(i, (i + 1) % count) for i in range(count)])  5.7 us
  transfers between devices with their start and end apart: 12, of which 9 were waited for; matrix products, arithmetic and copies ran while one was open for 18% of the time, Pallas kernels for 14%

profile of v21, /device:TPU:7, one launch (start us, length us, event | category | flops | bytes accessed | tf_op | source)
XLA Modules:
  0.0 111.5 jit_solution(9191223168620213773)
XLA Ops:
  1.6 4.1 %collective-permute-start = (bf16[4,1,64,128]{3,2,1,0:T(8,128)(2,1)S(1)}, bf16[4,1,64,128]{3,2,1,0:T(8,128)(2,1)S(1)}, u32[]{:S(2)}, u32[]{:S(2)}) collective-permute-start(bf16[4,1,64,128]{3,2,1,0:T(8,128)(2,1)S(1)} %get-tuple-element.41), channel_id=1, source_target_pairs={{0,8},{8,16},{16,24},{24,32},{32,40},{40,48},{48,56},{56,64},{64,7... | collective-permute-start | bytes 196616 | tf_op jit(solution)/shard_map/ppermute | solution.py:22
  5.9 1.1 %collective-permute-done = bf16[4,1,64,128]{3,2,1,0:T(8,128)(2,1)S(1)} collective-permute-done((bf16[4,1,64,128]{3,2,1,0:T(8,128)(2,1)S(1)}, bf16[4,1,64,128]{3,2,1,0:T(8,128)(2,1)S(1)}, u32[]{:S(2)}, u32[]{:S(2)}) %collective-permute-start) | collective-permute-done | bytes 65568 | tf_op jit(solution)/shard_map/ppermute | solution.py:22
  8.0 5.0 %collective-permute-done.1 = bf16[4,1,64,128]{3,2,1,0:T(8,128)(2,1)S(1)} collective-permute-done((bf16[4,1,64,128]{3,2,1,0:T(8,128)(2,1)S(1)}, bf16[4,1,64,128]{3,2,1,0:T(8,128)(2,1)S(1)}, u32[]{:S(2)}, u32[]{:S(2)}) %collective-permute-start.1) | collective-permute-done | bytes 65568 | tf_op jit(solution)/shard_map/ppermute | solution.py:24
  13.1 1.4 %collective-permute-start.2 = (bf16[4,6,1,128]{3,2,1,0:T(2,128)(2,1)S(1)}, bf16[4,6,1,128]{3,2,1,0:T(2,128)(2,1)S(1)}, u32[]{:S(2)}, u32[]{:S(2)}) collective-permute-start(bf16[4,6,1,128]{3,2,1,0:T(2,128)(2,1)S(1)} %get-tuple-element.38), channel_id=1, source_target_pairs={{0,2},{2,4},{4,6},{6,0},{1,3},{3,5},{5,7},{7,1},{8,10},{10,12},{12... | collective-permute-start | bytes 18440 | tf_op jit(solution)/shard_map/ppermute | solution.py:22
  14.4 1.5 %collective-permute-start.3 = (bf16[4,6,1,128]{3,2,1,0:T(2,128)(2,1)S(1)}, bf16[4,6,1,128]{3,2,1,0:T(2,128)(2,1)S(1)}, u32[]{:S(2)}, u32[]{:S(2)}) collective-permute-start(bf16[4,6,1,128]{3,2,1,0:T(2,128)(2,1)S(1)} %get-tuple-element.39), channel_id=1, source_target_pairs={{2,0},{4,2},{6,4},{0,6},{3,1},{5,3},{7,5},{1,7},{10,8},{12,10},{14... | collective-permute-start | bytes 18440 | tf_op jit(solution)/shard_map/ppermute | solution.py:24
  19.8 2.2 %reshape.237.refs_6_ = bf16[32,4096]{1,0:T(8,128)(2,1)} reshape(bf16[32,2,32,64]{3,2,1,0:T(8,128)(2,1)} %param.7) | data formatting | bytes 524288 | tf_op jit(solution)/shard_map/reshape | solution.py:331
  23.5 1.3 %copy.76.refs_1_ = f32[32,1]{1,0:T(8,128)} copy(f32[32,1]{0,1:T(1,128)} %bitcast.228) | data formatting | bytes 256 | tf_op jit(solution)/shard_map/reshape | solution.py:334
  24.9 1.4 %pad.4 = bf16[3,3,3,8,32]{4,3,2,1,0:T(8,128)(2,1)} pad(bf16[3,3,3,4,32]{4,3,2,1,0:T(4,128)(2,1)} %bitcast.227, bf16[]{:T(256)} %constant.43.clone.1), padding=0_0x0_0x0_0x0_4x0_0 | pad | bytes 20738 | tf_op jit(solution)/shard_map/jit(_pad)/pad | solution.py:244
  26.3 3.7 %collective-permute-done.4 = bf16[4,6,66,1]{3,2,1,0:T(8,128)(2,1)S(1)} collective-permute-done((bf16[4,6,66,1]{3,2,1,0:T(8,128)(2,1)S(1)}, bf16[4,6,66,1]{3,2,1,0:T(8,128)(2,1)S(1)}, u32[]{:S(2)}, u32[]{:S(2)}) %collective-permute-start.4) | collective-permute-done | bytes 3200 | tf_op jit(solution)/shard_map/ppermute | solution.py:22
  30.0 4.7 %collective-permute-done.5 = bf16[4,6,66,1]{3,2,1,0:T(8,128)(2,1)S(1)} collective-permute-done((bf16[4,6,66,1]{3,2,1,0:T(8,128)(2,1)S(1)}, bf16[4,6,66,1]{3,2,1,0:T(8,128)(2,1)S(1)}, u32[]{:S(2)}, u32[]{:S(2)}) %collective-permute-start.5) | collective-permute-done | bytes 3200 | tf_op jit(solution)/shard_map/ppermute | solution.py:24
  34.7 1.1 pad_maximum_fusion
  39.7 7.5 %copy.77.refs_5_ = bf16[256,108,128]{2,1,0:T(8,128)(2,1)} copy(bf16[256,108,128]{2,0,1:T(8,128)(2,1)S(1)} %bitcast.220) | data formatting | bytes 14155776 | tf_op jit(solution)/shard_map/reshape | solution.py:330
  47.3 16.3 %shard_map.75 = (bf16[32,4096]{1,0:T(8,128)(2,1)}, f32[32,108]{1,0:T(8,128)}, f32[32,1]{1,0:T(8,128)}, f32[396,4,128]{2,1,0:T(4,128)}, f32[396,4,128]{2,1,0:T(4,128)}) custom-call(bf16[32,108]{1,0:T(8,128)(2,1)} %copy.75.refs_0_, f32[32,1]{1,0:T(8,128)} %copy.76.refs_1_, bf16[2,128,128]{2,1,0:T(8,128)(2,1)} %add_convert_fusion.refs_2_, ...), custom_call_target="tpu_custom_call" | custom-call | tf_op jit(solution)/shard_map/pallas_call | solution.py:258
  63.6 1.9 %fusion.40 = (f32[6,66,4,1]{3,2,1,0:T(4,128)S(1)}, f32[6,66,4,1]{3,2,1,0:T(4,128)S(1)}) fusion(f32[6,66,4,128]{3,2,1,0:T(4,128)} %bitcast.223), kind=kLoop, calls=%fused_computation.97 | loop fusion | bytes 25344 | tf_op jit(solution)/shard_map/slice | solution.py:350
  65.9 1.7 %collective-permute-start.6 = (f32[6,66,4,1]{1,2,3,0:T(4,128)S(1)}, f32[6,66,4,1]{1,2,3,0:T(4,128)S(1)}, u32[]{:S(2)}, u32[]{:S(2)}) collective-permute-start(f32[6,66,4,1]{1,2,3,0:T(4,128)S(1)} %copy.88), channel_id=1, source_target_pairs={{0,1},{1,0},{2,3},{3,2},{4,5},{5,4},{6,7},{7,6},{8,9},{9,8},{10,11... | collective-permute-start | bytes 19016 | tf_op jit(solution)/shard_map/ppermute | solution.py:352
  68.0 1.9 %fusion.41 = (f32[6,66,4,1]{3,2,1,0:T(4,128)S(1)}, f32[6,66,4,1]{3,2,1,0:T(4,128)S(1)}) fusion(f32[6,66,4,128]{3,2,1,0:T(4,128)} %bitcast.221), kind=kLoop, calls=%fused_computation.98 | loop fusion | bytes 25344 | tf_op jit(solution)/shard_map/slice | solution.py:356
  72.3 1.4 %collective-permute-start.8 = (f32[6,1,4,128]{3,1,0,2:T(1,128)S(1)}, f32[6,1,4,128]{3,1,0,2:T(1,128)S(1)}, u32[]{:S(2)}, u32[]{:S(2)}) collective-permute-start(f32[6,1,4,128]{3,1,0,2:T(1,128)S(1)} %get-tuple-element.27), channel_id=1, source_target_pairs={{0,2},{2,4},{4,6},{6,0},{1,3},{3,5},{5,7},{7,1},{8,10},{10,12},{12... | collective-permute-start | bytes 36872 | tf_op jit(solution)/shard_map/ppermute | solution.py:296
  74.3 1.4 %collective-permute-start.9 = (f32[6,1,4,128]{3,1,0,2:T(1,128)S(1)}, f32[6,1,4,128]{3,1,0,2:T(1,128)S(1)}, u32[]{:S(2)}, u32[]{:S(2)}) collective-permute-start(f32[6,1,4,128]{3,1,0,2:T(1,128)S(1)} %get-tuple-element.26), channel_id=1, source_target_pairs={{2,0},{4,2},{6,4},{0,6},{3,1},{5,3},{7,5},{1,7},{10,8},{12,10},{14... | collective-permute-start | bytes 36872 | tf_op jit(solution)/shard_map/ppermute | solution.py:297
  77.0 4.3 %collective-permute-start.10 = (f32[1,64,4,128]{3,1,0,2:T(8,128)S(1)}, f32[1,64,4,128]{3,1,0,2:T(8,128)S(1)}, u32[]{:S(2)}, u32[]{:S(2)}) collective-permute-start(f32[1,64,4,128]{3,1,0,2:T(8,128)S(1)} %get-tuple-element.33), channel_id=1, source_target_pairs={{0,8},{8,16},{16,24},{24,32},{32,40},{40,48},{48,56},{56,64},{64,7... | collective-permute-start | bytes 393224 | tf_op jit(solution)/shard_map/ppermute | solution.py:296
  82.0 15.4 %shard_map.76 = f32[32,128]{1,0:T(8,128)} custom-call(f32[32,128]{1,0:T(8,128)} %maximum_maximum_fusion.1.refs_0_), custom_call_target="tpu_custom_call" | custom-call | tf_op jit(solution)/shard_map/pallas_call | solution.py:113
  98.9 2.3 %reshape.238 = bf16[32,2,32,64]{3,2,1,0:T(8,128)(2,1)} reshape(bf16[32,4096]{1,0:T(8,128)(2,1)} %get-tuple-element.9) | data formatting | bytes 524288 | tf_op jit(solution)/shard_map/reshape | solution.py:336
  101.2 1.4 %slice_reduce_fusion = f32[32]{0:T(128)} fusion(f32[32,128]{1,0:T(8,128)} %shard_map.76), kind=kLoop, calls=%fused_computation.87 | loop fusion | bytes 256 | tf_op jit(solution)/shard_map/slice | solution.py:346
  102.6 1.5 %collective-permute-start.11 = (f32[1,64,4,128]{3,1,0,2:T(8,128)S(1)}, f32[1,64,4,128]{3,1,0,2:T(8,128)S(1)}, u32[]{:S(2)}, u32[]{:S(2)}) collective-permute-start(f32[1,64,4,128]{3,1,0,2:T(8,128)S(1)} %get-tuple-element.32), channel_id=1, source_target_pairs={{8,0},{16,8},{24,16},{32,24},{40,32},{48,40},{56,48},{64,56},{72,6... | collective-permute-start | bytes 393224 | tf_op jit(solution)/shard_map/ppermute | solution.py:297
  104.1 6.6 %collective-permute-done.11 = f32[1,64,4,128]{3,1,0,2:T(8,128)S(1)} collective-permute-done((f32[1,64,4,128]{3,1,0,2:T(8,128)S(1)}, f32[1,64,4,128]{3,1,0,2:T(8,128)S(1)}, u32[]{:S(2)}, u32[]{:S(2)}) %collective-permute-start.11) | collective-permute-done | bytes 131104 | tf_op jit(solution)/shard_map/ppermute | solution.py:297
  (90 shorter events, 19.4 us)
Async XLA Ops:
  0.6 35.6 %copy-start.1 = (bf16[4,4,64,128]{3,2,1,0:T(8,128)(2,1)S(1)}, bf16[4,4,64,128]{3,2,1,0:T(8,128)(2,1)}, u32[]{:S(2)}) copy-start(bf16[4,4,64,128]{3,2,1,0:T(8,128)(2,1)} %param.4) | copy-start | bytes 786436
  1.6 5.5 %collective-permute-start = (bf16[4,1,64,128]{3,2,1,0:T(8,128)(2,1)S(1)}, bf16[4,1,64,128]{3,2,1,0:T(8,128)(2,1)S(1)}, u32[]{:S(2)}, u32[]{:S(2)}) collective-permute-start(bf16[4,1,64,128]{3,2,1,0:T(8,128)(2,1)S(1)} %get-tuple-element.41), channel_id=1, source_target_pairs={{0,8},{8,16},{16,24},{24,32},{32,40},{40,48},{48,56},{56,64},{64,7... | collective-permute-start | bytes 196616 | tf_op jit(solution)/shard_map/ppermute | solution.py:22
  5.7 7.3 %collective-permute-start.1 = (bf16[4,1,64,128]{3,2,1,0:T(8,128)(2,1)S(1)}, bf16[4,1,64,128]{3,2,1,0:T(8,128)(2,1)S(1)}, u32[]{:S(2)}, u32[]{:S(2)}) collective-permute-start(bf16[4,1,64,128]{3,2,1,0:T(8,128)(2,1)S(1)} %get-tuple-element.40), channel_id=1, source_target_pairs={{8,0},{16,8},{24,16},{32,24},{40,32},{48,40},{56,48},{64,56},{72,6... | collective-permute-start | bytes 196616 | tf_op jit(solution)/shard_map/ppermute | solution.py:24
  13.1 3.9 %collective-permute-start.2 = (bf16[4,6,1,128]{3,2,1,0:T(2,128)(2,1)S(1)}, bf16[4,6,1,128]{3,2,1,0:T(2,128)(2,1)S(1)}, u32[]{:S(2)}, u32[]{:S(2)}) collective-permute-start(bf16[4,6,1,128]{3,2,1,0:T(2,128)(2,1)S(1)} %get-tuple-element.38), channel_id=1, source_target_pairs={{0,2},{2,4},{4,6},{6,0},{1,3},{3,5},{5,7},{7,1},{8,10},{10,12},{12... | collective-permute-start | bytes 18440 | tf_op jit(solution)/shard_map/ppermute | solution.py:22
  14.4 2.8 %collective-permute-start.3 = (bf16[4,6,1,128]{3,2,1,0:T(2,128)(2,1)S(1)}, bf16[4,6,1,128]{3,2,1,0:T(2,128)(2,1)S(1)}, u32[]{:S(2)}, u32[]{:S(2)}) collective-permute-start(bf16[4,6,1,128]{3,2,1,0:T(2,128)(2,1)S(1)} %get-tuple-element.39), channel_id=1, source_target_pairs={{2,0},{4,2},{6,4},{0,6},{3,1},{5,3},{7,5},{1,7},{10,8},{12,10},{14... | collective-permute-start | bytes 18440 | tf_op jit(solution)/shard_map/ppermute | solution.py:24
  17.6 12.3 %collective-permute-start.4 = (bf16[4,6,66,1]{3,2,1,0:T(8,128)(2,1)S(1)}, bf16[4,6,66,1]{3,2,1,0:T(8,128)(2,1)S(1)}, u32[]{:S(2)}, u32[]{:S(2)}) collective-permute-start(bf16[4,6,66,1]{3,2,1,0:T(8,128)(2,1)S(1)} %get-tuple-element.35), channel_id=1, source_target_pairs={{0,1},{1,0},{2,3},{3,2},{4,5},{5,4},{6,7},{7,6},{8,9},{9,8},{10,11... | collective-permute-start | bytes 9512 | tf_op jit(solution)/shard_map/ppermute | solution.py:22
  18.5 16.2 %collective-permute-start.5 = (bf16[4,6,66,1]{3,2,1,0:T(8,128)(2,1)S(1)}, bf16[4,6,66,1]{3,2,1,0:T(8,128)(2,1)S(1)}, u32[]{:S(2)}, u32[]{:S(2)}) collective-permute-start(bf16[4,6,66,1]{3,2,1,0:T(8,128)(2,1)S(1)} %get-tuple-element.34), channel_id=1, source_target_pairs={{1,0},{0,1},{3,2},{2,3},{5,4},{4,5},{7,6},{6,7},{9,8},{8,9},{11,10... | collective-permute-start | bytes 9512 | tf_op jit(solution)/shard_map/ppermute | solution.py:24
  63.6 6.3 %copy-start = (f32[396,4,128]{2,1,0:T(4,128)S(1)}, f32[396,4,128]{2,1,0:T(4,128)}, u32[]{:S(2)}) copy-start(f32[396,4,128]{2,1,0:T(4,128)} %get-tuple-element.12) | copy-start | bytes 2433028
  65.9 5.3 %collective-permute-start.6 = (f32[6,66,4,1]{1,2,3,0:T(4,128)S(1)}, f32[6,66,4,1]{1,2,3,0:T(4,128)S(1)}, u32[]{:S(2)}, u32[]{:S(2)}) collective-permute-start(f32[6,66,4,1]{1,2,3,0:T(4,128)S(1)} %copy.88), channel_id=1, source_target_pairs={{0,1},{1,0},{2,3},{3,2},{4,5},{5,4},{6,7},{7,6},{8,9},{9,8},{10,11... | collective-permute-start | bytes 19016 | tf_op jit(solution)/shard_map/ppermute | solution.py:352
  67.9 3.8 %collective-permute-start.7 = (f32[6,66,4,1]{1,2,3,0:T(4,128)S(1)}, f32[6,66,4,1]{1,2,3,0:T(4,128)S(1)}, u32[]{:S(2)}, u32[]{:S(2)}) collective-permute-start(f32[6,66,4,1]{1,2,3,0:T(4,128)S(1)} %copy.91), channel_id=1, source_target_pairs={{1,0},{0,1},{3,2},{2,3},{5,4},{4,5},{7,6},{6,7},{9,8},{8,9},{11,10... | collective-permute-start | bytes 19016 | tf_op jit(solution)/shard_map/ppermute | solution.py:353
  71.1 10.2 %copy-start.3 = (f32[32,108]{1,0:T(8,128)S(1)}, f32[32,108]{1,0:T(8,128)}, u32[]{:S(2)}) copy-start(f32[32,108]{1,0:T(8,128)} %get-tuple-element.10) | copy-start | bytes 41476
  71.1 10.2 %copy-start.4 = (f32[32,1]{1,0:T(8,128)S(1)}, f32[32,1]{1,0:T(8,128)}, u32[]{:S(2)}) copy-start(f32[32,1]{1,0:T(8,128)} %get-tuple-element.11) | copy-start | bytes 388
  72.3 3.8 %collective-permute-start.8 = (f32[6,1,4,128]{3,1,0,2:T(1,128)S(1)}, f32[6,1,4,128]{3,1,0,2:T(1,128)S(1)}, u32[]{:S(2)}, u32[]{:S(2)}) collective-permute-start(f32[6,1,4,128]{3,1,0,2:T(1,128)S(1)} %get-tuple-element.27), channel_id=1, source_target_pairs={{0,2},{2,4},{4,6},{6,0},{1,3},{3,5},{5,7},{7,1},{8,10},{10,12},{12... | collective-permute-start | bytes 36872 | tf_op jit(solution)/shard_map/ppermute | solution.py:296
  74.3 2.6 %collective-permute-start.9 = (f32[6,1,4,128]{3,1,0,2:T(1,128)S(1)}, f32[6,1,4,128]{3,1,0,2:T(1,128)S(1)}, u32[]{:S(2)}, u32[]{:S(2)}) collective-permute-start(f32[6,1,4,128]{3,1,0,2:T(1,128)S(1)} %get-tuple-element.26), channel_id=1, source_target_pairs={{2,0},{4,2},{6,4},{0,6},{3,1},{5,3},{7,5},{1,7},{10,8},{12,10},{14... | collective-permute-start | bytes 36872 | tf_op jit(solution)/shard_map/ppermute | solution.py:297
  77.0 27.1 %collective-permute-start.10 = (f32[1,64,4,128]{3,1,0,2:T(8,128)S(1)}, f32[1,64,4,128]{3,1,0,2:T(8,128)S(1)}, u32[]{:S(2)}, u32[]{:S(2)}) collective-permute-start(f32[1,64,4,128]{3,1,0,2:T(8,128)S(1)} %get-tuple-element.33), channel_id=1, source_target_pairs={{0,8},{8,16},{16,24},{24,32},{32,40},{40,48},{48,56},{56,64},{64,7... | collective-permute-start | bytes 393224 | tf_op jit(solution)/shard_map/ppermute | solution.py:296
  102.6 8.1 %collective-permute-start.11 = (f32[1,64,4,128]{3,1,0,2:T(8,128)S(1)}, f32[1,64,4,128]{3,1,0,2:T(8,128)S(1)}, u32[]{:S(2)}, u32[]{:S(2)}) collective-permute-start(f32[1,64,4,128]{3,1,0,2:T(8,128)S(1)} %get-tuple-element.32), channel_id=1, source_target_pairs={{8,0},{16,8},{24,16},{32,24},{40,32},{48,40},{56,48},{64,56},{72,6... | collective-permute-start | bytes 393224 | tf_op jit(solution)/shard_map/ppermute | solution.py:297
  110.7 0.8 copy-start.2
